TPU v7x, 32 devices: a whole 2x2x4 slice. The times are simulated.
32 devices in a mesh: grp: 2 (over x), gx: 16 (over z, y, core).
Axes of the slice: x: 2, y: 2, z: 4, core: 2. Of those that a mesh axis runs over, the one named last changes fastest.
Arguments:
- grain_ids: int32 [96, 32, 512], P(('grp', 'gx')), parts along dimension 0, may hold values from 0 to 7
- jitter: bfloat16 [8, 96, 32, 512], P(None, ('grp', 'gx')), parts along dimension 1, may hold values from 0 to 0.5
- class_table: int32 [8, 8], replicated, may hold values from 0 to 3
- chosen: int32 [2], replicated, may hold values from 0 to 7
Outputs:
- order_params: float32 [8, 96, 32, 512], P(None, ('grp', 'gx')), parts along dimension 1
- correlation: float32 [2, 96, 32, 512], P(None, ('grp', 'gx')), parts along dimension 1
There are 2 independent parts, one for each index of `grp`. A program takes and returns all parts, laid end to end along the dimension named above; an argument that names none is the same for every part. Nothing has to cross between parts.
All inputs are finite; a program needn't handle non-finite values.
Results may differ from a plain program's by a relative error of at most 0.0003.
Values sent between devices are 32-bit elements; how exact they have to be, the bound alone decides.
No kernel may reach another device: no remote copies, remote signals or barrier semaphores. Data moves between devices by JAX's collectives and lax.ppermute only.
A program may use at most 128 MiB of HBM per device.

v0:
```python
import math

import jax
import jax.numpy as jnp
from jax import lax
from jax.sharding import PartitionSpec as P

STEPS = 3


HIGH = lax.Precision.HIGHEST


def with_halo(value, sides, width):
    for axis, dim in sides:
        peers, length = (lax.axis_size(axis), value.shape[dim])
        up = [(i, (i + 1) % peers) for i in range(peers)]
        down = [(j, i) for i, j in up]
        last = lax.slice_in_dim(value, length - width, length, axis=dim)
        initial = lax.slice_in_dim(value, 0, width, axis=dim)
        before = lax.ppermute(last, axis, up)
        after = lax.ppermute(initial, axis, down)
        value = jnp.concatenate([before, value, after], axis=dim)
    return value


def tables(length):
    index = lax.iota(jnp.int32, length)
    product = index[:, None] * index[None, :] % length
    angle = product.astype(jnp.float32) * (2.0 * math.pi / length)
    return (jnp.cos(angle), jnp.sin(angle))


def onehot_of(grain_ids):
    return (grain_ids[None] == lax.iota(jnp.int32, 8)[:, None, None, None]).astype(jnp.float32)


def levels_map(onehot, class_table):
    levels = 0.4 + 0.2 * class_table.astype(jnp.float32)
    return jnp.einsum("gi,gxzy->ixzy", levels, onehot, precision=HIGH)


def advance(extended, mobility):
    center = extended[:, 1:-1]
    lap = extended[:, 2:] + extended[:, :-2]
    lap = lap + jnp.roll(center, -1, 2) + jnp.roll(center, 1, 2)
    lap = lap + jnp.roll(center, -1, 3) + jnp.roll(center, 1, 3)
    lap = lap - 6.0 * center
    total = jnp.sum(center * center, axis=0)
    drive = -center + center * center * center + 3.0 * center * (total[None] - center * center)
    return center - 0.12 * mobility * (drive - lap)


def forward_planes(fields, cos_y, sin_y, cos_z, sin_z):
    real_y = jnp.dot(fields, cos_y, precision=HIGH)
    imag_y = -jnp.dot(fields, sin_y, precision=HIGH)
    real_z = jnp.einsum("kz,fxzy->fxky", cos_z, real_y, precision=HIGH) + jnp.einsum(
        "kz,fxzy->fxky", sin_z, imag_y, precision=HIGH
    )
    imag_z = jnp.einsum("kz,fxzy->fxky", cos_z, imag_y, precision=HIGH) - jnp.einsum(
        "kz,fxzy->fxky", sin_z, real_y, precision=HIGH
    )
    planes = fields.shape[1]
    return (
        real_z.reshape(fields.shape[0], planes, -1),
        imag_z.reshape(fields.shape[0], planes, -1),
    )


def line_power(real_part, imag_part, cos_x, sin_x, offset):
    real_x = jnp.einsum("kx,fxc->fkc", cos_x, real_part, precision=HIGH) + jnp.einsum(
        "kx,fxc->fkc", sin_x, imag_part, precision=HIGH
    )
    imag_x = jnp.einsum("kx,fxc->fkc", cos_x, imag_part, precision=HIGH) - jnp.einsum(
        "kx,fxc->fkc", sin_x, real_part, precision=HIGH
    )
    power = real_x * real_x + imag_x * imag_x
    freq_x = lax.iota(jnp.int32, power.shape[1])[:, None]
    column = offset + lax.iota(jnp.int32, power.shape[2])[None, :]
    keep = jnp.logical_not(jnp.logical_and(freq_x == 0, column == 0))
    power = power * keep.astype(jnp.float32)[None]
    back_real = jnp.einsum("kx,fkc->fxc", cos_x, power, precision=HIGH)
    back_imag = jnp.einsum("kx,fkc->fxc", sin_x, power, precision=HIGH)
    return (back_real, back_imag)


def inverse_planes(back_real, back_imag, cos_y, sin_y, cos_z, sin_z, depth, width, count):
    fields = back_real.shape[0]
    planes = back_real.shape[1]
    back_real = back_real.reshape(fields, planes, depth, width)
    back_imag = back_imag.reshape(fields, planes, depth, width)
    real_z = jnp.einsum("kz,fxky->fxzy", cos_z, back_real, precision=HIGH) - jnp.einsum(
        "kz,fxky->fxzy", sin_z, back_imag, precision=HIGH
    )
    imag_z = jnp.einsum("kz,fxky->fxzy", cos_z, back_imag, precision=HIGH) + jnp.einsum(
        "kz,fxky->fxzy", sin_z, back_real, precision=HIGH
    )
    result = jnp.dot(real_z, cos_y, precision=HIGH) - jnp.dot(imag_z, sin_y, precision=HIGH)
    return result / (count * count)


def shards(grain_ids, jitter, class_table, chosen):
    planes = grain_ids.shape[0]
    depth = grain_ids.shape[1]
    width = grain_ids.shape[2]
    devices = lax.axis_size("gx")
    onehot = onehot_of(grain_ids)
    eta = 0.6 * onehot + jitter.astype(jnp.float32)
    mobility = levels_map(onehot, class_table)
    for step in range(STEPS):
        extended = with_halo(eta, (("gx", 1),), 1)
        eta = advance(extended, mobility)
    select = (chosen[:, None] == lax.iota(jnp.int32, 8)[None, :]).astype(jnp.float32)
    fields = jnp.einsum("ki,ixzy->kxzy", select, eta, precision=HIGH)
    cos_y, sin_y = tables(width)
    cos_z, sin_z = tables(depth)
    total_x = planes * devices
    cos_x, sin_x = tables(total_x)
    count = float(total_x * depth * width)
    columns = depth * width // devices
    offset = lax.axis_index("gx") * columns
    real_part, imag_part = forward_planes(fields, cos_y, sin_y, cos_z, sin_z)
    stacked = jnp.concatenate([real_part, imag_part], axis=0)
    lines = lax.all_to_all(stacked, "gx", split_axis=2, concat_axis=1, tiled=True)
    back_real, back_imag = line_power(lines[:2], lines[2:], cos_x, sin_x, offset)
    returned = lax.all_to_all(
        jnp.concatenate([back_real, back_imag], axis=0),
        "gx",
        split_axis=1,
        concat_axis=2,
        tiled=True,
    )
    correlation = inverse_planes(
        returned[:2], returned[2:], cos_y, sin_y, cos_z, sin_z, depth, width, count
    )
    return (eta, correlation)


def solution(mesh):
    in_specs = (P(("grp", "gx"), None, None), P(None, ("grp", "gx"), None, None), P(), P())
    out_specs = (P(None, ("grp", "gx"), None, None), P(None, ("grp", "gx"), None, None))
    return jax.shard_map(shards, mesh=mesh, in_specs=in_specs, out_specs=out_specs, check_vma=False)
```

profile of v0, /device:TPU:0, one launch (start us, length us, event | category | flops | bytes accessed | tf_op | source)
XLA Modules:
  0.0 307.1 jit_solution(3220175203014402098)
XLA Ops:
  0.6 1.8 convert_add_fusion
  2.5 5.5 %collective-permute-start = (f32[8,1,32,512]{3,0,2,1:T(8,128)S(1)}, f32[8,1,32,512]{3,0,2,1:T(8,128)S(1)}, u32[]{:S(2)}, u32[]{:S(2)}) collective-permute-start(f32[8,1,32,512]{3,0,2,1:T(8,128)S(1)} %get-tuple-element.36), channel_id=1, source_target_pairs={{1,0},{2,1},{3,2},{4,3},{5,4},{6,5},{7,6},{8,7},{9,8},{10,9},{11,1... | collective-permute-start | bytes 1572872 | tf_op jit(solution)/shard_map/ppermute | solution.py:22
  8.0 0.4 fusion.241
  8.5 0.2 fusion.238
  8.6 0.3 copy-done
  8.9 0.3 copy-done.1
  9.3 14.6 %multiply_subtract_fusion.2 = f32[8,3,32,512]{3,0,2,1:T(8,128)S(1)} fusion(bf16[8,3,32,512]{3,2,1,0:T(8,128)(2,1)S(1)} %copy-done.1, s32[3,32,512]{2,1,0:T(8,128)S(1)} %copy-done), kind=kOutput, calls=%fused_computation.12 | output fusion | flops 4374535 | bytes 2555904 | tf_op jit(solution)/shard_map/sub | solution.py:50
  23.9 0.6 fusion.239
  24.6 2.2 fusion.16
  26.8 0.4 fusion.236
  27.3 0.2 fusion.233
  27.5 4.0 %collective-permute-start.2 = (f32[8,1,32,512]{3,0,2,1:T(8,128)S(1)}, f32[8,1,32,512]{3,0,2,1:T(8,128)S(1)}, u32[]{:S(2)}, u32[]{:S(2)}) collective-permute-start(f32[8,1,32,512]{3,0,2,1:T(8,128)S(1)} %get-tuple-element.26), channel_id=1, source_target_pairs={{1,0},{2,1},{3,2},{4,3},{5,4},{6,5},{7,6},{8,7},{9,8},{10,9},{11,1... | collective-permute-start | bytes 1572872 | tf_op jit(solution)/shard_map/ppermute | solution.py:22
  31.6 0.6 fusion.234
  32.1 6.1 %collective-permute-done.2 = f32[8,1,32,512]{3,0,2,1:T(8,128)S(1)} collective-permute-done((f32[8,1,32,512]{3,0,2,1:T(8,128)S(1)}, f32[8,1,32,512]{3,0,2,1:T(8,128)S(1)}, u32[]{:S(2)}, u32[]{:S(2)}) %collective-permute-start.2) | collective-permute-done | bytes 524320 | tf_op jit(solution)/shard_map/ppermute | solution.py:22
  38.2 4.6 %collective-permute-done.3 = f32[8,1,32,512]{3,0,2,1:T(8,128)S(1)} collective-permute-done((f32[8,1,32,512]{3,0,2,1:T(8,128)S(1)}, f32[8,1,32,512]{3,0,2,1:T(8,128)S(1)}, u32[]{:S(2)}, u32[]{:S(2)}) %collective-permute-start.3) | collective-permute-done | bytes 524320 | tf_op jit(solution)/shard_map/ppermute | solution.py:21
  42.8 34.6 %fusion.21 = f32[8,3,32,512]{3,0,2,1:T(8,128)S(1)} fusion(f32[8,3,32,512]{3,0,2,1:T(8,128)S(1)} %get-tuple-element.42, f32[8,3,32,512]{3,0,2,1:T(8,128)S(1)} %get-tuple-element.43, f32[8,1,32,512]{3,0,2,1:T(8,128)S(1)} %collective-permute-done.3, f32[8,1,32,512]{3,0,2,1:T(8,128)S(1)} %collective-permute-done.2, f32[8,3,1,512]{3,0,2,1:T(8,128)S(1)} %get-tuple-element.23, ...), kind=kOutput, calls=%fused_computation.24 | output fusion | flops 9879559 | bytes 12058624 | tf_op jit(solution)/shard_map/sub | solution.py:50
  77.5 0.4 fusion.231
  78.0 0.2 fusion.228
  78.2 0.2 collective-permute-start.4
  78.3 0.6 collective-permute-start.5
  78.9 0.6 fusion.229
  79.5 5.6 %collective-permute-done.4 = f32[8,1,32,512]{3,0,2,1:T(8,128)S(1)} collective-permute-done((f32[8,1,32,512]{3,0,2,1:T(8,128)S(1)}, f32[8,1,32,512]{3,0,2,1:T(8,128)S(1)}, u32[]{:S(2)}, u32[]{:S(2)}) %collective-permute-start.4) | collective-permute-done | bytes 524320 | tf_op jit(solution)/shard_map/ppermute | solution.py:22
  85.0 4.9 %collective-permute-done.5 = f32[8,1,32,512]{3,0,2,1:T(8,128)S(1)} collective-permute-done((f32[8,1,32,512]{3,0,2,1:T(8,128)S(1)}, f32[8,1,32,512]{3,0,2,1:T(8,128)S(1)}, u32[]{:S(2)}, u32[]{:S(2)}) %collective-permute-start.5) | collective-permute-done | bytes 524320 | tf_op jit(solution)/shard_map/ppermute | solution.py:21
  89.9 34.6 %fusion.26 = f32[8,3,32,512]{3,0,2,1:T(8,128)S(1)} fusion(f32[8,3,32,512]{3,0,2,1:T(8,128)S(1)} %fusion.21, f32[8,3,32,512]{3,0,2,1:T(8,128)S(1)} %get-tuple-element.43, f32[8,1,32,512]{3,0,2,1:T(8,128)S(1)} %collective-permute-done.5, f32[8,1,32,512]{3,0,2,1:T(8,128)S(1)} %collective-permute-done.4, f32[8,3,1,512]{3,0,2,1:T(8,128)S(1)} %get-tuple-element.13, ...), kind=kOutput, calls=%fused_computation.29 | output fusion | flops 9879559 | bytes 12058624 | tf_op jit(solution)/shard_map/sub | solution.py:50
  124.6 0.9 fusion.155
  125.5 5.1 %fusion.62 = f32[2,3,32,512]{3,2,1,0:T(8,128)S(1)} fusion(f32[2,3,32,512]{3,0,2,1:T(2,128)S(1)} %fusion.155), kind=kOutput, calls=%fused_computation.86 | convolution fusion | flops 607649792 | bytes 786432 | tf_op jit(solution)/shard_map/dot_general | solution.py:55
  130.6 5.1 %convolution_negate_fusion = f32[2,3,32,512]{3,2,1,0:T(8,128)S(1)} fusion(f32[2,3,32,512]{3,0,2,1:T(2,128)S(1)} %fusion.155), kind=kOutput, calls=%fused_computation.76 | convolution fusion | flops 607748096 | bytes 786432 | tf_op jit(solution)/shard_map/dot_general | solution.py:56
  135.7 0.6 fusion.116
  136.3 0.6 fusion.114
  136.9 0.6 fusion.52
  137.5 0.3 reshape.68
  137.9 0.6 fusion.51
  138.5 0.3 reshape.69
  138.8 0.4 pad_maximum_fusion.6
  139.2 20.3 %copy.46 = f32[4,3,16384]{0,1,2:T(4,128)} copy(f32[4,3,16384]{2,0,1:T(4,128)S(1)} %pad_maximum_fusion.6) | data formatting | bytes 1572864 | tf_op jit(solution)/shard_map/concatenate | solution.py:123
  159.5 24.8 %reshape.88 = f32[16,1,12288]{2,1,0:T(1,128)} reshape(f32[16384,3,4]{2,1,0:T(4,128)} %bitcast.118) | data formatting | bytes 1572864
  184.3 5.4 %all-to-all-start = ((f32[16,1,12288]{2,1,0:T(1,128)}), f32[16,1,12288]{2,1,0:T(1,128)S(1)}, u32[]{:S(2)}, u32[]{:S(2)}) async-start(f32[16,1,12288]{2,1,0:T(1,128)} %reshape.88), calls=%async_computation | async-start | bytes 1572864 | tf_op jit(solution)/shard_map/all_to_all | solution.py:124
  189.8 0.1 not_convert_fusion
  189.9 18.6 %all-to-all-done = f32[16,1,12288]{2,1,0:T(1,128)S(1)} async-done(((f32[16,1,12288]{2,1,0:T(1,128)}), f32[16,1,12288]{2,1,0:T(1,128)S(1)}, u32[]{:S(2)}, u32[]{:S(2)}) %all-to-all-start) | async-done | bytes 786464 | tf_op jit(solution)/shard_map/all_to_all | solution.py:124
  208.5 0.5 broadcast.133
  209.0 2.5 reduce
  211.5 33.0 %reshape.89 = f32[16384,3,4]{2,1,0:T(4,128)} reshape(f32[16,12288]{1,0:T(8,128)S(1)} %reduce) | data formatting | bytes 1572864
  244.5 18.5 %copy.81 = f32[4,3,16,1024]{3,2,0,1:T(8,128)S(1)} copy(f32[4,3,16,1024]{0,1,3,2:T(4,128)} %bitcast.119) | data formatting | bytes 1572864 | tf_op jit(solution)/shard_map/all_to_all | solution.py:124
  263.1 0.3 copy.51
  263.4 0.7 fusion.76
  264.1 0.3 copy.48
  264.4 0.7 fusion.80
  265.1 0.7 fusion.49
  265.7 0.7 fusion.55
  266.5 0.6 convolution_bitcast_fusion
  267.1 0.6 convolution_bitcast_fusion.1
  267.7 1.4 copy.58
  269.1 5.5 %all-to-all-start.1 = ((f32[4,48,1024]{2,0,1:T(4,128)}), f32[4,48,1024]{2,0,1:T(4,128)S(1)}, u32[]{:S(2)}, u32[]{:S(2)}) async-start(f32[4,48,1024]{2,0,1:T(4,128)} %copy.58), calls=%async_computation.1 | async-start | bytes 1572864 | tf_op jit(solution)/shard_map/all_to_all | solution.py:126
  274.6 2.1 copy.61
  276.7 16.7 %all-to-all-done.1 = f32[4,48,1024]{2,0,1:T(4,128)S(1)} async-done(((f32[4,48,1024]{2,0,1:T(4,128)}), f32[4,48,1024]{2,0,1:T(4,128)S(1)}, u32[]{:S(2)}, u32[]{:S(2)}) %all-to-all-start.1) | async-done | bytes 786464 | tf_op jit(solution)/shard_map/all_to_all | solution.py:126
  293.3 0.3 fusion.243
  293.6 0.1 copy.60
  293.8 0.5 fusion.110
  294.4 0.1 copy.59
  294.6 0.5 fusion.112
  295.1 0.6 fusion.47
  295.7 0.6 fusion.48
  296.3 5.1 %fusion.60 = f32[2,3,32,512]{3,2,1,0:T(8,128)S(1)} fusion(f32[2,3,32,512]{3,2,1,0:T(8,128)S(1)} %fusion.48), kind=kOutput, calls=%fused_computation.84 | convolution fusion | flops 607649792 | bytes 786432 | tf_op jit(solution)/shard_map/dot_general | solution.py:98
  301.3 5.6 %fusion.56 = f32[2,3,32,512]{3,2,1,0:T(8,128)} fusion(f32[2,3,32,512]{3,2,1,0:T(8,128)S(1)} %fusion.60, f32[2,3,32,512]{3,2,1,0:T(8,128)S(1)} %fusion.47), kind=kOutput, calls=%fused_computation.80 | convolution fusion | flops 607846400 | bytes 1179648 | tf_op jit(solution)/shard_map/dot_general | solution.py:98
  (24 shorter events, 0.7 us)
Async XLA Ops:
  2.5 22.0 %collective-permute-start = (f32[8,1,32,512]{3,0,2,1:T(8,128)S(1)}, f32[8,1,32,512]{3,0,2,1:T(8,128)S(1)}, u32[]{:S(2)}, u32[]{:S(2)}) collective-permute-start(f32[8,1,32,512]{3,0,2,1:T(8,128)S(1)} %get-tuple-element.36), channel_id=1, source_target_pairs={{1,0},{2,1},{3,2},{4,3},{5,4},{6,5},{7,6},{8,7},{9,8},{10,9},{11,1... | collective-permute-start | bytes 1572872 | tf_op jit(solution)/shard_map/ppermute | solution.py:22
  8.0 0.9 copy-start
  8.0 1.2 copy-start.1
  8.0 16.5 %collective-permute-start.1 = (f32[8,1,32,512]{3,0,2,1:T(8,128)S(1)}, f32[8,1,32,512]{3,0,2,1:T(8,128)S(1)}, u32[]{:S(2)}, u32[]{:S(2)}) collective-permute-start(f32[8,1,32,512]{3,0,2,1:T(8,128)S(1)} %get-tuple-element.37), channel_id=1, source_target_pairs={{0,1},{1,2},{2,3},{3,4},{4,5},{5,6},{6,7},{7,8},{8,9},{9,10},{10,1... | collective-permute-start | bytes 1572872 | tf_op jit(solution)/shard_map/ppermute | solution.py:21
  23.9 0.7 copy-start.2
  27.5 10.7 %collective-permute-start.2 = (f32[8,1,32,512]{3,0,2,1:T(8,128)S(1)}, f32[8,1,32,512]{3,0,2,1:T(8,128)S(1)}, u32[]{:S(2)}, u32[]{:S(2)}) collective-permute-start(f32[8,1,32,512]{3,0,2,1:T(8,128)S(1)} %get-tuple-element.26), channel_id=1, source_target_pairs={{1,0},{2,1},{3,2},{4,3},{5,4},{6,5},{7,6},{8,7},{9,8},{10,9},{11,1... | collective-permute-start | bytes 1572872 | tf_op jit(solution)/shard_map/ppermute | solution.py:22
  31.5 11.3 %collective-permute-start.3 = (f32[8,1,32,512]{3,0,2,1:T(8,128)S(1)}, f32[8,1,32,512]{3,0,2,1:T(8,128)S(1)}, u32[]{:S(2)}, u32[]{:S(2)}) collective-permute-start(f32[8,1,32,512]{3,0,2,1:T(8,128)S(1)} %get-tuple-element.27), channel_id=1, source_target_pairs={{0,1},{1,2},{2,3},{3,4},{4,5},{5,6},{6,7},{7,8},{8,9},{9,10},{10,1... | collective-permute-start | bytes 1572872 | tf_op jit(solution)/shard_map/ppermute | solution.py:21
  78.2 6.9 %collective-permute-start.4 = (f32[8,1,32,512]{3,0,2,1:T(8,128)S(1)}, f32[8,1,32,512]{3,0,2,1:T(8,128)S(1)}, u32[]{:S(2)}, u32[]{:S(2)}) collective-permute-start(f32[8,1,32,512]{3,0,2,1:T(8,128)S(1)} %get-tuple-element.16), channel_id=1, source_target_pairs={{1,0},{2,1},{3,2},{4,3},{5,4},{6,5},{7,6},{8,7},{9,8},{10,9},{11,1... | collective-permute-start | bytes 1572872 | tf_op jit(solution)/shard_map/ppermute | solution.py:22
  78.3 11.6 %collective-permute-start.5 = (f32[8,1,32,512]{3,0,2,1:T(8,128)S(1)}, f32[8,1,32,512]{3,0,2,1:T(8,128)S(1)}, u32[]{:S(2)}, u32[]{:S(2)}) collective-permute-start(f32[8,1,32,512]{3,0,2,1:T(8,128)S(1)} %get-tuple-element.17), channel_id=1, source_target_pairs={{0,1},{1,2},{2,3},{3,4},{4,5},{5,6},{6,7},{7,8},{8,9},{9,10},{10,1... | collective-permute-start | bytes 1572872 | tf_op jit(solution)/shard_map/ppermute | solution.py:21
  89.9 34.7 %copy-start.3 = (s32[2]{0:T(128)S(1)}, s32[2]{0:T(128)}, u32[]{:S(2)}) copy-start(s32[2]{0:T(128)} %param.7) | copy-start | bytes 28
  184.3 24.1 %all-to-all-start = ((f32[16,1,12288]{2,1,0:T(1,128)}), f32[16,1,12288]{2,1,0:T(1,128)S(1)}, u32[]{:S(2)}, u32[]{:S(2)}) async-start(f32[16,1,12288]{2,1,0:T(1,128)} %reshape.88), calls=%async_computation | async-start | bytes 1572864 | tf_op jit(solution)/shard_map/all_to_all | solution.py:124
  269.1 24.2 %all-to-all-start.1 = ((f32[4,48,1024]{2,0,1:T(4,128)}), f32[4,48,1024]{2,0,1:T(4,128)S(1)}, u32[]{:S(2)}, u32[]{:S(2)}) async-start(f32[4,48,1024]{2,0,1:T(4,128)} %copy.58), calls=%async_computation.1 | async-start | bytes 1572864 | tf_op jit(solution)/shard_map/all_to_all | solution.py:126
where the time goes:
time: 313 us; the launch traced here: 307 us
  local copies, waits for them, and re-layouts  107 us (34%)
  other arithmetic  88.8 us (28%)
  waiting for transfers between devices  56.3 us (18%)
  matrix products  32.5 us (10%)
  starting transfers between devices  21.2 us (7%)
    sub x3, other arithmetic, advance(): total[None] - center * center  83.9 us
    unnamed x11, local copies, waits for them, and re-layouts  60.6 us
    concatenate x1, local copies, waits for them, and re-layouts, shards(): stacked = jnp.concatenate([real_part, imag_part], axis=0)  20.3 us
    all_to_all x2, local copies, waits for them, and re-layouts, shards(): lax.all_to_all(stacked, 'gx', split_axis=2, concat_axis=1, tiled=True)  19 us
    all_to_all x1, waiting for transfers between devices, shards(): lax.all_to_all(stacked, 'gx', split_axis=2, concat_axis=1, tiled=True)  18.6 us
    all_to_all x1, waiting for transfers between devices, shards(): lax.all_to_all(jnp.concatenate([back_real, back_imag], axis=0), 'gx', spl...  16.7 us
    ppermute x3, waiting for transfers between devices, with_halo(): after = lax.ppermute(initial, axis, down)  11.7 us
    ppermute x3, starting transfers between devices, with_halo(): after = lax.ppermute(initial, axis, down)  9.67 us
  transfers between devices with their start and end apart: 8, of which 6 were waited for; matrix products, arithmetic and copies ran while one was open for 6% of the time, Pallas kernels for 0%

commit v1 on v0

v1 whole, which is shorter than its diff:
```python
import math

import jax
import jax.numpy as jnp
import ml_dtypes
import numpy as np
from jax import lax
from jax.experimental import pallas as pl
from jax.experimental.pallas import tpu as pltpu
from jax.sharding import PartitionSpec as P

STEPS = 3
GRAINS = 8
F32 = jnp.float32
BF16 = jnp.bfloat16
VMEM = pl.BlockSpec(memory_space=pltpu.VMEM)
SMEM = pl.BlockSpec(memory_space=pltpu.SMEM)
PARAMS = pltpu.CompilerParams(vmem_limit_bytes=48 * 2**20)


def halves(table):
    table = np.asarray(table, np.float32)
    high = table.astype(ml_dtypes.bfloat16)
    low = (table - high.astype(np.float32)).astype(ml_dtypes.bfloat16)
    return high, low


def phases(length, rows=None):
    index = np.arange(length)
    product = np.arange(length if rows is None else rows)[:, None] * index[None, :] % length
    angle = product * (2.0 * math.pi / length)
    return np.cos(angle), np.sin(angle)


def y_table(width):
    cos_y, sin_y = phases(width, width // 2)
    sin_y = -sin_y
    sin_y[0] = 1.0 - 2.0 * (np.arange(width) % 2)
    return np.concatenate([cos_y, sin_y], axis=0)


def z_tables(depth):
    cos_z, sin_z = phases(depth)
    two = np.eye(2)
    cos_z, sin_z = np.kron(two, cos_z), np.kron(two, sin_z)
    forward = np.block([[cos_z, -sin_z], [sin_z, cos_z]])
    half = 2 * depth
    forward_turned = np.concatenate([forward[:, half:], -forward[:, :half]], axis=1)
    inverse = np.block([[cos_z, sin_z], [-sin_z, cos_z]])
    inverse_turned = np.concatenate([-inverse[:, half:], inverse[:, :half]], axis=1)
    return (
        np.concatenate([forward, forward_turned], axis=1),
        np.concatenate([inverse, inverse_turned], axis=0),
    )


def split(value):
    high = value.astype(BF16)
    low = (value - high.astype(F32)).astype(BF16)
    return high, low


def dot3(left, right, contract=((1,), (0,))):
    def one(a, b):
        return lax.dot_general(a, b, (contract, ((), ())), preferred_element_type=F32)

    return one(left[0], right[0]) + (one(left[0], right[1]) + one(left[1], right[0]))


def start_kernel(chosen, jitter, grain_ids, p0, p1, p2, c0, c2):
    for plane, out in enumerate((p0, p1, p2)):
        ids = grain_ids[plane]

        def body(i, carry):
            base = jnp.where(ids == i, jnp.float32(0.6), jnp.float32(0.0))
            out[i] = base + jitter[i, plane].astype(F32)
            return carry

        lax.fori_loop(0, GRAINS, body, 0)
    for k in range(2):
        c0[k] = p0[chosen[k]]
        c2[k] = p2[chosen[k]]


def grain_of(start):
    ids = jnp.where(start[1] > 0.55, 1, 0)
    for g in range(2, GRAINS):
        ids = jnp.where(start[g] > 0.55, g, ids)
    return ids


def rate(classes, ids, i):
    def level(g):
        return 0.12 * (0.4 + 0.2 * classes[g, i].astype(F32))

    value = jnp.full(ids.shape, level(0), F32)
    for g in range(1, GRAINS):
        value = jnp.where(ids == g, level(g), value)
    return value


def squares(state):
    total = state[0] * state[0]
    for i in range(1, GRAINS):
        total = total + state[i] * state[i]
    return 5.0 + 3.0 * total


def update(e, before, after, total, mobility):
    depth, width = e.shape
    near = before + after
    near = near + (pltpu.roll(e, 1, 0) + pltpu.roll(e, depth - 1, 0))
    near = near + (pltpu.roll(e, 1, 1) + pltpu.roll(e, width - 1, 1))
    return e + mobility * (near - e * (total - 2.0 * (e * e)))


def step_plane(center, before, after, mobility, out):
    total = squares(center)

    def body(i, carry):
        out[i] = update(center[i], before[i], after[i], total, mobility[i])
        return carry

    lax.fori_loop(0, GRAINS, body, 0)


def rates_plane(classes, start, out):
    ids = grain_of(start)

    def body(i, carry):
        out[i] = rate(classes, ids, i)
        return carry

    lax.fori_loop(0, GRAINS, body, 0)


def main_kernel(
    chosen, classes, p0, p1, p2, prev1, next1, prev2, next2, prev3, next3, table_high, table_low,
    packed, eta1, eta2, rates, edge, fields,
):
    depth, width = p0.shape[1:]
    starts = (prev1, p0, p1, p2, next1)
    for k, start in enumerate(starts):
        rates_plane(classes, start, rates.at[k])
    row = (prev2,) + starts + (next2,)
    for k in range(5):
        step_plane(row[k + 1], row[k], row[k + 2], rates.at[k], eta1.at[k])
    for k in range(3):
        step_plane(eta1.at[k + 1], eta1.at[k], eta1.at[k + 2], rates.at[k + 1], eta2.at[k])
    for side, (far, mid, near, inner) in enumerate(((prev3, prev2, prev1, 0), (next3, next2, next1, 4))):
        ids = grain_of(mid)
        total0 = squares(mid)
        total1 = squares(eta1.at[inner])
        neighbour = 1 if side == 0 else 3
        for k in range(2):
            i = chosen[k]
            first = update(mid[i], far[k], near[i], total0, rate(classes, ids, i))
            edge[side, k] = update(eta1[inner, i], first, eta1[neighbour, i], total1, rates[inner, i])
    for k in range(3):
        total = squares(eta2.at[k])
        for f in range(2):
            i = chosen[f]
            before = edge[0, f] if k == 0 else eta2[k - 1, i]
            after = edge[1, f] if k == 2 else eta2[k + 1, i]
            value = update(eta2[k, i], before, after, total, rates[k + 1, i])
            base = k * 4 * depth + f * depth
            fields[base : base + depth] = value
            fields[base + 2 * depth : base + 3 * depth] = value
    full = dot3((table_high[...], table_low[...]), split(fields[...]), ((1,), (1,)))
    slots = width // 2
    lanes = 4 * depth
    real_lane = lax.broadcasted_iota(jnp.int32, (slots, lanes), 1) < 2 * depth
    for k in range(3):
        part = full[:, k * lanes : (k + 1) * lanes]
        part = jnp.where(real_lane, part[:slots], part[slots:])
        if len(packed.shape) == 3 and packed.shape[0] == 3:
            packed[k] = part
        else:
            devices, rows, _ = packed.shape
            rows = rows // 3
            packed[:, k * rows : (k + 1) * rows, :] = part.reshape(devices, rows, lanes)


def rest_kernel(
    classes, p0, p1, p2, prev1, next1, prev2, next2, prev3, next3, eta1, eta2, out, rates, edge, other
):
    for far, mid, near, inner, neighbour, side in (
        (prev3, prev2, prev1, 0, 1, 0),
        (next3, next2, next1, 4, 3, 1),
    ):
        rates_plane(classes, mid, rates)
        step_plane(mid, far, near, rates, other)
        rates_plane(classes, near, rates)
        step_plane(eta1.at[inner], other, eta1.at[neighbour], rates, edge.at[side])
    row = (edge.at[0], eta2.at[0], eta2.at[1], eta2.at[2], edge.at[1])
    for k, start in enumerate((p0, p1, p2)):
        rates_plane(classes, start, rates)
        step_plane(row[k + 1], row[k], row[k + 2], rates, out.at[:, k])


def line_kernel(
    lines, zf_high, zf_low, zi_high, zi_low, xf_high, xf_low, out, r1, r2, gathered, scale
):
    rows, lanes = lines.shape
    total_x = xf_high.shape[0]
    slots = rows // total_x
    half = lanes // 2
    zf = (zf_high[...], zf_low[...])
    xf = (xf_high[...], xf_low[...])
    turned = dot3(split(lines[...]), zf)
    r1[...] = turned[:, :lanes]
    r2[...] = turned[:, lanes:]
    real_lane = lax.broadcasted_iota(jnp.int32, (total_x, lanes), 1) < half
    mixed = lines[pl.ds(0, total_x, stride=slots), :]
    pair = jnp.concatenate(
        [jnp.where(real_lane, mixed, 0.0), jnp.where(real_lane, pltpu.roll(mixed, half, 1), 0.0)], axis=0
    )
    pair = dot3(split(pair), zf)
    for j in range(slots):
        at = slice(j * lanes, (j + 1) * lanes)
        gathered[:total_x, at] = r1[pl.ds(j, total_x, stride=slots), :]
        gathered[total_x:, at] = r2[pl.ds(j, total_x, stride=slots), :]
    for j in range(2):
        at = slice((slots + j) * lanes, (slots + j + 1) * lanes)
        gathered[:total_x, at] = pair[j * total_x : (j + 1) * total_x, :lanes]
        gathered[total_x:, at] = pair[j * total_x : (j + 1) * total_x, lanes:]
    spectrum = dot3(xf, split(gathered[...]))

    def power(j):
        part = spectrum[:, j * lanes : (j + 1) * lanes]
        part = part * part
        return part + pltpu.roll(part, half, 1)

    first = lax.axis_index("gx") == 0
    lane = lax.broadcasted_iota(jnp.int32, (total_x, lanes), 1)
    line = lax.broadcasted_iota(jnp.int32, (total_x, lanes), 0)
    constant = jnp.logical_and(line == 0, jnp.logical_or(lane == 0, lane == half // 2))
    powers = []
    for j in range(slots):
        value = jnp.where(real_lane, power(j), 0.0) * (2.0 * scale)
        if j == 0:
            special = jnp.where(real_lane, power(slots), power(slots + 1)) * scale
            special = jnp.where(constant, 0.0, special)
            value = jnp.where(first, special, value)
        powers.append(value)
    powers = split(jnp.concatenate(powers, axis=1))
    cos_x = (xf[0][:, :total_x], xf[1][:, :total_x])
    sin_x = (xf[0][:, total_x:], xf[1][:, total_x:])
    for target, matrix in ((r1, cos_x), (r2, sin_x)):
        back = dot3(matrix, powers)
        for j in range(slots):
            target[pl.ds(j, total_x, stride=slots), :] = back[:, j * lanes : (j + 1) * lanes]
    zi = (zi_high[...], zi_low[...])
    out[...] = dot3(split(r1[...]), (zi[0][:lanes], zi[1][:lanes])) + dot3(
        split(r2[...]), (zi[0][lanes:], zi[1][lanes:])
    )


def finish_kernel(returned, table_high, table_low, out):
    fields, planes, depth, width = out.shape
    lanes = 2 * fields * depth
    half = lanes // 2
    slots = width // 2
    stacked = []
    for k in range(planes):
        if returned.shape[0] == planes:
            part = returned[k]
        else:
            devices, rows, _ = returned.shape
            rows = rows // planes
            part = returned[:, k * rows : (k + 1) * rows, :].reshape(slots, lanes)
        part = part.T
        stacked.append(jnp.concatenate([part[:half], part[half:]], axis=1))
    stacked = split(jnp.concatenate(stacked, axis=0))
    result = dot3(stacked, (table_high[...], table_low[...]))
    for k in range(planes):
        for f in range(fields):
            base = k * half + f * depth
            out[f, k] = result[base : base + depth]


def call(kernel, outs, in_specs, *args, scratch=(), flops=0, moved=0):
    return pl.pallas_call(
        kernel,
        out_shape=outs,
        in_specs=in_specs,
        out_specs=jax.tree.map(lambda _: VMEM, outs),
        scratch_shapes=scratch,
        compiler_params=PARAMS,
        cost_estimate=pl.CostEstimate(flops=flops, bytes_accessed=moved, transcendentals=0),
    )(*args)


def shards(grain_ids, jitter, class_table, chosen):
    planes, depth, width = grain_ids.shape
    devices = lax.axis_size("gx")
    total_x = planes * devices
    count = float(total_x * depth * width)
    slots = width // 2
    share = slots // devices
    lanes = 4 * depth
    up = [(i, (i + 1) % devices) for i in range(devices)]
    down = [(j, i) for i, j in up]
    aligned = share % 8 == 0

    def shape(*dims):
        return jax.ShapeDtypeStruct(dims, F32)

    plane = (GRAINS, depth, width)
    table = [jnp.asarray(part) for part in halves(y_table(width))]
    z_forward, z_inverse = z_tables(depth)
    z_parts = [jnp.asarray(part) for matrix in (z_forward, z_inverse) for part in halves(matrix)]
    x_parts = [jnp.asarray(part) for part in halves(np.concatenate(phases(total_x), axis=1))]

    two = (2, depth, width)
    p0, p1, p2, c0, c2 = call(
        start_kernel,
        (shape(*plane), shape(*plane), shape(*plane), shape(*two), shape(*two)),
        [SMEM, VMEM, VMEM],
        chosen, jitter, grain_ids,
        flops=2**21, moved=2**22,
    )
    prev1 = lax.ppermute(p2, "gx", up)
    next1 = lax.ppermute(p0, "gx", down)
    prev2 = lax.ppermute(p1, "gx", up)
    next2 = lax.ppermute(p1, "gx", down)
    prev3 = lax.ppermute(c0, "gx", up)
    next3 = lax.ppermute(c2, "gx", down)
    late0, late2, prev3, next3 = lax.optimization_barrier((p0, p2, prev3, next3))
    prev3_all = lax.ppermute(late0, "gx", up)
    next3_all = lax.ppermute(late2, "gx", down)
    packed_shape = (devices, planes * share, lanes) if aligned else (planes, slots, lanes)
    packed, eta1, eta2 = call(
        main_kernel,
        (shape(*packed_shape), shape(5, *plane), shape(3, *plane)),
        [SMEM, SMEM] + [VMEM] * 11,
        chosen, class_table, p0, p1, p2, prev1, next1, prev2, next2, prev3, next3, *table,
        scratch=[
            pltpu.VMEM((5, *plane), F32),
            pltpu.VMEM((2, *two), F32),
            pltpu.VMEM((planes * lanes, width), F32),
        ],
        flops=2**28, moved=2**24,
    )
    if aligned:
        lines = lax.all_to_all(packed, "gx", split_axis=0, concat_axis=0, tiled=True)
    else:
        lines = lax.all_to_all(packed, "gx", split_axis=1, concat_axis=0, tiled=True)
    lines = lines.reshape(total_x * share, lanes)
    order_params = call(
        rest_kernel,
        shape(GRAINS, planes, depth, width),
        [SMEM] + [VMEM] * 11,
        class_table, p0, p1, p2, prev1, next1, prev2, next2, prev3_all, next3_all, eta1, eta2,
        scratch=[pltpu.VMEM(plane, F32), pltpu.VMEM((2, *plane), F32), pltpu.VMEM(plane, F32)],
        flops=2**26, moved=2**24,
    )

    def lines_body(*refs):
        line_kernel(*refs, scale=1.0 / (count * count))

    back = call(
        lines_body,
        shape(total_x * share, lanes),
        [VMEM] * 7,
        lines, *z_parts, *x_parts,
        scratch=[
            pltpu.VMEM((total_x * share, lanes), F32),
            pltpu.VMEM((total_x * share, lanes), F32),
            pltpu.VMEM((2 * total_x, (share + 2) * lanes), F32),
        ],
        flops=2**28, moved=2**22,
    )
    back = back.reshape(devices, planes * share, lanes)
    returned = lax.all_to_all(back, "gx", split_axis=0, concat_axis=0, tiled=True)
    if not aligned:
        returned = returned.reshape(devices, planes, share, lanes).transpose(1, 0, 2, 3)
        returned = returned.reshape(planes, slots, lanes)
    correlation = call(
        finish_kernel,
        shape(2, planes, depth, width),
        [VMEM] * 3,
        returned, *table,
        flops=2**28, moved=2**22,
    )
    return (order_params, correlation)


def solution(mesh):
    in_specs = (P(("grp", "gx"), None, None), P(None, ("grp", "gx"), None, None), P(), P())
    out_specs = (P(None, ("grp", "gx"), None, None), P(None, ("grp", "gx"), None, None))
    return jax.shard_map(shards, mesh=mesh, in_specs=in_specs, out_specs=out_specs, check_vma=False)
```

time: 313 us -> 114 us (0.36); the launches traced: 307 us -> 113 us
  local copies, waits for them, and re-layouts: 107 us -> 9.01 us
  other arithmetic: 88.8 us -> 0 us
  matrix products: 32.5 us -> 0 us
  Pallas kernels: 0 us -> 30.6 us
  blocking collectives: 0 us -> 20.6 us
  waiting for transfers between devices: 56.3 us -> 37.8 us
  starting transfers between devices: 21.2 us -> 14.2 us
    sub x3 -> x0, other arithmetic: 83.9 us -> none  [advance(): total[None] - center * center]
    unnamed x11 -> x42, local copies, waits for them, and re-layouts: 60.6 us -> 9.01 us
    all_to_all x2 -> x1, waiting for transfers between devices: 35.2 us -> 0.01 us  [shards(): lax.all_to_all(back, 'gx', split_axis=0, concat_axis=0, tiled=True)]
    dot_general x20 -> x0, matrix products: 32.5 us -> none  [the longest x1 5.6 us: inverse_planes(): jnp.dot(imag_z, sin_y, precision=HIGH)]
    pallas_call x0 -> x5, Pallas kernels: none -> 30.6 us  [call(): pl.pallas_call(kernel, out_shape=outs, in_specs=in_specs, out_specs=jax.t...]
    concatenate x2 -> x0, local copies, waits for them, and re-layouts: 21.7 us -> none  [the longest x1 20.3 us: shards(): stacked = jnp.concatenate([real_part, imag_part], axis=0)]
    all_to_all x0 -> x1, blocking collectives: none -> 20.6 us  [shards(): lax.all_to_all(packed, 'gx', split_axis=0, concat_axis=0, tiled=True)]
    all_to_all x2 -> x0, local copies, waits for them, and re-layouts: 19 us -> none  [shards(): lax.all_to_all(stacked, 'gx', split_axis=2, concat_axis=1, tiled=True)]
  transfers between devices with their start and end apart: 8 -> 9, of which waited for: 6 -> 3; matrix products, arithmetic and copies ran while one was open for 6% -> 0% of each run, Pallas kernels for 0% -> 11%
where the time goes in v1:
time: 114 us; the launch traced here: 113 us
  waiting for transfers between devices  37.8 us (33%)
  Pallas kernels  30.6 us (27%)
  blocking collectives  20.6 us (18%)
  starting transfers between devices  14.2 us (12%)
  local copies, waits for them, and re-layouts  9.01 us (8%)
    pallas_call x5, Pallas kernels, call(): pl.pallas_call(kernel, out_shape=outs, in_specs=in_specs, out_specs=jax.t...  30.6 us
    all_to_all x1, blocking collectives, shards(): lax.all_to_all(packed, 'gx', split_axis=0, concat_axis=0, tiled=True)  20.6 us
    ppermute x1, waiting for transfers between devices, shards(): prev3 = lax.ppermute(c0, 'gx', up)  18.4 us
    ppermute x1, waiting for transfers between devices, shards(): prev3_all = lax.ppermute(late0, 'gx', up)  13.3 us
    unnamed x42, local copies, waits for them, and re-layouts  9.01 us
    ppermute x1, waiting for transfers between devices, shards(): next3 = lax.ppermute(c2, 'gx', down)  6.07 us
    ppermute x1, starting transfers between devices, shards(): next1 = lax.ppermute(p0, 'gx', down)  5.5 us
    ppermute x1, starting transfers between devices, shards(): next3_all = lax.ppermute(late2, 'gx', down)  4.12 us
  transfers between devices with their start and end apart: 9, of which 3 were waited for; matrix products, arithmetic and copies ran while one was open for 0% of the time, Pallas kernels for 11%

profile of v1, /device:TPU:0, one launch (start us, length us, event | category | flops | bytes accessed | tf_op | source)
XLA Modules:
  0.0 113.1 jit_solution(2864507235098024086)
XLA Ops:
  0.6 0.0 copy-start.10
  0.6 1.1 copy-done.10
  1.8 0.0 copy-start.11
  1.8 0.9 copy-done.11
  2.7 0.0 copy-start.20
  2.7 0.7 copy-done.20
  3.3 0.8 shard_map.131
  4.2 5.5 %collective-permute-start.1 = (f32[8,32,512]{2,1,0:T(8,128)S(1)}, f32[8,32,512]{2,1,0:T(8,128)S(1)}, u32[]{:S(2)}, u32[]{:S(2)}) collective-permute-start(f32[8,32,512]{2,1,0:T(8,128)S(1)} %get-tuple-element.19.p0), channel_id=1, source_target_pairs={{1,0},{2,1},{3,2},{4,3},{5,4},{6,5},{7,6},{8,7},{9,8},{10,9},{11,1... | collective-permute-start | bytes 1572872 | tf_op jit(solution)/shard_map/ppermute | solution.py:324
  9.7 0.7 collective-permute-start.3
  10.4 0.0 collective-permute-start.2
  10.4 0.0 collective-permute-start
  10.4 0.0 collective-permute-start.4
  10.4 18.4 %collective-permute-done.4.prev3 = f32[2,32,512]{2,1,0:T(8,128)S(1)} collective-permute-done((f32[2,32,512]{2,1,0:T(8,128)S(1)}, f32[2,32,512]{2,1,0:T(8,128)S(1)}, u32[]{:S(2)}, u32[]{:S(2)}) %collective-permute-start.4) | collective-permute-done | bytes 131104 | tf_op jit(solution)/shard_map/ppermute | solution.py:327
  28.8 0.0 collective-permute-start.5
  28.8 6.1 %collective-permute-done.5.next3 = f32[2,32,512]{2,1,0:T(8,128)S(1)} collective-permute-done((f32[2,32,512]{2,1,0:T(8,128)S(1)}, f32[2,32,512]{2,1,0:T(8,128)S(1)}, u32[]{:S(2)}, u32[]{:S(2)}) %collective-permute-start.5) | collective-permute-done | bytes 131104 | tf_op jit(solution)/shard_map/ppermute | solution.py:328
  34.9 0.0 collective-permute-done.1.next1
  34.9 0.0 collective-permute-done.3.next2
  34.9 0.0 copy-start.4
  34.9 0.0 collective-permute-done.2.prev2
  34.9 0.0 copy-start.6
  34.9 0.0 collective-permute-done.prev1
  34.9 0.0 copy-start
  34.9 1.4 %copy-done = bf16[512,512]{1,0:T(8,128)(2,1)S(1)} copy-done((bf16[512,512]{1,0:T(8,128)(2,1)S(1)}, bf16[512,512]{1,0:T(8,128)(2,1)}, u32[]{:S(2)}) %copy-start) | copy-done | bytes 524312
  36.3 0.0 copy-start.2
  36.3 1.0 copy-done.2
  37.3 0.0 copy-start.16
  37.4 0.7 copy-done.16
  38.0 0.0 copy-start.8
  38.0 0.0 copy-start.12
  38.0 0.0 copy-start.13
  38.0 0.0 copy-start.14
  38.0 0.0 copy-start.15
  38.1 0.0 copy-start.18
  38.1 0.0 copy-start.19
  38.1 12.8 %shard_map.132 = (f32[16,48,128]{2,1,0:T(8,128)S(1)}, f32[5,8,32,512]{3,2,1,0:T(8,128)}, f32[3,8,32,512]{3,2,1,0:T(8,128)}) custom-call(s32[2]{0:T(128)S(1)} %copy-done.20, s32[8,8]{1,0:T(8,128)S(1)} %copy-done.16, f32[8,32,512]{2,1,0:T(8,128)S(1)} %get-tuple-element.19.p0, f32[8,32,512]{2,1,0:T(8,128)S(1)} %get-tuple-element.15.p1, ...), custom_call_target="tpu_custom_call" | custom-call | flops 268435456 | bytes 16777216 | tf_op jit(solution)/shard_map/pallas_call | solution.py:283
  50.9 0.0 copy-done.4
  50.9 0.0 copy-done.6
  50.9 0.0 copy-done.8
  50.9 0.0 copy-start.17
  50.9 20.6 %all_to_all.10 = f32[16,48,128]{2,1,0:T(8,128)S(1)} all-to-all(f32[16,48,128]{2,1,0:T(8,128)S(1)} %get-tuple-element.25), channel_id=1, replica_groups=mesh['grp'=2,'gx'=16] {'gx'}, dimensions={0} | all-to-all | bytes 786432 | tf_op jit(solution)/shard_map/all_to_all | solution.py:346
  71.5 0.0 copy-done.12
  71.5 0.0 copy-done.13
  71.5 0.0 copy-done.14
  71.5 0.0 copy-done.15
  71.5 0.0 copy-done.18
  71.6 0.0 copy-done.19
  71.6 3.2 %shard_map.134 = f32[768,128]{1,0:T(8,128)} custom-call(f32[768,128]{1,0:T(8,128)S(1)} %bitcast.2, bf16[128,256]{1,0:T(8,128)(2,1)S(1)} %copy-done.15, bf16[128,256]{1,0:T(8,128)(2,1)S(1)} %copy-done.14, bf16[256,128]{1,0:T(8,128)(2,1)S(1)} %copy-done.13, bf16[256,128]{1,0:T(8,128)(2,1)S(1)} %copy-done.12, bf16[48,96]{1,0:T(8,128)(2,1)S(1)} %copy-done.19, ...), custom_call_target="tpu_custom_call" | custom-call | flops 268435456 | bytes 4194304 | tf_op jit(solution)/shard_map/pallas_call | solution.py:283
  74.8 3.6 %all-to-all-start.1 = ((f32[16,48,128]{2,1,0:T(8,128)}), f32[16,48,128]{2,1,0:T(8,128)S(1)}, u32[]{:S(2)}, u32[]{:S(2)}) async-start(f32[16,48,128]{2,1,0:T(8,128)} %bitcast.1), calls=%async_computation.1 | async-start | bytes 786432 | tf_op jit(solution)/shard_map/all_to_all | solution.py:375
  78.3 0.4 collective-permute-start.6
  78.7 4.1 %collective-permute-start.7 = (f32[8,32,512]{2,1,0:T(8,128)S(1)}, f32[8,32,512]{2,1,0:T(8,128)S(1)}, u32[]{:S(2)}, u32[]{:S(2)}) collective-permute-start(f32[8,32,512]{2,1,0:T(8,128)S(1)} %get-tuple-element.20.p2), channel_id=1, source_target_pairs={{1,0},{2,1},{3,2},{4,3},{5,4},{6,5},{7,6},{8,7},{9,8},{10,9},{11,1... | collective-permute-start | bytes 1572872 | tf_op jit(solution)/shard_map/ppermute | solution.py:331
  82.8 13.3 %collective-permute-done.6.prev3 = f32[8,32,512]{2,1,0:T(8,128)S(1)} collective-permute-done((f32[8,32,512]{2,1,0:T(8,128)S(1)}, f32[8,32,512]{2,1,0:T(8,128)S(1)}, u32[]{:S(2)}, u32[]{:S(2)}) %collective-permute-start.6) | collective-permute-done | bytes 524320 | tf_op jit(solution)/shard_map/ppermute | solution.py:330
  96.2 0.0 collective-permute-done.7.next3
  96.2 0.0 copy-done.17
  96.2 0.0 copy-start.5
  96.2 1.0 copy-done.5
  97.2 0.0 copy-start.7
  97.2 1.0 copy-done.7
  98.3 0.0 copy-start.9
  98.3 1.0 copy-done.9
  99.3 12.4 %shard_map.133 = f32[8,3,32,512]{3,2,1,0:T(8,128)} custom-call(s32[8,8]{1,0:T(8,128)S(1)} %copy-done.17, f32[8,32,512]{2,1,0:T(8,128)S(1)} %get-tuple-element.19.p0, f32[8,32,512]{2,1,0:T(8,128)S(1)} %get-tuple-element.15.p1, f32[8,32,512]{2,1,0:T(8,128)S(1)} %get-tuple-element.20.p2, f32[8,32,512]{2,1,0:T(8,128)S(1)} %copy-done.9, ...), custom_call_target="tpu_custom_call" | custom-call | flops 67108864 | bytes 16777216 | tf_op jit(solution)/shard_map/pallas_call | solution.py:283
  111.7 0.0 all-to-all-done.1.returned
  111.7 0.0 copy-done.1
  111.7 0.0 copy-done.3
  111.7 1.3 %shard_map.135 = f32[2,3,32,512]{3,2,1,0:T(8,128)} custom-call(f32[16,48,128]{2,1,0:T(8,128)S(1)} %all-to-all-done.1.returned, bf16[512,512]{1,0:T(8,128)(2,1)S(1)} %copy-done.3, bf16[512,512]{1,0:T(8,128)(2,1)S(1)} %copy-done.1), custom_call_target="tpu_custom_call" | custom-call | flops 268435456 | bytes 4194304 | tf_op jit(solution)/shard_map/pallas_call | solution.py:283
  (2 shorter events, 0.0 us)
Async XLA Ops:
  0.6 1.1 %copy-start.10 = (bf16[8,3,32,512]{3,2,1,0:T(8,128)(2,1)S(1)}, bf16[8,3,32,512]{3,2,1,0:T(8,128)(2,1)}, u32[]{:S(2)}) copy-start(bf16[8,3,32,512]{3,2,1,0:T(8,128)(2,1)} %jitter.1) | copy-start | bytes 2359300
  1.8 0.9 copy-start.11
  2.7 0.7 copy-start.20
  4.2 30.7 %collective-permute-start.1 = (f32[8,32,512]{2,1,0:T(8,128)S(1)}, f32[8,32,512]{2,1,0:T(8,128)S(1)}, u32[]{:S(2)}, u32[]{:S(2)}) collective-permute-start(f32[8,32,512]{2,1,0:T(8,128)S(1)} %get-tuple-element.19.p0), channel_id=1, source_target_pairs={{1,0},{2,1},{3,2},{4,3},{5,4},{6,5},{7,6},{8,7},{9,8},{10,9},{11,1... | collective-permute-start | bytes 1572872 | tf_op jit(solution)/shard_map/ppermute | solution.py:324
  9.7 25.2 %collective-permute-start.3 = (f32[8,32,512]{2,1,0:T(8,128)S(1)}, f32[8,32,512]{2,1,0:T(8,128)S(1)}, u32[]{:S(2)}, u32[]{:S(2)}) collective-permute-start(f32[8,32,512]{2,1,0:T(8,128)S(1)} %get-tuple-element.15.p1), channel_id=1, source_target_pairs={{1,0},{2,1},{3,2},{4,3},{5,4},{6,5},{7,6},{8,7},{9,8},{10,9},{11,1... | collective-permute-start | bytes 1572872 | tf_op jit(solution)/shard_map/ppermute | solution.py:326
  10.4 24.5 %collective-permute-start.2 = (f32[8,32,512]{2,1,0:T(8,128)S(1)}, f32[8,32,512]{2,1,0:T(8,128)S(1)}, u32[]{:S(2)}, u32[]{:S(2)}) collective-permute-start(f32[8,32,512]{2,1,0:T(8,128)S(1)} %get-tuple-element.15.p1), channel_id=1, source_target_pairs={{0,1},{1,2},{2,3},{3,4},{4,5},{5,6},{6,7},{7,8},{8,9},{9,10},{10,1... | collective-permute-start | bytes 1572872 | tf_op jit(solution)/shard_map/ppermute | solution.py:325
  10.4 24.5 %collective-permute-start = (f32[8,32,512]{2,1,0:T(8,128)S(1)}, f32[8,32,512]{2,1,0:T(8,128)S(1)}, u32[]{:S(2)}, u32[]{:S(2)}) collective-permute-start(f32[8,32,512]{2,1,0:T(8,128)S(1)} %get-tuple-element.20.p2), channel_id=1, source_target_pairs={{0,1},{1,2},{2,3},{3,4},{4,5},{5,6},{6,7},{7,8},{8,9},{9,10},{10,1... | collective-permute-start | bytes 1572872 | tf_op jit(solution)/shard_map/ppermute | solution.py:323
  10.4 18.4 %collective-permute-start.4 = (f32[2,32,512]{2,1,0:T(8,128)S(1)}, f32[2,32,512]{2,1,0:T(8,128)S(1)}, u32[]{:S(2)}, u32[]{:S(2)}) collective-permute-start(f32[2,32,512]{2,1,0:T(8,128)S(1)} %get-tuple-element.17), channel_id=1, source_target_pairs={{0,1},{1,2},{2,3},{3,4},{4,5},{5,6},{6,7},{7,8},{8,9},{9,10},{10,1... | collective-permute-start | bytes 393224 | tf_op jit(solution)/shard_map/ppermute | solution.py:327
  28.8 6.1 %collective-permute-start.5 = (f32[2,32,512]{2,1,0:T(8,128)S(1)}, f32[2,32,512]{2,1,0:T(8,128)S(1)}, u32[]{:S(2)}, u32[]{:S(2)}) collective-permute-start(f32[2,32,512]{2,1,0:T(8,128)S(1)} %get-tuple-element.18), channel_id=1, source_target_pairs={{1,0},{2,1},{3,2},{4,3},{5,4},{6,5},{7,6},{8,7},{9,8},{10,9},{11,1... | collective-permute-start | bytes 393224 | tf_op jit(solution)/shard_map/ppermute | solution.py:328
  34.9 16.1 %copy-start.4 = (f32[8,32,512]{2,1,0:T(8,128)}, f32[8,32,512]{2,1,0:T(8,128)S(1)}, u32[]{:S(2)}) copy-start(f32[8,32,512]{2,1,0:T(8,128)S(1)} %collective-permute-done.3.next2) | copy-start | bytes 1572868
  34.9 16.0 %copy-start.6 = (f32[8,32,512]{2,1,0:T(8,128)}, f32[8,32,512]{2,1,0:T(8,128)S(1)}, u32[]{:S(2)}) copy-start(f32[8,32,512]{2,1,0:T(8,128)S(1)} %collective-permute-done.2.prev2) | copy-start | bytes 1572868
  34.9 1.4 %copy-start = (bf16[512,512]{1,0:T(8,128)(2,1)S(1)}, bf16[512,512]{1,0:T(8,128)(2,1)}, u32[]{:S(2)}) copy-start(bf16[512,512]{1,0:T(8,128)(2,1)} %constant.17.clone.table_low) | copy-start | bytes 1572868
  36.3 1.0 copy-start.2
  37.3 0.7 copy-start.16
  38.0 12.9 %copy-start.8 = (f32[8,32,512]{2,1,0:T(8,128)}, f32[8,32,512]{2,1,0:T(8,128)S(1)}, u32[]{:S(2)}) copy-start(f32[8,32,512]{2,1,0:T(8,128)S(1)} %collective-permute-done.prev1) | copy-start | bytes 1572868
  38.0 33.5 %copy-start.12 = (bf16[256,128]{1,0:T(8,128)(2,1)S(1)}, bf16[256,128]{1,0:T(8,128)(2,1)}, u32[]{:S(2)}) copy-start(bf16[256,128]{1,0:T(8,128)(2,1)} %constant.21.clone.refs_4_) | copy-start | bytes 196612
  38.0 33.5 %copy-start.13 = (bf16[256,128]{1,0:T(8,128)(2,1)S(1)}, bf16[256,128]{1,0:T(8,128)(2,1)}, u32[]{:S(2)}) copy-start(bf16[256,128]{1,0:T(8,128)(2,1)} %constant.20.clone.refs_3_) | copy-start | bytes 196612
  38.0 33.5 %copy-start.14 = (bf16[128,256]{1,0:T(8,128)(2,1)S(1)}, bf16[128,256]{1,0:T(8,128)(2,1)}, u32[]{:S(2)}) copy-start(bf16[128,256]{1,0:T(8,128)(2,1)} %constant.19.clone.refs_2_) | copy-start | bytes 196612
  38.0 33.5 %copy-start.15 = (bf16[128,256]{1,0:T(8,128)(2,1)S(1)}, bf16[128,256]{1,0:T(8,128)(2,1)}, u32[]{:S(2)}) copy-start(bf16[128,256]{1,0:T(8,128)(2,1)} %constant.18.clone.refs_1_) | copy-start | bytes 196612
  38.1 33.5 %copy-start.18 = (bf16[48,96]{1,0:T(8,128)(2,1)S(1)}, bf16[48,96]{1,0:T(8,128)(2,1)}, u32[]{:S(2)}) copy-start(bf16[48,96]{1,0:T(8,128)(2,1)} %constant.23.clone.refs_6_) | copy-start | bytes 27652
  38.1 33.5 %copy-start.19 = (bf16[48,96]{1,0:T(8,128)(2,1)S(1)}, bf16[48,96]{1,0:T(8,128)(2,1)}, u32[]{:S(2)}) copy-start(bf16[48,96]{1,0:T(8,128)(2,1)} %constant.22.clone.refs_5_) | copy-start | bytes 27652
  50.9 45.3 %copy-start.17 = (s32[8,8]{1,0:T(8,128)S(1)}, s32[8,8]{1,0:T(8,128)}, u32[]{:S(2)}) copy-start(s32[8,8]{1,0:T(8,128)} %classes.3) | copy-start | bytes 772
  74.8 37.0 %all-to-all-start.1 = ((f32[16,48,128]{2,1,0:T(8,128)}), f32[16,48,128]{2,1,0:T(8,128)S(1)}, u32[]{:S(2)}, u32[]{:S(2)}) async-start(f32[16,48,128]{2,1,0:T(8,128)} %bitcast.1), calls=%async_computation.1 | async-start | bytes 786432 | tf_op jit(solution)/shard_map/all_to_all | solution.py:375
  78.3 17.8 %collective-permute-start.6 = (f32[8,32,512]{2,1,0:T(8,128)S(1)}, f32[8,32,512]{2,1,0:T(8,128)S(1)}, u32[]{:S(2)}, u32[]{:S(2)}) collective-permute-start(f32[8,32,512]{2,1,0:T(8,128)S(1)} %get-tuple-element.19.p0), channel_id=1, source_target_pairs={{0,1},{1,2},{2,3},{3,4},{4,5},{5,6},{6,7},{7,8},{8,9},{9,10},{10,1... | collective-permute-start | bytes 1572872 | tf_op jit(solution)/shard_map/ppermute | solution.py:330
  78.7 17.5 %collective-permute-start.7 = (f32[8,32,512]{2,1,0:T(8,128)S(1)}, f32[8,32,512]{2,1,0:T(8,128)S(1)}, u32[]{:S(2)}, u32[]{:S(2)}) collective-permute-start(f32[8,32,512]{2,1,0:T(8,128)S(1)} %get-tuple-element.20.p2), channel_id=1, source_target_pairs={{1,0},{2,1},{3,2},{4,3},{5,4},{6,5},{7,6},{8,7},{9,8},{10,9},{11,1... | collective-permute-start | bytes 1572872 | tf_op jit(solution)/shard_map/ppermute | solution.py:331
  96.2 1.0 copy-start.5
  97.2 1.0 copy-start.7
  98.3 1.0 copy-start.9
  99.3 12.4 %copy-start.1 = (bf16[512,512]{1,0:T(8,128)(2,1)S(1)}, bf16[512,512]{1,0:T(8,128)(2,1)}, u32[]{:S(2)}) copy-start(bf16[512,512]{1,0:T(8,128)(2,1)} %constant.17.clone.table_low) | copy-start | bytes 1572868
  99.3 12.4 %copy-start.3 = (bf16[512,512]{1,0:T(8,128)(2,1)S(1)}, bf16[512,512]{1,0:T(8,128)(2,1)}, u32[]{:S(2)}) copy-start(bf16[512,512]{1,0:T(8,128)(2,1)} %constant.16.clone.table_high) | copy-start | bytes 1572868

commit v2 on v1

--- a/solution.py
+++ b/solution.py
@@ -14,8 +14,8 @@
 F32 = jnp.float32
 BF16 = jnp.bfloat16
 VMEM = pl.BlockSpec(memory_space=pltpu.VMEM)
-SMEM = pl.BlockSpec(memory_space=pltpu.SMEM)
-PARAMS = pltpu.CompilerParams(vmem_limit_bytes=48 * 2**20)
+ANY = pl.BlockSpec(memory_space=pl.ANY)
+PARAMS = pltpu.CompilerParams(vmem_limit_bytes=28 * 2**20)
 
 
 def halves(table):
@@ -67,19 +67,51 @@
     return one(left[0], right[0]) + (one(left[0], right[1]) + one(left[1], right[0]))
 
 
-def start_kernel(chosen, jitter, grain_ids, p0, p1, p2, c0, c2):
-    for plane, out in enumerate((p0, p1, p2)):
+def fetch(pairs, semaphores):
+    copies = [pltpu.make_async_copy(src, dst, semaphores.at[k]) for k, (src, dst) in enumerate(pairs)]
+    for copy in copies:
+        copy.start()
+    return copies
+
+
+def pair_of(chosen):
+    first, second = chosen[0], chosen[1]
+    second = jnp.where(second == first, lax.rem(first + 1, GRAINS), second)
+    return first, second
+
+
+def others_of(chosen):
+    first, second = pair_of(chosen)
+    low, high = jnp.minimum(first, second), jnp.maximum(first, second)
+
+    def other(r):
+        i = r + (r >= low).astype(jnp.int32)
+        return i + (i >= high).astype(jnp.int32)
+
+    return other
+
+
+def start_kernel(chosen_any, jitter_any, ids_any, to_next, to_prev, c0, c2, chosen, jitter, grain_ids, semaphores):
+    planes = grain_ids.shape[0]
+    pairs = []
+    for k in range(planes):
+        pairs.append((jitter_any.at[:, k], jitter.at[:, k]))
+        pairs.append((ids_any.at[k], grain_ids.at[k]))
+    pairs.append((chosen_any, chosen))
+    copies = fetch(pairs, semaphores)
+    for plane, outs in enumerate(((to_prev.at[0],), (to_prev.at[1], to_next.at[0]), (to_next.at[1],))):
+        copies[2 * plane].wait()
+        copies[2 * plane + 1].wait()
         ids = grain_ids[plane]
-
-        def body(i, carry):
+        for i in range(GRAINS):
             base = jnp.where(ids == i, jnp.float32(0.6), jnp.float32(0.0))
-            out[i] = base + jitter[i, plane].astype(F32)
-            return carry
-
-        lax.fori_loop(0, GRAINS, body, 0)
-    for k in range(2):
-        c0[k] = p0[chosen[k]]
-        c2[k] = p2[chosen[k]]
+            value = base + jitter[i, plane].astype(F32)
+            for out in outs:
+                out[i] = value
+    copies[-1].wait()
+    for k, i in enumerate(pair_of(chosen)):
+        c0[k] = to_prev[0, i]
+        c2[k] = to_next[1, i]
 
 
 def grain_of(start):
@@ -134,46 +166,86 @@
     lax.fori_loop(0, GRAINS, body, 0)
 
 
-def main_kernel(
-    chosen, classes, p0, p1, p2, prev1, next1, prev2, next2, prev3, next3, table_high, table_low,
-    packed, eta1, eta2, rates, edge, fields,
+def inner_kernel(chosen_any, classes_any, to_next, to_prev, rates, middle, r0, r2, chosen, classes, semaphores):
+    copies = fetch(((chosen_any, chosen), (classes_any, classes)), semaphores)
+    row = (to_prev.at[0], to_prev.at[1], to_next.at[1])
+    for copy in copies:
+        copy.wait()
+    other = others_of(chosen)
+
+    def body(r, carry):
+        i = other(r)
+        r0[r] = to_prev[0, i]
+        r2[r] = to_next[1, i]
+        return carry
+
+    lax.fori_loop(0, GRAINS - 2, body, 0)
+    for k in range(3):
+        rates_plane(classes, row[k], rates.at[k])
+    step_plane(row[1], row[0], row[2], rates.at[1], middle)
+
+
+def near_kernel(
+    classes_any, to_next, to_prev, prev, nxt, rates, middle, edge_rates, eta1, eta2, classes, semaphores
 ):
-    depth, width = p0.shape[1:]
-    starts = (prev1, p0, p1, p2, next1)
-    for k, start in enumerate(starts):
-        rates_plane(classes, start, rates.at[k])
-    row = (prev2,) + starts + (next2,)
-    for k in range(5):
-        step_plane(row[k + 1], row[k], row[k + 2], rates.at[k], eta1.at[k])
-    for k in range(3):
-        step_plane(eta1.at[k + 1], eta1.at[k], eta1.at[k + 2], rates.at[k + 1], eta2.at[k])
-    for side, (far, mid, near, inner) in enumerate(((prev3, prev2, prev1, 0), (next3, next2, next1, 4))):
+    copies = fetch(((classes_any, classes),), semaphores)
+    p0, p1, p2 = to_prev.at[0], to_prev.at[1], to_next.at[1]
+    step_plane(p0, prev.at[1], p1, rates.at[0], eta1.at[1])
+    step_plane(p2, p1, nxt.at[0], rates.at[2], eta1.at[2])
+    copies[0].wait()
+    rates_plane(classes, prev.at[1], edge_rates.at[0])
+    rates_plane(classes, nxt.at[0], edge_rates.at[1])
+    step_plane(middle, eta1.at[1], eta1.at[2], rates.at[1], eta2.at[1])
+    step_plane(prev.at[1], prev.at[0], p0, edge_rates.at[0], eta1.at[0])
+    step_plane(nxt.at[0], p2, nxt.at[1], edge_rates.at[1], eta1.at[3])
+    step_plane(eta1.at[1], eta1.at[0], middle, rates.at[0], eta2.at[0])
+    step_plane(eta1.at[2], middle, eta1.at[3], rates.at[2], eta2.at[2])
+
+
+def pair_kernel(
+    chosen_any, classes_any, prev, nxt, prev3, next3, rates, edge_rates, eta1, eta2, high_any, low_any,
+    packed, final, chosen, classes, high, low, edge, fields, semaphores,
+):
+    copies = fetch(
+        ((chosen_any, chosen), (classes_any, classes), (high_any, high), (low_any, low)), semaphores
+    )
+    depth, width = final.shape[2:]
+    totals = [squares(eta2.at[k]) for k in range(3)]
+    copies[0].wait()
+    copies[1].wait()
+    pair = pair_of(chosen)
+    for side, (far, mid, near) in enumerate(((prev3, prev.at[0], prev.at[1]), (next3, nxt.at[1], nxt.at[0]))):
+        inner, neighbour = (0, 1) if side == 0 else (3, 2)
         ids = grain_of(mid)
         total0 = squares(mid)
         total1 = squares(eta1.at[inner])
-        neighbour = 1 if side == 0 else 3
-        for k in range(2):
-            i = chosen[k]
+        for k, i in enumerate(pair):
             first = update(mid[i], far[k], near[i], total0, rate(classes, ids, i))
-            edge[side, k] = update(eta1[inner, i], first, eta1[neighbour, i], total1, rates[inner, i])
+            edge[side, k] = update(eta1[inner, i], first, eta1[neighbour, i], total1, edge_rates[side, i])
+    repeated = chosen[1] == chosen[0]
     for k in range(3):
-        total = squares(eta2.at[k])
-        for f in range(2):
-            i = chosen[f]
+        values = []
+        for f, i in enumerate(pair):
             before = edge[0, f] if k == 0 else eta2[k - 1, i]
             after = edge[1, f] if k == 2 else eta2[k + 1, i]
-            value = update(eta2[k, i], before, after, total, rates[k + 1, i])
+            value = update(eta2[k, i], before, after, totals[k], rates[k, i])
+            final[f, k] = value
+            values.append(value)
+        values[1] = jnp.where(repeated, values[0], values[1])
+        for f in range(2):
             base = k * 4 * depth + f * depth
-            fields[base : base + depth] = value
-            fields[base + 2 * depth : base + 3 * depth] = value
-    full = dot3((table_high[...], table_low[...]), split(fields[...]), ((1,), (1,)))
+            fields[base : base + depth] = values[f]
+            fields[base + 2 * depth : base + 3 * depth] = values[f]
+    copies[2].wait()
+    copies[3].wait()
+    full = dot3((high[...], low[...]), split(fields[...]), ((1,), (1,)))
     slots = width // 2
     lanes = 4 * depth
     real_lane = lax.broadcasted_iota(jnp.int32, (slots, lanes), 1) < 2 * depth
     for k in range(3):
         part = full[:, k * lanes : (k + 1) * lanes]
         part = jnp.where(real_lane, part[:slots], part[slots:])
-        if len(packed.shape) == 3 and packed.shape[0] == 3:
+        if packed.shape[0] == 3:
             packed[k] = part
         else:
             devices, rows, _ = packed.shape
@@ -182,20 +254,40 @@
 
 
 def rest_kernel(
-    classes, p0, p1, p2, prev1, next1, prev2, next2, prev3, next3, eta1, eta2, out, rates, edge, other
+    chosen_any, classes_any, prev, nxt, prev3, next3, rates, edge_rates, eta1, eta2, final,
+    out, chosen, classes, edge, semaphores,
 ):
-    for far, mid, near, inner, neighbour, side in (
-        (prev3, prev2, prev1, 0, 1, 0),
-        (next3, next2, next1, 4, 3, 1),
-    ):
-        rates_plane(classes, mid, rates)
-        step_plane(mid, far, near, rates, other)
-        rates_plane(classes, near, rates)
-        step_plane(eta1.at[inner], other, eta1.at[neighbour], rates, edge.at[side])
-    row = (edge.at[0], eta2.at[0], eta2.at[1], eta2.at[2], edge.at[1])
-    for k, start in enumerate((p0, p1, p2)):
-        rates_plane(classes, start, rates)
-        step_plane(row[k + 1], row[k], row[k + 2], rates, out.at[:, k])
+    copies = fetch(((chosen_any, chosen), (classes_any, classes)), semaphores)
+    for copy in copies:
+        copy.wait()
+    other = others_of(chosen)
+    rest = GRAINS - 2
+    for side, (far, mid, near) in enumerate(((prev3, prev.at[0], prev.at[1]), (next3, nxt.at[1], nxt.at[0]))):
+        inner, neighbour = (0, 1) if side == 0 else (3, 2)
+        ids = grain_of(mid)
+        total0 = squares(mid)
+        total1 = squares(eta1.at[inner])
+
+        def body(r, carry):
+            i = other(r)
+            first = update(mid[i], far[r], near[i], total0, rate(classes, ids, i))
+            edge[side, r] = update(eta1[inner, i], first, eta1[neighbour, i], total1, edge_rates[side, i])
+            return carry
+
+        lax.fori_loop(0, rest, body, 0)
+    for k in range(3):
+        total = squares(eta2.at[k])
+
+        def last(r, carry):
+            i = other(r)
+            before = edge[0, r] if k == 0 else eta2[k - 1, i]
+            after = edge[1, r] if k == 2 else eta2[k + 1, i]
+            out[i, k] = update(eta2[k, i], before, after, total, rates[k, i])
+            return carry
+
+        lax.fori_loop(0, rest, last, 0)
+        for f, i in enumerate(pair_of(chosen)):
+            out[i, k] = final[f, k]
 
 
 def line_kernel(
@@ -312,35 +404,61 @@
     z_parts = [jnp.asarray(part) for matrix in (z_forward, z_inverse) for part in halves(matrix)]
     x_parts = [jnp.asarray(part) for part in halves(np.concatenate(phases(total_x), axis=1))]
 
-    two = (2, depth, width)
-    p0, p1, p2, c0, c2 = call(
+    two = (2, *plane)
+    six = (GRAINS - 2, depth, width)
+    small = [pltpu.SMEM((2,), jnp.int32), pltpu.SMEM((GRAINS, GRAINS), jnp.int32)]
+    to_next, to_prev, c0, c2 = call(
         start_kernel,
-        (shape(*plane), shape(*plane), shape(*plane), shape(*two), shape(*two)),
-        [SMEM, VMEM, VMEM],
+        (shape(*two), shape(*two), shape(2, depth, width), shape(2, depth, width)),
+        [ANY] * 3,
         chosen, jitter, grain_ids,
+        scratch=[
+            small[0],
+            pltpu.VMEM(jitter.shape, jitter.dtype),
+            pltpu.VMEM(grain_ids.shape, jnp.int32),
+            pltpu.SemaphoreType.DMA((2 * planes + 1,)),
+        ],
         flops=2**21, moved=2**22,
     )
-    prev1 = lax.ppermute(p2, "gx", up)
-    next1 = lax.ppermute(p0, "gx", down)
-    prev2 = lax.ppermute(p1, "gx", up)
-    next2 = lax.ppermute(p1, "gx", down)
+    prev = lax.ppermute(to_next, "gx", up)
+    nxt = lax.ppermute(to_prev, "gx", down)
+    rates, middle, r0, r2 = call(
+        inner_kernel,
+        (shape(planes, *plane), shape(*plane), shape(*six), shape(*six)),
+        [ANY] * 2 + [VMEM] * 2,
+        chosen, class_table, to_next, to_prev,
+        scratch=[*small, pltpu.SemaphoreType.DMA((2,))],
+        flops=2**24, moved=2**22,
+    )
+    c0, c2, prev, nxt = lax.optimization_barrier((c0, c2, prev, nxt))
     prev3 = lax.ppermute(c0, "gx", up)
     next3 = lax.ppermute(c2, "gx", down)
-    late0, late2, prev3, next3 = lax.optimization_barrier((p0, p2, prev3, next3))
-    prev3_all = lax.ppermute(late0, "gx", up)
-    next3_all = lax.ppermute(late2, "gx", down)
+    edge_rates, eta1, eta2 = call(
+        near_kernel,
+        (shape(*two), shape(4, *plane), shape(planes, *plane)),
+        [ANY] + [VMEM] * 6,
+        class_table, to_next, to_prev, prev, nxt, rates, middle,
+        scratch=[small[1], pltpu.SemaphoreType.DMA((1,))],
+        flops=2**25, moved=2**24,
+    )
+    r0, r2, prev3, next3 = lax.optimization_barrier((r0, r2, prev3, next3))
+    prev3_rest = lax.ppermute(r0, "gx", up)
+    next3_rest = lax.ppermute(r2, "gx", down)
     packed_shape = (devices, planes * share, lanes) if aligned else (planes, slots, lanes)
-    packed, eta1, eta2 = call(
-        main_kernel,
-        (shape(*packed_shape), shape(5, *plane), shape(3, *plane)),
-        [SMEM, SMEM] + [VMEM] * 11,
-        chosen, class_table, p0, p1, p2, prev1, next1, prev2, next2, prev3, next3, *table,
+    packed, final = call(
+        pair_kernel,
+        (shape(*packed_shape), shape(2, planes, depth, width)),
+        [ANY] * 2 + [VMEM] * 8 + [ANY] * 2,
+        chosen, class_table, prev, nxt, prev3, next3, rates, edge_rates, eta1, eta2, *table,
         scratch=[
-            pltpu.VMEM((5, *plane), F32),
-            pltpu.VMEM((2, *two), F32),
+            *small,
+            pltpu.VMEM(table[0].shape, BF16),
+            pltpu.VMEM(table[1].shape, BF16),
+            pltpu.VMEM((2, 2, depth, width), F32),
             pltpu.VMEM((planes * lanes, width), F32),
+            pltpu.SemaphoreType.DMA((4,)),
         ],
-        flops=2**28, moved=2**24,
+        flops=2**28, moved=2**23,
     )
     if aligned:
         lines = lax.all_to_all(packed, "gx", split_axis=0, concat_axis=0, tiled=True)
@@ -350,11 +468,12 @@
     order_params = call(
         rest_kernel,
         shape(GRAINS, planes, depth, width),
-        [SMEM] + [VMEM] * 11,
-        class_table, p0, p1, p2, prev1, next1, prev2, next2, prev3_all, next3_all, eta1, eta2,
-        scratch=[pltpu.VMEM(plane, F32), pltpu.VMEM((2, *plane), F32), pltpu.VMEM(plane, F32)],
+        [ANY] * 2 + [VMEM] * 9,
+        chosen, class_table, prev, nxt, prev3_rest, next3_rest, rates, edge_rates, eta1, eta2, final,
+        scratch=[*small, pltpu.VMEM((2, *six), F32), pltpu.SemaphoreType.DMA((2,))],
         flops=2**26, moved=2**24,
     )
+    lines, order_params = lax.optimization_barrier((lines, order_params))
 
     def lines_body(*refs):
         line_kernel(*refs, scale=1.0 / (count * count))

time: 114 us -> 111 us (0.974)
  waiting for transfers between devices: 37.8 us -> 24.5 us
  starting transfers between devices: 14.2 us -> 27.1 us
  local copies, waits for them, and re-layouts: 9.01 us -> 18.3 us
  Pallas kernels: 30.6 us -> 23.5 us
  blocking collectives: 20.6 us -> 15.7 us
    ppermute x1, waiting for transfers between devices: 18.4 us -> 0.01 us  [shards(): prev3 = lax.ppermute(c0, 'gx', up)]
    ppermute x1, starting transfers between devices: 0.01 us -> 11.9 us  [shards(): prev3 = lax.ppermute(c0, 'gx', up)]
    ppermute x6 -> x4, waiting for transfers between devices: 13.4 us -> 24.4 us  [the longest x1 12.5 us: shards(): prev = lax.ppermute(to_next, 'gx', up)]
    unnamed x42 -> x58, local copies, waits for them, and re-layouts: 9.01 us -> 18.3 us
    pallas_call x5 -> x7, Pallas kernels: 30.6 us -> 23.5 us  [call(): pl.pallas_call(kernel, out_shape=outs, in_specs=in_specs, out_specs=jax.t...]
    ppermute x1, waiting for transfers between devices: 6.07 us -> 0.01 us  [shards(): next3 = lax.ppermute(c2, 'gx', down)]
    all_to_all x1, blocking collectives: 20.6 us -> 15.7 us  [shards(): lax.all_to_all(back, 'gx', split_axis=0, concat_axis=0, tiled=True)]
    all_to_all x1, starting transfers between devices: 3.55 us -> 5.13 us  [shards(): lax.all_to_all(packed, 'gx', split_axis=0, concat_axis=0, tiled=True)]
  transfers between devices with their start and end apart: 9 -> 7, of which waited for: 3 -> 2; matrix products, arithmetic and copies ran while one was open for 0% -> 0% of each run, Pallas kernels for 11% -> 15%
where the time goes in v2:
time: 111 us; the launch traced here: 110 us
  starting transfers between devices  27.1 us (24%)
  waiting for transfers between devices  24.5 us (22%)
  Pallas kernels  23.5 us (21%)
  local copies, waits for them, and re-layouts  18.3 us (16%)
  blocking collectives  15.7 us (14%)
    pallas_call x7, Pallas kernels, call(): pl.pallas_call(kernel, out_shape=outs, in_specs=in_specs, out_specs=jax.t...  23.5 us
    unnamed x58, local copies, waits for them, and re-layouts  18.3 us
    all_to_all x1, blocking collectives, shards(): lax.all_to_all(back, 'gx', split_axis=0, concat_axis=0, tiled=True)  15.7 us
    ppermute x1, waiting for transfers between devices, shards(): prev = lax.ppermute(to_next, 'gx', up)  12.5 us
    ppermute x1, waiting for transfers between devices, shards(): prev3_rest = lax.ppermute(r0, 'gx', up)  11.9 us
    ppermute x1, starting transfers between devices, shards(): prev3 = lax.ppermute(c0, 'gx', up)  11.9 us
    all_to_all x1, starting transfers between devices, shards(): lax.all_to_all(packed, 'gx', split_axis=0, concat_axis=0, tiled=True)  5.13 us
    ppermute x1, starting transfers between devices, shards(): nxt = lax.ppermute(to_prev, 'gx', down)  5.06 us
  transfers between devices with their start and end apart: 7, of which 2 were waited for; matrix products, arithmetic and copies ran while one was open for 0% of the time, Pallas kernels for 15%

profile of v2, /device:TPU:0, one launch (start us, length us, event | category | flops | bytes accessed | tf_op | source)
XLA Modules:
  0.0 110.0 jit_solution(3629539944362895403)
XLA Ops:
  0.6 0.0 copy-start.11
  0.6 1.1 %copy-done.11 = bf16[8,3,32,512]{3,2,1,0:T(8,128)(2,1)S(1)} copy-done((bf16[8,3,32,512]{3,2,1,0:T(8,128)(2,1)S(1)}, bf16[8,3,32,512]{3,2,1,0:T(8,128)(2,1)}, u32[]{:S(2)}) %copy-start.11) | copy-done | bytes 786456
  1.8 0.0 copy-start.15
  1.8 0.9 copy-done.15
  2.7 0.0 copy-start.24
  2.7 0.7 copy-done.24
  3.3 0.0 copy-start.21
  3.3 0.9 shard_map.131
  4.3 0.5 collective-permute-start
  4.8 5.1 %collective-permute-start.1 = (f32[2,8,32,512]{3,2,1,0:T(8,128)S(1)}, f32[2,8,32,512]{3,2,1,0:T(8,128)S(1)}, u32[]{:S(2)}, u32[]{:S(2)}) collective-permute-start(f32[2,8,32,512]{3,2,1,0:T(8,128)S(1)} %get-tuple-element.28.to_prev), channel_id=1, source_target_pairs={{1,0},{2,1},{3,2},{4,3},{5,4},{6,5},{7,6},{8,7},{9,8},{10,9},{11,1... | collective-permute-start | bytes 3145736 | tf_op jit(solution)/shard_map/ppermute | solution.py:424
  9.8 12.5 %collective-permute-done.prev = f32[2,8,32,512]{3,2,1,0:T(8,128)S(1)} collective-permute-done((f32[2,8,32,512]{3,2,1,0:T(8,128)S(1)}, f32[2,8,32,512]{3,2,1,0:T(8,128)S(1)}, u32[]{:S(2)}, u32[]{:S(2)}) %collective-permute-start) | collective-permute-done | bytes 1048608 | tf_op jit(solution)/shard_map/ppermute | solution.py:423
  22.4 0.0 collective-permute-done.1.nxt
  22.4 0.0 copy-start
  22.4 11.9 %collective-permute-start.2 = (f32[2,32,512]{2,1,0:T(8,128)S(1)}, f32[2,32,512]{2,1,0:T(8,128)S(1)}, u32[]{:S(2)}, u32[]{:S(2)}) collective-permute-start(f32[2,32,512]{2,1,0:T(8,128)S(1)} %get-tuple-element.33), channel_id=1, source_target_pairs={{0,1},{1,2},{2,3},{3,4},{4,5},{5,6},{6,7},{7,8},{8,9},{9,10},{10,1... | collective-permute-start | bytes 393224 | tf_op jit(solution)/shard_map/ppermute | solution.py:434
  34.3 0.0 collective-permute-start.3
  34.3 0.0 copy-start.20
  34.3 0.7 copy-done.20
  35.0 0.7 copy-done.25
  35.6 2.7 %shard_map.132 = (f32[3,8,32,512]{3,2,1,0:T(8,128)S(1)}, f32[8,32,512]{2,1,0:T(8,128)S(1)}, f32[6,32,512]{2,1,0:T(8,128)S(1)}, f32[6,32,512]{2,1,0:T(8,128)S(1)}) custom-call(s32[2]{0:T(128)S(1)} %copy-done.25, s32[8,8]{1,0:T(8,128)S(1)} %copy-done.20, f32[2,8,32,512]{3,2,1,0:T(8,128)S(1)} %get-tuple-element.27.to_next, ...), custom_call_target="tpu_custom_call" | custom-call | flops 16777216 | bytes 4194304 | tf_op jit(solution)/shard_map/pallas_call | solution.py:375
  38.4 0.0 copy-start.27
  38.4 0.8 copy-done.27
  39.1 0.7 copy-done.28
  39.9 0.0 copy-done.21
  39.9 7.3 %shard_map.133 = (f32[2,8,32,512]{3,2,1,0:T(8,128)S(1)}, f32[4,8,32,512]{3,2,1,0:T(8,128)S(1)}, f32[3,8,32,512]{3,2,1,0:T(8,128)S(1)}) custom-call(s32[8,8]{1,0:T(8,128)S(1)} %copy-done.21, f32[2,8,32,512]{3,2,1,0:T(8,128)S(1)} %get-tuple-element.27.to_next, f32[2,8,32,512]{3,2,1,0:T(8,128)S(1)} %get-tuple-element.28.to_prev, ...), custom_call_target="tpu_custom_call" | custom-call | flops 33554432 | bytes 16777216 | tf_op jit(solution)/shard_map/pallas_call | solution.py:375
  47.2 0.0 copy-start.2
  47.2 0.0 copy-start.4
  47.2 0.0 copy-start.6
  47.2 0.0 collective-permute-done.2.prev3
  47.3 0.0 collective-permute-done.3.next3
  47.3 0.0 copy-done
  47.3 0.0 copy-done.8
  47.3 0.0 copy-done.9
  47.3 2.7 %shard_map.134 = (f32[16,48,128]{2,1,0:T(8,128)S(1)}, f32[2,3,32,512]{3,2,1,0:T(8,128)S(1)}) custom-call(s32[2]{0:T(128)S(1)} %copy-done.25, s32[8,8]{1,0:T(8,128)S(1)} %copy-done.21, f32[2,8,32,512]{3,2,1,0:T(8,128)S(1)} %collective-permute-done.prev, f32[2,8,32,512]{3,2,1,0:T(8,128)S(1)} %collective-permute-done.1.nxt, ...), custom_call_target="tpu_custom_call" | custom-call | flops 268435456 | bytes 8388608 | tf_op jit(solution)/shard_map/pallas_call | solution.py:375
  50.0 0.0 copy-done.2
  50.0 0.0 copy-done.4
  50.0 0.0 copy-done.6
  50.0 0.0 copy-start.12
  50.0 0.8 copy-done.12
  50.8 0.8 copy-done.13
  51.5 5.1 %all-to-all-start = ((f32[16,48,128]{2,1,0:T(8,128)}), f32[16,48,128]{2,1,0:T(8,128)S(1)}, u32[]{:S(2)}, u32[]{:S(2)}) async-start(f32[16,48,128]{2,1,0:T(8,128)} %copy-done.12), calls=%async_computation | async-start | bytes 786432 | tf_op jit(solution)/shard_map/all_to_all | solution.py:464
  56.7 0.4 collective-permute-start.4
  57.1 4.1 %collective-permute-start.5 = (f32[6,32,512]{2,1,0:T(8,128)}, f32[6,32,512]{2,1,0:T(8,128)S(1)}, u32[]{:S(2)}, u32[]{:S(2)}) collective-permute-start(f32[6,32,512]{2,1,0:T(8,128)} %copy-done.27), channel_id=1, source_target_pairs={{1,0},{2,1},{3,2},{4,3},{5,4},{6,5},{7,6},{8,7},{9,8},{10,9},{11,1... | collective-permute-start | bytes 1179656 | tf_op jit(solution)/shard_map/ppermute | solution.py:446
  61.2 11.9 %collective-permute-done.4.prev3 = f32[6,32,512]{2,1,0:T(8,128)S(1)} collective-permute-done((f32[6,32,512]{2,1,0:T(8,128)}, f32[6,32,512]{2,1,0:T(8,128)S(1)}, u32[]{:S(2)}, u32[]{:S(2)}) %collective-permute-start.4) | collective-permute-done | bytes 393248 | tf_op jit(solution)/shard_map/ppermute | solution.py:445
  73.1 0.0 collective-permute-done.5.next3
  73.1 1.2 %copy-done.1 = f32[2,8,32,512]{3,2,1,0:T(8,128)S(1)} copy-done((f32[2,8,32,512]{3,2,1,0:T(8,128)S(1)}, f32[2,8,32,512]{3,2,1,0:T(8,128)}, u32[]{:S(2)}) %copy-start.1) | copy-done | bytes 1048600
  74.3 1.6 %copy-done.3 = f32[4,8,32,512]{3,2,1,0:T(8,128)S(1)} copy-done((f32[4,8,32,512]{3,2,1,0:T(8,128)S(1)}, f32[4,8,32,512]{3,2,1,0:T(8,128)}, u32[]{:S(2)}) %copy-start.3) | copy-done | bytes 2097176
  75.9 1.4 %copy-done.5 = f32[3,8,32,512]{3,2,1,0:T(8,128)S(1)} copy-done((f32[3,8,32,512]{3,2,1,0:T(8,128)S(1)}, f32[3,8,32,512]{3,2,1,0:T(8,128)}, u32[]{:S(2)}) %copy-start.5) | copy-done | bytes 1572888
  77.3 1.2 %copy-done.7 = f32[2,8,32,512]{3,2,1,0:T(8,128)S(1)} copy-done((f32[2,8,32,512]{3,2,1,0:T(8,128)S(1)}, f32[2,8,32,512]{3,2,1,0:T(8,128)}, u32[]{:S(2)}) %copy-start.7) | copy-done | bytes 1048600
  78.5 1.0 copy-done.14
  79.5 0.7 copy-done.26
  80.2 6.1 %shard_map.135 = f32[8,3,32,512]{3,2,1,0:T(8,128)} custom-call(s32[2]{0:T(128)S(1)} %copy-done.26, s32[8,8]{1,0:T(8,128)S(1)} %copy-done.21, f32[2,8,32,512]{3,2,1,0:T(8,128)S(1)} %collective-permute-done.prev, f32[2,8,32,512]{3,2,1,0:T(8,128)S(1)} %copy-done.1, f32[6,32,512]{2,1,0:T(8,128)S(1)} %collective-permute-done.4.prev3, ...), custom_call_target="tpu_custom_call" | custom-call | flops 67108864 | bytes 16777216 | tf_op jit(solution)/shard_map/pallas_call | solution.py:375
  86.3 0.0 copy-start.10
  86.3 0.0 all-to-all-done
  86.3 0.0 copy-done.22
  86.3 0.0 copy-start.16
  86.4 0.9 copy-done.16
  87.2 0.8 copy-done.17
  88.1 0.8 copy-done.18
  88.9 0.8 copy-done.19
  89.8 0.7 copy-done.23
  90.5 2.5 %shard_map.136 = f32[768,128]{1,0:T(8,128)S(1)} custom-call(f32[768,128]{1,0:T(8,128)S(1)} %bitcast.2, bf16[128,256]{1,0:T(8,128)(2,1)S(1)} %copy-done.19, bf16[128,256]{1,0:T(8,128)(2,1)S(1)} %copy-done.18, bf16[256,128]{1,0:T(8,128)(2,1)S(1)} %copy-done.17, bf16[256,128]{1,0:T(8,128)(2,1)S(1)} %copy-done.16, bf16[48,96]{1,0:T(8,128)(2,1)S(1)} %copy-done.23, ...), custom_call_target="tpu_custom_call" | custom-call | flops 268435456 | bytes 4194304 | tf_op jit(solution)/shard_map/pallas_call | solution.py:375
  92.9 15.7 %all_to_all.10.returned = f32[16,48,128]{2,1,0:T(8,128)S(1)} all-to-all(f32[16,48,128]{2,1,0:T(8,128)S(1)} %bitcast.3), channel_id=1, replica_groups=mesh['grp'=2,'gx'=16] {'gx'}, dimensions={0} | all-to-all | bytes 786432 | tf_op jit(solution)/shard_map/all_to_all | solution.py:494
  108.7 0.0 copy-done.10
  108.7 1.3 %shard_map.137 = f32[2,3,32,512]{3,2,1,0:T(8,128)} custom-call(f32[16,48,128]{2,1,0:T(8,128)S(1)} %all_to_all.10.returned, bf16[512,512]{1,0:T(8,128)(2,1)S(1)} %copy-done.10, bf16[512,512]{1,0:T(8,128)(2,1)S(1)} %copy-done.8), custom_call_target="tpu_custom_call" | custom-call | flops 268435456 | bytes 4194304 | tf_op jit(solution)/shard_map/pallas_call | solution.py:375
  (16 shorter events, 0.0 us)
Async XLA Ops:
  0.6 1.1 %copy-start.11 = (bf16[8,3,32,512]{3,2,1,0:T(8,128)(2,1)S(1)}, bf16[8,3,32,512]{3,2,1,0:T(8,128)(2,1)}, u32[]{:S(2)}) copy-start(bf16[8,3,32,512]{3,2,1,0:T(8,128)(2,1)} %jitter_any.1) | copy-start | bytes 2359300
  1.8 0.9 copy-start.15
  2.7 0.7 copy-start.24
  3.3 36.5 %copy-start.21 = (s32[8,8]{1,0:T(8,128)S(1)}, s32[8,8]{1,0:T(8,128)}, u32[]{:S(2)}) copy-start(s32[8,8]{1,0:T(8,128)} %classes_any.7) | copy-start | bytes 772
  4.3 18.1 %collective-permute-start = (f32[2,8,32,512]{3,2,1,0:T(8,128)S(1)}, f32[2,8,32,512]{3,2,1,0:T(8,128)S(1)}, u32[]{:S(2)}, u32[]{:S(2)}) collective-permute-start(f32[2,8,32,512]{3,2,1,0:T(8,128)S(1)} %get-tuple-element.27.to_next), channel_id=1, source_target_pairs={{0,1},{1,2},{2,3},{3,4},{4,5},{5,6},{6,7},{7,8},{8,9},{9,10},{10,1... | collective-permute-start | bytes 3145736 | tf_op jit(solution)/shard_map/ppermute | solution.py:423
  4.8 17.6 %collective-permute-start.1 = (f32[2,8,32,512]{3,2,1,0:T(8,128)S(1)}, f32[2,8,32,512]{3,2,1,0:T(8,128)S(1)}, u32[]{:S(2)}, u32[]{:S(2)}) collective-permute-start(f32[2,8,32,512]{3,2,1,0:T(8,128)S(1)} %get-tuple-element.28.to_prev), channel_id=1, source_target_pairs={{1,0},{2,1},{3,2},{4,3},{5,4},{6,5},{7,6},{8,7},{9,8},{10,9},{11,1... | collective-permute-start | bytes 3145736 | tf_op jit(solution)/shard_map/ppermute | solution.py:424
  22.4 24.9 %copy-start = (f32[2,8,32,512]{3,2,1,0:T(8,128)}, f32[2,8,32,512]{3,2,1,0:T(8,128)S(1)}, u32[]{:S(2)}) copy-start(f32[2,8,32,512]{3,2,1,0:T(8,128)S(1)} %collective-permute-done.1.nxt) | copy-start | bytes 3145732
  22.4 24.9 %collective-permute-start.2 = (f32[2,32,512]{2,1,0:T(8,128)S(1)}, f32[2,32,512]{2,1,0:T(8,128)S(1)}, u32[]{:S(2)}, u32[]{:S(2)}) collective-permute-start(f32[2,32,512]{2,1,0:T(8,128)S(1)} %get-tuple-element.33), channel_id=1, source_target_pairs={{0,1},{1,2},{2,3},{3,4},{4,5},{5,6},{6,7},{7,8},{8,9},{9,10},{10,1... | collective-permute-start | bytes 393224 | tf_op jit(solution)/shard_map/ppermute | solution.py:434
  34.3 13.0 %collective-permute-start.3 = (f32[2,32,512]{2,1,0:T(8,128)S(1)}, f32[2,32,512]{2,1,0:T(8,128)S(1)}, u32[]{:S(2)}, u32[]{:S(2)}) collective-permute-start(f32[2,32,512]{2,1,0:T(8,128)S(1)} %get-tuple-element.34), channel_id=1, source_target_pairs={{1,0},{2,1},{3,2},{4,3},{5,4},{6,5},{7,6},{8,7},{9,8},{10,9},{11,1... | collective-permute-start | bytes 393224 | tf_op jit(solution)/shard_map/ppermute | solution.py:435
  34.3 0.7 copy-start.20
  35.0 0.7 copy-start.25
  38.4 0.8 copy-start.27
  39.1 0.7 copy-start.28
  39.9 7.4 %copy-start.8 = (bf16[512,512]{1,0:T(8,128)(2,1)S(1)}, bf16[512,512]{1,0:T(8,128)(2,1)}, u32[]{:S(2)}) copy-start(bf16[512,512]{1,0:T(8,128)(2,1)} %constant.17.clone.low_any.table_low) | copy-start | bytes 1572868
  39.9 7.4 %copy-start.9 = (bf16[512,512]{1,0:T(8,128)(2,1)S(1)}, bf16[512,512]{1,0:T(8,128)(2,1)}, u32[]{:S(2)}) copy-start(bf16[512,512]{1,0:T(8,128)(2,1)} %constant.16.clone.high_any.table_high) | copy-start | bytes 1572868
  47.2 2.8 %copy-start.2 = (f32[4,8,32,512]{3,2,1,0:T(8,128)}, f32[4,8,32,512]{3,2,1,0:T(8,128)S(1)}, u32[]{:S(2)}) copy-start(f32[4,8,32,512]{3,2,1,0:T(8,128)S(1)} %get-tuple-element.40.eta1) | copy-start | bytes 6291460
  47.2 2.8 %copy-start.4 = (f32[3,8,32,512]{3,2,1,0:T(8,128)}, f32[3,8,32,512]{3,2,1,0:T(8,128)S(1)}, u32[]{:S(2)}) copy-start(f32[3,8,32,512]{3,2,1,0:T(8,128)S(1)} %get-tuple-element.41.eta2) | copy-start | bytes 4718596
  47.2 2.8 %copy-start.6 = (f32[2,8,32,512]{3,2,1,0:T(8,128)}, f32[2,8,32,512]{3,2,1,0:T(8,128)S(1)}, u32[]{:S(2)}) copy-start(f32[2,8,32,512]{3,2,1,0:T(8,128)S(1)} %get-tuple-element.39.edge_rates) | copy-start | bytes 3145732
  50.0 0.8 copy-start.12
  50.8 0.8 copy-start.13
  51.5 34.8 %all-to-all-start = ((f32[16,48,128]{2,1,0:T(8,128)}), f32[16,48,128]{2,1,0:T(8,128)S(1)}, u32[]{:S(2)}, u32[]{:S(2)}) async-start(f32[16,48,128]{2,1,0:T(8,128)} %copy-done.12), calls=%async_computation | async-start | bytes 786432 | tf_op jit(solution)/shard_map/all_to_all | solution.py:464
  56.7 16.4 %collective-permute-start.4 = (f32[6,32,512]{2,1,0:T(8,128)}, f32[6,32,512]{2,1,0:T(8,128)S(1)}, u32[]{:S(2)}, u32[]{:S(2)}) collective-permute-start(f32[6,32,512]{2,1,0:T(8,128)} %copy-done.28), channel_id=1, source_target_pairs={{0,1},{1,2},{2,3},{3,4},{4,5},{5,6},{6,7},{7,8},{8,9},{9,10},{10,1... | collective-permute-start | bytes 1179656 | tf_op jit(solution)/shard_map/ppermute | solution.py:445
  57.1 16.0 %collective-permute-start.5 = (f32[6,32,512]{2,1,0:T(8,128)}, f32[6,32,512]{2,1,0:T(8,128)S(1)}, u32[]{:S(2)}, u32[]{:S(2)}) collective-permute-start(f32[6,32,512]{2,1,0:T(8,128)} %copy-done.27), channel_id=1, source_target_pairs={{1,0},{2,1},{3,2},{4,3},{5,4},{6,5},{7,6},{8,7},{9,8},{10,9},{11,1... | collective-permute-start | bytes 1179656 | tf_op jit(solution)/shard_map/ppermute | solution.py:446
  73.1 1.2 %copy-start.1 = (f32[2,8,32,512]{3,2,1,0:T(8,128)S(1)}, f32[2,8,32,512]{3,2,1,0:T(8,128)}, u32[]{:S(2)}) copy-start(f32[2,8,32,512]{3,2,1,0:T(8,128)} %copy-done) | copy-start | bytes 3145732
  74.3 1.6 %copy-start.3 = (f32[4,8,32,512]{3,2,1,0:T(8,128)S(1)}, f32[4,8,32,512]{3,2,1,0:T(8,128)}, u32[]{:S(2)}) copy-start(f32[4,8,32,512]{3,2,1,0:T(8,128)} %copy-done.2) | copy-start | bytes 6291460
  75.9 1.4 %copy-start.5 = (f32[3,8,32,512]{3,2,1,0:T(8,128)S(1)}, f32[3,8,32,512]{3,2,1,0:T(8,128)}, u32[]{:S(2)}) copy-start(f32[3,8,32,512]{3,2,1,0:T(8,128)} %copy-done.4) | copy-start | bytes 4718596
  77.3 1.2 %copy-start.7 = (f32[2,8,32,512]{3,2,1,0:T(8,128)S(1)}, f32[2,8,32,512]{3,2,1,0:T(8,128)}, u32[]{:S(2)}) copy-start(f32[2,8,32,512]{3,2,1,0:T(8,128)} %copy-done.6) | copy-start | bytes 3145732
  78.5 1.0 copy-start.14
  79.5 0.7 copy-start.26
  80.2 6.1 %copy-start.22 = (bf16[48,96]{1,0:T(8,128)(2,1)S(1)}, bf16[48,96]{1,0:T(8,128)(2,1)}, u32[]{:S(2)}) copy-start(bf16[48,96]{1,0:T(8,128)(2,1)} %constant.23.clone.refs_6_) | copy-start | bytes 27652
  86.3 22.4 %copy-start.10 = (bf16[512,512]{1,0:T(8,128)(2,1)S(1)}, bf16[512,512]{1,0:T(8,128)(2,1)}, u32[]{:S(2)}) copy-start(bf16[512,512]{1,0:T(8,128)(2,1)} %constant.16.clone.high_any.table_high) | copy-start | bytes 1572868
  86.3 0.9 copy-start.16
  87.2 0.8 copy-start.17
  88.1 0.8 copy-start.18
  88.9 0.8 copy-start.19
  89.8 0.7 copy-start.23

commit v3 on v2

--- a/solution.py
+++ b/solution.py
@@ -14,8 +14,8 @@
 F32 = jnp.float32
 BF16 = jnp.bfloat16
 VMEM = pl.BlockSpec(memory_space=pltpu.VMEM)
-ANY = pl.BlockSpec(memory_space=pl.ANY)
-PARAMS = pltpu.CompilerParams(vmem_limit_bytes=28 * 2**20)
+ANY = pl.BlockSpec(memory_space=pltpu.HBM)
+MIB = 2**20
 
 
 def halves(table):
@@ -253,13 +253,11 @@
             packed[:, k * rows : (k + 1) * rows, :] = part.reshape(devices, rows, lanes)
 
 
-def rest_kernel(
-    chosen_any, classes_any, prev, nxt, prev3, next3, rates, edge_rates, eta1, eta2, final,
-    out, chosen, classes, edge, semaphores,
-):
-    copies = fetch(((chosen_any, chosen), (classes_any, classes)), semaphores)
-    for copy in copies:
+def rest_kernel(*refs):
+    sources, out, targets, edge, semaphores = refs[:11], refs[11], refs[12:23], refs[23], refs[24]
+    for copy in fetch(list(zip(sources, targets)), semaphores):
         copy.wait()
+    chosen, classes, prev, nxt, prev3, next3, rates, edge_rates, eta1, eta2, final = targets
     other = others_of(chosen)
     rest = GRAINS - 2
     for side, (far, mid, near) in enumerate(((prev3, prev.at[0], prev.at[1]), (next3, nxt.at[1], nxt.at[0]))):
@@ -348,7 +346,8 @@
     )
 
 
-def finish_kernel(returned, table_high, table_low, out):
+def finish_kernel(returned, high_any, low_any, out, high, low, semaphores):
+    copies = fetch(((high_any, high), (low_any, low)), semaphores)
     fields, planes, depth, width = out.shape
     lanes = 2 * fields * depth
     half = lanes // 2
@@ -364,23 +363,25 @@
         part = part.T
         stacked.append(jnp.concatenate([part[:half], part[half:]], axis=1))
     stacked = split(jnp.concatenate(stacked, axis=0))
-    result = dot3(stacked, (table_high[...], table_low[...]))
+    for copy in copies:
+        copy.wait()
+    result = dot3(stacked, (high[...], low[...]))
     for k in range(planes):
         for f in range(fields):
             base = k * half + f * depth
             out[f, k] = result[base : base + depth]
 
 
-def call(kernel, outs, in_specs, *args, scratch=(), flops=0, moved=0):
+def call(kernel, outs, in_specs, *args, scratch=(), flops=0, moved=0, limit=12):
     return pl.pallas_call(
         kernel,
         out_shape=outs,
         in_specs=in_specs,
         out_specs=jax.tree.map(lambda _: VMEM, outs),
         scratch_shapes=scratch,
-        compiler_params=PARAMS,
+        compiler_params=pltpu.CompilerParams(vmem_limit_bytes=limit * MIB),
         cost_estimate=pl.CostEstimate(flops=flops, bytes_accessed=moved, transcendentals=0),
-    )(*args)
+    )(*[pltpu.with_memory_space_constraint(a, pltpu.HBM) if b is ANY else a for a, b in zip(args, in_specs)])
 
 
 def shards(grain_ids, jitter, class_table, chosen):
@@ -430,7 +431,7 @@
         scratch=[*small, pltpu.SemaphoreType.DMA((2,))],
         flops=2**24, moved=2**22,
     )
-    c0, c2, prev, nxt = lax.optimization_barrier((c0, c2, prev, nxt))
+    c0, c2, r0, r2, prev, nxt = lax.optimization_barrier((c0, c2, r0, r2, prev, nxt))
     prev3 = lax.ppermute(c0, "gx", up)
     next3 = lax.ppermute(c2, "gx", down)
     edge_rates, eta1, eta2 = call(
@@ -441,7 +442,6 @@
         scratch=[small[1], pltpu.SemaphoreType.DMA((1,))],
         flops=2**25, moved=2**24,
     )
-    r0, r2, prev3, next3 = lax.optimization_barrier((r0, r2, prev3, next3))
     prev3_rest = lax.ppermute(r0, "gx", up)
     next3_rest = lax.ppermute(r2, "gx", down)
     packed_shape = (devices, planes * share, lanes) if aligned else (planes, slots, lanes)
@@ -460,21 +460,12 @@
         ],
         flops=2**28, moved=2**23,
     )
+    packed, prev3_rest, next3_rest = lax.optimization_barrier((packed, prev3_rest, next3_rest))
     if aligned:
         lines = lax.all_to_all(packed, "gx", split_axis=0, concat_axis=0, tiled=True)
     else:
         lines = lax.all_to_all(packed, "gx", split_axis=1, concat_axis=0, tiled=True)
     lines = lines.reshape(total_x * share, lanes)
-    order_params = call(
-        rest_kernel,
-        shape(GRAINS, planes, depth, width),
-        [ANY] * 2 + [VMEM] * 9,
-        chosen, class_table, prev, nxt, prev3_rest, next3_rest, rates, edge_rates, eta1, eta2, final,
-        scratch=[*small, pltpu.VMEM((2, *six), F32), pltpu.SemaphoreType.DMA((2,))],
-        flops=2**26, moved=2**24,
-    )
-    lines, order_params = lax.optimization_barrier((lines, order_params))
-
     def lines_body(*refs):
         line_kernel(*refs, scale=1.0 / (count * count))
 
@@ -495,11 +486,31 @@
     if not aligned:
         returned = returned.reshape(devices, planes, share, lanes).transpose(1, 0, 2, 3)
         returned = returned.reshape(planes, slots, lanes)
+    late = (chosen, class_table, prev, nxt, prev3_rest, next3_rest, rates, edge_rates, eta1, eta2, final)
+    late, _ = lax.optimization_barrier((late, back))
+    order_params = call(
+        rest_kernel,
+        shape(GRAINS, planes, depth, width),
+        [ANY] * 11,
+        *late,
+        scratch=[
+            *small,
+            *[pltpu.VMEM(value.shape, F32) for value in late[2:]],
+            pltpu.VMEM((2, *six), F32),
+            pltpu.SemaphoreType.DMA((11,)),
+        ],
+        flops=2**26, moved=2**24, limit=24,
+    )
     correlation = call(
         finish_kernel,
         shape(2, planes, depth, width),
-        [VMEM] * 3,
+        [VMEM] + [ANY] * 2,
         returned, *table,
+        scratch=[
+            pltpu.VMEM(table[0].shape, BF16),
+            pltpu.VMEM(table[1].shape, BF16),
+            pltpu.SemaphoreType.DMA((2,)),
+        ],
         flops=2**28, moved=2**22,
     )
     return (order_params, correlation)

time: 111 us -> 90.1 us (0.81)
  local copies, waits for them, and re-layouts: 18.3 us -> 0.84 us
  waiting for transfers between devices: 24.5 us -> 12.6 us
  Pallas kernels: 23.5 us -> 29.8 us
  blocking collectives: 15.7 us -> 17.3 us
  starting transfers between devices: 27.1 us -> 28.3 us
    unnamed x58 -> x30, local copies, waits for them, and re-layouts: 18.3 us -> 0.84 us
    ppermute x1, starting transfers between devices: 0.41 us -> 14.7 us  [shards(): prev3_rest = lax.ppermute(r0, 'gx', up)]
    ppermute x1, waiting for transfers between devices: 11.9 us -> 0.01 us  [shards(): prev3_rest = lax.ppermute(r0, 'gx', up)]
    ppermute x1, starting transfers between devices: 11.9 us -> 0.51 us  [shards(): prev3 = lax.ppermute(c0, 'gx', up)]
    pallas_call x7, Pallas kernels: 23.5 us -> 29.8 us  [call(): pl.pallas_call(kernel, out_shape=outs, in_specs=in_specs, out_specs=jax.t...]
    ppermute x1, starting transfers between devices: 4.08 us -> 0.01 us  [shards(): next3_rest = lax.ppermute(r2, 'gx', down)]
    ppermute x1, starting transfers between devices: 0.01 us -> 3.94 us  [shards(): next3 = lax.ppermute(c2, 'gx', down)]
    all_to_all x1, waiting for transfers between devices: 0.01 us -> 2.94 us  [shards(): lax.all_to_all(back, 'gx', split_axis=0, concat_axis=0, tiled=True)]
  transfers between devices with their start and end apart: 7 -> 7, of which waited for: 2 -> 2; matrix products, arithmetic and copies ran while one was open for 0% -> 0% of each run, Pallas kernels for 15% -> 25%
where the time goes in v3:
time: 90.1 us; the launch traced here: 89.7 us
  Pallas kernels  29.8 us (33%)
  starting transfers between devices  28.3 us (31%)
  blocking collectives  17.3 us (19%)
  waiting for transfers between devices  12.6 us (14%)
    pallas_call x7, Pallas kernels, call(): pl.pallas_call(kernel, out_shape=outs, in_specs=in_specs, out_specs=jax.t...  29.8 us
    all_to_all x1, blocking collectives, shards(): lax.all_to_all(packed, 'gx', split_axis=0, concat_axis=0, tiled=True)  17.3 us
    ppermute x1, starting transfers between devices, shards(): prev3_rest = lax.ppermute(r0, 'gx', up)  14.7 us
    ppermute x1, waiting for transfers between devices, shards(): prev = lax.ppermute(to_next, 'gx', up)  9.65 us
    ppermute x1, starting transfers between devices, shards(): nxt = lax.ppermute(to_prev, 'gx', down)  5.06 us
    ppermute x1, starting transfers between devices, shards(): next3 = lax.ppermute(c2, 'gx', down)  3.94 us
    all_to_all x1, starting transfers between devices, shards(): lax.all_to_all(back, 'gx', split_axis=0, concat_axis=0, tiled=True)  3.55 us
    all_to_all x1, waiting for transfers between devices, shards(): lax.all_to_all(back, 'gx', split_axis=0, concat_axis=0, tiled=True)  2.94 us
  transfers between devices with their start and end apart: 7, of which 2 were waited for; matrix products, arithmetic and copies ran while one was open for 0% of the time, Pallas kernels for 25%

profile of v3, /device:TPU:0, one launch (start us, length us, event | category | flops | bytes accessed | tf_op | source)
XLA Modules:
  0.0 89.7 jit_solution(5713067766300344959)
XLA Ops:
  0.6 1.3 %shard_map.131 = (f32[2,8,32,512]{3,2,1,0:T(8,128)S(1)}, f32[2,8,32,512]{3,2,1,0:T(8,128)S(1)}, f32[2,32,512]{2,1,0:T(8,128)S(1)}, f32[2,32,512]{2,1,0:T(8,128)S(1)}) custom-call(s32[2]{0:T(128)} %refs_0_, bf16[8,3,32,512]{3,2,1,0:T(8,128)(2,1)} %jitter_any.1, s32[3,32,512]{2,1,0:T(8,128)} %ids_any.1), custom_call_target="tpu_custom_call" | custom-call | flops 2097152 | bytes 4194304 | tf_op jit(solution)/shard_map/pallas_call | solution.py:376
  2.0 0.5 collective-permute-start
  2.5 5.1 %collective-permute-start.1 = (f32[2,8,32,512]{3,2,1,0:T(8,128)S(1)}, f32[2,8,32,512]{3,2,1,0:T(8,128)S(1)}, u32[]{:S(2)}, u32[]{:S(2)}) collective-permute-start(f32[2,8,32,512]{3,2,1,0:T(8,128)S(1)} %get-tuple-element.38.to_prev), channel_id=1, source_target_pairs={{1,0},{2,1},{3,2},{4,3},{5,4},{6,5},{7,6},{8,7},{9,8},{10,9},{11,1... | collective-permute-start | bytes 3145736 | tf_op jit(solution)/shard_map/ppermute | solution.py:425
  7.5 2.9 %shard_map.132 = (f32[3,8,32,512]{3,2,1,0:T(8,128)S(1)}, f32[8,32,512]{2,1,0:T(8,128)S(1)}, f32[6,32,512]{2,1,0:T(8,128)S(1)}, f32[6,32,512]{2,1,0:T(8,128)S(1)}) custom-call(s32[2]{0:T(128)} %refs_0_, s32[8,8]{1,0:T(8,128)} %refs_1_.1, f32[2,8,32,512]{3,2,1,0:T(8,128)S(1)} %get-tuple-element.37.to_next, f32[2,8,32,512]{3,2,1,0:T(8,128)S(1)} %get-tuple-element.38.to_prev), custom_call_target="tpu_custom_call" | custom-call | flops 16777216 | bytes 4194304 | tf_op jit(solution)/shard_map/pallas_call | solution.py:376
  10.4 0.0 copy-start
  10.4 9.7 %collective-permute-done.prev.refs_2_ = f32[2,8,32,512]{3,2,1,0:T(8,128)S(1)} collective-permute-done((f32[2,8,32,512]{3,2,1,0:T(8,128)S(1)}, f32[2,8,32,512]{3,2,1,0:T(8,128)S(1)}, u32[]{:S(2)}, u32[]{:S(2)}) %collective-permute-start) | collective-permute-done | bytes 1048608 | tf_op jit(solution)/shard_map/ppermute | solution.py:424
  20.0 0.0 copy-start.1
  20.1 0.0 collective-permute-done.1.nxt.refs_3_
  20.1 0.0 copy-start.2
  20.1 14.7 %collective-permute-start.4 = (f32[6,32,512]{2,1,0:T(8,128)S(1)}, f32[6,32,512]{2,1,0:T(8,128)S(1)}, u32[]{:S(2)}, u32[]{:S(2)}) collective-permute-start(f32[6,32,512]{2,1,0:T(8,128)S(1)} %get-tuple-element.51), channel_id=1, source_target_pairs={{0,1},{1,2},{2,3},{3,4},{4,5},{5,6},{6,7},{7,8},{8,9},{9,10},{10,1... | collective-permute-start | bytes 1179656 | tf_op jit(solution)/shard_map/ppermute | solution.py:445
  34.8 0.0 collective-permute-start.5
  34.8 0.5 collective-permute-start.2
  35.3 3.9 %collective-permute-start.3 = (f32[2,32,512]{2,1,0:T(8,128)S(1)}, f32[2,32,512]{2,1,0:T(8,128)S(1)}, u32[]{:S(2)}, u32[]{:S(2)}) collective-permute-start(f32[2,32,512]{2,1,0:T(8,128)S(1)} %get-tuple-element.44), channel_id=1, source_target_pairs={{1,0},{2,1},{3,2},{4,3},{5,4},{6,5},{7,6},{8,7},{9,8},{10,9},{11,1... | collective-permute-start | bytes 393224 | tf_op jit(solution)/shard_map/ppermute | solution.py:436
  39.2 7.2 %shard_map.133 = (f32[2,8,32,512]{3,2,1,0:T(8,128)S(1)}, f32[4,8,32,512]{3,2,1,0:T(8,128)S(1)}, f32[3,8,32,512]{3,2,1,0:T(8,128)S(1)}) custom-call(s32[8,8]{1,0:T(8,128)} %refs_1_.1, f32[2,8,32,512]{3,2,1,0:T(8,128)S(1)} %get-tuple-element.37.to_next, f32[2,8,32,512]{3,2,1,0:T(8,128)S(1)} %get-tuple-element.38.to_prev, ...), custom_call_target="tpu_custom_call" | custom-call | flops 33554432 | bytes 16777216 | tf_op jit(solution)/shard_map/pallas_call | solution.py:376
  46.4 0.0 copy-start.3
  46.4 0.0 copy-start.4
  46.4 0.0 copy-start.5
  46.4 0.0 collective-permute-done.2.prev3
  46.4 0.0 collective-permute-done.3.next3
  46.4 0.0 copy-done
  46.5 0.0 copy-done.1
  46.5 0.0 copy-done.2
  46.5 0.0 copy-start.7
  46.5 0.0 copy-start.8
  46.5 0.0 copy-start.9
  46.5 0.0 copy-start.10
  46.5 0.0 copy-start.11
  46.5 0.0 copy-start.12
  46.6 3.5 %shard_map.134 = (f32[16,48,128]{2,1,0:T(8,128)S(1)}, f32[2,3,32,512]{3,2,1,0:T(8,128)S(1)}) custom-call(s32[2]{0:T(128)} %refs_0_, s32[8,8]{1,0:T(8,128)} %refs_1_.1, f32[2,8,32,512]{3,2,1,0:T(8,128)S(1)} %collective-permute-done.prev.refs_2_, f32[2,8,32,512]{3,2,1,0:T(8,128)S(1)} %collective-permute-done.1.nxt.refs_3_, ...), custom_call_target="tpu_custom_call" | custom-call | flops 268435456 | bytes 8388608 | tf_op jit(solution)/shard_map/pallas_call | solution.py:376
  50.0 0.0 copy-done.3
  50.0 0.0 copy-done.4
  50.1 0.0 copy-done.5
  50.1 0.0 copy-start.6
  50.1 0.8 copy-done.6
  50.8 0.0 collective-permute-done.4.refs_4_
  50.9 0.0 copy-start.13
  50.9 0.0 collective-permute-done.5.refs_5_
  50.9 0.0 copy-start.14
  50.9 17.3 %all_to_all.10 = f32[16,48,128]{2,1,0:T(8,128)S(1)} all-to-all(f32[16,48,128]{2,1,0:T(8,128)S(1)} %get-tuple-element.56), channel_id=1, replica_groups=mesh['grp'=2,'gx'=16] {'gx'}, dimensions={0} | all-to-all | bytes 786432 | tf_op jit(solution)/shard_map/all_to_all | solution.py:465
  68.2 0.0 copy-done.7
  68.2 0.0 copy-done.8
  68.2 0.0 copy-done.9
  68.2 0.0 copy-done.10
  68.2 0.0 copy-done.11
  68.2 0.0 copy-done.12
  68.2 3.2 %shard_map.135 = f32[768,128]{1,0:T(8,128)} custom-call(f32[768,128]{1,0:T(8,128)S(1)} %bitcast.2, bf16[128,256]{1,0:T(8,128)(2,1)S(1)} %copy-done.10, bf16[128,256]{1,0:T(8,128)(2,1)S(1)} %copy-done.9, bf16[256,128]{1,0:T(8,128)(2,1)S(1)} %copy-done.8, bf16[256,128]{1,0:T(8,128)(2,1)S(1)} %copy-done.7, bf16[48,96]{1,0:T(8,128)(2,1)S(1)} %copy-done.12, ...), custom_call_target="tpu_custom_call" | custom-call | flops 268435456 | bytes 4194304 | tf_op jit(solution)/shard_map/pallas_call | solution.py:376
  71.4 3.6 %all-to-all-start.1 = ((f32[16,48,128]{2,1,0:T(8,128)}), f32[16,48,128]{2,1,0:T(8,128)S(1)}, u32[]{:S(2)}, u32[]{:S(2)}) async-start(f32[16,48,128]{2,1,0:T(8,128)} %bitcast.1), calls=%async_computation.1 | async-start | bytes 786432 | tf_op jit(solution)/shard_map/all_to_all | solution.py:485
  75.0 0.0 copy-done.13
  75.0 0.0 copy-done.14
  75.0 9.2 %shard_map.136 = f32[8,3,32,512]{3,2,1,0:T(8,128)} custom-call(s32[2]{0:T(128)} %refs_0_, s32[8,8]{1,0:T(8,128)} %refs_1_.1, f32[2,8,32,512]{3,2,1,0:T(8,128)} %copy-done.1, f32[2,8,32,512]{3,2,1,0:T(8,128)} %copy-done.2, f32[6,32,512]{2,1,0:T(8,128)} %copy-done.13, f32[6,32,512]{2,1,0:T(8,128)} %copy-done.14, f32[3,8,32,512]{3,2,1,0:T(8,128)} %copy-done, ...), custom_call_target="tpu_custom_call" | custom-call | flops 67108864 | bytes 16777216 | tf_op jit(solution)/shard_map/pallas_call | solution.py:376
  84.2 2.9 %all-to-all-done.1.returned = f32[16,48,128]{2,1,0:T(8,128)S(1)} async-done(((f32[16,48,128]{2,1,0:T(8,128)}), f32[16,48,128]{2,1,0:T(8,128)S(1)}, u32[]{:S(2)}, u32[]{:S(2)}) %all-to-all-start.1) | async-done | bytes 393248 | tf_op jit(solution)/shard_map/all_to_all | solution.py:485
  87.1 2.5 %shard_map.137 = f32[2,3,32,512]{3,2,1,0:T(8,128)} custom-call(f32[16,48,128]{2,1,0:T(8,128)S(1)} %all-to-all-done.1.returned, bf16[512,512]{1,0:T(8,128)(2,1)} %constant.16.clone.high_any, bf16[512,512]{1,0:T(8,128)(2,1)} %constant.17.clone.low_any), custom_call_target="tpu_custom_call" | custom-call | flops 268435456 | bytes 4194304 | tf_op jit(solution)/shard_map/pallas_call | solution.py:376
Async XLA Ops:
  2.0 18.1 %collective-permute-start = (f32[2,8,32,512]{3,2,1,0:T(8,128)S(1)}, f32[2,8,32,512]{3,2,1,0:T(8,128)S(1)}, u32[]{:S(2)}, u32[]{:S(2)}) collective-permute-start(f32[2,8,32,512]{3,2,1,0:T(8,128)S(1)} %get-tuple-element.37.to_next), channel_id=1, source_target_pairs={{0,1},{1,2},{2,3},{3,4},{4,5},{5,6},{6,7},{7,8},{8,9},{9,10},{10,1... | collective-permute-start | bytes 3145736 | tf_op jit(solution)/shard_map/ppermute | solution.py:424
  2.5 17.6 %collective-permute-start.1 = (f32[2,8,32,512]{3,2,1,0:T(8,128)S(1)}, f32[2,8,32,512]{3,2,1,0:T(8,128)S(1)}, u32[]{:S(2)}, u32[]{:S(2)}) collective-permute-start(f32[2,8,32,512]{3,2,1,0:T(8,128)S(1)} %get-tuple-element.38.to_prev), channel_id=1, source_target_pairs={{1,0},{2,1},{3,2},{4,3},{5,4},{6,5},{7,6},{8,7},{9,8},{10,9},{11,1... | collective-permute-start | bytes 3145736 | tf_op jit(solution)/shard_map/ppermute | solution.py:425
  10.4 36.1 %copy-start = (f32[3,8,32,512]{3,2,1,0:T(8,128)}, f32[3,8,32,512]{3,2,1,0:T(8,128)S(1)}, u32[]{:S(2)}) copy-start(f32[3,8,32,512]{3,2,1,0:T(8,128)S(1)} %get-tuple-element.63.rates.refs_6_) | copy-start | bytes 4718596
  20.0 26.4 %copy-start.1 = (f32[2,8,32,512]{3,2,1,0:T(8,128)}, f32[2,8,32,512]{3,2,1,0:T(8,128)S(1)}, u32[]{:S(2)}) copy-start(f32[2,8,32,512]{3,2,1,0:T(8,128)S(1)} %collective-permute-done.prev.refs_2_) | copy-start | bytes 3145732
  20.1 26.4 %copy-start.2 = (f32[2,8,32,512]{3,2,1,0:T(8,128)}, f32[2,8,32,512]{3,2,1,0:T(8,128)S(1)}, u32[]{:S(2)}) copy-start(f32[2,8,32,512]{3,2,1,0:T(8,128)S(1)} %collective-permute-done.1.nxt.refs_3_) | copy-start | bytes 3145732
  20.1 30.8 %collective-permute-start.4 = (f32[6,32,512]{2,1,0:T(8,128)S(1)}, f32[6,32,512]{2,1,0:T(8,128)S(1)}, u32[]{:S(2)}, u32[]{:S(2)}) collective-permute-start(f32[6,32,512]{2,1,0:T(8,128)S(1)} %get-tuple-element.51), channel_id=1, source_target_pairs={{0,1},{1,2},{2,3},{3,4},{4,5},{5,6},{6,7},{7,8},{8,9},{9,10},{10,1... | collective-permute-start | bytes 1179656 | tf_op jit(solution)/shard_map/ppermute | solution.py:445
  34.8 16.1 %collective-permute-start.5 = (f32[6,32,512]{2,1,0:T(8,128)S(1)}, f32[6,32,512]{2,1,0:T(8,128)S(1)}, u32[]{:S(2)}, u32[]{:S(2)}) collective-permute-start(f32[6,32,512]{2,1,0:T(8,128)S(1)} %get-tuple-element.52), channel_id=1, source_target_pairs={{1,0},{2,1},{3,2},{4,3},{5,4},{6,5},{7,6},{8,7},{9,8},{10,9},{11,1... | collective-permute-start | bytes 1179656 | tf_op jit(solution)/shard_map/ppermute | solution.py:446
  34.8 11.7 %collective-permute-start.2 = (f32[2,32,512]{2,1,0:T(8,128)S(1)}, f32[2,32,512]{2,1,0:T(8,128)S(1)}, u32[]{:S(2)}, u32[]{:S(2)}) collective-permute-start(f32[2,32,512]{2,1,0:T(8,128)S(1)} %get-tuple-element.43), channel_id=1, source_target_pairs={{0,1},{1,2},{2,3},{3,4},{4,5},{5,6},{6,7},{7,8},{8,9},{9,10},{10,1... | collective-permute-start | bytes 393224 | tf_op jit(solution)/shard_map/ppermute | solution.py:435
  35.3 11.2 %collective-permute-start.3 = (f32[2,32,512]{2,1,0:T(8,128)S(1)}, f32[2,32,512]{2,1,0:T(8,128)S(1)}, u32[]{:S(2)}, u32[]{:S(2)}) collective-permute-start(f32[2,32,512]{2,1,0:T(8,128)S(1)} %get-tuple-element.44), channel_id=1, source_target_pairs={{1,0},{2,1},{3,2},{4,3},{5,4},{6,5},{7,6},{8,7},{9,8},{10,9},{11,1... | collective-permute-start | bytes 393224 | tf_op jit(solution)/shard_map/ppermute | solution.py:436
  46.4 3.6 %copy-start.3 = (f32[4,8,32,512]{3,2,1,0:T(8,128)}, f32[4,8,32,512]{3,2,1,0:T(8,128)S(1)}, u32[]{:S(2)}) copy-start(f32[4,8,32,512]{3,2,1,0:T(8,128)S(1)} %get-tuple-element.65.eta1.refs_8_) | copy-start | bytes 6291460
  46.4 3.6 %copy-start.4 = (f32[3,8,32,512]{3,2,1,0:T(8,128)}, f32[3,8,32,512]{3,2,1,0:T(8,128)S(1)}, u32[]{:S(2)}) copy-start(f32[3,8,32,512]{3,2,1,0:T(8,128)S(1)} %get-tuple-element.66.eta2.refs_9_) | copy-start | bytes 4718596
  46.4 3.6 %copy-start.5 = (f32[2,8,32,512]{3,2,1,0:T(8,128)}, f32[2,8,32,512]{3,2,1,0:T(8,128)S(1)}, u32[]{:S(2)}) copy-start(f32[2,8,32,512]{3,2,1,0:T(8,128)S(1)} %get-tuple-element.64.edge_rates.refs_7_) | copy-start | bytes 3145732
  46.5 21.7 %copy-start.7 = (bf16[256,128]{1,0:T(8,128)(2,1)S(1)}, bf16[256,128]{1,0:T(8,128)(2,1)}, u32[]{:S(2)}) copy-start(bf16[256,128]{1,0:T(8,128)(2,1)} %constant.21.clone.refs_4_) | copy-start | bytes 196612
  46.5 21.7 %copy-start.8 = (bf16[256,128]{1,0:T(8,128)(2,1)S(1)}, bf16[256,128]{1,0:T(8,128)(2,1)}, u32[]{:S(2)}) copy-start(bf16[256,128]{1,0:T(8,128)(2,1)} %constant.20.clone.refs_3_) | copy-start | bytes 196612
  46.5 21.7 %copy-start.9 = (bf16[128,256]{1,0:T(8,128)(2,1)S(1)}, bf16[128,256]{1,0:T(8,128)(2,1)}, u32[]{:S(2)}) copy-start(bf16[128,256]{1,0:T(8,128)(2,1)} %constant.19.clone.refs_2_) | copy-start | bytes 196612
  46.5 21.7 %copy-start.10 = (bf16[128,256]{1,0:T(8,128)(2,1)S(1)}, bf16[128,256]{1,0:T(8,128)(2,1)}, u32[]{:S(2)}) copy-start(bf16[128,256]{1,0:T(8,128)(2,1)} %constant.18.clone.refs_1_) | copy-start | bytes 196612
  46.5 21.7 %copy-start.11 = (bf16[48,96]{1,0:T(8,128)(2,1)S(1)}, bf16[48,96]{1,0:T(8,128)(2,1)}, u32[]{:S(2)}) copy-start(bf16[48,96]{1,0:T(8,128)(2,1)} %constant.23.clone.refs_6_) | copy-start | bytes 27652
  46.5 21.7 %copy-start.12 = (bf16[48,96]{1,0:T(8,128)(2,1)S(1)}, bf16[48,96]{1,0:T(8,128)(2,1)}, u32[]{:S(2)}) copy-start(bf16[48,96]{1,0:T(8,128)(2,1)} %constant.22.clone.refs_5_) | copy-start | bytes 27652
  50.1 0.8 copy-start.6
  50.9 24.1 %copy-start.13 = (f32[6,32,512]{2,1,0:T(8,128)}, f32[6,32,512]{2,1,0:T(8,128)S(1)}, u32[]{:S(2)}) copy-start(f32[6,32,512]{2,1,0:T(8,128)S(1)} %collective-permute-done.4.refs_4_) | copy-start | bytes 1179652
  50.9 24.1 %copy-start.14 = (f32[6,32,512]{2,1,0:T(8,128)}, f32[6,32,512]{2,1,0:T(8,128)S(1)}, u32[]{:S(2)}) copy-start(f32[6,32,512]{2,1,0:T(8,128)S(1)} %collective-permute-done.5.refs_5_) | copy-start | bytes 1179652
  71.4 15.7 %all-to-all-start.1 = ((f32[16,48,128]{2,1,0:T(8,128)}), f32[16,48,128]{2,1,0:T(8,128)S(1)}, u32[]{:S(2)}, u32[]{:S(2)}) async-start(f32[16,48,128]{2,1,0:T(8,128)} %bitcast.1), calls=%async_computation.1 | async-start | bytes 786432 | tf_op jit(solution)/shard_map/all_to_all | solution.py:485

commit v4 on v3

--- a/solution.py
+++ b/solution.py
@@ -85,23 +85,23 @@
     low, high = jnp.minimum(first, second), jnp.maximum(first, second)
 
     def other(r):
-        i = r + (r >= low).astype(jnp.int32)
-        return i + (i >= high).astype(jnp.int32)
+        i = jnp.where(r >= low, r + 1, r)
+        return jnp.where(i >= high, i + 1, i)
 
     return other
 
 
-def start_kernel(chosen_any, jitter_any, ids_any, to_next, to_prev, c0, c2, chosen, jitter, grain_ids, semaphores):
+def start_kernel(chosen_any, jitter_any, ids_any, p0, p2, up2, down2, chosen, jitter, grain_ids, semaphores):
     planes = grain_ids.shape[0]
     pairs = []
-    for k in range(planes):
+    for k in (2, 0, 1):
         pairs.append((jitter_any.at[:, k], jitter.at[:, k]))
         pairs.append((ids_any.at[k], grain_ids.at[k]))
     pairs.append((chosen_any, chosen))
     copies = fetch(pairs, semaphores)
-    for plane, outs in enumerate(((to_prev.at[0],), (to_prev.at[1], to_next.at[0]), (to_next.at[1],))):
-        copies[2 * plane].wait()
-        copies[2 * plane + 1].wait()
+    for step, (plane, outs) in enumerate(((2, (p2,)), (0, (p0,)), (1, (up2, down2)))):
+        copies[2 * step].wait()
+        copies[2 * step + 1].wait()
         ids = grain_ids[plane]
         for i in range(GRAINS):
             base = jnp.where(ids == i, jnp.float32(0.6), jnp.float32(0.0))
@@ -110,9 +110,8 @@
                 out[i] = value
     copies[-1].wait()
     for k, i in enumerate(pair_of(chosen)):
-        c0[k] = to_prev[0, i]
-        c2[k] = to_next[1, i]
-
+        up2[GRAINS + k] = p0[i]
+        down2[GRAINS + k] = p2[i]
 
 def grain_of(start):
     ids = jnp.where(start[1] > 0.55, 1, 0)
@@ -166,69 +165,64 @@
     lax.fori_loop(0, GRAINS, body, 0)
 
 
-def inner_kernel(chosen_any, classes_any, to_next, to_prev, rates, middle, r0, r2, chosen, classes, semaphores):
+def inner_kernel(chosen_any, classes_any, p0, p2, up2, rates, middle, r0, r2, chosen, classes, semaphores):
     copies = fetch(((chosen_any, chosen), (classes_any, classes)), semaphores)
-    row = (to_prev.at[0], to_prev.at[1], to_next.at[1])
+    row = (p0, up2, p2)
     for copy in copies:
         copy.wait()
     other = others_of(chosen)
-
-    def body(r, carry):
+    for r in range(GRAINS - 2):
         i = other(r)
-        r0[r] = to_prev[0, i]
-        r2[r] = to_next[1, i]
-        return carry
-
-    lax.fori_loop(0, GRAINS - 2, body, 0)
+        r0[r] = p0[i]
+        r2[r] = p2[i]
     for k in range(3):
         rates_plane(classes, row[k], rates.at[k])
-    step_plane(row[1], row[0], row[2], rates.at[1], middle)
+    step_plane(up2, p0, p2, rates.at[1], middle)
 
 
 def near_kernel(
-    classes_any, to_next, to_prev, prev, nxt, rates, middle, edge_rates, eta1, eta2, classes, semaphores
+    classes_any, p0, p2, up2, prev1, next1, rates, middle, edge_rates, inner1, middle2, classes, semaphores
 ):
     copies = fetch(((classes_any, classes),), semaphores)
-    p0, p1, p2 = to_prev.at[0], to_prev.at[1], to_next.at[1]
-    step_plane(p0, prev.at[1], p1, rates.at[0], eta1.at[1])
-    step_plane(p2, p1, nxt.at[0], rates.at[2], eta1.at[2])
+    step_plane(p0, prev1, up2, rates.at[0], inner1.at[0])
+    step_plane(p2, up2, next1, rates.at[2], inner1.at[1])
     copies[0].wait()
-    rates_plane(classes, prev.at[1], edge_rates.at[0])
-    rates_plane(classes, nxt.at[0], edge_rates.at[1])
-    step_plane(middle, eta1.at[1], eta1.at[2], rates.at[1], eta2.at[1])
-    step_plane(prev.at[1], prev.at[0], p0, edge_rates.at[0], eta1.at[0])
-    step_plane(nxt.at[0], p2, nxt.at[1], edge_rates.at[1], eta1.at[3])
-    step_plane(eta1.at[1], eta1.at[0], middle, rates.at[0], eta2.at[0])
-    step_plane(eta1.at[2], middle, eta1.at[3], rates.at[2], eta2.at[2])
+    rates_plane(classes, prev1, edge_rates.at[0])
+    rates_plane(classes, next1, edge_rates.at[1])
+    step_plane(middle, inner1.at[0], inner1.at[1], rates.at[1], middle2)
 
 
 def pair_kernel(
-    chosen_any, classes_any, prev, nxt, prev3, next3, rates, edge_rates, eta1, eta2, high_any, low_any,
-    packed, final, chosen, classes, high, low, edge, fields, semaphores,
+    chosen_any, classes_any, p0, p2, prev1, next1, prev2, next2, rates, edge_rates, middle, inner1, middle2,
+    high_any, low_any, packed, outer1, side2, final_any, chosen, classes, high, low, edge, fields, final, semaphores,
 ):
     copies = fetch(
         ((chosen_any, chosen), (classes_any, classes), (high_any, high), (low_any, low)), semaphores
     )
+    step_plane(prev1, prev2, p0, edge_rates.at[0], outer1.at[0])
+    step_plane(next1, p2, next2, edge_rates.at[1], outer1.at[1])
+    step_plane(inner1.at[0], outer1.at[0], middle, rates.at[0], side2.at[0])
+    step_plane(inner1.at[1], middle, outer1.at[1], rates.at[2], side2.at[1])
+    eta2 = (side2.at[0], middle2, side2.at[1])
     depth, width = final.shape[2:]
-    totals = [squares(eta2.at[k]) for k in range(3)]
+    totals = [squares(state) for state in eta2]
     copies[0].wait()
     copies[1].wait()
     pair = pair_of(chosen)
-    for side, (far, mid, near) in enumerate(((prev3, prev.at[0], prev.at[1]), (next3, nxt.at[1], nxt.at[0]))):
-        inner, neighbour = (0, 1) if side == 0 else (3, 2)
+    for side, (mid, near) in enumerate(((prev2, prev1), (next2, next1))):
         ids = grain_of(mid)
         total0 = squares(mid)
-        total1 = squares(eta1.at[inner])
+        total1 = squares(outer1.at[side])
         for k, i in enumerate(pair):
-            first = update(mid[i], far[k], near[i], total0, rate(classes, ids, i))
-            edge[side, k] = update(eta1[inner, i], first, eta1[neighbour, i], total1, edge_rates[side, i])
+            first = update(mid[i], mid[GRAINS + k], near[i], total0, rate(classes, ids, i))
+            edge[side, k] = update(outer1[side, i], first, inner1[side, i], total1, edge_rates[side, i])
     repeated = chosen[1] == chosen[0]
     for k in range(3):
         values = []
         for f, i in enumerate(pair):
-            before = edge[0, f] if k == 0 else eta2[k - 1, i]
-            after = edge[1, f] if k == 2 else eta2[k + 1, i]
-            value = update(eta2[k, i], before, after, totals[k], rates[k, i])
+            before = edge[0, f] if k == 0 else eta2[k - 1][i]
+            after = edge[1, f] if k == 2 else eta2[k + 1][i]
+            value = update(eta2[k][i], before, after, totals[k], rates[k, i])
             final[f, k] = value
             values.append(value)
         values[1] = jnp.where(repeated, values[0], values[1])
@@ -236,6 +230,8 @@
             base = k * 4 * depth + f * depth
             fields[base : base + depth] = values[f]
             fields[base + 2 * depth : base + 3 * depth] = values[f]
+    out_copy = pltpu.make_async_copy(final, final_any, semaphores.at[4])
+    out_copy.start()
     copies[2].wait()
     copies[3].wait()
     full = dot3((high[...], low[...]), split(fields[...]), ((1,), (1,)))
@@ -251,36 +247,45 @@
             devices, rows, _ = packed.shape
             rows = rows // 3
             packed[:, k * rows : (k + 1) * rows, :] = part.reshape(devices, rows, lanes)
+    out_copy.wait()
 
 
 def rest_kernel(*refs):
-    sources, out, targets, edge, semaphores = refs[:11], refs[11], refs[12:23], refs[23], refs[24]
-    for copy in fetch(list(zip(sources, targets)), semaphores):
+    count = (len(refs) - 3) // 2
+    sources, out, targets = refs[:count], refs[count], refs[count + 1 : 2 * count + 1]
+    edge, semaphores = refs[-2:]
+    copies = fetch(list(zip(sources, targets)), semaphores)
+    (
+        chosen, classes, prev2, prev1, prev3, next2, next1, next3, outer1, inner1, edge_rates,
+        middle2, side2, rates, final,
+    ) = targets
+    for copy in copies[:11]:
         copy.wait()
-    chosen, classes, prev, nxt, prev3, next3, rates, edge_rates, eta1, eta2, final = targets
     other = others_of(chosen)
     rest = GRAINS - 2
-    for side, (far, mid, near) in enumerate(((prev3, prev.at[0], prev.at[1]), (next3, nxt.at[1], nxt.at[0]))):
-        inner, neighbour = (0, 1) if side == 0 else (3, 2)
+    for side, (far, mid, near) in enumerate(((prev3, prev2, prev1), (next3, next2, next1))):
         ids = grain_of(mid)
         total0 = squares(mid)
-        total1 = squares(eta1.at[inner])
+        total1 = squares(outer1.at[side])
 
         def body(r, carry):
             i = other(r)
             first = update(mid[i], far[r], near[i], total0, rate(classes, ids, i))
-            edge[side, r] = update(eta1[inner, i], first, eta1[neighbour, i], total1, edge_rates[side, i])
+            edge[side, r] = update(outer1[side, i], first, inner1[side, i], total1, edge_rates[side, i])
             return carry
 
         lax.fori_loop(0, rest, body, 0)
+    for copy in copies[11:]:
+        copy.wait()
+    eta2 = (side2.at[0], middle2, side2.at[1])
     for k in range(3):
-        total = squares(eta2.at[k])
+        total = squares(eta2[k])
 
         def last(r, carry):
             i = other(r)
-            before = edge[0, r] if k == 0 else eta2[k - 1, i]
-            after = edge[1, r] if k == 2 else eta2[k + 1, i]
-            out[i, k] = update(eta2[k, i], before, after, total, rates[k, i])
+            before = edge[0, r] if k == 0 else eta2[k - 1][i]
+            after = edge[1, r] if k == 2 else eta2[k + 1][i]
+            out[i, k] = update(eta2[k][i], before, after, total, rates[k, i])
             return carry
 
         lax.fori_loop(0, rest, last, 0)
@@ -372,12 +377,12 @@
             out[f, k] = result[base : base + depth]
 
 
-def call(kernel, outs, in_specs, *args, scratch=(), flops=0, moved=0, limit=12):
+def call(kernel, outs, in_specs, *args, scratch=(), flops=0, moved=0, limit=12, out_specs=None):
     return pl.pallas_call(
         kernel,
         out_shape=outs,
         in_specs=in_specs,
-        out_specs=jax.tree.map(lambda _: VMEM, outs),
+        out_specs=out_specs or jax.tree.map(lambda _: VMEM, outs),
         scratch_shapes=scratch,
         compiler_params=pltpu.CompilerParams(vmem_limit_bytes=limit * MIB),
         cost_estimate=pl.CostEstimate(flops=flops, bytes_accessed=moved, transcendentals=0),
@@ -408,9 +413,10 @@
     two = (2, *plane)
     six = (GRAINS - 2, depth, width)
     small = [pltpu.SMEM((2,), jnp.int32), pltpu.SMEM((GRAINS, GRAINS), jnp.int32)]
-    to_next, to_prev, c0, c2 = call(
+    ten = (GRAINS + 2, depth, width)
+    p0, p2, up2, down2 = call(
         start_kernel,
-        (shape(*two), shape(*two), shape(2, depth, width), shape(2, depth, width)),
+        (shape(*plane), shape(*plane), shape(*ten), shape(*ten)),
         [ANY] * 3,
         chosen, jitter, grain_ids,
         scratch=[
@@ -421,46 +427,47 @@
         ],
         flops=2**21, moved=2**22,
     )
-    prev = lax.ppermute(to_next, "gx", up)
-    nxt = lax.ppermute(to_prev, "gx", down)
+    prev1 = lax.ppermute(p2, "gx", up)
+    next1 = lax.ppermute(p0, "gx", down)
+    prev2 = lax.ppermute(up2, "gx", up)
+    next2 = lax.ppermute(down2, "gx", down)
     rates, middle, r0, r2 = call(
         inner_kernel,
         (shape(planes, *plane), shape(*plane), shape(*six), shape(*six)),
-        [ANY] * 2 + [VMEM] * 2,
-        chosen, class_table, to_next, to_prev,
+        [ANY] * 2 + [VMEM] * 3,
+        chosen, class_table, p0, p2, up2,
         scratch=[*small, pltpu.SemaphoreType.DMA((2,))],
         flops=2**24, moved=2**22,
     )
-    c0, c2, r0, r2, prev, nxt = lax.optimization_barrier((c0, c2, r0, r2, prev, nxt))
-    prev3 = lax.ppermute(c0, "gx", up)
-    next3 = lax.ppermute(c2, "gx", down)
-    edge_rates, eta1, eta2 = call(
+    prev3 = lax.ppermute(r0, "gx", up)
+    next3 = lax.ppermute(r2, "gx", down)
+    edge_rates, inner1, middle2 = call(
         near_kernel,
-        (shape(*two), shape(4, *plane), shape(planes, *plane)),
-        [ANY] + [VMEM] * 6,
-        class_table, to_next, to_prev, prev, nxt, rates, middle,
+        (shape(*two), shape(*two), shape(*plane)),
+        [ANY] + [VMEM] * 7,
+        class_table, p0, p2, up2, prev1, next1, rates, middle,
         scratch=[small[1], pltpu.SemaphoreType.DMA((1,))],
         flops=2**25, moved=2**24,
     )
-    prev3_rest = lax.ppermute(r0, "gx", up)
-    next3_rest = lax.ppermute(r2, "gx", down)
     packed_shape = (devices, planes * share, lanes) if aligned else (planes, slots, lanes)
-    packed, final = call(
+    packed, outer1, side2, final = call(
         pair_kernel,
-        (shape(*packed_shape), shape(2, planes, depth, width)),
-        [ANY] * 2 + [VMEM] * 8 + [ANY] * 2,
-        chosen, class_table, prev, nxt, prev3, next3, rates, edge_rates, eta1, eta2, *table,
+        (shape(*packed_shape), shape(*two), shape(*two), shape(2, planes, depth, width)),
+        [ANY] * 2 + [VMEM] * 11 + [ANY] * 2,
+        chosen, class_table, p0, p2, prev1, next1, prev2, next2, rates, edge_rates, middle, inner1, middle2, *table,
         scratch=[
             *small,
             pltpu.VMEM(table[0].shape, BF16),
             pltpu.VMEM(table[1].shape, BF16),
             pltpu.VMEM((2, 2, depth, width), F32),
             pltpu.VMEM((planes * lanes, width), F32),
-            pltpu.SemaphoreType.DMA((4,)),
+            pltpu.VMEM((2, planes, depth, width), F32),
+            pltpu.SemaphoreType.DMA((5,)),
         ],
+        out_specs=(VMEM, VMEM, VMEM, ANY),
         flops=2**28, moved=2**23,
     )
-    packed, prev3_rest, next3_rest = lax.optimization_barrier((packed, prev3_rest, next3_rest))
+    packed, prev3, next3 = lax.optimization_barrier((packed, prev3, next3))
     if aligned:
         lines = lax.all_to_all(packed, "gx", split_axis=0, concat_axis=0, tiled=True)
     else:
@@ -486,18 +493,21 @@
     if not aligned:
         returned = returned.reshape(devices, planes, share, lanes).transpose(1, 0, 2, 3)
         returned = returned.reshape(planes, slots, lanes)
-    late = (chosen, class_table, prev, nxt, prev3_rest, next3_rest, rates, edge_rates, eta1, eta2, final)
+    late = (
+        chosen, class_table, prev2, prev1, prev3, next2, next1, next3, outer1, inner1, edge_rates,
+        middle2, side2, rates, final,
+    )
     late, _ = lax.optimization_barrier((late, back))
     order_params = call(
         rest_kernel,
         shape(GRAINS, planes, depth, width),
-        [ANY] * 11,
+        [ANY] * len(late),
         *late,
         scratch=[
             *small,
             *[pltpu.VMEM(value.shape, F32) for value in late[2:]],
             pltpu.VMEM((2, *six), F32),
-            pltpu.SemaphoreType.DMA((11,)),
+            pltpu.SemaphoreType.DMA((len(late),)),
         ],
         flops=2**26, moved=2**24, limit=24,
     )

time: 90.1 us -> 85.9 us (0.953)
  blocking collectives: 17.3 us -> 32 us
  starting transfers between devices: 28.3 us -> 18 us
  waiting for transfers between devices: 12.6 us -> 5.82 us
  Pallas kernels: 29.8 us -> 27.7 us
    all_to_all x1, blocking collectives: 17.3 us -> 32 us  [shards(): lax.all_to_all(packed, 'gx', split_axis=0, concat_axis=0, tiled=True)]
    ppermute x6, starting transfers between devices: 24.7 us -> 14.5 us  [the longest x1 5.06 us: shards(): next2 = lax.ppermute(down2, 'gx', down)]
    ppermute x6, waiting for transfers between devices: 9.67 us -> 1.96 us  [the longest x1 1.95 us: shards(): next1 = lax.ppermute(p0, 'gx', down)]
    pallas_call x7, Pallas kernels: 29.8 us -> 27.7 us  [call(): pl.pallas_call(kernel, out_shape=outs, in_specs=in_specs, out_specs=out_s...]
    all_to_all x1, waiting for transfers between devices: 2.94 us -> 3.86 us  [shards(): lax.all_to_all(back, 'gx', split_axis=0, concat_axis=0, tiled=True)]
  transfers between devices with their start and end apart: 7 -> 7, of which waited for: 2 -> 2; matrix products, arithmetic and copies ran while one was open for 0% -> 0% of each run, Pallas kernels for 25% -> 24%
where the time goes in v4:
time: 85.9 us; the launch traced here: 85.6 us
  blocking collectives  32 us (37%)
  Pallas kernels  27.7 us (32%)
  starting transfers between devices  18 us (21%)
  waiting for transfers between devices  5.82 us (7%)
  local copies, waits for them, and re-layouts  1.09 us (1%)
  between operations  0.95 us (1%)
    all_to_all x1, blocking collectives, shards(): lax.all_to_all(packed, 'gx', split_axis=0, concat_axis=0, tiled=True)  32 us
    pallas_call x7, Pallas kernels, call(): pl.pallas_call(kernel, out_shape=outs, in_specs=in_specs, out_specs=out_s...  27.7 us
    ppermute x1, starting transfers between devices, shards(): next2 = lax.ppermute(down2, 'gx', down)  5.06 us
    ppermute x1, starting transfers between devices, shards(): next1 = lax.ppermute(p0, 'gx', down)  4.44 us
    ppermute x1, starting transfers between devices, shards(): next3 = lax.ppermute(r2, 'gx', down)  4.41 us
    all_to_all x1, waiting for transfers between devices, shards(): lax.all_to_all(back, 'gx', split_axis=0, concat_axis=0, tiled=True)  3.86 us
    all_to_all x1, starting transfers between devices, shards(): lax.all_to_all(back, 'gx', split_axis=0, concat_axis=0, tiled=True)  3.56 us
    ppermute x1, waiting for transfers between devices, shards(): next1 = lax.ppermute(p0, 'gx', down)  1.95 us
  transfers between devices with their start and end apart: 7, of which 2 were waited for; matrix products, arithmetic and copies ran while one was open for 0% of the time, Pallas kernels for 24%

profile of v4, /device:TPU:0, one launch (start us, length us, event | category | flops | bytes accessed | tf_op | source)
XLA Modules:
  0.0 85.6 jit_solution(10520794583185758561)
XLA Ops:
  0.6 1.3 %shard_map.131 = (f32[8,32,512]{2,1,0:T(8,128)S(1)}, f32[8,32,512]{2,1,0:T(8,128)S(1)}, f32[10,32,512]{2,1,0:T(8,128)S(1)}, f32[10,32,512]{2,1,0:T(8,128)S(1)}) custom-call(s32[2]{0:T(128)} %refs_0_, bf16[8,3,32,512]{3,2,1,0:T(8,128)(2,1)} %jitter_any.1, s32[3,32,512]{2,1,0:T(8,128)} %ids_any.1), custom_call_target="tpu_custom_call" | custom-call | flops 2097152 | bytes 4194304 | tf_op jit(solution)/shard_map/pallas_call | solution.py:381
  2.0 0.5 collective-permute-start.1
  2.5 5.1 %collective-permute-start.3 = (f32[10,32,512]{2,1,0:T(8,128)S(1)}, f32[10,32,512]{2,1,0:T(8,128)S(1)}, u32[]{:S(2)}, u32[]{:S(2)}) collective-permute-start(f32[10,32,512]{2,1,0:T(8,128)S(1)} %get-tuple-element.38), channel_id=1, source_target_pairs={{1,0},{2,1},{3,2},{4,3},{5,4},{6,5},{7,6},{8,7},{9,8},{10,9},{11,1... | collective-permute-start | bytes 1966088 | tf_op jit(solution)/shard_map/ppermute | solution.py:433
  7.5 0.0 collective-permute-start
  7.5 4.4 %collective-permute-start.2 = (f32[8,32,512]{2,1,0:T(8,128)S(1)}, f32[8,32,512]{2,1,0:T(8,128)S(1)}, u32[]{:S(2)}, u32[]{:S(2)}) collective-permute-start(f32[8,32,512]{2,1,0:T(8,128)S(1)} %get-tuple-element.37.p0), channel_id=1, source_target_pairs={{1,0},{2,1},{3,2},{4,3},{5,4},{6,5},{7,6},{8,7},{9,8},{10,9},{11,1... | collective-permute-start | bytes 1572872 | tf_op jit(solution)/shard_map/ppermute | solution.py:431
  12.0 2.8 %shard_map.132 = (f32[3,8,32,512]{3,2,1,0:T(8,128)S(1)}, f32[8,32,512]{2,1,0:T(8,128)S(1)}, f32[6,32,512]{2,1,0:T(8,128)S(1)}, f32[6,32,512]{2,1,0:T(8,128)S(1)}) custom-call(s32[2]{0:T(128)} %refs_0_, s32[8,8]{1,0:T(8,128)} %refs_1_.1, f32[8,32,512]{2,1,0:T(8,128)S(1)} %get-tuple-element.37.p0, f32[8,32,512]{2,1,0:T(8,128)S(1)} %get-tuple-element.36.p2, ...), custom_call_target="tpu_custom_call" | custom-call | flops 16777216 | bytes 4194304 | tf_op jit(solution)/shard_map/pallas_call | solution.py:381
  14.8 0.0 copy-start
  14.8 0.1 collective-permute-start.4
  14.9 0.0 collective-permute-done.1.prev1.refs_3_
  14.9 0.0 copy-start.1
  14.9 4.4 %collective-permute-start.5 = (f32[6,32,512]{2,1,0:T(8,128)S(1)}, f32[6,32,512]{2,1,0:T(8,128)S(1)}, u32[]{:S(2)}, u32[]{:S(2)}) collective-permute-start(f32[6,32,512]{2,1,0:T(8,128)S(1)} %get-tuple-element.46), channel_id=1, source_target_pairs={{1,0},{2,1},{3,2},{4,3},{5,4},{6,5},{7,6},{8,7},{9,8},{10,9},{11,1... | collective-permute-start | bytes 1179656 | tf_op jit(solution)/shard_map/ppermute | solution.py:443
  19.3 1.9 %collective-permute-done.2.next1.refs_6_ = f32[8,32,512]{2,1,0:T(8,128)S(1)} collective-permute-done((f32[8,32,512]{2,1,0:T(8,128)S(1)}, f32[8,32,512]{2,1,0:T(8,128)S(1)}, u32[]{:S(2)}, u32[]{:S(2)}) %collective-permute-start.2) | collective-permute-done | bytes 524320 | tf_op jit(solution)/shard_map/ppermute | solution.py:431
  21.2 0.0 copy-start.2
  21.3 3.5 %shard_map.133 = (f32[2,8,32,512]{3,2,1,0:T(8,128)S(1)}, f32[2,8,32,512]{3,2,1,0:T(8,128)S(1)}, f32[8,32,512]{2,1,0:T(8,128)S(1)}) custom-call(s32[8,8]{1,0:T(8,128)} %refs_1_.1, f32[8,32,512]{2,1,0:T(8,128)S(1)} %get-tuple-element.37.p0, f32[8,32,512]{2,1,0:T(8,128)S(1)} %get-tuple-element.36.p2, f32[10,32,512]{2,1,0:T(8,128)S(1)} %get-tuple-element.35.up2, ...), custom_call_target="tpu_custom_call" | custom-call | flops 33554432 | bytes 16777216 | tf_op jit(solution)/shard_map/pallas_call | solution.py:381
  24.7 0.0 copy-start.3
  24.8 0.0 copy-start.4
  24.8 0.0 copy-start.7
  24.8 0.0 collective-permute-done.3.next2.refs_5_
  24.8 0.0 copy-start.5
  24.8 0.0 collective-permute-done.prev2.refs_2_
  24.8 0.0 copy-start.6
  24.8 0.0 copy-done
  24.8 0.0 copy-done.1
  24.8 0.0 copy-done.2
  24.9 0.0 copy-start.11
  24.9 0.0 copy-start.12
  24.9 0.0 copy-start.13
  24.9 0.0 copy-start.14
  24.9 0.0 copy-start.15
  24.9 0.0 copy-start.16
  24.9 6.0 %shard_map.134 = (f32[16,48,128]{2,1,0:T(8,128)S(1)}, f32[2,8,32,512]{3,2,1,0:T(8,128)S(1)}, f32[2,8,32,512]{3,2,1,0:T(8,128)S(1)}, f32[2,3,32,512]{3,2,1,0:T(8,128)S(1)}) custom-call(s32[2]{0:T(128)} %refs_0_, s32[8,8]{1,0:T(8,128)} %refs_1_.1, f32[8,32,512]{2,1,0:T(8,128)S(1)} %get-tuple-element.37.p0, f32[8,32,512]{2,1,0:T(8,128)S(1)} %get-tuple-element.36.p2, ...), custom_call_target="tpu_custom_call" | custom-call | flops 268435456 | bytes 8388608 | tf_op jit(solution)/shard_map/pallas_call | solution.py:381
  30.9 0.0 copy-done.3
  31.0 0.0 copy-done.4
  31.0 0.0 copy-done.7
  31.0 0.0 copy-done.5
  31.0 0.0 copy-done.6
  31.0 0.0 copy-start.9
  31.0 1.0 %copy-done.9 = f32[2,8,32,512]{3,2,1,0:T(8,128)} copy-done((f32[2,8,32,512]{3,2,1,0:T(8,128)}, f32[2,8,32,512]{3,2,1,0:T(8,128)S(1)}, u32[]{:S(2)}) %copy-start.9) | copy-done | bytes 1048600
  32.0 0.0 copy-start.8
  32.0 0.0 copy-start.10
  32.0 0.0 collective-permute-done.4.refs_4_
  32.0 0.0 copy-start.17
  32.0 0.0 collective-permute-done.5.refs_7_
  32.0 0.0 copy-start.18
  32.0 32.0 %all_to_all.10 = f32[16,48,128]{2,1,0:T(8,128)S(1)} all-to-all(f32[16,48,128]{2,1,0:T(8,128)S(1)} %get-tuple-element.52), channel_id=1, replica_groups=mesh['grp'=2,'gx'=16] {'gx'}, dimensions={0} | all-to-all | bytes 786432 | tf_op jit(solution)/shard_map/all_to_all | solution.py:472
  64.0 0.0 copy-done.17
  64.0 0.0 copy-done.11
  64.0 0.0 copy-done.12
  64.0 0.0 copy-done.13
  64.1 0.0 copy-done.14
  64.1 0.0 copy-done.15
  64.1 0.0 copy-done.16
  64.1 3.2 %shard_map.135 = f32[768,128]{1,0:T(8,128)} custom-call(f32[768,128]{1,0:T(8,128)S(1)} %bitcast.2, bf16[128,256]{1,0:T(8,128)(2,1)S(1)} %copy-done.14, bf16[128,256]{1,0:T(8,128)(2,1)S(1)} %copy-done.13, bf16[256,128]{1,0:T(8,128)(2,1)S(1)} %copy-done.12, bf16[256,128]{1,0:T(8,128)(2,1)S(1)} %copy-done.11, bf16[48,96]{1,0:T(8,128)(2,1)S(1)} %copy-done.16, ...), custom_call_target="tpu_custom_call" | custom-call | flops 268435456 | bytes 4194304 | tf_op jit(solution)/shard_map/pallas_call | solution.py:381
  67.3 0.0 copy-done.8
  67.3 0.0 copy-done.10
  67.3 0.0 copy-done.18
  67.3 3.6 %all-to-all-start.1 = ((f32[16,48,128]{2,1,0:T(8,128)}), f32[16,48,128]{2,1,0:T(8,128)S(1)}, u32[]{:S(2)}, u32[]{:S(2)}) async-start(f32[16,48,128]{2,1,0:T(8,128)} %bitcast.1), calls=%async_computation.1 | async-start | bytes 786432 | tf_op jit(solution)/shard_map/all_to_all | solution.py:492
  70.9 8.3 %shard_map.136 = f32[8,3,32,512]{3,2,1,0:T(8,128)} custom-call(s32[2]{0:T(128)} %refs_0_, s32[8,8]{1,0:T(8,128)} %refs_1_.1, f32[10,32,512]{2,1,0:T(8,128)} %copy-done.6, f32[8,32,512]{2,1,0:T(8,128)} %copy-done.1, f32[6,32,512]{2,1,0:T(8,128)} %copy-done.17, f32[10,32,512]{2,1,0:T(8,128)} %copy-done.5, f32[8,32,512]{2,1,0:T(8,128)} %copy-done.2, ...), custom_call_target="tpu_custom_call" | custom-call | flops 67108864 | bytes 16777216 | tf_op jit(solution)/shard_map/pallas_call | solution.py:381
  79.2 3.9 %all-to-all-done.1.returned = f32[16,48,128]{2,1,0:T(8,128)S(1)} async-done(((f32[16,48,128]{2,1,0:T(8,128)}), f32[16,48,128]{2,1,0:T(8,128)S(1)}, u32[]{:S(2)}, u32[]{:S(2)}) %all-to-all-start.1) | async-done | bytes 393248 | tf_op jit(solution)/shard_map/all_to_all | solution.py:492
  83.1 2.5 %shard_map.137 = f32[2,3,32,512]{3,2,1,0:T(8,128)} custom-call(f32[16,48,128]{2,1,0:T(8,128)S(1)} %all-to-all-done.1.returned, bf16[512,512]{1,0:T(8,128)(2,1)} %constant.16.clone.high_any, bf16[512,512]{1,0:T(8,128)(2,1)} %constant.17.clone.low_any), custom_call_target="tpu_custom_call" | custom-call | flops 268435456 | bytes 4194304 | tf_op jit(solution)/shard_map/pallas_call | solution.py:381
Async XLA Ops:
  2.0 12.9 %collective-permute-start.1 = (f32[8,32,512]{2,1,0:T(8,128)S(1)}, f32[8,32,512]{2,1,0:T(8,128)S(1)}, u32[]{:S(2)}, u32[]{:S(2)}) collective-permute-start(f32[8,32,512]{2,1,0:T(8,128)S(1)} %get-tuple-element.36.p2), channel_id=1, source_target_pairs={{0,1},{1,2},{2,3},{3,4},{4,5},{5,6},{6,7},{7,8},{8,9},{9,10},{10,1... | collective-permute-start | bytes 1572872 | tf_op jit(solution)/shard_map/ppermute | solution.py:430
  2.5 22.3 %collective-permute-start.3 = (f32[10,32,512]{2,1,0:T(8,128)S(1)}, f32[10,32,512]{2,1,0:T(8,128)S(1)}, u32[]{:S(2)}, u32[]{:S(2)}) collective-permute-start(f32[10,32,512]{2,1,0:T(8,128)S(1)} %get-tuple-element.38), channel_id=1, source_target_pairs={{1,0},{2,1},{3,2},{4,3},{5,4},{6,5},{7,6},{8,7},{9,8},{10,9},{11,1... | collective-permute-start | bytes 1966088 | tf_op jit(solution)/shard_map/ppermute | solution.py:433
  7.5 17.3 %collective-permute-start = (f32[10,32,512]{2,1,0:T(8,128)S(1)}, f32[10,32,512]{2,1,0:T(8,128)S(1)}, u32[]{:S(2)}, u32[]{:S(2)}) collective-permute-start(f32[10,32,512]{2,1,0:T(8,128)S(1)} %get-tuple-element.35.up2), channel_id=1, source_target_pairs={{0,1},{1,2},{2,3},{3,4},{4,5},{5,6},{6,7},{7,8},{8,9},{9,10},{10,1... | collective-permute-start | bytes 1966088 | tf_op jit(solution)/shard_map/ppermute | solution.py:432
  7.5 13.7 %collective-permute-start.2 = (f32[8,32,512]{2,1,0:T(8,128)S(1)}, f32[8,32,512]{2,1,0:T(8,128)S(1)}, u32[]{:S(2)}, u32[]{:S(2)}) collective-permute-start(f32[8,32,512]{2,1,0:T(8,128)S(1)} %get-tuple-element.37.p0), channel_id=1, source_target_pairs={{1,0},{2,1},{3,2},{4,3},{5,4},{6,5},{7,6},{8,7},{9,8},{10,9},{11,1... | collective-permute-start | bytes 1572872 | tf_op jit(solution)/shard_map/ppermute | solution.py:431
  14.8 10.0 %copy-start = (f32[3,8,32,512]{3,2,1,0:T(8,128)}, f32[3,8,32,512]{3,2,1,0:T(8,128)S(1)}, u32[]{:S(2)}) copy-start(f32[3,8,32,512]{3,2,1,0:T(8,128)S(1)} %get-tuple-element.66.rates.refs_13_) | copy-start | bytes 4718596
  14.8 17.2 %collective-permute-start.4 = (f32[6,32,512]{2,1,0:T(8,128)S(1)}, f32[6,32,512]{2,1,0:T(8,128)S(1)}, u32[]{:S(2)}, u32[]{:S(2)}) collective-permute-start(f32[6,32,512]{2,1,0:T(8,128)S(1)} %get-tuple-element.45), channel_id=1, source_target_pairs={{0,1},{1,2},{2,3},{3,4},{4,5},{5,6},{6,7},{7,8},{8,9},{9,10},{10,1... | collective-permute-start | bytes 1179656 | tf_op jit(solution)/shard_map/ppermute | solution.py:442
  14.9 10.0 %copy-start.1 = (f32[8,32,512]{2,1,0:T(8,128)}, f32[8,32,512]{2,1,0:T(8,128)S(1)}, u32[]{:S(2)}) copy-start(f32[8,32,512]{2,1,0:T(8,128)S(1)} %collective-permute-done.1.prev1.refs_3_) | copy-start | bytes 1572868
  14.9 17.1 %collective-permute-start.5 = (f32[6,32,512]{2,1,0:T(8,128)S(1)}, f32[6,32,512]{2,1,0:T(8,128)S(1)}, u32[]{:S(2)}, u32[]{:S(2)}) collective-permute-start(f32[6,32,512]{2,1,0:T(8,128)S(1)} %get-tuple-element.46), channel_id=1, source_target_pairs={{1,0},{2,1},{3,2},{4,3},{5,4},{6,5},{7,6},{8,7},{9,8},{10,9},{11,1... | collective-permute-start | bytes 1179656 | tf_op jit(solution)/shard_map/ppermute | solution.py:443
  21.2 3.6 %copy-start.2 = (f32[8,32,512]{2,1,0:T(8,128)}, f32[8,32,512]{2,1,0:T(8,128)S(1)}, u32[]{:S(2)}) copy-start(f32[8,32,512]{2,1,0:T(8,128)S(1)} %collective-permute-done.2.next1.refs_6_) | copy-start | bytes 1572868
  24.7 6.2 %copy-start.3 = (f32[2,8,32,512]{3,2,1,0:T(8,128)}, f32[2,8,32,512]{3,2,1,0:T(8,128)S(1)}, u32[]{:S(2)}) copy-start(f32[2,8,32,512]{3,2,1,0:T(8,128)S(1)} %get-tuple-element.63.edge_rates.refs_10_) | copy-start | bytes 3145732
  24.8 6.2 %copy-start.4 = (f32[2,8,32,512]{3,2,1,0:T(8,128)}, f32[2,8,32,512]{3,2,1,0:T(8,128)S(1)}, u32[]{:S(2)}) copy-start(f32[2,8,32,512]{3,2,1,0:T(8,128)S(1)} %get-tuple-element.62.inner1.refs_9_) | copy-start | bytes 3145732
  24.8 6.2 %copy-start.7 = (f32[8,32,512]{2,1,0:T(8,128)}, f32[8,32,512]{2,1,0:T(8,128)S(1)}, u32[]{:S(2)}) copy-start(f32[8,32,512]{2,1,0:T(8,128)S(1)} %get-tuple-element.64.middle2.refs_11_) | copy-start | bytes 1572868
  24.8 6.2 %copy-start.5 = (f32[10,32,512]{2,1,0:T(8,128)}, f32[10,32,512]{2,1,0:T(8,128)S(1)}, u32[]{:S(2)}) copy-start(f32[10,32,512]{2,1,0:T(8,128)S(1)} %collective-permute-done.3.next2.refs_5_) | copy-start | bytes 1966084
  24.8 6.2 %copy-start.6 = (f32[10,32,512]{2,1,0:T(8,128)}, f32[10,32,512]{2,1,0:T(8,128)S(1)}, u32[]{:S(2)}) copy-start(f32[10,32,512]{2,1,0:T(8,128)S(1)} %collective-permute-done.prev2.refs_2_) | copy-start | bytes 1966084
  24.9 39.2 %copy-start.11 = (bf16[256,128]{1,0:T(8,128)(2,1)S(1)}, bf16[256,128]{1,0:T(8,128)(2,1)}, u32[]{:S(2)}) copy-start(bf16[256,128]{1,0:T(8,128)(2,1)} %constant.21.clone.refs_4_) | copy-start | bytes 196612
  24.9 39.2 %copy-start.12 = (bf16[256,128]{1,0:T(8,128)(2,1)S(1)}, bf16[256,128]{1,0:T(8,128)(2,1)}, u32[]{:S(2)}) copy-start(bf16[256,128]{1,0:T(8,128)(2,1)} %constant.20.clone.refs_3_) | copy-start | bytes 196612
  24.9 39.2 %copy-start.13 = (bf16[128,256]{1,0:T(8,128)(2,1)S(1)}, bf16[128,256]{1,0:T(8,128)(2,1)}, u32[]{:S(2)}) copy-start(bf16[128,256]{1,0:T(8,128)(2,1)} %constant.19.clone.refs_2_) | copy-start | bytes 196612
  24.9 39.2 %copy-start.14 = (bf16[128,256]{1,0:T(8,128)(2,1)S(1)}, bf16[128,256]{1,0:T(8,128)(2,1)}, u32[]{:S(2)}) copy-start(bf16[128,256]{1,0:T(8,128)(2,1)} %constant.18.clone.refs_1_) | copy-start | bytes 196612
  24.9 39.2 %copy-start.15 = (bf16[48,96]{1,0:T(8,128)(2,1)S(1)}, bf16[48,96]{1,0:T(8,128)(2,1)}, u32[]{:S(2)}) copy-start(bf16[48,96]{1,0:T(8,128)(2,1)} %constant.23.clone.refs_6_) | copy-start | bytes 27652
  24.9 39.2 %copy-start.16 = (bf16[48,96]{1,0:T(8,128)(2,1)S(1)}, bf16[48,96]{1,0:T(8,128)(2,1)}, u32[]{:S(2)}) copy-start(bf16[48,96]{1,0:T(8,128)(2,1)} %constant.22.clone.refs_5_) | copy-start | bytes 27652
  31.0 1.0 %copy-start.9 = (f32[2,8,32,512]{3,2,1,0:T(8,128)}, f32[2,8,32,512]{3,2,1,0:T(8,128)S(1)}, u32[]{:S(2)}) copy-start(f32[2,8,32,512]{3,2,1,0:T(8,128)S(1)} %get-tuple-element.65.refs_12_) | copy-start | bytes 3145732
  32.0 35.3 %copy-start.8 = (f32[2,8,32,512]{3,2,1,0:T(8,128)}, f32[2,8,32,512]{3,2,1,0:T(8,128)S(1)}, u32[]{:S(2)}) copy-start(f32[2,8,32,512]{3,2,1,0:T(8,128)S(1)} %get-tuple-element.61.refs_8_) | copy-start | bytes 3145732
  32.0 35.3 %copy-start.10 = (f32[2,3,32,512]{3,2,1,0:T(8,128)}, f32[2,3,32,512]{3,2,1,0:T(8,128)S(1)}, u32[]{:S(2)}) copy-start(f32[2,3,32,512]{3,2,1,0:T(8,128)S(1)} %get-tuple-element.67.refs_14_) | copy-start | bytes 1179652
  32.0 32.0 %copy-start.17 = (f32[6,32,512]{2,1,0:T(8,128)}, f32[6,32,512]{2,1,0:T(8,128)S(1)}, u32[]{:S(2)}) copy-start(f32[6,32,512]{2,1,0:T(8,128)S(1)} %collective-permute-done.4.refs_4_) | copy-start | bytes 1179652
  32.0 35.3 %copy-start.18 = (f32[6,32,512]{2,1,0:T(8,128)}, f32[6,32,512]{2,1,0:T(8,128)S(1)}, u32[]{:S(2)}) copy-start(f32[6,32,512]{2,1,0:T(8,128)S(1)} %collective-permute-done.5.refs_7_) | copy-start | bytes 1179652
  67.3 15.7 %all-to-all-start.1 = ((f32[16,48,128]{2,1,0:T(8,128)}), f32[16,48,128]{2,1,0:T(8,128)S(1)}, u32[]{:S(2)}, u32[]{:S(2)}) async-start(f32[16,48,128]{2,1,0:T(8,128)} %bitcast.1), calls=%async_computation.1 | async-start | bytes 786432 | tf_op jit(solution)/shard_map/all_to_all | solution.py:492

commit v5 on v4

--- a/solution.py
+++ b/solution.py
@@ -147,22 +147,14 @@
 
 def step_plane(center, before, after, mobility, out):
     total = squares(center)
-
-    def body(i, carry):
+    for i in range(GRAINS):
         out[i] = update(center[i], before[i], after[i], total, mobility[i])
-        return carry
-
-    lax.fori_loop(0, GRAINS, body, 0)
 
 
 def rates_plane(classes, start, out):
     ids = grain_of(start)
-
-    def body(i, carry):
+    for i in range(GRAINS):
         out[i] = rate(classes, ids, i)
-        return carry
-
-    lax.fori_loop(0, GRAINS, body, 0)
 
 
 def inner_kernel(chosen_any, classes_any, p0, p2, up2, rates, middle, r0, r2, chosen, classes, semaphores):
@@ -267,28 +259,20 @@
         ids = grain_of(mid)
         total0 = squares(mid)
         total1 = squares(outer1.at[side])
-
-        def body(r, carry):
+        for r in range(rest):
             i = other(r)
             first = update(mid[i], far[r], near[i], total0, rate(classes, ids, i))
             edge[side, r] = update(outer1[side, i], first, inner1[side, i], total1, edge_rates[side, i])
-            return carry
-
-        lax.fori_loop(0, rest, body, 0)
     for copy in copies[11:]:
         copy.wait()
     eta2 = (side2.at[0], middle2, side2.at[1])
     for k in range(3):
         total = squares(eta2[k])
-
-        def last(r, carry):
+        for r in range(rest):
             i = other(r)
             before = edge[0, r] if k == 0 else eta2[k - 1][i]
             after = edge[1, r] if k == 2 else eta2[k + 1][i]
             out[i, k] = update(eta2[k][i], before, after, total, rates[k, i])
-            return carry
-
-        lax.fori_loop(0, rest, last, 0)
         for f, i in enumerate(pair_of(chosen)):
             out[i, k] = final[f, k]
 
@@ -439,6 +423,7 @@
         scratch=[*small, pltpu.SemaphoreType.DMA((2,))],
         flops=2**24, moved=2**22,
     )
+    r0, r2, prev1, next1 = lax.optimization_barrier((r0, r2, prev1, next1))
     prev3 = lax.ppermute(r0, "gx", up)
     next3 = lax.ppermute(r2, "gx", down)
     edge_rates, inner1, middle2 = call(

time: 85.9 us -> 81 us (0.943)
  Pallas kernels: 27.7 us -> 21.1 us
  waiting for transfers between devices: 5.82 us -> 10.6 us
  blocking collectives: 32 us -> 28.1 us
    pallas_call x7, Pallas kernels: 27.7 us -> 21.1 us  [call(): pl.pallas_call(kernel, out_shape=outs, in_specs=in_specs, out_specs=out_s...]
    ppermute x1, starting transfers between devices: 0.06 us -> 5.07 us  [shards(): prev3 = lax.ppermute(r0, 'gx', up)]
    ppermute x1, waiting for transfers between devices: 0.01 us -> 4.7 us  [shards(): prev1 = lax.ppermute(p2, 'gx', up)]
    ppermute x1, starting transfers between devices: 4.41 us -> 0.01 us  [shards(): next3 = lax.ppermute(r2, 'gx', down)]
    all_to_all x1, blocking collectives: 32 us -> 28.1 us  [shards(): lax.all_to_all(packed, 'gx', split_axis=0, concat_axis=0, tiled=True)]
    ppermute x1, waiting for transfers between devices: 1.95 us -> 0.29 us  [shards(): next1 = lax.ppermute(p0, 'gx', down)]
    all_to_all x1, waiting for transfers between devices: 3.86 us -> 5.41 us  [shards(): lax.all_to_all(back, 'gx', split_axis=0, concat_axis=0, tiled=True)]
    ppermute x1, starting transfers between devices: 4.44 us -> 5.5 us  [shards(): next1 = lax.ppermute(p0, 'gx', down)]
  transfers between devices with their start and end apart: 7 -> 7, of which waited for: 2 -> 4; matrix products, arithmetic and copies ran while one was open for 0% -> 0% of each run, Pallas kernels for 24% -> 17%
where the time goes in v5:
time: 81 us; the launch traced here: 80.7 us
  blocking collectives  28.1 us (35%)
  Pallas kernels  21.1 us (26%)
  starting transfers between devices  18.8 us (23%)
  waiting for transfers between devices  10.6 us (13%)
  local copies, waits for them, and re-layouts  1.08 us (1%)
  between operations  1.05 us (1%)
    all_to_all x1, blocking collectives, shards(): lax.all_to_all(packed, 'gx', split_axis=0, concat_axis=0, tiled=True)  28.1 us
    pallas_call x7, Pallas kernels, call(): pl.pallas_call(kernel, out_shape=outs, in_specs=in_specs, out_specs=out_s...  21.1 us
    ppermute x1, starting transfers between devices, shards(): next1 = lax.ppermute(p0, 'gx', down)  5.5 us
    all_to_all x1, waiting for transfers between devices, shards(): lax.all_to_all(back, 'gx', split_axis=0, concat_axis=0, tiled=True)  5.41 us
    ppermute x1, starting transfers between devices, shards(): prev3 = lax.ppermute(r0, 'gx', up)  5.07 us
    ppermute x1, waiting for transfers between devices, shards(): prev1 = lax.ppermute(p2, 'gx', up)  4.7 us
    ppermute x1, starting transfers between devices, shards(): next2 = lax.ppermute(down2, 'gx', down)  4.44 us
    all_to_all x1, starting transfers between devices, shards(): lax.all_to_all(back, 'gx', split_axis=0, concat_axis=0, tiled=True)  3.74 us
  transfers between devices with their start and end apart: 7, of which 4 were waited for; matrix products, arithmetic and copies ran while one was open for 0% of the time, Pallas kernels for 17%

profile of v5, /device:TPU:0, one launch (start us, length us, event | category | flops | bytes accessed | tf_op | source)
XLA Modules:
  0.0 80.7 jit_solution(13450253982322313405)
XLA Ops:
  0.6 1.3 %shard_map.131 = (f32[8,32,512]{2,1,0:T(8,128)S(1)}, f32[8,32,512]{2,1,0:T(8,128)S(1)}, f32[10,32,512]{2,1,0:T(8,128)S(1)}, f32[10,32,512]{2,1,0:T(8,128)S(1)}) custom-call(s32[2]{0:T(128)} %refs_0_, bf16[8,3,32,512]{3,2,1,0:T(8,128)(2,1)} %jitter_any.1, s32[3,32,512]{2,1,0:T(8,128)} %ids_any.1), custom_call_target="tpu_custom_call" | custom-call | flops 2097152 | bytes 4194304 | tf_op jit(solution)/shard_map/pallas_call | solution.py:365
  2.0 5.5 %collective-permute-start.2 = (f32[8,32,512]{2,1,0:T(8,128)S(1)}, f32[8,32,512]{2,1,0:T(8,128)S(1)}, u32[]{:S(2)}, u32[]{:S(2)}) collective-permute-start(f32[8,32,512]{2,1,0:T(8,128)S(1)} %get-tuple-element.40.p0), channel_id=1, source_target_pairs={{1,0},{2,1},{3,2},{4,3},{5,4},{6,5},{7,6},{8,7},{9,8},{10,9},{11,1... | collective-permute-start | bytes 1572872 | tf_op jit(solution)/shard_map/ppermute | solution.py:415
  7.5 0.0 collective-permute-start.1
  7.5 4.4 %collective-permute-start.3 = (f32[10,32,512]{2,1,0:T(8,128)S(1)}, f32[10,32,512]{2,1,0:T(8,128)S(1)}, u32[]{:S(2)}, u32[]{:S(2)}) collective-permute-start(f32[10,32,512]{2,1,0:T(8,128)S(1)} %get-tuple-element.46), channel_id=1, source_target_pairs={{1,0},{2,1},{3,2},{4,3},{5,4},{6,5},{7,6},{8,7},{9,8},{10,9},{11,1... | collective-permute-start | bytes 1966088 | tf_op jit(solution)/shard_map/ppermute | solution.py:417
  11.9 0.0 collective-permute-start
  11.9 1.9 %shard_map.132 = (f32[3,8,32,512]{3,2,1,0:T(8,128)S(1)}, f32[8,32,512]{2,1,0:T(8,128)S(1)}, f32[6,32,512]{2,1,0:T(8,128)S(1)}, f32[6,32,512]{2,1,0:T(8,128)S(1)}) custom-call(s32[2]{0:T(128)} %refs_0_, s32[8,8]{1,0:T(8,128)} %refs_1_.1, f32[8,32,512]{2,1,0:T(8,128)S(1)} %get-tuple-element.40.p0, f32[8,32,512]{2,1,0:T(8,128)S(1)} %get-tuple-element.41.p2, ...), custom_call_target="tpu_custom_call" | custom-call | flops 16777216 | bytes 4194304 | tf_op jit(solution)/shard_map/pallas_call | solution.py:365
  13.9 0.0 copy-start
  13.9 0.3 collective-permute-done.2.next1.refs_6_
  14.2 0.0 copy-start.1
  14.2 4.7 %collective-permute-done.1.prev1.refs_3_ = f32[8,32,512]{2,1,0:T(8,128)S(1)} collective-permute-done((f32[8,32,512]{2,1,0:T(8,128)S(1)}, f32[8,32,512]{2,1,0:T(8,128)S(1)}, u32[]{:S(2)}, u32[]{:S(2)}) %collective-permute-start.1) | collective-permute-done | bytes 524320 | tf_op jit(solution)/shard_map/ppermute | solution.py:414
  18.9 0.0 copy-start.2
  18.9 5.1 %collective-permute-start.4 = (f32[6,32,512]{2,1,0:T(8,128)S(1)}, f32[6,32,512]{2,1,0:T(8,128)S(1)}, u32[]{:S(2)}, u32[]{:S(2)}) collective-permute-start(f32[6,32,512]{2,1,0:T(8,128)S(1)} %get-tuple-element.53), channel_id=1, source_target_pairs={{0,1},{1,2},{2,3},{3,4},{4,5},{5,6},{6,7},{7,8},{8,9},{9,10},{10,1... | collective-permute-start | bytes 1179656 | tf_op jit(solution)/shard_map/ppermute | solution.py:427
  23.9 0.0 collective-permute-start.5
  23.9 1.7 %shard_map.133 = (f32[2,8,32,512]{3,2,1,0:T(8,128)S(1)}, f32[2,8,32,512]{3,2,1,0:T(8,128)S(1)}, f32[8,32,512]{2,1,0:T(8,128)S(1)}) custom-call(s32[8,8]{1,0:T(8,128)} %refs_1_.1, f32[8,32,512]{2,1,0:T(8,128)S(1)} %get-tuple-element.40.p0, f32[8,32,512]{2,1,0:T(8,128)S(1)} %get-tuple-element.41.p2, f32[10,32,512]{2,1,0:T(8,128)S(1)} %get-tuple-element.39.up2, ...), custom_call_target="tpu_custom_call" | custom-call | flops 33554432 | bytes 16777216 | tf_op jit(solution)/shard_map/pallas_call | solution.py:365
  25.6 0.0 copy-start.3
  25.6 0.0 copy-start.4
  25.6 0.0 copy-start.7
  25.6 0.0 collective-permute-done.3.next2.refs_5_
  25.7 0.0 copy-start.5
  25.7 0.2 collective-permute-done.prev2.refs_2_
  25.9 0.0 copy-start.6
  25.9 0.0 copy-done
  25.9 0.0 copy-done.1
  25.9 0.0 copy-done.2
  25.9 0.0 copy-start.11
  25.9 0.0 copy-start.12
  25.9 0.0 copy-start.13
  25.9 0.0 copy-start.14
  25.9 0.0 copy-start.15
  26.0 0.0 copy-start.16
  26.0 3.8 %shard_map.134 = (f32[16,48,128]{2,1,0:T(8,128)S(1)}, f32[2,8,32,512]{3,2,1,0:T(8,128)S(1)}, f32[2,8,32,512]{3,2,1,0:T(8,128)S(1)}, f32[2,3,32,512]{3,2,1,0:T(8,128)S(1)}) custom-call(s32[2]{0:T(128)} %refs_0_, s32[8,8]{1,0:T(8,128)} %refs_1_.1, f32[8,32,512]{2,1,0:T(8,128)S(1)} %get-tuple-element.40.p0, f32[8,32,512]{2,1,0:T(8,128)S(1)} %get-tuple-element.41.p2, ...), custom_call_target="tpu_custom_call" | custom-call | flops 268435456 | bytes 8388608 | tf_op jit(solution)/shard_map/pallas_call | solution.py:365
  29.8 0.0 copy-done.3
  29.8 0.0 copy-done.4
  29.8 0.0 copy-done.7
  29.8 0.0 copy-done.5
  29.8 0.0 copy-done.6
  29.9 0.0 copy-start.9
  29.9 1.0 %copy-done.9 = f32[2,8,32,512]{3,2,1,0:T(8,128)} copy-done((f32[2,8,32,512]{3,2,1,0:T(8,128)}, f32[2,8,32,512]{3,2,1,0:T(8,128)S(1)}, u32[]{:S(2)}) %copy-start.9) | copy-done | bytes 1048600
  30.9 0.0 copy-start.8
  30.9 0.0 copy-start.10
  30.9 0.0 collective-permute-done.4.refs_4_
  30.9 0.0 copy-start.17
  30.9 0.0 collective-permute-done.5.refs_7_
  30.9 0.0 copy-start.18
  30.9 28.1 %all_to_all.10 = f32[16,48,128]{2,1,0:T(8,128)S(1)} all-to-all(f32[16,48,128]{2,1,0:T(8,128)S(1)} %get-tuple-element.60), channel_id=1, replica_groups=mesh['grp'=2,'gx'=16] {'gx'}, dimensions={0} | all-to-all | bytes 786432 | tf_op jit(solution)/shard_map/all_to_all | solution.py:457
  59.0 0.0 copy-done.17
  59.0 0.0 copy-done.11
  59.0 0.0 copy-done.12
  59.0 0.0 copy-done.13
  59.0 0.0 copy-done.14
  59.0 0.0 copy-done.15
  59.0 0.0 copy-done.16
  59.0 3.2 %shard_map.135 = f32[768,128]{1,0:T(8,128)} custom-call(f32[768,128]{1,0:T(8,128)S(1)} %bitcast.2, bf16[128,256]{1,0:T(8,128)(2,1)S(1)} %copy-done.14, bf16[128,256]{1,0:T(8,128)(2,1)S(1)} %copy-done.13, bf16[256,128]{1,0:T(8,128)(2,1)S(1)} %copy-done.12, bf16[256,128]{1,0:T(8,128)(2,1)S(1)} %copy-done.11, bf16[48,96]{1,0:T(8,128)(2,1)S(1)} %copy-done.16, ...), custom_call_target="tpu_custom_call" | custom-call | flops 268435456 | bytes 4194304 | tf_op jit(solution)/shard_map/pallas_call | solution.py:365
  62.2 0.0 copy-done.8
  62.2 0.0 copy-done.10
  62.2 0.0 copy-done.18
  62.2 3.7 %all-to-all-start.1 = ((f32[16,48,128]{2,1,0:T(8,128)}), f32[16,48,128]{2,1,0:T(8,128)S(1)}, u32[]{:S(2)}, u32[]{:S(2)}) async-start(f32[16,48,128]{2,1,0:T(8,128)} %bitcast.1), calls=%async_computation.1 | async-start | bytes 786432 | tf_op jit(solution)/shard_map/all_to_all | solution.py:477
  66.0 6.6 %shard_map.136 = f32[8,3,32,512]{3,2,1,0:T(8,128)} custom-call(s32[2]{0:T(128)} %refs_0_, s32[8,8]{1,0:T(8,128)} %refs_1_.1, f32[10,32,512]{2,1,0:T(8,128)} %copy-done.6, f32[8,32,512]{2,1,0:T(8,128)} %copy-done.2, f32[6,32,512]{2,1,0:T(8,128)} %copy-done.17, f32[10,32,512]{2,1,0:T(8,128)} %copy-done.5, f32[8,32,512]{2,1,0:T(8,128)} %copy-done.1, ...), custom_call_target="tpu_custom_call" | custom-call | flops 67108864 | bytes 16777216 | tf_op jit(solution)/shard_map/pallas_call | solution.py:365
  72.6 5.4 %all-to-all-done.1.returned = f32[16,48,128]{2,1,0:T(8,128)S(1)} async-done(((f32[16,48,128]{2,1,0:T(8,128)}), f32[16,48,128]{2,1,0:T(8,128)S(1)}, u32[]{:S(2)}, u32[]{:S(2)}) %all-to-all-start.1) | async-done | bytes 393248 | tf_op jit(solution)/shard_map/all_to_all | solution.py:477
  78.0 2.5 %shard_map.137 = f32[2,3,32,512]{3,2,1,0:T(8,128)} custom-call(f32[16,48,128]{2,1,0:T(8,128)S(1)} %all-to-all-done.1.returned, bf16[512,512]{1,0:T(8,128)(2,1)} %constant.16.clone.high_any, bf16[512,512]{1,0:T(8,128)(2,1)} %constant.17.clone.low_any), custom_call_target="tpu_custom_call" | custom-call | flops 268435456 | bytes 4194304 | tf_op jit(solution)/shard_map/pallas_call | solution.py:365
Async XLA Ops:
  2.0 12.2 %collective-permute-start.2 = (f32[8,32,512]{2,1,0:T(8,128)S(1)}, f32[8,32,512]{2,1,0:T(8,128)S(1)}, u32[]{:S(2)}, u32[]{:S(2)}) collective-permute-start(f32[8,32,512]{2,1,0:T(8,128)S(1)} %get-tuple-element.40.p0), channel_id=1, source_target_pairs={{1,0},{2,1},{3,2},{4,3},{5,4},{6,5},{7,6},{8,7},{9,8},{10,9},{11,1... | collective-permute-start | bytes 1572872 | tf_op jit(solution)/shard_map/ppermute | solution.py:415
  7.5 11.4 %collective-permute-start.1 = (f32[8,32,512]{2,1,0:T(8,128)S(1)}, f32[8,32,512]{2,1,0:T(8,128)S(1)}, u32[]{:S(2)}, u32[]{:S(2)}) collective-permute-start(f32[8,32,512]{2,1,0:T(8,128)S(1)} %get-tuple-element.41.p2), channel_id=1, source_target_pairs={{0,1},{1,2},{2,3},{3,4},{4,5},{5,6},{6,7},{7,8},{8,9},{9,10},{10,1... | collective-permute-start | bytes 1572872 | tf_op jit(solution)/shard_map/ppermute | solution.py:414
  7.5 18.2 %collective-permute-start.3 = (f32[10,32,512]{2,1,0:T(8,128)S(1)}, f32[10,32,512]{2,1,0:T(8,128)S(1)}, u32[]{:S(2)}, u32[]{:S(2)}) collective-permute-start(f32[10,32,512]{2,1,0:T(8,128)S(1)} %get-tuple-element.46), channel_id=1, source_target_pairs={{1,0},{2,1},{3,2},{4,3},{5,4},{6,5},{7,6},{8,7},{9,8},{10,9},{11,1... | collective-permute-start | bytes 1966088 | tf_op jit(solution)/shard_map/ppermute | solution.py:417
  11.9 14.0 %collective-permute-start = (f32[10,32,512]{2,1,0:T(8,128)S(1)}, f32[10,32,512]{2,1,0:T(8,128)S(1)}, u32[]{:S(2)}, u32[]{:S(2)}) collective-permute-start(f32[10,32,512]{2,1,0:T(8,128)S(1)} %get-tuple-element.39.up2), channel_id=1, source_target_pairs={{0,1},{1,2},{2,3},{3,4},{4,5},{5,6},{6,7},{7,8},{8,9},{9,10},{10,1... | collective-permute-start | bytes 1966088 | tf_op jit(solution)/shard_map/ppermute | solution.py:416
  13.9 12.0 %copy-start = (f32[3,8,32,512]{3,2,1,0:T(8,128)}, f32[3,8,32,512]{3,2,1,0:T(8,128)S(1)}, u32[]{:S(2)}) copy-start(f32[3,8,32,512]{3,2,1,0:T(8,128)S(1)} %get-tuple-element.74.rates.refs_13_) | copy-start | bytes 4718596
  14.2 11.7 %copy-start.1 = (f32[8,32,512]{2,1,0:T(8,128)}, f32[8,32,512]{2,1,0:T(8,128)S(1)}, u32[]{:S(2)}) copy-start(f32[8,32,512]{2,1,0:T(8,128)S(1)} %collective-permute-done.2.next1.refs_6_) | copy-start | bytes 1572868
  18.9 7.0 %copy-start.2 = (f32[8,32,512]{2,1,0:T(8,128)}, f32[8,32,512]{2,1,0:T(8,128)S(1)}, u32[]{:S(2)}) copy-start(f32[8,32,512]{2,1,0:T(8,128)S(1)} %collective-permute-done.1.prev1.refs_3_) | copy-start | bytes 1572868
  18.9 12.0 %collective-permute-start.4 = (f32[6,32,512]{2,1,0:T(8,128)S(1)}, f32[6,32,512]{2,1,0:T(8,128)S(1)}, u32[]{:S(2)}, u32[]{:S(2)}) collective-permute-start(f32[6,32,512]{2,1,0:T(8,128)S(1)} %get-tuple-element.53), channel_id=1, source_target_pairs={{0,1},{1,2},{2,3},{3,4},{4,5},{5,6},{6,7},{7,8},{8,9},{9,10},{10,1... | collective-permute-start | bytes 1179656 | tf_op jit(solution)/shard_map/ppermute | solution.py:427
  23.9 6.9 %collective-permute-start.5 = (f32[6,32,512]{2,1,0:T(8,128)S(1)}, f32[6,32,512]{2,1,0:T(8,128)S(1)}, u32[]{:S(2)}, u32[]{:S(2)}) collective-permute-start(f32[6,32,512]{2,1,0:T(8,128)S(1)} %get-tuple-element.54), channel_id=1, source_target_pairs={{1,0},{2,1},{3,2},{4,3},{5,4},{6,5},{7,6},{8,7},{9,8},{10,9},{11,1... | collective-permute-start | bytes 1179656 | tf_op jit(solution)/shard_map/ppermute | solution.py:428
  25.6 4.2 %copy-start.3 = (f32[2,8,32,512]{3,2,1,0:T(8,128)}, f32[2,8,32,512]{3,2,1,0:T(8,128)S(1)}, u32[]{:S(2)}) copy-start(f32[2,8,32,512]{3,2,1,0:T(8,128)S(1)} %get-tuple-element.71.edge_rates.refs_10_) | copy-start | bytes 3145732
  25.6 4.2 %copy-start.4 = (f32[2,8,32,512]{3,2,1,0:T(8,128)}, f32[2,8,32,512]{3,2,1,0:T(8,128)S(1)}, u32[]{:S(2)}) copy-start(f32[2,8,32,512]{3,2,1,0:T(8,128)S(1)} %get-tuple-element.70.inner1.refs_9_) | copy-start | bytes 3145732
  25.6 4.2 %copy-start.7 = (f32[8,32,512]{2,1,0:T(8,128)}, f32[8,32,512]{2,1,0:T(8,128)S(1)}, u32[]{:S(2)}) copy-start(f32[8,32,512]{2,1,0:T(8,128)S(1)} %get-tuple-element.72.middle2.refs_11_) | copy-start | bytes 1572868
  25.7 4.2 %copy-start.5 = (f32[10,32,512]{2,1,0:T(8,128)}, f32[10,32,512]{2,1,0:T(8,128)S(1)}, u32[]{:S(2)}) copy-start(f32[10,32,512]{2,1,0:T(8,128)S(1)} %collective-permute-done.3.next2.refs_5_) | copy-start | bytes 1966084
  25.9 4.0 %copy-start.6 = (f32[10,32,512]{2,1,0:T(8,128)}, f32[10,32,512]{2,1,0:T(8,128)S(1)}, u32[]{:S(2)}) copy-start(f32[10,32,512]{2,1,0:T(8,128)S(1)} %collective-permute-done.prev2.refs_2_) | copy-start | bytes 1966084
  25.9 33.1 %copy-start.11 = (bf16[256,128]{1,0:T(8,128)(2,1)S(1)}, bf16[256,128]{1,0:T(8,128)(2,1)}, u32[]{:S(2)}) copy-start(bf16[256,128]{1,0:T(8,128)(2,1)} %constant.21.clone.refs_4_) | copy-start | bytes 196612
  25.9 33.1 %copy-start.12 = (bf16[256,128]{1,0:T(8,128)(2,1)S(1)}, bf16[256,128]{1,0:T(8,128)(2,1)}, u32[]{:S(2)}) copy-start(bf16[256,128]{1,0:T(8,128)(2,1)} %constant.20.clone.refs_3_) | copy-start | bytes 196612
  25.9 33.0 %copy-start.13 = (bf16[128,256]{1,0:T(8,128)(2,1)S(1)}, bf16[128,256]{1,0:T(8,128)(2,1)}, u32[]{:S(2)}) copy-start(bf16[128,256]{1,0:T(8,128)(2,1)} %constant.19.clone.refs_2_) | copy-start | bytes 196612
  25.9 33.0 %copy-start.14 = (bf16[128,256]{1,0:T(8,128)(2,1)S(1)}, bf16[128,256]{1,0:T(8,128)(2,1)}, u32[]{:S(2)}) copy-start(bf16[128,256]{1,0:T(8,128)(2,1)} %constant.18.clone.refs_1_) | copy-start | bytes 196612
  25.9 33.0 %copy-start.15 = (bf16[48,96]{1,0:T(8,128)(2,1)S(1)}, bf16[48,96]{1,0:T(8,128)(2,1)}, u32[]{:S(2)}) copy-start(bf16[48,96]{1,0:T(8,128)(2,1)} %constant.23.clone.refs_6_) | copy-start | bytes 27652
  26.0 33.0 %copy-start.16 = (bf16[48,96]{1,0:T(8,128)(2,1)S(1)}, bf16[48,96]{1,0:T(8,128)(2,1)}, u32[]{:S(2)}) copy-start(bf16[48,96]{1,0:T(8,128)(2,1)} %constant.22.clone.refs_5_) | copy-start | bytes 27652
  29.9 1.0 %copy-start.9 = (f32[2,8,32,512]{3,2,1,0:T(8,128)}, f32[2,8,32,512]{3,2,1,0:T(8,128)S(1)}, u32[]{:S(2)}) copy-start(f32[2,8,32,512]{3,2,1,0:T(8,128)S(1)} %get-tuple-element.73.refs_12_) | copy-start | bytes 3145732
  30.9 31.4 %copy-start.8 = (f32[2,8,32,512]{3,2,1,0:T(8,128)}, f32[2,8,32,512]{3,2,1,0:T(8,128)S(1)}, u32[]{:S(2)}) copy-start(f32[2,8,32,512]{3,2,1,0:T(8,128)S(1)} %get-tuple-element.69.refs_8_) | copy-start | bytes 3145732
  30.9 31.4 %copy-start.10 = (f32[2,3,32,512]{3,2,1,0:T(8,128)}, f32[2,3,32,512]{3,2,1,0:T(8,128)S(1)}, u32[]{:S(2)}) copy-start(f32[2,3,32,512]{3,2,1,0:T(8,128)S(1)} %get-tuple-element.75.refs_14_) | copy-start | bytes 1179652
  30.9 28.1 %copy-start.17 = (f32[6,32,512]{2,1,0:T(8,128)}, f32[6,32,512]{2,1,0:T(8,128)S(1)}, u32[]{:S(2)}) copy-start(f32[6,32,512]{2,1,0:T(8,128)S(1)} %collective-permute-done.4.refs_4_) | copy-start | bytes 1179652
  30.9 31.4 %copy-start.18 = (f32[6,32,512]{2,1,0:T(8,128)}, f32[6,32,512]{2,1,0:T(8,128)S(1)}, u32[]{:S(2)}) copy-start(f32[6,32,512]{2,1,0:T(8,128)S(1)} %collective-permute-done.5.refs_7_) | copy-start | bytes 1179652
  62.2 15.7 %all-to-all-start.1 = ((f32[16,48,128]{2,1,0:T(8,128)}), f32[16,48,128]{2,1,0:T(8,128)S(1)}, u32[]{:S(2)}, u32[]{:S(2)}) async-start(f32[16,48,128]{2,1,0:T(8,128)} %bitcast.1), calls=%async_computation.1 | async-start | bytes 786432 | tf_op jit(solution)/shard_map/all_to_all | solution.py:477

commit v6 on v5

--- a/solution.py
+++ b/solution.py
@@ -49,7 +49,7 @@
     inverse = np.block([[cos_z, sin_z], [-sin_z, cos_z]])
     inverse_turned = np.concatenate([-inverse[:, half:], inverse[:, :half]], axis=1)
     return (
-        np.concatenate([forward, forward_turned], axis=1),
+        np.concatenate([forward, forward_turned], axis=0),
         np.concatenate([inverse, inverse_turned], axis=0),
     )
 
@@ -172,31 +172,38 @@
     step_plane(up2, p0, p2, rates.at[1], middle)
 
 
-def near_kernel(
-    classes_any, p0, p2, up2, prev1, next1, rates, middle, edge_rates, inner1, middle2, classes, semaphores
-):
+def groups(ref, count, base=0):
+    return [ref.at[pl.ds(base + k * GRAINS, GRAINS)] for k in range(count)]
+
+
+def near_kernel(classes_any, p0, p2, up2, prev1, next1, rates, middle, near_out, classes, semaphores):
+    edge0, edge1, inner0, inner2, middle2 = groups(near_out, 5)
     copies = fetch(((classes_any, classes),), semaphores)
-    step_plane(p0, prev1, up2, rates.at[0], inner1.at[0])
-    step_plane(p2, up2, next1, rates.at[2], inner1.at[1])
+    step_plane(p0, prev1, up2, rates.at[0], inner0)
+    step_plane(p2, up2, next1, rates.at[2], inner2)
     copies[0].wait()
-    rates_plane(classes, prev1, edge_rates.at[0])
-    rates_plane(classes, next1, edge_rates.at[1])
-    step_plane(middle, inner1.at[0], inner1.at[1], rates.at[1], middle2)
+    rates_plane(classes, prev1, edge0)
+    rates_plane(classes, next1, edge1)
+    step_plane(middle, inner0, inner2, rates.at[1], middle2)
 
 
 def pair_kernel(
-    chosen_any, classes_any, p0, p2, prev1, next1, prev2, next2, rates, edge_rates, middle, inner1, middle2,
-    high_any, low_any, packed, outer1, side2, final_any, chosen, classes, high, low, edge, fields, final, semaphores,
+    chosen_any, classes_any, p0, p2, prev1, next1, prev2, next2, rates, middle, near_out, high_any, low_any,
+    packed, late, chosen, classes, high, low, edge, fields, semaphores,
 ):
     copies = fetch(
         ((chosen_any, chosen), (classes_any, classes), (high_any, high), (low_any, low)), semaphores
     )
-    step_plane(prev1, prev2, p0, edge_rates.at[0], outer1.at[0])
-    step_plane(next1, p2, next2, edge_rates.at[1], outer1.at[1])
-    step_plane(inner1.at[0], outer1.at[0], middle, rates.at[0], side2.at[0])
-    step_plane(inner1.at[1], middle, outer1.at[1], rates.at[2], side2.at[1])
-    eta2 = (side2.at[0], middle2, side2.at[1])
-    depth, width = final.shape[2:]
+    near_state = groups(near_out, 5)
+    edge_rates, inner1, middle2 = near_state[:2], near_state[2:4], near_state[4]
+    late_state = groups(late, 4)
+    outer1, side2 = late_state[:2], late_state[2:]
+    step_plane(prev1, prev2, p0, edge_rates[0], outer1[0])
+    step_plane(next1, p2, next2, edge_rates[1], outer1[1])
+    step_plane(inner1[0], outer1[0], middle, rates.at[0], side2[0])
+    step_plane(inner1[1], middle, outer1[1], rates.at[2], side2[1])
+    eta2 = (side2[0], middle2, side2[1])
+    depth, width = late.shape[1:]
     totals = [squares(state) for state in eta2]
     copies[0].wait()
     copies[1].wait()
@@ -204,10 +211,10 @@
     for side, (mid, near) in enumerate(((prev2, prev1), (next2, next1))):
         ids = grain_of(mid)
         total0 = squares(mid)
-        total1 = squares(outer1.at[side])
+        total1 = squares(outer1[side])
         for k, i in enumerate(pair):
             first = update(mid[i], mid[GRAINS + k], near[i], total0, rate(classes, ids, i))
-            edge[side, k] = update(outer1[side, i], first, inner1[side, i], total1, edge_rates[side, i])
+            edge[side, k] = update(outer1[side][i], first, inner1[side][i], total1, edge_rates[side][i])
     repeated = chosen[1] == chosen[0]
     for k in range(3):
         values = []
@@ -215,31 +222,33 @@
             before = edge[0, f] if k == 0 else eta2[k - 1][i]
             after = edge[1, f] if k == 2 else eta2[k + 1][i]
             value = update(eta2[k][i], before, after, totals[k], rates[k, i])
-            final[f, k] = value
+            late[4 * GRAINS + 3 * f + k] = value
             values.append(value)
         values[1] = jnp.where(repeated, values[0], values[1])
         for f in range(2):
-            base = k * 4 * depth + f * depth
+            base = k * 2 * depth + f * depth
             fields[base : base + depth] = values[f]
-            fields[base + 2 * depth : base + 3 * depth] = values[f]
-    out_copy = pltpu.make_async_copy(final, final_any, semaphores.at[4])
-    out_copy.start()
     copies[2].wait()
     copies[3].wait()
     full = dot3((high[...], low[...]), split(fields[...]), ((1,), (1,)))
     slots = width // 2
     lanes = 4 * depth
-    real_lane = lax.broadcasted_iota(jnp.int32, (slots, lanes), 1) < 2 * depth
+    half = lanes // 2
+    real_lane = lax.broadcasted_iota(jnp.int32, (slots, lanes), 1) < half
     for k in range(3):
-        part = full[:, k * lanes : (k + 1) * lanes]
-        part = jnp.where(real_lane, part[:slots], part[slots:])
+        at = slice(k // 2 * lanes, k // 2 * lanes + lanes)
+        cosine, sine = full[:slots, at], full[slots:, at]
+        if k % 2:
+            cosine = pltpu.roll(cosine, half, 1)
+        else:
+            sine = pltpu.roll(sine, half, 1)
+        part = jnp.where(real_lane, cosine, sine)
         if packed.shape[0] == 3:
             packed[k] = part
         else:
             devices, rows, _ = packed.shape
             rows = rows // 3
             packed[:, k * rows : (k + 1) * rows, :] = part.reshape(devices, rows, lanes)
-    out_copy.wait()
 
 
 def rest_kernel(*refs):
@@ -247,25 +256,25 @@
     sources, out, targets = refs[:count], refs[count], refs[count + 1 : 2 * count + 1]
     edge, semaphores = refs[-2:]
     copies = fetch(list(zip(sources, targets)), semaphores)
-    (
-        chosen, classes, prev2, prev1, prev3, next2, next1, next3, outer1, inner1, edge_rates,
-        middle2, side2, rates, final,
-    ) = targets
-    for copy in copies[:11]:
+    chosen, classes, prev2, prev1, prev3, next2, next1, next3, near_out, late, rates = targets
+    near_state = groups(near_out, 5)
+    edge_rates, inner1, middle2 = near_state[:2], near_state[2:4], near_state[4]
+    late_state = groups(late, 4)
+    outer1, side2 = late_state[:2], late_state[2:]
+    for copy in copies[:10]:
         copy.wait()
     other = others_of(chosen)
     rest = GRAINS - 2
     for side, (far, mid, near) in enumerate(((prev3, prev2, prev1), (next3, next2, next1))):
         ids = grain_of(mid)
         total0 = squares(mid)
-        total1 = squares(outer1.at[side])
+        total1 = squares(outer1[side])
         for r in range(rest):
             i = other(r)
             first = update(mid[i], far[r], near[i], total0, rate(classes, ids, i))
-            edge[side, r] = update(outer1[side, i], first, inner1[side, i], total1, edge_rates[side, i])
-    for copy in copies[11:]:
-        copy.wait()
-    eta2 = (side2.at[0], middle2, side2.at[1])
+            edge[side, r] = update(outer1[side][i], first, inner1[side][i], total1, edge_rates[side][i])
+    copies[10].wait()
+    eta2 = (side2[0], middle2, side2[1])
     for k in range(3):
         total = squares(eta2[k])
         for r in range(rest):
@@ -274,41 +283,50 @@
             after = edge[1, r] if k == 2 else eta2[k + 1][i]
             out[i, k] = update(eta2[k][i], before, after, total, rates[k, i])
         for f, i in enumerate(pair_of(chosen)):
-            out[i, k] = final[f, k]
-
-
-def line_kernel(
-    lines, zf_high, zf_low, zi_high, zi_low, xf_high, xf_low, out, r1, r2, gathered, scale
-):
+            out[i, k] = late[4 * GRAINS + 3 * f + k]
+
+
+def line_kernel(lines, z_forward, z_inverse, x_both, out, wide, tall, scale):
     rows, lanes = lines.shape
-    total_x = xf_high.shape[0]
+    total_x = wide.shape[0] // 3
     slots = rows // total_x
     half = lanes // 2
-    zf = (zf_high[...], zf_low[...])
-    xf = (xf_high[...], xf_low[...])
-    turned = dot3(split(lines[...]), zf)
-    r1[...] = turned[:, :lanes]
-    r2[...] = turned[:, lanes:]
+
+    def over_x(pieces):
+        for j, piece in enumerate(pieces):
+            at = slice(j * lanes, (j + 1) * lanes)
+            high, low = split(piece)
+            wide[:total_x, at] = high
+            wide[total_x : 2 * total_x, at] = low
+            wide[2 * total_x :, at] = high
+        both = jnp.dot(x_both[...], wide[...], preferred_element_type=F32)
+        return both[:total_x], both[total_x:]
+
+    def put(row, even, odd):
+        at = slice(row * total_x, (row + 1) * total_x)
+        for base, value in ((0, even), (lanes, odd)):
+            high, low = split(value)
+            tall[0, at, base : base + lanes] = high
+            tall[1, at, base : base + lanes] = low
+
     real_lane = lax.broadcasted_iota(jnp.int32, (total_x, lanes), 1) < half
-    mixed = lines[pl.ds(0, total_x, stride=slots), :]
-    pair = jnp.concatenate(
-        [jnp.where(real_lane, mixed, 0.0), jnp.where(real_lane, pltpu.roll(mixed, half, 1), 0.0)], axis=0
-    )
-    pair = dot3(split(pair), zf)
+    even, odd = over_x([lines[pl.ds(j, total_x, stride=slots), :] for j in range(slots)])
     for j in range(slots):
         at = slice(j * lanes, (j + 1) * lanes)
-        gathered[:total_x, at] = r1[pl.ds(j, total_x, stride=slots), :]
-        gathered[total_x:, at] = r2[pl.ds(j, total_x, stride=slots), :]
-    for j in range(2):
-        at = slice((slots + j) * lanes, (slots + j + 1) * lanes)
-        gathered[:total_x, at] = pair[j * total_x : (j + 1) * total_x, :lanes]
-        gathered[total_x:, at] = pair[j * total_x : (j + 1) * total_x, lanes:]
-    spectrum = dot3(xf, split(gathered[...]))
+        put(j, even[:, at], odd[:, at])
+    first_even, first_odd = even[:, :lanes], odd[:, :lanes]
+    put(slots, jnp.where(real_lane, first_even, 0.0), jnp.where(real_lane, first_odd, 0.0))
+    put(
+        slots + 1,
+        jnp.where(real_lane, pltpu.roll(first_even, half, 1), 0.0),
+        jnp.where(real_lane, pltpu.roll(first_odd, half, 1), 0.0),
+    )
+    spectrum = dot3((tall[0], tall[1]), (z_forward[0], z_forward[1]))
+    spectrum = spectrum * spectrum
+    spectrum = spectrum + pltpu.roll(spectrum, half, 1)
 
     def power(j):
-        part = spectrum[:, j * lanes : (j + 1) * lanes]
-        part = part * part
-        return part + pltpu.roll(part, half, 1)
+        return spectrum[j * total_x : (j + 1) * total_x]
 
     first = lax.axis_index("gx") == 0
     lane = lax.broadcasted_iota(jnp.int32, (total_x, lanes), 1)
@@ -322,21 +340,16 @@
             special = jnp.where(constant, 0.0, special)
             value = jnp.where(first, special, value)
         powers.append(value)
-    powers = split(jnp.concatenate(powers, axis=1))
-    cos_x = (xf[0][:, :total_x], xf[1][:, :total_x])
-    sin_x = (xf[0][:, total_x:], xf[1][:, total_x:])
-    for target, matrix in ((r1, cos_x), (r2, sin_x)):
-        back = dot3(matrix, powers)
-        for j in range(slots):
-            target[pl.ds(j, total_x, stride=slots), :] = back[:, j * lanes : (j + 1) * lanes]
-    zi = (zi_high[...], zi_low[...])
-    out[...] = dot3(split(r1[...]), (zi[0][:lanes], zi[1][:lanes])) + dot3(
-        split(r2[...]), (zi[0][lanes:], zi[1][lanes:])
-    )
-
-
-def finish_kernel(returned, high_any, low_any, out, high, low, semaphores):
-    copies = fetch(((high_any, high), (low_any, low)), semaphores)
+    even, odd = over_x(powers)
+    for j in range(slots):
+        at = slice(j * lanes, (j + 1) * lanes)
+        put(j, even[:, at], odd[:, at])
+    back = dot3((tall[0, :rows], tall[1, :rows]), (z_inverse[0], z_inverse[1]))
+    for j in range(slots):
+        out[pl.ds(j, total_x, stride=slots), :] = back[j * total_x : (j + 1) * total_x]
+
+
+def finish_kernel(returned, high, low, out):
     fields, planes, depth, width = out.shape
     lanes = 2 * fields * depth
     half = lanes // 2
@@ -352,8 +365,6 @@
         part = part.T
         stacked.append(jnp.concatenate([part[:half], part[half:]], axis=1))
     stacked = split(jnp.concatenate(stacked, axis=0))
-    for copy in copies:
-        copy.wait()
     result = dot3(stacked, (high[...], low[...]))
     for k in range(planes):
         for f in range(fields):
@@ -361,16 +372,17 @@
             out[f, k] = result[base : base + depth]
 
 
-def call(kernel, outs, in_specs, *args, scratch=(), flops=0, moved=0, limit=12, out_specs=None):
+def call(kernel, outs, in_specs, *args, scratch=(), flops=0, moved=0, limit=12):
+    args = [pltpu.with_memory_space_constraint(a, pltpu.HBM) if b is ANY else a for a, b in zip(args, in_specs)]
     return pl.pallas_call(
         kernel,
         out_shape=outs,
         in_specs=in_specs,
-        out_specs=out_specs or jax.tree.map(lambda _: VMEM, outs),
+        out_specs=jax.tree.map(lambda _: VMEM, outs),
         scratch_shapes=scratch,
         compiler_params=pltpu.CompilerParams(vmem_limit_bytes=limit * MIB),
         cost_estimate=pl.CostEstimate(flops=flops, bytes_accessed=moved, transcendentals=0),
-    )(*[pltpu.with_memory_space_constraint(a, pltpu.HBM) if b is ANY else a for a, b in zip(args, in_specs)])
+    )(*args)
 
 
 def shards(grain_ids, jitter, class_table, chosen):
@@ -391,8 +403,9 @@
     plane = (GRAINS, depth, width)
     table = [jnp.asarray(part) for part in halves(y_table(width))]
     z_forward, z_inverse = z_tables(depth)
-    z_parts = [jnp.asarray(part) for matrix in (z_forward, z_inverse) for part in halves(matrix)]
-    x_parts = [jnp.asarray(part) for part in halves(np.concatenate(phases(total_x), axis=1))]
+    z_parts = [jnp.asarray(np.stack(halves(matrix))) for matrix in (z_forward, z_inverse)]
+    x_high, x_low = halves(np.concatenate(phases(total_x), axis=0))
+    x_both = jnp.asarray(np.concatenate([x_high, x_high, x_low], axis=1))
 
     two = (2, *plane)
     six = (GRAINS - 2, depth, width)
@@ -426,50 +439,47 @@
     r0, r2, prev1, next1 = lax.optimization_barrier((r0, r2, prev1, next1))
     prev3 = lax.ppermute(r0, "gx", up)
     next3 = lax.ppermute(r2, "gx", down)
-    edge_rates, inner1, middle2 = call(
+    near_out = call(
         near_kernel,
-        (shape(*two), shape(*two), shape(*plane)),
+        shape(5 * GRAINS, depth, width),
         [ANY] + [VMEM] * 7,
         class_table, p0, p2, up2, prev1, next1, rates, middle,
         scratch=[small[1], pltpu.SemaphoreType.DMA((1,))],
         flops=2**25, moved=2**24,
     )
     packed_shape = (devices, planes * share, lanes) if aligned else (planes, slots, lanes)
-    packed, outer1, side2, final = call(
+    packed, late_out = call(
         pair_kernel,
-        (shape(*packed_shape), shape(*two), shape(*two), shape(2, planes, depth, width)),
-        [ANY] * 2 + [VMEM] * 11 + [ANY] * 2,
-        chosen, class_table, p0, p2, prev1, next1, prev2, next2, rates, edge_rates, middle, inner1, middle2, *table,
+        (shape(*packed_shape), shape(4 * GRAINS + 2 * planes, depth, width)),
+        [ANY] * 2 + [VMEM] * 9 + [ANY] * 2,
+        chosen, class_table, p0, p2, prev1, next1, prev2, next2, rates, middle, near_out, *table,
         scratch=[
             *small,
             pltpu.VMEM(table[0].shape, BF16),
             pltpu.VMEM(table[1].shape, BF16),
             pltpu.VMEM((2, 2, depth, width), F32),
-            pltpu.VMEM((planes * lanes, width), F32),
-            pltpu.VMEM((2, planes, depth, width), F32),
-            pltpu.SemaphoreType.DMA((5,)),
+            pltpu.VMEM(((planes + 1) // 2 * lanes, width), F32),
+            pltpu.SemaphoreType.DMA((4,)),
         ],
-        out_specs=(VMEM, VMEM, VMEM, ANY),
-        flops=2**28, moved=2**23,
-    )
-    packed, prev3, next3 = lax.optimization_barrier((packed, prev3, next3))
+        flops=2**28, moved=2**23, limit=50,
+    )
     if aligned:
         lines = lax.all_to_all(packed, "gx", split_axis=0, concat_axis=0, tiled=True)
     else:
         lines = lax.all_to_all(packed, "gx", split_axis=1, concat_axis=0, tiled=True)
     lines = lines.reshape(total_x * share, lanes)
+    lines, prev3, next3 = lax.optimization_barrier((lines, prev3, next3))
     def lines_body(*refs):
         line_kernel(*refs, scale=1.0 / (count * count))
 
     back = call(
         lines_body,
         shape(total_x * share, lanes),
-        [VMEM] * 7,
-        lines, *z_parts, *x_parts,
+        [VMEM] * 4,
+        lines, *z_parts, x_both,
         scratch=[
-            pltpu.VMEM((total_x * share, lanes), F32),
-            pltpu.VMEM((total_x * share, lanes), F32),
-            pltpu.VMEM((2 * total_x, (share + 2) * lanes), F32),
+            pltpu.VMEM((3 * total_x, share * lanes), BF16),
+            pltpu.VMEM((2, total_x * (share + 2), 2 * lanes), BF16),
         ],
         flops=2**28, moved=2**22,
     )
@@ -478,10 +488,7 @@
     if not aligned:
         returned = returned.reshape(devices, planes, share, lanes).transpose(1, 0, 2, 3)
         returned = returned.reshape(planes, slots, lanes)
-    late = (
-        chosen, class_table, prev2, prev1, prev3, next2, next1, next3, outer1, inner1, edge_rates,
-        middle2, side2, rates, final,
-    )
+    late = (chosen, class_table, prev2, prev1, prev3, next2, next1, next3, near_out, late_out, rates)
     late, _ = lax.optimization_barrier((late, back))
     order_params = call(
         rest_kernel,
@@ -499,13 +506,8 @@
     correlation = call(
         finish_kernel,
         shape(2, planes, depth, width),
-        [VMEM] + [ANY] * 2,
+        [VMEM] * 3,
         returned, *table,
-        scratch=[
-            pltpu.VMEM(table[0].shape, BF16),
-            pltpu.VMEM(table[1].shape, BF16),
-            pltpu.SemaphoreType.DMA((2,)),
-        ],
         flops=2**28, moved=2**22,
     )
     return (order_params, correlation)

time: 81 us -> 85.9 us (1.060)
  blocking collectives: 28.1 us -> 0 us
  waiting for transfers between devices: 10.6 us -> 28.8 us
  starting transfers between devices: 18.8 us -> 30.1 us
  Pallas kernels: 21.1 us -> 23.3 us
  local copies, waits for them, and re-layouts: 1.08 us -> 2.41 us
    all_to_all x1 -> x0, blocking collectives: 28.1 us -> none  [shards(): lax.all_to_all(packed, 'gx', split_axis=0, concat_axis=0, tiled=True)]
    ppermute x1, waiting for transfers between devices: 0.01 us -> 11.9 us  [shards(): prev3 = lax.ppermute(r0, 'gx', up)]
    all_to_all x0 -> x1, starting transfers between devices: none -> 11.9 us  [shards(): lax.all_to_all(packed, 'gx', split_axis=0, concat_axis=0, tiled=True)]
    ppermute x1, waiting for transfers between devices: 0.29 us -> 7.29 us  [shards(): next1 = lax.ppermute(p0, 'gx', down)]
    ppermute x1, starting transfers between devices: 5.07 us -> 0.46 us  [shards(): prev3 = lax.ppermute(r0, 'gx', up)]
    ppermute x1, starting transfers between devices: 0.01 us -> 4.05 us  [shards(): next3 = lax.ppermute(r2, 'gx', down)]
    pallas_call x7, Pallas kernels: 21.1 us -> 23.3 us  [call(): pl.pallas_call(kernel, out_shape=outs, in_specs=in_specs, out_specs=jax.t...]
    unnamed x38 -> x34, local copies, waits for them, and re-layouts: 1.08 us -> 2.41 us
  transfers between devices with their start and end apart: 7 -> 8, of which waited for: 4 -> 4; matrix products, arithmetic and copies ran while one was open for 0% -> 0% of each run, Pallas kernels for 17% -> 13%
where the time goes in v6:
time: 85.9 us; the launch traced here: 85.5 us
  starting transfers between devices  30.1 us (35%)
  waiting for transfers between devices  28.8 us (34%)
  Pallas kernels  23.3 us (27%)
  local copies, waits for them, and re-layouts  2.41 us (3%)
  between operations  0.88 us (1%)
    pallas_call x7, Pallas kernels, call(): pl.pallas_call(kernel, out_shape=outs, in_specs=in_specs, out_specs=jax.t...  23.3 us
    ppermute x1, waiting for transfers between devices, shards(): prev3 = lax.ppermute(r0, 'gx', up)  11.9 us
    all_to_all x1, starting transfers between devices, shards(): lax.all_to_all(packed, 'gx', split_axis=0, concat_axis=0, tiled=True)  11.9 us
    ppermute x1, waiting for transfers between devices, shards(): next1 = lax.ppermute(p0, 'gx', down)  7.29 us
    ppermute x1, starting transfers between devices, shards(): next2 = lax.ppermute(down2, 'gx', down)  5.5 us
    all_to_all x1, waiting for transfers between devices, shards(): lax.all_to_all(back, 'gx', split_axis=0, concat_axis=0, tiled=True)  4.9 us
    ppermute x1, waiting for transfers between devices, shards(): prev1 = lax.ppermute(p2, 'gx', up)  4.71 us
    ppermute x1, starting transfers between devices, shards(): next1 = lax.ppermute(p0, 'gx', down)  4.44 us
  transfers between devices with their start and end apart: 8, of which 4 were waited for; matrix products, arithmetic and copies ran while one was open for 0% of the time, Pallas kernels for 13%

profile of v6, /device:TPU:0, one launch (start us, length us, event | category | flops | bytes accessed | tf_op | source)
XLA Modules:
  0.0 85.5 jit_solution(17007596299804431206)
XLA Ops:
  0.6 1.3 %shard_map.104 = (f32[8,32,512]{2,1,0:T(8,128)S(1)}, f32[8,32,512]{2,1,0:T(8,128)S(1)}, f32[10,32,512]{2,1,0:T(8,128)S(1)}, f32[10,32,512]{2,1,0:T(8,128)S(1)}) custom-call(s32[2]{0:T(128)} %refs_0_, bf16[8,3,32,512]{3,2,1,0:T(8,128)(2,1)} %jitter_any.1, s32[3,32,512]{2,1,0:T(8,128)} %ids_any.1), custom_call_target="tpu_custom_call" | custom-call | flops 2097152 | bytes 4194304 | tf_op jit(solution)/shard_map/pallas_call | solution.py:377
  2.0 5.5 %collective-permute-start.3 = (f32[10,32,512]{2,1,0:T(8,128)S(1)}, f32[10,32,512]{2,1,0:T(8,128)S(1)}, u32[]{:S(2)}, u32[]{:S(2)}) collective-permute-start(f32[10,32,512]{2,1,0:T(8,128)S(1)} %get-tuple-element.37), channel_id=1, source_target_pairs={{1,0},{2,1},{3,2},{4,3},{5,4},{6,5},{7,6},{8,7},{9,8},{10,9},{11,1... | collective-permute-start | bytes 1966088 | tf_op jit(solution)/shard_map/ppermute | solution.py:430
  7.5 0.0 collective-permute-start
  7.5 4.4 %collective-permute-start.2 = (f32[8,32,512]{2,1,0:T(8,128)S(1)}, f32[8,32,512]{2,1,0:T(8,128)S(1)}, u32[]{:S(2)}, u32[]{:S(2)}) collective-permute-start(f32[8,32,512]{2,1,0:T(8,128)S(1)} %get-tuple-element.31.p0), channel_id=1, source_target_pairs={{1,0},{2,1},{3,2},{4,3},{5,4},{6,5},{7,6},{8,7},{9,8},{10,9},{11,1... | collective-permute-start | bytes 1572872 | tf_op jit(solution)/shard_map/ppermute | solution.py:428
  11.9 0.0 collective-permute-start.1
  11.9 1.9 %shard_map.105 = (f32[3,8,32,512]{3,2,1,0:T(8,128)S(1)}, f32[8,32,512]{2,1,0:T(8,128)S(1)}, f32[6,32,512]{2,1,0:T(8,128)S(1)}, f32[6,32,512]{2,1,0:T(8,128)S(1)}) custom-call(s32[2]{0:T(128)} %refs_0_, s32[8,8]{1,0:T(8,128)} %refs_1_.1, f32[8,32,512]{2,1,0:T(8,128)S(1)} %get-tuple-element.31.p0, f32[8,32,512]{2,1,0:T(8,128)S(1)} %get-tuple-element.32.p2, ...), custom_call_target="tpu_custom_call" | custom-call | flops 16777216 | bytes 4194304 | tf_op jit(solution)/shard_map/pallas_call | solution.py:377
  13.9 0.0 copy-start.1
  13.9 0.0 copy-start.10
  13.9 0.0 copy-start.12
  13.9 7.3 %collective-permute-done.2.next1.refs_6_ = f32[8,32,512]{2,1,0:T(8,128)S(1)} collective-permute-done((f32[8,32,512]{2,1,0:T(8,128)S(1)}, f32[8,32,512]{2,1,0:T(8,128)S(1)}, u32[]{:S(2)}, u32[]{:S(2)}) %collective-permute-start.2) | collective-permute-done | bytes 524320 | tf_op jit(solution)/shard_map/ppermute | solution.py:428
  21.2 0.0 copy-start.2
  21.2 4.7 %collective-permute-done.1.prev1.refs_3_ = f32[8,32,512]{2,1,0:T(8,128)S(1)} collective-permute-done((f32[8,32,512]{2,1,0:T(8,128)S(1)}, f32[8,32,512]{2,1,0:T(8,128)S(1)}, u32[]{:S(2)}, u32[]{:S(2)}) %collective-permute-start.1) | collective-permute-done | bytes 524320 | tf_op jit(solution)/shard_map/ppermute | solution.py:427
  25.9 0.0 copy-start.3
  25.9 1.7 %shard_map.106.near_out.refs_8_ = f32[40,32,512]{2,1,0:T(8,128)S(1)} custom-call(s32[8,8]{1,0:T(8,128)} %refs_1_.1, f32[8,32,512]{2,1,0:T(8,128)S(1)} %get-tuple-element.31.p0, f32[8,32,512]{2,1,0:T(8,128)S(1)} %get-tuple-element.32.p2, f32[10,32,512]{2,1,0:T(8,128)S(1)} %get-tuple-element.30.up2, f32[8,32,512]{2,1,0:T(8,128)S(1)} %collective-permute-done.1.prev1.refs_3_, ...), custom_call_target="tpu_custom_call" | custom-call | flops 33554432 | bytes 16777216 | tf_op jit(solution)/shard_map/pallas_call | solution.py:377
  27.6 0.0 copy-done.1
  27.6 0.0 copy-done.10
  27.6 0.0 copy-done.12
  27.6 0.0 copy-start
  27.6 1.5 %copy-done = f32[40,32,512]{2,1,0:T(8,128)} copy-done((f32[40,32,512]{2,1,0:T(8,128)}, f32[40,32,512]{2,1,0:T(8,128)S(1)}, u32[]{:S(2)}) %copy-start) | copy-done | bytes 2621464
  29.1 0.0 copy-start.7
  29.1 0.0 copy-start.8
  29.1 0.0 collective-permute-done.3.next2.refs_5_
  29.1 0.0 copy-start.14
  29.1 0.0 copy-start.13
  29.1 0.0 copy-start.11
  29.2 0.0 copy-start.9
  29.2 0.0 collective-permute-done.prev2.refs_2_
  29.2 0.0 copy-done.2
  29.2 0.0 copy-done.3
  29.2 0.8 copy-done.14
  30.0 0.0 copy-start.4
  30.0 7.0 %shard_map.107 = (f32[16,48,128]{2,1,0:T(8,128)}, f32[38,32,512]{2,1,0:T(8,128)}) custom-call(s32[2]{0:T(128)} %refs_0_, s32[8,8]{1,0:T(8,128)} %refs_1_.1, f32[8,32,512]{2,1,0:T(8,128)S(1)} %get-tuple-element.31.p0, f32[8,32,512]{2,1,0:T(8,128)S(1)} %get-tuple-element.32.p2, f32[8,32,512]{2,1,0:T(8,128)S(1)} %collective-permute-done.1.prev1.refs_3_, ...), custom_call_target="tpu_custom_call" | custom-call | flops 268435456 | bytes 8388608 | tf_op jit(solution)/shard_map/pallas_call | solution.py:377
  37.0 0.0 copy-done.4
  37.0 11.9 %all-to-all-start = ((f32[16,48,128]{2,1,0:T(8,128)}), f32[16,48,128]{2,1,0:T(8,128)S(1)}, u32[]{:S(2)}, u32[]{:S(2)}) async-start(f32[16,48,128]{2,1,0:T(8,128)} %get-tuple-element.40), calls=%async_computation | async-start | bytes 786432 | tf_op jit(solution)/shard_map/all_to_all | solution.py:467
  48.9 0.0 copy-done.13
  48.9 0.5 collective-permute-start.4
  49.4 0.0 copy-done.11
  49.4 4.0 %collective-permute-start.5 = (f32[6,32,512]{2,1,0:T(8,128)S(1)}, f32[6,32,512]{2,1,0:T(8,128)S(1)}, u32[]{:S(2)}, u32[]{:S(2)}) collective-permute-start(f32[6,32,512]{2,1,0:T(8,128)S(1)} %copy-done.11), channel_id=1, source_target_pairs={{1,0},{2,1},{3,2},{4,3},{5,4},{6,5},{7,6},{8,7},{9,8},{10,9},{11,1... | collective-permute-start | bytes 1179656 | tf_op jit(solution)/shard_map/ppermute | solution.py:441
  53.4 11.9 %collective-permute-done.4.refs_4_ = f32[6,32,512]{2,1,0:T(8,128)S(1)} collective-permute-done((f32[6,32,512]{2,1,0:T(8,128)S(1)}, f32[6,32,512]{2,1,0:T(8,128)S(1)}, u32[]{:S(2)}, u32[]{:S(2)}) %collective-permute-start.4) | collective-permute-done | bytes 393248 | tf_op jit(solution)/shard_map/ppermute | solution.py:440
  65.3 0.0 copy-start.15
  65.3 0.0 collective-permute-done.5.refs_7_
  65.3 0.0 copy-start.16
  65.3 0.0 all-to-all-done
  65.3 0.0 copy-done.7
  65.3 0.0 copy-done.8
  65.3 0.0 copy-done.9
  65.3 2.9 %shard_map.108 = f32[768,128]{1,0:T(8,128)} custom-call(f32[768,128]{1,0:T(8,128)S(1)} %bitcast.2, bf16[2,256,128]{2,1,0:T(8,128)(2,1)S(1)} %copy-done.8, bf16[2,256,128]{2,1,0:T(8,128)(2,1)S(1)} %copy-done.7, bf16[96,144]{1,0:T(8,128)(2,1)S(1)} %copy-done.9), custom_call_target="tpu_custom_call" | custom-call | flops 268435456 | bytes 4194304 | tf_op jit(solution)/shard_map/pallas_call | solution.py:377
  68.2 3.8 %all-to-all-start.1 = ((f32[16,48,128]{2,1,0:T(8,128)}), f32[16,48,128]{2,1,0:T(8,128)S(1)}, u32[]{:S(2)}, u32[]{:S(2)}) async-start(f32[16,48,128]{2,1,0:T(8,128)} %bitcast.1), calls=%async_computation.1 | async-start | bytes 786432 | tf_op jit(solution)/shard_map/all_to_all | solution.py:487
  72.0 0.0 copy-done.15
  72.0 0.0 copy-done.16
  72.0 0.0 copy-start.5
  72.0 0.0 copy-start.6
  72.0 7.2 %shard_map.109 = f32[8,3,32,512]{3,2,1,0:T(8,128)} custom-call(s32[2]{0:T(128)} %refs_0_, s32[8,8]{1,0:T(8,128)} %refs_1_.1, f32[10,32,512]{2,1,0:T(8,128)} %copy-done.4, f32[8,32,512]{2,1,0:T(8,128)} %copy-done.3, f32[6,32,512]{2,1,0:T(8,128)} %copy-done.15, f32[10,32,512]{2,1,0:T(8,128)} %copy-done.14, f32[8,32,512]{2,1,0:T(8,128)} %copy-done.2, ...), custom_call_target="tpu_custom_call" | custom-call | flops 67108864 | bytes 16777216 | tf_op jit(solution)/shard_map/pallas_call | solution.py:377
  79.3 4.9 %all-to-all-done.1.returned = f32[16,48,128]{2,1,0:T(8,128)S(1)} async-done(((f32[16,48,128]{2,1,0:T(8,128)}), f32[16,48,128]{2,1,0:T(8,128)S(1)}, u32[]{:S(2)}, u32[]{:S(2)}) %all-to-all-start.1) | async-done | bytes 393248 | tf_op jit(solution)/shard_map/all_to_all | solution.py:487
  84.2 0.0 copy-done.5
  84.2 0.0 copy-done.6
  84.2 1.3 %shard_map.110 = f32[2,3,32,512]{3,2,1,0:T(8,128)} custom-call(f32[16,48,128]{2,1,0:T(8,128)S(1)} %all-to-all-done.1.returned, bf16[512,512]{1,0:T(8,128)(2,1)S(1)} %copy-done.6, bf16[512,512]{1,0:T(8,128)(2,1)S(1)} %copy-done.5), custom_call_target="tpu_custom_call" | custom-call | flops 268435456 | bytes 4194304 | tf_op jit(solution)/shard_map/pallas_call | solution.py:377
Async XLA Ops:
  2.0 27.2 %collective-permute-start.3 = (f32[10,32,512]{2,1,0:T(8,128)S(1)}, f32[10,32,512]{2,1,0:T(8,128)S(1)}, u32[]{:S(2)}, u32[]{:S(2)}) collective-permute-start(f32[10,32,512]{2,1,0:T(8,128)S(1)} %get-tuple-element.37), channel_id=1, source_target_pairs={{1,0},{2,1},{3,2},{4,3},{5,4},{6,5},{7,6},{8,7},{9,8},{10,9},{11,1... | collective-permute-start | bytes 1966088 | tf_op jit(solution)/shard_map/ppermute | solution.py:430
  7.5 21.7 %collective-permute-start = (f32[10,32,512]{2,1,0:T(8,128)S(1)}, f32[10,32,512]{2,1,0:T(8,128)S(1)}, u32[]{:S(2)}, u32[]{:S(2)}) collective-permute-start(f32[10,32,512]{2,1,0:T(8,128)S(1)} %get-tuple-element.30.up2), channel_id=1, source_target_pairs={{0,1},{1,2},{2,3},{3,4},{4,5},{5,6},{6,7},{7,8},{8,9},{9,10},{10,1... | collective-permute-start | bytes 1966088 | tf_op jit(solution)/shard_map/ppermute | solution.py:429
  7.5 13.7 %collective-permute-start.2 = (f32[8,32,512]{2,1,0:T(8,128)S(1)}, f32[8,32,512]{2,1,0:T(8,128)S(1)}, u32[]{:S(2)}, u32[]{:S(2)}) collective-permute-start(f32[8,32,512]{2,1,0:T(8,128)S(1)} %get-tuple-element.31.p0), channel_id=1, source_target_pairs={{1,0},{2,1},{3,2},{4,3},{5,4},{6,5},{7,6},{8,7},{9,8},{10,9},{11,1... | collective-permute-start | bytes 1572872 | tf_op jit(solution)/shard_map/ppermute | solution.py:428
  11.9 14.0 %collective-permute-start.1 = (f32[8,32,512]{2,1,0:T(8,128)S(1)}, f32[8,32,512]{2,1,0:T(8,128)S(1)}, u32[]{:S(2)}, u32[]{:S(2)}) collective-permute-start(f32[8,32,512]{2,1,0:T(8,128)S(1)} %get-tuple-element.32.p2), channel_id=1, source_target_pairs={{0,1},{1,2},{2,3},{3,4},{4,5},{5,6},{6,7},{7,8},{8,9},{9,10},{10,1... | collective-permute-start | bytes 1572872 | tf_op jit(solution)/shard_map/ppermute | solution.py:427
  13.9 13.7 %copy-start.1 = (f32[3,8,32,512]{3,2,1,0:T(8,128)}, f32[3,8,32,512]{3,2,1,0:T(8,128)S(1)}, u32[]{:S(2)}) copy-start(f32[3,8,32,512]{3,2,1,0:T(8,128)S(1)} %get-tuple-element.57.rates.refs_10_) | copy-start | bytes 4718596
  13.9 13.7 %copy-start.10 = (f32[6,32,512]{2,1,0:T(8,128)}, f32[6,32,512]{2,1,0:T(8,128)S(1)}, u32[]{:S(2)}) copy-start(f32[6,32,512]{2,1,0:T(8,128)S(1)} %get-tuple-element.42) | copy-start | bytes 1179652
  13.9 13.7 %copy-start.12 = (f32[6,32,512]{2,1,0:T(8,128)}, f32[6,32,512]{2,1,0:T(8,128)S(1)}, u32[]{:S(2)}) copy-start(f32[6,32,512]{2,1,0:T(8,128)S(1)} %get-tuple-element.41) | copy-start | bytes 1179652
  21.2 8.0 %copy-start.2 = (f32[8,32,512]{2,1,0:T(8,128)}, f32[8,32,512]{2,1,0:T(8,128)S(1)}, u32[]{:S(2)}) copy-start(f32[8,32,512]{2,1,0:T(8,128)S(1)} %collective-permute-done.2.next1.refs_6_) | copy-start | bytes 1572868
  25.9 3.3 %copy-start.3 = (f32[8,32,512]{2,1,0:T(8,128)}, f32[8,32,512]{2,1,0:T(8,128)S(1)}, u32[]{:S(2)}) copy-start(f32[8,32,512]{2,1,0:T(8,128)S(1)} %collective-permute-done.1.prev1.refs_3_) | copy-start | bytes 1572868
  27.6 1.5 %copy-start = (f32[40,32,512]{2,1,0:T(8,128)}, f32[40,32,512]{2,1,0:T(8,128)S(1)}, u32[]{:S(2)}) copy-start(f32[40,32,512]{2,1,0:T(8,128)S(1)} %shard_map.106.near_out.refs_8_) | copy-start | bytes 7864324
  29.1 36.2 %copy-start.7 = (bf16[2,256,128]{2,1,0:T(8,128)(2,1)S(1)}, bf16[2,256,128]{2,1,0:T(8,128)(2,1)}, u32[]{:S(2)}) copy-start(bf16[2,256,128]{2,1,0:T(8,128)(2,1)} %constant.13.clone.refs_2_) | copy-start | bytes 393220
  29.1 36.2 %copy-start.8 = (bf16[2,256,128]{2,1,0:T(8,128)(2,1)S(1)}, bf16[2,256,128]{2,1,0:T(8,128)(2,1)}, u32[]{:S(2)}) copy-start(bf16[2,256,128]{2,1,0:T(8,128)(2,1)} %constant.12.clone.refs_1_) | copy-start | bytes 393220
  29.1 0.9 %copy-start.14 = (f32[10,32,512]{2,1,0:T(8,128)}, f32[10,32,512]{2,1,0:T(8,128)S(1)}, u32[]{:S(2)}) copy-start(f32[10,32,512]{2,1,0:T(8,128)S(1)} %collective-permute-done.3.next2.refs_5_) | copy-start | bytes 1966084
  29.1 19.8 %copy-start.13 = (f32[6,32,512]{2,1,0:T(8,128)S(1)}, f32[6,32,512]{2,1,0:T(8,128)}, u32[]{:S(2)}) copy-start(f32[6,32,512]{2,1,0:T(8,128)} %copy-done.12) | copy-start | bytes 1179652
  29.1 20.2 %copy-start.11 = (f32[6,32,512]{2,1,0:T(8,128)S(1)}, f32[6,32,512]{2,1,0:T(8,128)}, u32[]{:S(2)}) copy-start(f32[6,32,512]{2,1,0:T(8,128)} %copy-done.10) | copy-start | bytes 1179652
  29.2 36.2 %copy-start.9 = (bf16[96,144]{1,0:T(8,128)(2,1)S(1)}, bf16[96,144]{1,0:T(8,128)(2,1)}, u32[]{:S(2)}) copy-start(bf16[96,144]{1,0:T(8,128)(2,1)} %constant.14.clone.refs_3_) | copy-start | bytes 82948
  30.0 7.0 %copy-start.4 = (f32[10,32,512]{2,1,0:T(8,128)}, f32[10,32,512]{2,1,0:T(8,128)S(1)}, u32[]{:S(2)}) copy-start(f32[10,32,512]{2,1,0:T(8,128)S(1)} %collective-permute-done.prev2.refs_2_) | copy-start | bytes 1966084
  37.0 28.3 %all-to-all-start = ((f32[16,48,128]{2,1,0:T(8,128)}), f32[16,48,128]{2,1,0:T(8,128)S(1)}, u32[]{:S(2)}, u32[]{:S(2)}) async-start(f32[16,48,128]{2,1,0:T(8,128)} %get-tuple-element.40), calls=%async_computation | async-start | bytes 786432 | tf_op jit(solution)/shard_map/all_to_all | solution.py:467
  48.9 16.4 %collective-permute-start.4 = (f32[6,32,512]{2,1,0:T(8,128)S(1)}, f32[6,32,512]{2,1,0:T(8,128)S(1)}, u32[]{:S(2)}, u32[]{:S(2)}) collective-permute-start(f32[6,32,512]{2,1,0:T(8,128)S(1)} %copy-done.13), channel_id=1, source_target_pairs={{0,1},{1,2},{2,3},{3,4},{4,5},{5,6},{6,7},{7,8},{8,9},{9,10},{10,1... | collective-permute-start | bytes 1179656 | tf_op jit(solution)/shard_map/ppermute | solution.py:440
  49.4 15.9 %collective-permute-start.5 = (f32[6,32,512]{2,1,0:T(8,128)S(1)}, f32[6,32,512]{2,1,0:T(8,128)S(1)}, u32[]{:S(2)}, u32[]{:S(2)}) collective-permute-start(f32[6,32,512]{2,1,0:T(8,128)S(1)} %copy-done.11), channel_id=1, source_target_pairs={{1,0},{2,1},{3,2},{4,3},{5,4},{6,5},{7,6},{8,7},{9,8},{10,9},{11,1... | collective-permute-start | bytes 1179656 | tf_op jit(solution)/shard_map/ppermute | solution.py:441
  65.3 6.7 %copy-start.15 = (f32[6,32,512]{2,1,0:T(8,128)}, f32[6,32,512]{2,1,0:T(8,128)S(1)}, u32[]{:S(2)}) copy-start(f32[6,32,512]{2,1,0:T(8,128)S(1)} %collective-permute-done.4.refs_4_) | copy-start | bytes 1179652
  65.3 6.7 %copy-start.16 = (f32[6,32,512]{2,1,0:T(8,128)}, f32[6,32,512]{2,1,0:T(8,128)S(1)}, u32[]{:S(2)}) copy-start(f32[6,32,512]{2,1,0:T(8,128)S(1)} %collective-permute-done.5.refs_7_) | copy-start | bytes 1179652
  68.2 16.0 %all-to-all-start.1 = ((f32[16,48,128]{2,1,0:T(8,128)}), f32[16,48,128]{2,1,0:T(8,128)S(1)}, u32[]{:S(2)}, u32[]{:S(2)}) async-start(f32[16,48,128]{2,1,0:T(8,128)} %bitcast.1), calls=%async_computation.1 | async-start | bytes 786432 | tf_op jit(solution)/shard_map/all_to_all | solution.py:487
  72.0 12.2 %copy-start.5 = (bf16[512,512]{1,0:T(8,128)(2,1)S(1)}, bf16[512,512]{1,0:T(8,128)(2,1)}, u32[]{:S(2)}) copy-start(bf16[512,512]{1,0:T(8,128)(2,1)} %constant.11.clone.low_any.low) | copy-start | bytes 1572868
  72.0 12.1 %copy-start.6 = (bf16[512,512]{1,0:T(8,128)(2,1)S(1)}, bf16[512,512]{1,0:T(8,128)(2,1)}, u32[]{:S(2)}) copy-start(bf16[512,512]{1,0:T(8,128)(2,1)} %constant.10.clone.high_any.high) | copy-start | bytes 1572868

commit v7 on v6

--- a/solution.py
+++ b/solution.py
@@ -91,27 +91,21 @@
     return other
 
 
-def start_kernel(chosen_any, jitter_any, ids_any, p0, p2, up2, down2, chosen, jitter, grain_ids, semaphores):
+def start_kernel(jitter_any, ids_any, p0, p1, p2, jitter, grain_ids, semaphores):
     planes = grain_ids.shape[0]
     pairs = []
-    for k in (2, 0, 1):
+    for k in range(planes):
         pairs.append((jitter_any.at[:, k], jitter.at[:, k]))
         pairs.append((ids_any.at[k], grain_ids.at[k]))
-    pairs.append((chosen_any, chosen))
     copies = fetch(pairs, semaphores)
-    for step, (plane, outs) in enumerate(((2, (p2,)), (0, (p0,)), (1, (up2, down2)))):
-        copies[2 * step].wait()
-        copies[2 * step + 1].wait()
-        ids = grain_ids[plane]
+    for k, out in enumerate((p0, p1, p2)):
+        copies[2 * k].wait()
+        copies[2 * k + 1].wait()
+        ids = grain_ids[k]
         for i in range(GRAINS):
             base = jnp.where(ids == i, jnp.float32(0.6), jnp.float32(0.0))
-            value = base + jitter[i, plane].astype(F32)
-            for out in outs:
-                out[i] = value
-    copies[-1].wait()
-    for k, i in enumerate(pair_of(chosen)):
-        up2[GRAINS + k] = p0[i]
-        down2[GRAINS + k] = p2[i]
+            out[i] = base + jitter[i, k].astype(F32)
+
 
 def grain_of(start):
     ids = jnp.where(start[1] > 0.55, 1, 0)
@@ -157,53 +151,64 @@
         out[i] = rate(classes, ids, i)
 
 
-def inner_kernel(chosen_any, classes_any, p0, p2, up2, rates, middle, r0, r2, chosen, classes, semaphores):
+def inner_kernel(
+    chosen_any, classes_any, p0, p1, p2, up2, down2, r0, r2, rates, middle, chosen, classes, semaphores
+):
     copies = fetch(((chosen_any, chosen), (classes_any, classes)), semaphores)
-    row = (p0, up2, p2)
+    for i in range(GRAINS):
+        up2[i] = p1[i]
+        down2[i] = p1[i]
     for copy in copies:
         copy.wait()
+    for k, i in enumerate(pair_of(chosen)):
+        up2[GRAINS + k] = p0[i]
+        down2[GRAINS + k] = p2[i]
     other = others_of(chosen)
     for r in range(GRAINS - 2):
         i = other(r)
         r0[r] = p0[i]
         r2[r] = p2[i]
-    for k in range(3):
-        rates_plane(classes, row[k], rates.at[k])
-    step_plane(up2, p0, p2, rates.at[1], middle)
+    for k, start in enumerate((p0, p1, p2)):
+        rates_plane(classes, start, rates.at[k])
+    step_plane(p1, p0, p2, rates.at[1], middle)
 
 
 def groups(ref, count, base=0):
     return [ref.at[pl.ds(base + k * GRAINS, GRAINS)] for k in range(count)]
 
 
-def near_kernel(classes_any, p0, p2, up2, prev1, next1, rates, middle, near_out, classes, semaphores):
+def near_kernel(classes_any, p0, p1, p2, prev1, next1, rates, middle, near_out, classes, semaphores):
     edge0, edge1, inner0, inner2, middle2 = groups(near_out, 5)
     copies = fetch(((classes_any, classes),), semaphores)
-    step_plane(p0, prev1, up2, rates.at[0], inner0)
-    step_plane(p2, up2, next1, rates.at[2], inner2)
+    step_plane(p0, prev1, p1, rates.at[0], inner0)
+    step_plane(p2, p1, next1, rates.at[2], inner2)
     copies[0].wait()
     rates_plane(classes, prev1, edge0)
     rates_plane(classes, next1, edge1)
     step_plane(middle, inner0, inner2, rates.at[1], middle2)
 
 
-def pair_kernel(
-    chosen_any, classes_any, p0, p2, prev1, next1, prev2, next2, rates, middle, near_out, high_any, low_any,
-    packed, late, chosen, classes, high, low, edge, fields, semaphores,
-):
-    copies = fetch(
-        ((chosen_any, chosen), (classes_any, classes), (high_any, high), (low_any, low)), semaphores
-    )
-    near_state = groups(near_out, 5)
-    edge_rates, inner1, middle2 = near_state[:2], near_state[2:4], near_state[4]
-    late_state = groups(late, 4)
-    outer1, side2 = late_state[:2], late_state[2:]
+def second_step(p0, p2, prev1, next1, prev2, next2, rates, middle, near_state, outer1, side2):
+    edge_rates, inner1 = near_state[:2], near_state[2:4]
     step_plane(prev1, prev2, p0, edge_rates[0], outer1[0])
     step_plane(next1, p2, next2, edge_rates[1], outer1[1])
     step_plane(inner1[0], outer1[0], middle, rates.at[0], side2[0])
     step_plane(inner1[1], middle, outer1[1], rates.at[2], side2[1])
+
+
+def pair_kernel(
+    chosen_any, classes_any, p0, p2, prev1, next1, prev2, next2, rates, middle, near_out, high_any, low_any,
+    packed, chosen, classes, high, low, second, edge, fields, semaphores,
+):
+    copies = fetch(
+        ((chosen_any, chosen), (classes_any, classes), (high_any, high), (low_any, low)), semaphores
+    )
+    near_state = groups(near_out, 5)
+    edge_rates, inner1, middle2 = near_state[:2], near_state[2:4], near_state[4]
+    outer1, side2 = groups(second, 2), groups(second, 2, 2 * GRAINS)
+    second_step(p0, p2, prev1, next1, prev2, next2, rates, middle, near_state, outer1, side2)
     eta2 = (side2[0], middle2, side2[1])
-    depth, width = late.shape[1:]
+    depth, width = p0.shape[1:]
     totals = [squares(state) for state in eta2]
     copies[0].wait()
     copies[1].wait()
@@ -222,7 +227,6 @@
             before = edge[0, f] if k == 0 else eta2[k - 1][i]
             after = edge[1, f] if k == 2 else eta2[k + 1][i]
             value = update(eta2[k][i], before, after, totals[k], rates[k, i])
-            late[4 * GRAINS + 3 * f + k] = value
             values.append(value)
         values[1] = jnp.where(repeated, values[0], values[1])
         for f in range(2):
@@ -252,38 +256,35 @@
 
 
 def rest_kernel(*refs):
-    count = (len(refs) - 3) // 2
+    count = (len(refs) - 4) // 2
     sources, out, targets = refs[:count], refs[count], refs[count + 1 : 2 * count + 1]
-    edge, semaphores = refs[-2:]
+    second, edge, semaphores = refs[-3:]
     copies = fetch(list(zip(sources, targets)), semaphores)
-    chosen, classes, prev2, prev1, prev3, next2, next1, next3, near_out, late, rates = targets
+    chosen, classes, p0, p2, prev1, next1, prev2, next2, near_out, middle, rates, prev3, next3 = targets
     near_state = groups(near_out, 5)
     edge_rates, inner1, middle2 = near_state[:2], near_state[2:4], near_state[4]
-    late_state = groups(late, 4)
-    outer1, side2 = late_state[:2], late_state[2:]
-    for copy in copies[:10]:
+    outer1, side2 = groups(second, 2), groups(second, 2, 2 * GRAINS)
+    for copy in copies:
         copy.wait()
+    second_step(p0, p2, prev1, next1, prev2, next2, rates, middle, near_state, outer1, side2)
     other = others_of(chosen)
-    rest = GRAINS - 2
+    pair = pair_of(chosen)
+    places = [(pair[k], GRAINS + k, None) for k in range(2)] + [(other(r), None, r) for r in range(GRAINS - 2)]
     for side, (far, mid, near) in enumerate(((prev3, prev2, prev1), (next3, next2, next1))):
         ids = grain_of(mid)
         total0 = squares(mid)
         total1 = squares(outer1[side])
-        for r in range(rest):
-            i = other(r)
-            first = update(mid[i], far[r], near[i], total0, rate(classes, ids, i))
-            edge[side, r] = update(outer1[side][i], first, inner1[side][i], total1, edge_rates[side][i])
-    copies[10].wait()
+        for k, (i, early, late) in enumerate(places):
+            third = far[late] if early is None else mid[early]
+            first = update(mid[i], third, near[i], total0, rate(classes, ids, i))
+            edge[side, k] = update(outer1[side][i], first, inner1[side][i], total1, edge_rates[side][i])
     eta2 = (side2[0], middle2, side2[1])
-    for k in range(3):
-        total = squares(eta2[k])
-        for r in range(rest):
-            i = other(r)
-            before = edge[0, r] if k == 0 else eta2[k - 1][i]
-            after = edge[1, r] if k == 2 else eta2[k + 1][i]
-            out[i, k] = update(eta2[k][i], before, after, total, rates[k, i])
-        for f, i in enumerate(pair_of(chosen)):
-            out[i, k] = late[4 * GRAINS + 3 * f + k]
+    for plane in range(3):
+        total = squares(eta2[plane])
+        for k, (i, _, _) in enumerate(places):
+            before = edge[0, k] if plane == 0 else eta2[plane - 1][i]
+            after = edge[1, k] if plane == 2 else eta2[plane + 1][i]
+            out[i, plane] = update(eta2[plane][i], before, after, total, rates[plane, i])
 
 
 def line_kernel(lines, z_forward, z_inverse, x_both, out, wide, tall, scale):
@@ -411,31 +412,30 @@
     six = (GRAINS - 2, depth, width)
     small = [pltpu.SMEM((2,), jnp.int32), pltpu.SMEM((GRAINS, GRAINS), jnp.int32)]
     ten = (GRAINS + 2, depth, width)
-    p0, p2, up2, down2 = call(
+    p0, p1, p2 = call(
         start_kernel,
-        (shape(*plane), shape(*plane), shape(*ten), shape(*ten)),
-        [ANY] * 3,
-        chosen, jitter, grain_ids,
+        (shape(*plane), shape(*plane), shape(*plane)),
+        [ANY] * 2,
+        jitter, grain_ids,
         scratch=[
-            small[0],
             pltpu.VMEM(jitter.shape, jitter.dtype),
             pltpu.VMEM(grain_ids.shape, jnp.int32),
-            pltpu.SemaphoreType.DMA((2 * planes + 1,)),
+            pltpu.SemaphoreType.DMA((2 * planes,)),
         ],
         flops=2**21, moved=2**22,
     )
     prev1 = lax.ppermute(p2, "gx", up)
     next1 = lax.ppermute(p0, "gx", down)
+    up2, down2, r0, r2, rates, middle = call(
+        inner_kernel,
+        (shape(*ten), shape(*ten), shape(*six), shape(*six), shape(planes, *plane), shape(*plane)),
+        [ANY] * 2 + [VMEM] * 3,
+        chosen, class_table, p0, p1, p2,
+        scratch=[*small, pltpu.SemaphoreType.DMA((2,))],
+        flops=2**24, moved=2**22,
+    )
     prev2 = lax.ppermute(up2, "gx", up)
     next2 = lax.ppermute(down2, "gx", down)
-    rates, middle, r0, r2 = call(
-        inner_kernel,
-        (shape(planes, *plane), shape(*plane), shape(*six), shape(*six)),
-        [ANY] * 2 + [VMEM] * 3,
-        chosen, class_table, p0, p2, up2,
-        scratch=[*small, pltpu.SemaphoreType.DMA((2,))],
-        flops=2**24, moved=2**22,
-    )
     r0, r2, prev1, next1 = lax.optimization_barrier((r0, r2, prev1, next1))
     prev3 = lax.ppermute(r0, "gx", up)
     next3 = lax.ppermute(r2, "gx", down)
@@ -443,32 +443,33 @@
         near_kernel,
         shape(5 * GRAINS, depth, width),
         [ANY] + [VMEM] * 7,
-        class_table, p0, p2, up2, prev1, next1, rates, middle,
+        class_table, p0, p1, p2, prev1, next1, rates, middle,
         scratch=[small[1], pltpu.SemaphoreType.DMA((1,))],
         flops=2**25, moved=2**24,
     )
     packed_shape = (devices, planes * share, lanes) if aligned else (planes, slots, lanes)
-    packed, late_out = call(
+    packed = call(
         pair_kernel,
-        (shape(*packed_shape), shape(4 * GRAINS + 2 * planes, depth, width)),
+        shape(*packed_shape),
         [ANY] * 2 + [VMEM] * 9 + [ANY] * 2,
         chosen, class_table, p0, p2, prev1, next1, prev2, next2, rates, middle, near_out, *table,
         scratch=[
             *small,
             pltpu.VMEM(table[0].shape, BF16),
             pltpu.VMEM(table[1].shape, BF16),
+            pltpu.VMEM((4 * GRAINS, depth, width), F32),
             pltpu.VMEM((2, 2, depth, width), F32),
             pltpu.VMEM(((planes + 1) // 2 * lanes, width), F32),
             pltpu.SemaphoreType.DMA((4,)),
         ],
-        flops=2**28, moved=2**23, limit=50,
-    )
+        flops=2**28, moved=2**23,
+    )
+    packed, prev3, next3 = lax.optimization_barrier((packed, prev3, next3))
     if aligned:
         lines = lax.all_to_all(packed, "gx", split_axis=0, concat_axis=0, tiled=True)
     else:
         lines = lax.all_to_all(packed, "gx", split_axis=1, concat_axis=0, tiled=True)
     lines = lines.reshape(total_x * share, lanes)
-    lines, prev3, next3 = lax.optimization_barrier((lines, prev3, next3))
     def lines_body(*refs):
         line_kernel(*refs, scale=1.0 / (count * count))
 
@@ -488,7 +489,7 @@
     if not aligned:
         returned = returned.reshape(devices, planes, share, lanes).transpose(1, 0, 2, 3)
         returned = returned.reshape(planes, slots, lanes)
-    late = (chosen, class_table, prev2, prev1, prev3, next2, next1, next3, near_out, late_out, rates)
+    late = (chosen, class_table, p0, p2, prev1, next1, prev2, next2, near_out, middle, rates, prev3, next3)
     late, _ = lax.optimization_barrier((late, back))
     order_params = call(
         rest_kernel,
@@ -498,7 +499,8 @@
         scratch=[
             *small,
             *[pltpu.VMEM(value.shape, F32) for value in late[2:]],
-            pltpu.VMEM((2, *six), F32),
+            pltpu.VMEM((4 * GRAINS, depth, width), F32),
+            pltpu.VMEM((2, *plane), F32),
             pltpu.SemaphoreType.DMA((len(late),)),
         ],
         flops=2**26, moved=2**24, limit=24,

time: 85.9 us -> 78.4 us (0.913)
  blocking collectives: 0 us -> 28.1 us
  waiting for transfers between devices: 28.8 us -> 8.4 us
  starting transfers between devices: 30.1 us -> 18.9 us
  local copies, waits for them, and re-layouts: 2.41 us -> 0.08 us
  Pallas kernels: 23.3 us -> 21.9 us
    all_to_all x0 -> x1, blocking collectives: none -> 28.1 us  [shards(): lax.all_to_all(packed, 'gx', split_axis=0, concat_axis=0, tiled=True)]
    all_to_all x1 -> x0, starting transfers between devices: 11.9 us -> none  [shards(): lax.all_to_all(packed, 'gx', split_axis=0, concat_axis=0, tiled=True)]
    ppermute x1, waiting for transfers between devices: 11.9 us -> 0.85 us  [shards(): prev3 = lax.ppermute(r0, 'gx', up)]
    ppermute x1, waiting for transfers between devices: 7.29 us -> 0.16 us  [shards(): next1 = lax.ppermute(p0, 'gx', down)]
    ppermute x1, starting transfers between devices: 0.46 us -> 5.07 us  [shards(): prev3 = lax.ppermute(r0, 'gx', up)]
    ppermute x1, starting transfers between devices: 4.05 us -> 0.01 us  [shards(): next3 = lax.ppermute(r2, 'gx', down)]
    all_to_all x1, waiting for transfers between devices: 4.9 us -> 2.46 us  [shards(): lax.all_to_all(back, 'gx', split_axis=0, concat_axis=0, tiled=True)]
    unnamed x34 -> x32, local copies, waits for them, and re-layouts: 2.41 us -> 0.08 us
  transfers between devices with their start and end apart: 8 -> 7, of which waited for: 4 -> 5; matrix products, arithmetic and copies ran while one was open for 0% -> 0% of each run, Pallas kernels for 13% -> 21%
where the time goes in v7:
time: 78.4 us; the launch traced here: 78.1 us
  blocking collectives  28.1 us (36%)
  Pallas kernels  21.9 us (28%)
  starting transfers between devices  18.9 us (24%)
  waiting for transfers between devices  8.4 us (11%)
  between operations  0.86 us (1%)
    all_to_all x1, blocking collectives, shards(): lax.all_to_all(packed, 'gx', split_axis=0, concat_axis=0, tiled=True)  28.1 us
    pallas_call x7, Pallas kernels, call(): pl.pallas_call(kernel, out_shape=outs, in_specs=in_specs, out_specs=jax.t...  21.9 us
    ppermute x1, starting transfers between devices, shards(): next1 = lax.ppermute(p0, 'gx', down)  5.5 us
    ppermute x1, starting transfers between devices, shards(): prev3 = lax.ppermute(r0, 'gx', up)  5.07 us
    ppermute x1, waiting for transfers between devices, shards(): prev1 = lax.ppermute(p2, 'gx', up)  4.7 us
    ppermute x1, starting transfers between devices, shards(): next2 = lax.ppermute(down2, 'gx', down)  4.49 us
    all_to_all x1, starting transfers between devices, shards(): lax.all_to_all(back, 'gx', split_axis=0, concat_axis=0, tiled=True)  3.73 us
    all_to_all x1, waiting for transfers between devices, shards(): lax.all_to_all(back, 'gx', split_axis=0, concat_axis=0, tiled=True)  2.46 us
  transfers between devices with their start and end apart: 7, of which 5 were waited for; matrix products, arithmetic and copies ran while one was open for 0% of the time, Pallas kernels for 21%

profile of v7, /device:TPU:0, one launch (start us, length us, event | category | flops | bytes accessed | tf_op | source)
XLA Modules:
  0.0 78.1 jit_solution(13160070907731054814)
XLA Ops:
  0.6 1.3 %shard_map.104 = (f32[8,32,512]{2,1,0:T(8,128)S(1)}, f32[8,32,512]{2,1,0:T(8,128)S(1)}, f32[8,32,512]{2,1,0:T(8,128)S(1)}) custom-call(bf16[8,3,32,512]{3,2,1,0:T(8,128)(2,1)} %jitter_any.1, s32[3,32,512]{2,1,0:T(8,128)} %ids_any.1), custom_call_target="tpu_custom_call" | custom-call | flops 2097152 | bytes 4194304 | tf_op jit(solution)/shard_map/pallas_call | solution.py:378
  1.9 0.0 copy-start.2
  1.9 0.0 copy-start.3
  1.9 5.5 %collective-permute-start.1 = (f32[8,32,512]{2,1,0:T(8,128)S(1)}, f32[8,32,512]{2,1,0:T(8,128)S(1)}, u32[]{:S(2)}, u32[]{:S(2)}) collective-permute-start(f32[8,32,512]{2,1,0:T(8,128)S(1)} %get-tuple-element.49.p0.refs_2_), channel_id=1, source_target_pairs={{1,0},{2,1},{3,2},{4,3},{5,4},{6,5},{7,6},{8,7},{9,8},{10,9},{11,1... | collective-permute-start | bytes 1572872 | tf_op jit(solution)/shard_map/ppermute | solution.py:428
  7.4 0.0 collective-permute-start
  7.4 2.0 %shard_map.105 = (f32[10,32,512]{2,1,0:T(8,128)S(1)}, f32[10,32,512]{2,1,0:T(8,128)S(1)}, f32[6,32,512]{2,1,0:T(8,128)S(1)}, f32[6,32,512]{2,1,0:T(8,128)S(1)}, ...) custom-call(s32[2]{0:T(128)} %refs_0_, s32[8,8]{1,0:T(8,128)} %refs_1_.1, ...), custom_call_target="tpu_custom_call" | custom-call | flops 16777216 | bytes 4194304 | tf_op jit(solution)/shard_map/pallas_call | solution.py:378
  9.4 0.0 copy-start.1
  9.4 0.0 copy-start.6
  9.4 0.1 collective-permute-start.2
  9.5 4.5 %collective-permute-start.3 = (f32[10,32,512]{2,1,0:T(8,128)S(1)}, f32[10,32,512]{2,1,0:T(8,128)S(1)}, u32[]{:S(2)}, u32[]{:S(2)}) collective-permute-start(f32[10,32,512]{2,1,0:T(8,128)S(1)} %get-tuple-element.39), channel_id=1, source_target_pairs={{1,0},{2,1},{3,2},{4,3},{5,4},{6,5},{7,6},{8,7},{9,8},{10,9},{11,1... | collective-permute-start | bytes 1966088 | tf_op jit(solution)/shard_map/ppermute | solution.py:438
  14.0 0.2 collective-permute-done.1.next1.refs_5_
  14.1 0.0 copy-start.4
  14.1 4.7 %collective-permute-done.prev1.refs_4_ = f32[8,32,512]{2,1,0:T(8,128)S(1)} collective-permute-done((f32[8,32,512]{2,1,0:T(8,128)S(1)}, f32[8,32,512]{2,1,0:T(8,128)S(1)}, u32[]{:S(2)}, u32[]{:S(2)}) %collective-permute-start) | collective-permute-done | bytes 524320 | tf_op jit(solution)/shard_map/ppermute | solution.py:427
  18.8 0.0 copy-start.5
  18.8 5.1 %collective-permute-start.4 = (f32[6,32,512]{2,1,0:T(8,128)S(1)}, f32[6,32,512]{2,1,0:T(8,128)S(1)}, u32[]{:S(2)}, u32[]{:S(2)}) collective-permute-start(f32[6,32,512]{2,1,0:T(8,128)S(1)} %get-tuple-element.42), channel_id=1, source_target_pairs={{0,1},{1,2},{2,3},{3,4},{4,5},{5,6},{6,7},{7,8},{8,9},{9,10},{10,1... | collective-permute-start | bytes 1179656 | tf_op jit(solution)/shard_map/ppermute | solution.py:440
  23.9 0.0 collective-permute-start.5
  23.9 1.7 %shard_map.106.near_out.refs_8_ = f32[40,32,512]{2,1,0:T(8,128)S(1)} custom-call(s32[8,8]{1,0:T(8,128)} %refs_1_.1, f32[8,32,512]{2,1,0:T(8,128)S(1)} %get-tuple-element.49.p0.refs_2_, f32[8,32,512]{2,1,0:T(8,128)S(1)} %get-tuple-element.33.p1, f32[8,32,512]{2,1,0:T(8,128)S(1)} %get-tuple-element.50.p2.refs_3_, ...), custom_call_target="tpu_custom_call" | custom-call | flops 33554432 | bytes 16777216 | tf_op jit(solution)/shard_map/pallas_call | solution.py:378
  25.6 0.0 copy-start
  25.6 0.0 copy-start.11
  25.6 0.0 copy-start.12
  25.6 0.0 copy-start.13
  25.6 0.2 collective-permute-done.2.prev2.refs_6_
  25.9 0.0 copy-start.7
  25.9 0.0 collective-permute-done.3.next2.refs_7_
  25.9 0.0 copy-done.2
  25.9 0.0 copy-done.3
  25.9 0.0 copy-done.1
  25.9 0.0 copy-done.6
  25.9 0.0 copy-done.4
  25.9 0.0 copy-done.5
  25.9 0.0 copy-start.8
  25.9 3.3 %shard_map.107 = f32[16,48,128]{2,1,0:T(8,128)S(1)} custom-call(s32[2]{0:T(128)} %refs_0_, s32[8,8]{1,0:T(8,128)} %refs_1_.1, f32[8,32,512]{2,1,0:T(8,128)S(1)} %get-tuple-element.49.p0.refs_2_, f32[8,32,512]{2,1,0:T(8,128)S(1)} %get-tuple-element.50.p2.refs_3_, f32[8,32,512]{2,1,0:T(8,128)S(1)} %collective-permute-done.prev1.refs_4_, ...), custom_call_target="tpu_custom_call" | custom-call | flops 268435456 | bytes 8388608 | tf_op jit(solution)/shard_map/pallas_call | solution.py:378
  29.2 0.0 copy-done
  29.2 0.0 copy-done.7
  29.2 0.0 copy-done.8
  29.2 0.8 %collective-permute-done.4.refs_11_ = f32[6,32,512]{2,1,0:T(8,128)S(1)} collective-permute-done((f32[6,32,512]{2,1,0:T(8,128)S(1)}, f32[6,32,512]{2,1,0:T(8,128)S(1)}, u32[]{:S(2)}, u32[]{:S(2)}) %collective-permute-start.4) | collective-permute-done | bytes 393248 | tf_op jit(solution)/shard_map/ppermute | solution.py:440
  30.1 0.0 copy-start.14
  30.1 0.0 collective-permute-done.5.refs_12_
  30.1 0.0 copy-start.15
  30.1 28.1 %all_to_all.10 = f32[16,48,128]{2,1,0:T(8,128)S(1)} all-to-all(f32[16,48,128]{2,1,0:T(8,128)S(1)} %shard_map.107), channel_id=1, replica_groups=mesh['grp'=2,'gx'=16] {'gx'}, dimensions={0} | all-to-all | bytes 786432 | tf_op jit(solution)/shard_map/all_to_all | solution.py:469
  58.1 0.0 copy-done.11
  58.1 0.0 copy-done.12
  58.1 0.0 copy-done.13
  58.2 2.9 %shard_map.108 = f32[768,128]{1,0:T(8,128)} custom-call(f32[768,128]{1,0:T(8,128)S(1)} %bitcast.2, bf16[2,256,128]{2,1,0:T(8,128)(2,1)S(1)} %copy-done.12, bf16[2,256,128]{2,1,0:T(8,128)(2,1)S(1)} %copy-done.11, bf16[96,144]{1,0:T(8,128)(2,1)S(1)} %copy-done.13), custom_call_target="tpu_custom_call" | custom-call | flops 268435456 | bytes 4194304 | tf_op jit(solution)/shard_map/pallas_call | solution.py:378
  61.1 0.0 copy-done.15
  61.1 3.7 %all-to-all-start.1 = ((f32[16,48,128]{2,1,0:T(8,128)}), f32[16,48,128]{2,1,0:T(8,128)S(1)}, u32[]{:S(2)}, u32[]{:S(2)}) async-start(f32[16,48,128]{2,1,0:T(8,128)} %bitcast.1), calls=%async_computation.1 | async-start | bytes 786432 | tf_op jit(solution)/shard_map/all_to_all | solution.py:488
  64.8 0.0 copy-done.14
  64.8 0.0 copy-start.9
  64.8 0.0 copy-start.10
  64.8 9.5 %shard_map.109 = f32[8,3,32,512]{3,2,1,0:T(8,128)} custom-call(s32[2]{0:T(128)} %refs_0_, s32[8,8]{1,0:T(8,128)} %refs_1_.1, f32[8,32,512]{2,1,0:T(8,128)} %copy-done.2, f32[8,32,512]{2,1,0:T(8,128)} %copy-done.3, f32[8,32,512]{2,1,0:T(8,128)} %copy-done.5, f32[8,32,512]{2,1,0:T(8,128)} %copy-done.4, f32[10,32,512]{2,1,0:T(8,128)} %copy-done.7, ...), custom_call_target="tpu_custom_call" | custom-call | flops 67108864 | bytes 16777216 | tf_op jit(solution)/shard_map/pallas_call | solution.py:378
  74.3 2.5 %all-to-all-done.1.returned = f32[16,48,128]{2,1,0:T(8,128)S(1)} async-done(((f32[16,48,128]{2,1,0:T(8,128)}), f32[16,48,128]{2,1,0:T(8,128)S(1)}, u32[]{:S(2)}, u32[]{:S(2)}) %all-to-all-start.1) | async-done | bytes 393248 | tf_op jit(solution)/shard_map/all_to_all | solution.py:488
  76.8 0.0 copy-done.9
  76.8 0.0 copy-done.10
  76.8 1.3 %shard_map.110 = f32[2,3,32,512]{3,2,1,0:T(8,128)} custom-call(f32[16,48,128]{2,1,0:T(8,128)S(1)} %all-to-all-done.1.returned, bf16[512,512]{1,0:T(8,128)(2,1)S(1)} %copy-done.10, bf16[512,512]{1,0:T(8,128)(2,1)S(1)} %copy-done.9), custom_call_target="tpu_custom_call" | custom-call | flops 268435456 | bytes 4194304 | tf_op jit(solution)/shard_map/pallas_call | solution.py:378
Async XLA Ops:
  1.9 24.0 %copy-start.2 = (f32[8,32,512]{2,1,0:T(8,128)}, f32[8,32,512]{2,1,0:T(8,128)S(1)}, u32[]{:S(2)}) copy-start(f32[8,32,512]{2,1,0:T(8,128)S(1)} %get-tuple-element.49.p0.refs_2_) | copy-start | bytes 1572868
  1.9 23.9 %copy-start.3 = (f32[8,32,512]{2,1,0:T(8,128)}, f32[8,32,512]{2,1,0:T(8,128)S(1)}, u32[]{:S(2)}) copy-start(f32[8,32,512]{2,1,0:T(8,128)S(1)} %get-tuple-element.50.p2.refs_3_) | copy-start | bytes 1572868
  1.9 12.2 %collective-permute-start.1 = (f32[8,32,512]{2,1,0:T(8,128)S(1)}, f32[8,32,512]{2,1,0:T(8,128)S(1)}, u32[]{:S(2)}, u32[]{:S(2)}) collective-permute-start(f32[8,32,512]{2,1,0:T(8,128)S(1)} %get-tuple-element.49.p0.refs_2_), channel_id=1, source_target_pairs={{1,0},{2,1},{3,2},{4,3},{5,4},{6,5},{7,6},{8,7},{9,8},{10,9},{11,1... | collective-permute-start | bytes 1572872 | tf_op jit(solution)/shard_map/ppermute | solution.py:428
  7.4 11.4 %collective-permute-start = (f32[8,32,512]{2,1,0:T(8,128)S(1)}, f32[8,32,512]{2,1,0:T(8,128)S(1)}, u32[]{:S(2)}, u32[]{:S(2)}) collective-permute-start(f32[8,32,512]{2,1,0:T(8,128)S(1)} %get-tuple-element.50.p2.refs_3_), channel_id=1, source_target_pairs={{0,1},{1,2},{2,3},{3,4},{4,5},{5,6},{6,7},{7,8},{8,9},{9,10},{10,1... | collective-permute-start | bytes 1572872 | tf_op jit(solution)/shard_map/ppermute | solution.py:427
  9.4 16.5 %copy-start.1 = (f32[3,8,32,512]{3,2,1,0:T(8,128)}, f32[3,8,32,512]{3,2,1,0:T(8,128)S(1)}, u32[]{:S(2)}) copy-start(f32[3,8,32,512]{3,2,1,0:T(8,128)S(1)} %get-tuple-element.57.rates.refs_10_) | copy-start | bytes 4718596
  9.4 16.5 %copy-start.6 = (f32[8,32,512]{2,1,0:T(8,128)}, f32[8,32,512]{2,1,0:T(8,128)S(1)}, u32[]{:S(2)}) copy-start(f32[8,32,512]{2,1,0:T(8,128)S(1)} %get-tuple-element.56.middle.refs_9_) | copy-start | bytes 1572868
  9.4 16.4 %collective-permute-start.2 = (f32[10,32,512]{2,1,0:T(8,128)S(1)}, f32[10,32,512]{2,1,0:T(8,128)S(1)}, u32[]{:S(2)}, u32[]{:S(2)}) collective-permute-start(f32[10,32,512]{2,1,0:T(8,128)S(1)} %get-tuple-element.38), channel_id=1, source_target_pairs={{0,1},{1,2},{2,3},{3,4},{4,5},{5,6},{6,7},{7,8},{8,9},{9,10},{10,1... | collective-permute-start | bytes 1966088 | tf_op jit(solution)/shard_map/ppermute | solution.py:437
  9.5 16.4 %collective-permute-start.3 = (f32[10,32,512]{2,1,0:T(8,128)S(1)}, f32[10,32,512]{2,1,0:T(8,128)S(1)}, u32[]{:S(2)}, u32[]{:S(2)}) collective-permute-start(f32[10,32,512]{2,1,0:T(8,128)S(1)} %get-tuple-element.39), channel_id=1, source_target_pairs={{1,0},{2,1},{3,2},{4,3},{5,4},{6,5},{7,6},{8,7},{9,8},{10,9},{11,1... | collective-permute-start | bytes 1966088 | tf_op jit(solution)/shard_map/ppermute | solution.py:438
  14.1 11.8 %copy-start.4 = (f32[8,32,512]{2,1,0:T(8,128)}, f32[8,32,512]{2,1,0:T(8,128)S(1)}, u32[]{:S(2)}) copy-start(f32[8,32,512]{2,1,0:T(8,128)S(1)} %collective-permute-done.1.next1.refs_5_) | copy-start | bytes 1572868
  18.8 7.1 %copy-start.5 = (f32[8,32,512]{2,1,0:T(8,128)}, f32[8,32,512]{2,1,0:T(8,128)S(1)}, u32[]{:S(2)}) copy-start(f32[8,32,512]{2,1,0:T(8,128)S(1)} %collective-permute-done.prev1.refs_4_) | copy-start | bytes 1572868
  18.8 11.2 %collective-permute-start.4 = (f32[6,32,512]{2,1,0:T(8,128)S(1)}, f32[6,32,512]{2,1,0:T(8,128)S(1)}, u32[]{:S(2)}, u32[]{:S(2)}) collective-permute-start(f32[6,32,512]{2,1,0:T(8,128)S(1)} %get-tuple-element.42), channel_id=1, source_target_pairs={{0,1},{1,2},{2,3},{3,4},{4,5},{5,6},{6,7},{7,8},{8,9},{9,10},{10,1... | collective-permute-start | bytes 1179656 | tf_op jit(solution)/shard_map/ppermute | solution.py:440
  23.9 6.2 %collective-permute-start.5 = (f32[6,32,512]{2,1,0:T(8,128)S(1)}, f32[6,32,512]{2,1,0:T(8,128)S(1)}, u32[]{:S(2)}, u32[]{:S(2)}) collective-permute-start(f32[6,32,512]{2,1,0:T(8,128)S(1)} %get-tuple-element.43), channel_id=1, source_target_pairs={{1,0},{2,1},{3,2},{4,3},{5,4},{6,5},{7,6},{8,7},{9,8},{10,9},{11,1... | collective-permute-start | bytes 1179656 | tf_op jit(solution)/shard_map/ppermute | solution.py:441
  25.6 3.6 %copy-start = (f32[40,32,512]{2,1,0:T(8,128)}, f32[40,32,512]{2,1,0:T(8,128)S(1)}, u32[]{:S(2)}) copy-start(f32[40,32,512]{2,1,0:T(8,128)S(1)} %shard_map.106.near_out.refs_8_) | copy-start | bytes 7864324
  25.6 32.5 %copy-start.11 = (bf16[2,256,128]{2,1,0:T(8,128)(2,1)S(1)}, bf16[2,256,128]{2,1,0:T(8,128)(2,1)}, u32[]{:S(2)}) copy-start(bf16[2,256,128]{2,1,0:T(8,128)(2,1)} %constant.13.clone.refs_2_) | copy-start | bytes 393220
  25.6 32.5 %copy-start.12 = (bf16[2,256,128]{2,1,0:T(8,128)(2,1)S(1)}, bf16[2,256,128]{2,1,0:T(8,128)(2,1)}, u32[]{:S(2)}) copy-start(bf16[2,256,128]{2,1,0:T(8,128)(2,1)} %constant.12.clone.refs_1_) | copy-start | bytes 393220
  25.6 32.5 %copy-start.13 = (bf16[96,144]{1,0:T(8,128)(2,1)S(1)}, bf16[96,144]{1,0:T(8,128)(2,1)}, u32[]{:S(2)}) copy-start(bf16[96,144]{1,0:T(8,128)(2,1)} %constant.14.clone.refs_3_) | copy-start | bytes 82948
  25.9 3.4 %copy-start.7 = (f32[10,32,512]{2,1,0:T(8,128)}, f32[10,32,512]{2,1,0:T(8,128)S(1)}, u32[]{:S(2)}) copy-start(f32[10,32,512]{2,1,0:T(8,128)S(1)} %collective-permute-done.2.prev2.refs_6_) | copy-start | bytes 1966084
  25.9 3.3 %copy-start.8 = (f32[10,32,512]{2,1,0:T(8,128)}, f32[10,32,512]{2,1,0:T(8,128)S(1)}, u32[]{:S(2)}) copy-start(f32[10,32,512]{2,1,0:T(8,128)S(1)} %collective-permute-done.3.next2.refs_7_) | copy-start | bytes 1966084
  30.1 34.7 %copy-start.14 = (f32[6,32,512]{2,1,0:T(8,128)}, f32[6,32,512]{2,1,0:T(8,128)S(1)}, u32[]{:S(2)}) copy-start(f32[6,32,512]{2,1,0:T(8,128)S(1)} %collective-permute-done.4.refs_11_) | copy-start | bytes 1179652
  30.1 31.0 %copy-start.15 = (f32[6,32,512]{2,1,0:T(8,128)}, f32[6,32,512]{2,1,0:T(8,128)S(1)}, u32[]{:S(2)}) copy-start(f32[6,32,512]{2,1,0:T(8,128)S(1)} %collective-permute-done.5.refs_12_) | copy-start | bytes 1179652
  61.1 15.7 %all-to-all-start.1 = ((f32[16,48,128]{2,1,0:T(8,128)}), f32[16,48,128]{2,1,0:T(8,128)S(1)}, u32[]{:S(2)}, u32[]{:S(2)}) async-start(f32[16,48,128]{2,1,0:T(8,128)} %bitcast.1), calls=%async_computation.1 | async-start | bytes 786432 | tf_op jit(solution)/shard_map/all_to_all | solution.py:488
  64.8 12.0 %copy-start.9 = (bf16[512,512]{1,0:T(8,128)(2,1)S(1)}, bf16[512,512]{1,0:T(8,128)(2,1)}, u32[]{:S(2)}) copy-start(bf16[512,512]{1,0:T(8,128)(2,1)} %constant.11.clone.low_any.low) | copy-start | bytes 1572868
  64.8 12.0 %copy-start.10 = (bf16[512,512]{1,0:T(8,128)(2,1)S(1)}, bf16[512,512]{1,0:T(8,128)(2,1)}, u32[]{:S(2)}) copy-start(bf16[512,512]{1,0:T(8,128)(2,1)} %constant.10.clone.high_any.high) | copy-start | bytes 1572868

commit v8 on v7

--- a/solution.py
+++ b/solution.py
@@ -10,6 +10,7 @@
 from jax.sharding import PartitionSpec as P
 
 STEPS = 3
+SOON = 3
 GRAINS = 8
 F32 = jnp.float32
 BF16 = jnp.bfloat16
@@ -152,7 +153,7 @@
 
 
 def inner_kernel(
-    chosen_any, classes_any, p0, p1, p2, up2, down2, r0, r2, rates, middle, chosen, classes, semaphores
+    chosen_any, classes_any, p0, p1, p2, up2, down2, r0, r2, l0, l2, rates, middle, chosen, classes, semaphores
 ):
     copies = fetch(((chosen_any, chosen), (classes_any, classes)), semaphores)
     for i in range(GRAINS):
@@ -166,8 +167,11 @@
     other = others_of(chosen)
     for r in range(GRAINS - 2):
         i = other(r)
-        r0[r] = p0[i]
-        r2[r] = p2[i]
+        for soon, late, start in ((r0, l0, p0), (r2, l2, p2)):
+            if r < SOON:
+                soon[r] = start[i]
+            else:
+                late[r - SOON] = start[i]
     for k, start in enumerate((p0, p1, p2)):
         rates_plane(classes, start, rates.at[k])
     step_plane(p1, p0, p2, rates.at[1], middle)
@@ -260,7 +264,7 @@
     sources, out, targets = refs[:count], refs[count], refs[count + 1 : 2 * count + 1]
     second, edge, semaphores = refs[-3:]
     copies = fetch(list(zip(sources, targets)), semaphores)
-    chosen, classes, p0, p2, prev1, next1, prev2, next2, near_out, middle, rates, prev3, next3 = targets
+    chosen, classes, p0, p2, prev1, next1, prev2, next2, near_out, middle, rates, prev3, next3, prev4, next4 = targets
     near_state = groups(near_out, 5)
     edge_rates, inner1, middle2 = near_state[:2], near_state[2:4], near_state[4]
     outer1, side2 = groups(second, 2), groups(second, 2, 2 * GRAINS)
@@ -270,12 +274,15 @@
     other = others_of(chosen)
     pair = pair_of(chosen)
     places = [(pair[k], GRAINS + k, None) for k in range(2)] + [(other(r), None, r) for r in range(GRAINS - 2)]
-    for side, (far, mid, near) in enumerate(((prev3, prev2, prev1), (next3, next2, next1))):
+    for side, (soon, far, mid, near) in enumerate(((prev3, prev4, prev2, prev1), (next3, next4, next2, next1))):
         ids = grain_of(mid)
         total0 = squares(mid)
         total1 = squares(outer1[side])
         for k, (i, early, late) in enumerate(places):
-            third = far[late] if early is None else mid[early]
+            if early is not None:
+                third = mid[early]
+            else:
+                third = soon[late] if late < SOON else far[late - SOON]
             first = update(mid[i], third, near[i], total0, rate(classes, ids, i))
             edge[side, k] = update(outer1[side][i], first, inner1[side][i], total1, edge_rates[side][i])
     eta2 = (side2[0], middle2, side2[1])
@@ -409,7 +416,7 @@
     x_both = jnp.asarray(np.concatenate([x_high, x_high, x_low], axis=1))
 
     two = (2, *plane)
-    six = (GRAINS - 2, depth, width)
+    soon, last = (SOON, depth, width), (GRAINS - 2 - SOON, depth, width)
     small = [pltpu.SMEM((2,), jnp.int32), pltpu.SMEM((GRAINS, GRAINS), jnp.int32)]
     ten = (GRAINS + 2, depth, width)
     p0, p1, p2 = call(
@@ -426,9 +433,12 @@
     )
     prev1 = lax.ppermute(p2, "gx", up)
     next1 = lax.ppermute(p0, "gx", down)
-    up2, down2, r0, r2, rates, middle = call(
+    up2, down2, r0, r2, l0, l2, rates, middle = call(
         inner_kernel,
-        (shape(*ten), shape(*ten), shape(*six), shape(*six), shape(planes, *plane), shape(*plane)),
+        (
+            shape(*ten), shape(*ten), shape(*soon), shape(*soon), shape(*last), shape(*last),
+            shape(planes, *plane), shape(*plane),
+        ),
         [ANY] * 2 + [VMEM] * 3,
         chosen, class_table, p0, p1, p2,
         scratch=[*small, pltpu.SemaphoreType.DMA((2,))],
@@ -436,9 +446,11 @@
     )
     prev2 = lax.ppermute(up2, "gx", up)
     next2 = lax.ppermute(down2, "gx", down)
-    r0, r2, prev1, next1 = lax.optimization_barrier((r0, r2, prev1, next1))
+    r0, r2, l0, l2, prev1, next1 = lax.optimization_barrier((r0, r2, l0, l2, prev1, next1))
     prev3 = lax.ppermute(r0, "gx", up)
     next3 = lax.ppermute(r2, "gx", down)
+    prev4 = lax.ppermute(l0, "gx", up)
+    next4 = lax.ppermute(l2, "gx", down)
     near_out = call(
         near_kernel,
         shape(5 * GRAINS, depth, width),
@@ -470,6 +482,7 @@
     else:
         lines = lax.all_to_all(packed, "gx", split_axis=1, concat_axis=0, tiled=True)
     lines = lines.reshape(total_x * share, lanes)
+    lines, prev4, next4 = lax.optimization_barrier((lines, prev4, next4))
     def lines_body(*refs):
         line_kernel(*refs, scale=1.0 / (count * count))
 
@@ -489,7 +502,7 @@
     if not aligned:
         returned = returned.reshape(devices, planes, share, lanes).transpose(1, 0, 2, 3)
         returned = returned.reshape(planes, slots, lanes)
-    late = (chosen, class_table, p0, p2, prev1, next1, prev2, next2, near_out, middle, rates, prev3, next3)
+    late = (chosen, class_table, p0, p2, prev1, next1, prev2, next2, near_out, middle, rates, prev3, next3, prev4, next4)
     late, _ = lax.optimization_barrier((late, back))
     order_params = call(
         rest_kernel,

time: 78.4 us -> 78.7 us (level)
  blocking collectives: 28.1 us -> 0 us
  starting transfers between devices: 18.9 us -> 37.3 us
  waiting for transfers between devices: 8.4 us -> 17.3 us
    all_to_all x1 -> x0, blocking collectives: 28.1 us -> none  [shards(): lax.all_to_all(packed, 'gx', split_axis=0, concat_axis=0, tiled=True)]
    all_to_all x0 -> x1, starting transfers between devices: none -> 14 us  [shards(): lax.all_to_all(packed, 'gx', split_axis=0, concat_axis=0, tiled=True)]
    ppermute x0 -> x2, waiting for transfers between devices: none -> 9.81 us  [the longest x1 9.81 us: shards(): prev4 = lax.ppermute(l0, 'gx', up)]
    ppermute x0 -> x2, starting transfers between devices: none -> 4.49 us  [the longest x1 4.08 us: shards(): next4 = lax.ppermute(l2, 'gx', down)]
    ppermute x1, waiting for transfers between devices: 0.85 us -> 0.01 us  [shards(): prev3 = lax.ppermute(r0, 'gx', up)]
  transfers between devices with their start and end apart: 7 -> 10, of which waited for: 5 -> 5; matrix products, arithmetic and copies ran while one was open for 0% -> 0% of each run, Pallas kernels for 21% -> 22%
where the time goes in v8:
time: 78.7 us; the launch traced here: 78.3 us
  starting transfers between devices  37.3 us (47%)
  Pallas kernels  22.6 us (29%)
  waiting for transfers between devices  17.3 us (22%)
  between operations  0.95 us (1%)
    pallas_call x7, Pallas kernels, call(): pl.pallas_call(kernel, out_shape=outs, in_specs=in_specs, out_specs=jax.t...  22.6 us
    all_to_all x1, starting transfers between devices, shards(): lax.all_to_all(packed, 'gx', split_axis=0, concat_axis=0, tiled=True)  14 us
    ppermute x1, waiting for transfers between devices, shards(): prev4 = lax.ppermute(l0, 'gx', up)  9.81 us
    ppermute x1, starting transfers between devices, shards(): next1 = lax.ppermute(p0, 'gx', down)  5.5 us
    ppermute x1, starting transfers between devices, shards(): prev3 = lax.ppermute(r0, 'gx', up)  5.07 us
    ppermute x1, waiting for transfers between devices, shards(): prev1 = lax.ppermute(p2, 'gx', up)  4.7 us
    ppermute x1, starting transfers between devices, shards(): next2 = lax.ppermute(down2, 'gx', down)  4.49 us
    ppermute x1, starting transfers between devices, shards(): next4 = lax.ppermute(l2, 'gx', down)  4.08 us
  transfers between devices with their start and end apart: 10, of which 5 were waited for; matrix products, arithmetic and copies ran while one was open for 0% of the time, Pallas kernels for 22%

profile of v8, /device:TPU:0, one launch (start us, length us, event | category | flops | bytes accessed | tf_op | source)
XLA Modules:
  0.0 78.3 jit_solution(13784277262099341679)
XLA Ops:
  0.6 1.3 %shard_map.104 = (f32[8,32,512]{2,1,0:T(8,128)S(1)}, f32[8,32,512]{2,1,0:T(8,128)S(1)}, f32[8,32,512]{2,1,0:T(8,128)S(1)}) custom-call(bf16[8,3,32,512]{3,2,1,0:T(8,128)(2,1)} %jitter_any.1, s32[3,32,512]{2,1,0:T(8,128)} %ids_any.1), custom_call_target="tpu_custom_call" | custom-call | flops 2097152 | bytes 4194304 | tf_op jit(solution)/shard_map/pallas_call | solution.py:385
  1.9 0.0 copy-start.2
  1.9 0.0 copy-start.3
  1.9 5.5 %collective-permute-start.1 = (f32[8,32,512]{2,1,0:T(8,128)S(1)}, f32[8,32,512]{2,1,0:T(8,128)S(1)}, u32[]{:S(2)}, u32[]{:S(2)}) collective-permute-start(f32[8,32,512]{2,1,0:T(8,128)S(1)} %get-tuple-element.65.p0.refs_2_), channel_id=1, source_target_pairs={{1,0},{2,1},{3,2},{4,3},{5,4},{6,5},{7,6},{8,7},{9,8},{10,9},{11,1... | collective-permute-start | bytes 1572872 | tf_op jit(solution)/shard_map/ppermute | solution.py:435
  7.4 0.0 collective-permute-start
  7.4 2.0 %shard_map.105 = (f32[10,32,512]{2,1,0:T(8,128)S(1)}, f32[10,32,512]{2,1,0:T(8,128)S(1)}, f32[3,32,512]{2,1,0:T(8,128)S(1)}, f32[3,32,512]{2,1,0:T(8,128)S(1)}, ...) custom-call(s32[2]{0:T(128)} %refs_0_, ...), custom_call_target="tpu_custom_call" | custom-call | flops 16777216 | bytes 4194304 | tf_op jit(solution)/shard_map/pallas_call | solution.py:385
  9.4 0.0 copy-start.1
  9.4 0.0 copy-start.6
  9.4 0.1 collective-permute-start.2
  9.5 4.5 %collective-permute-start.3 = (f32[10,32,512]{2,1,0:T(8,128)S(1)}, f32[10,32,512]{2,1,0:T(8,128)S(1)}, u32[]{:S(2)}, u32[]{:S(2)}) collective-permute-start(f32[10,32,512]{2,1,0:T(8,128)S(1)} %get-tuple-element.50), channel_id=1, source_target_pairs={{1,0},{2,1},{3,2},{4,3},{5,4},{6,5},{7,6},{8,7},{9,8},{10,9},{11,1... | collective-permute-start | bytes 1966088 | tf_op jit(solution)/shard_map/ppermute | solution.py:448
  14.0 0.2 collective-permute-done.1.next1.refs_5_
  14.1 0.0 copy-start.4
  14.1 4.7 %collective-permute-done.prev1.refs_4_ = f32[8,32,512]{2,1,0:T(8,128)S(1)} collective-permute-done((f32[8,32,512]{2,1,0:T(8,128)S(1)}, f32[8,32,512]{2,1,0:T(8,128)S(1)}, u32[]{:S(2)}, u32[]{:S(2)}) %collective-permute-start) | collective-permute-done | bytes 524320 | tf_op jit(solution)/shard_map/ppermute | solution.py:434
  18.8 0.0 copy-start.5
  18.8 5.1 %collective-permute-start.4 = (f32[3,32,512]{2,1,0:T(8,128)S(1)}, f32[3,32,512]{2,1,0:T(8,128)S(1)}, u32[]{:S(2)}, u32[]{:S(2)}) collective-permute-start(f32[3,32,512]{2,1,0:T(8,128)S(1)} %get-tuple-element.53), channel_id=1, source_target_pairs={{0,1},{1,2},{2,3},{3,4},{4,5},{5,6},{6,7},{7,8},{8,9},{9,10},{10,1... | collective-permute-start | bytes 589832 | tf_op jit(solution)/shard_map/ppermute | solution.py:450
  23.9 0.0 collective-permute-start.5
  23.9 1.7 %shard_map.106.near_out.refs_8_ = f32[40,32,512]{2,1,0:T(8,128)S(1)} custom-call(s32[8,8]{1,0:T(8,128)} %refs_1_.1, f32[8,32,512]{2,1,0:T(8,128)S(1)} %get-tuple-element.65.p0.refs_2_, f32[8,32,512]{2,1,0:T(8,128)S(1)} %get-tuple-element.42.p1, f32[8,32,512]{2,1,0:T(8,128)S(1)} %get-tuple-element.66.p2.refs_3_, ...), custom_call_target="tpu_custom_call" | custom-call | flops 33554432 | bytes 16777216 | tf_op jit(solution)/shard_map/pallas_call | solution.py:385
  25.6 0.0 copy-start
  25.6 0.0 copy-start.11
  25.6 0.0 copy-start.12
  25.6 0.0 copy-start.13
  25.6 0.2 collective-permute-done.2.prev2.refs_6_
  25.9 0.0 copy-start.7
  25.9 0.0 collective-permute-done.3.next2.refs_7_
  25.9 0.0 copy-done.2
  25.9 0.0 copy-done.3
  25.9 0.0 copy-done.1
  25.9 0.0 copy-done.6
  25.9 0.0 copy-done.4
  25.9 0.0 copy-done.5
  25.9 0.0 copy-start.8
  25.9 4.0 %shard_map.107 = f32[16,48,128]{2,1,0:T(8,128)} custom-call(s32[2]{0:T(128)} %refs_0_, s32[8,8]{1,0:T(8,128)} %refs_1_.1, f32[8,32,512]{2,1,0:T(8,128)S(1)} %get-tuple-element.65.p0.refs_2_, f32[8,32,512]{2,1,0:T(8,128)S(1)} %get-tuple-element.66.p2.refs_3_, f32[8,32,512]{2,1,0:T(8,128)S(1)} %collective-permute-done.prev1.refs_4_, ...), custom_call_target="tpu_custom_call" | custom-call | flops 268435456 | bytes 8388608 | tf_op jit(solution)/shard_map/pallas_call | solution.py:385
  30.0 0.0 copy-done
  30.0 0.0 copy-done.7
  30.0 0.0 copy-done.8
  30.0 0.0 collective-permute-done.4.refs_11_
  30.0 0.0 copy-start.14
  30.0 0.0 collective-permute-done.5.refs_12_
  30.0 0.0 copy-start.15
  30.0 14.0 %all-to-all-start = ((f32[16,48,128]{2,1,0:T(8,128)}), f32[16,48,128]{2,1,0:T(8,128)S(1)}, u32[]{:S(2)}, u32[]{:S(2)}) async-start(f32[16,48,128]{2,1,0:T(8,128)} %shard_map.107), calls=%async_computation | async-start | bytes 786432 | tf_op jit(solution)/shard_map/all_to_all | solution.py:481
  44.0 0.4 collective-permute-start.6
  44.4 4.1 %collective-permute-start.7 = (f32[3,32,512]{2,1,0:T(8,128)S(1)}, f32[3,32,512]{2,1,0:T(8,128)S(1)}, u32[]{:S(2)}, u32[]{:S(2)}) collective-permute-start(f32[3,32,512]{2,1,0:T(8,128)S(1)} %get-tuple-element.59), channel_id=1, source_target_pairs={{1,0},{2,1},{3,2},{4,3},{5,4},{6,5},{7,6},{8,7},{9,8},{10,9},{11,1... | collective-permute-start | bytes 589832 | tf_op jit(solution)/shard_map/ppermute | solution.py:453
  48.5 9.8 %collective-permute-done.6.refs_13_ = f32[3,32,512]{2,1,0:T(8,128)S(1)} collective-permute-done((f32[3,32,512]{2,1,0:T(8,128)S(1)}, f32[3,32,512]{2,1,0:T(8,128)S(1)}, u32[]{:S(2)}, u32[]{:S(2)}) %collective-permute-start.6) | collective-permute-done | bytes 196640 | tf_op jit(solution)/shard_map/ppermute | solution.py:452
  58.3 0.0 copy-start.16
  58.3 0.0 collective-permute-done.7.refs_14_
  58.3 0.0 copy-start.17
  58.3 0.0 all-to-all-done
  58.3 0.0 copy-done.11
  58.3 0.0 copy-done.12
  58.3 0.0 copy-done.13
  58.4 2.9 %shard_map.108 = f32[768,128]{1,0:T(8,128)} custom-call(f32[768,128]{1,0:T(8,128)S(1)} %bitcast.2, bf16[2,256,128]{2,1,0:T(8,128)(2,1)S(1)} %copy-done.12, bf16[2,256,128]{2,1,0:T(8,128)(2,1)S(1)} %copy-done.11, bf16[96,144]{1,0:T(8,128)(2,1)S(1)} %copy-done.13), custom_call_target="tpu_custom_call" | custom-call | flops 268435456 | bytes 4194304 | tf_op jit(solution)/shard_map/pallas_call | solution.py:385
  61.2 3.7 %all-to-all-start.1 = ((f32[16,48,128]{2,1,0:T(8,128)}), f32[16,48,128]{2,1,0:T(8,128)S(1)}, u32[]{:S(2)}, u32[]{:S(2)}) async-start(f32[16,48,128]{2,1,0:T(8,128)} %bitcast.1), calls=%async_computation.1 | async-start | bytes 786432 | tf_op jit(solution)/shard_map/all_to_all | solution.py:501
  65.0 0.0 copy-done.14
  65.0 0.0 copy-done.15
  65.0 0.0 copy-done.16
  65.0 0.0 copy-done.17
  65.0 0.0 copy-start.9
  65.0 0.0 copy-start.10
  65.0 9.5 %shard_map.109 = f32[8,3,32,512]{3,2,1,0:T(8,128)} custom-call(s32[2]{0:T(128)} %refs_0_, s32[8,8]{1,0:T(8,128)} %refs_1_.1, f32[8,32,512]{2,1,0:T(8,128)} %copy-done.2, f32[8,32,512]{2,1,0:T(8,128)} %copy-done.3, f32[8,32,512]{2,1,0:T(8,128)} %copy-done.5, f32[8,32,512]{2,1,0:T(8,128)} %copy-done.4, f32[10,32,512]{2,1,0:T(8,128)} %copy-done.7, ...), custom_call_target="tpu_custom_call" | custom-call | flops 67108864 | bytes 16777216 | tf_op jit(solution)/shard_map/pallas_call | solution.py:385
  74.5 2.4 %all-to-all-done.1.returned = f32[16,48,128]{2,1,0:T(8,128)S(1)} async-done(((f32[16,48,128]{2,1,0:T(8,128)}), f32[16,48,128]{2,1,0:T(8,128)S(1)}, u32[]{:S(2)}, u32[]{:S(2)}) %all-to-all-start.1) | async-done | bytes 393248 | tf_op jit(solution)/shard_map/all_to_all | solution.py:501
  76.9 0.0 copy-done.9
  76.9 0.0 copy-done.10
  76.9 1.3 %shard_map.110 = f32[2,3,32,512]{3,2,1,0:T(8,128)} custom-call(f32[16,48,128]{2,1,0:T(8,128)S(1)} %all-to-all-done.1.returned, bf16[512,512]{1,0:T(8,128)(2,1)S(1)} %copy-done.10, bf16[512,512]{1,0:T(8,128)(2,1)S(1)} %copy-done.9), custom_call_target="tpu_custom_call" | custom-call | flops 268435456 | bytes 4194304 | tf_op jit(solution)/shard_map/pallas_call | solution.py:385
Async XLA Ops:
  1.9 24.0 %copy-start.2 = (f32[8,32,512]{2,1,0:T(8,128)}, f32[8,32,512]{2,1,0:T(8,128)S(1)}, u32[]{:S(2)}) copy-start(f32[8,32,512]{2,1,0:T(8,128)S(1)} %get-tuple-element.65.p0.refs_2_) | copy-start | bytes 1572868
  1.9 23.9 %copy-start.3 = (f32[8,32,512]{2,1,0:T(8,128)}, f32[8,32,512]{2,1,0:T(8,128)S(1)}, u32[]{:S(2)}) copy-start(f32[8,32,512]{2,1,0:T(8,128)S(1)} %get-tuple-element.66.p2.refs_3_) | copy-start | bytes 1572868
  1.9 12.2 %collective-permute-start.1 = (f32[8,32,512]{2,1,0:T(8,128)S(1)}, f32[8,32,512]{2,1,0:T(8,128)S(1)}, u32[]{:S(2)}, u32[]{:S(2)}) collective-permute-start(f32[8,32,512]{2,1,0:T(8,128)S(1)} %get-tuple-element.65.p0.refs_2_), channel_id=1, source_target_pairs={{1,0},{2,1},{3,2},{4,3},{5,4},{6,5},{7,6},{8,7},{9,8},{10,9},{11,1... | collective-permute-start | bytes 1572872 | tf_op jit(solution)/shard_map/ppermute | solution.py:435
  7.4 11.4 %collective-permute-start = (f32[8,32,512]{2,1,0:T(8,128)S(1)}, f32[8,32,512]{2,1,0:T(8,128)S(1)}, u32[]{:S(2)}, u32[]{:S(2)}) collective-permute-start(f32[8,32,512]{2,1,0:T(8,128)S(1)} %get-tuple-element.66.p2.refs_3_), channel_id=1, source_target_pairs={{0,1},{1,2},{2,3},{3,4},{4,5},{5,6},{6,7},{7,8},{8,9},{9,10},{10,1... | collective-permute-start | bytes 1572872 | tf_op jit(solution)/shard_map/ppermute | solution.py:434
  9.4 16.5 %copy-start.1 = (f32[3,8,32,512]{3,2,1,0:T(8,128)}, f32[3,8,32,512]{3,2,1,0:T(8,128)S(1)}, u32[]{:S(2)}) copy-start(f32[3,8,32,512]{3,2,1,0:T(8,128)S(1)} %get-tuple-element.73.rates.refs_10_) | copy-start | bytes 4718596
  9.4 16.5 %copy-start.6 = (f32[8,32,512]{2,1,0:T(8,128)}, f32[8,32,512]{2,1,0:T(8,128)S(1)}, u32[]{:S(2)}) copy-start(f32[8,32,512]{2,1,0:T(8,128)S(1)} %get-tuple-element.72.middle.refs_9_) | copy-start | bytes 1572868
  9.4 16.4 %collective-permute-start.2 = (f32[10,32,512]{2,1,0:T(8,128)S(1)}, f32[10,32,512]{2,1,0:T(8,128)S(1)}, u32[]{:S(2)}, u32[]{:S(2)}) collective-permute-start(f32[10,32,512]{2,1,0:T(8,128)S(1)} %get-tuple-element.49), channel_id=1, source_target_pairs={{0,1},{1,2},{2,3},{3,4},{4,5},{5,6},{6,7},{7,8},{8,9},{9,10},{10,1... | collective-permute-start | bytes 1966088 | tf_op jit(solution)/shard_map/ppermute | solution.py:447
  9.5 16.4 %collective-permute-start.3 = (f32[10,32,512]{2,1,0:T(8,128)S(1)}, f32[10,32,512]{2,1,0:T(8,128)S(1)}, u32[]{:S(2)}, u32[]{:S(2)}) collective-permute-start(f32[10,32,512]{2,1,0:T(8,128)S(1)} %get-tuple-element.50), channel_id=1, source_target_pairs={{1,0},{2,1},{3,2},{4,3},{5,4},{6,5},{7,6},{8,7},{9,8},{10,9},{11,1... | collective-permute-start | bytes 1966088 | tf_op jit(solution)/shard_map/ppermute | solution.py:448
  14.1 11.8 %copy-start.4 = (f32[8,32,512]{2,1,0:T(8,128)}, f32[8,32,512]{2,1,0:T(8,128)S(1)}, u32[]{:S(2)}) copy-start(f32[8,32,512]{2,1,0:T(8,128)S(1)} %collective-permute-done.1.next1.refs_5_) | copy-start | bytes 1572868
  18.8 7.1 %copy-start.5 = (f32[8,32,512]{2,1,0:T(8,128)}, f32[8,32,512]{2,1,0:T(8,128)S(1)}, u32[]{:S(2)}) copy-start(f32[8,32,512]{2,1,0:T(8,128)S(1)} %collective-permute-done.prev1.refs_4_) | copy-start | bytes 1572868
  18.8 11.1 %collective-permute-start.4 = (f32[3,32,512]{2,1,0:T(8,128)S(1)}, f32[3,32,512]{2,1,0:T(8,128)S(1)}, u32[]{:S(2)}, u32[]{:S(2)}) collective-permute-start(f32[3,32,512]{2,1,0:T(8,128)S(1)} %get-tuple-element.53), channel_id=1, source_target_pairs={{0,1},{1,2},{2,3},{3,4},{4,5},{5,6},{6,7},{7,8},{8,9},{9,10},{10,1... | collective-permute-start | bytes 589832 | tf_op jit(solution)/shard_map/ppermute | solution.py:450
  23.9 6.1 %collective-permute-start.5 = (f32[3,32,512]{2,1,0:T(8,128)S(1)}, f32[3,32,512]{2,1,0:T(8,128)S(1)}, u32[]{:S(2)}, u32[]{:S(2)}) collective-permute-start(f32[3,32,512]{2,1,0:T(8,128)S(1)} %get-tuple-element.54), channel_id=1, source_target_pairs={{1,0},{2,1},{3,2},{4,3},{5,4},{6,5},{7,6},{8,7},{9,8},{10,9},{11,1... | collective-permute-start | bytes 589832 | tf_op jit(solution)/shard_map/ppermute | solution.py:451
  25.6 4.4 %copy-start = (f32[40,32,512]{2,1,0:T(8,128)}, f32[40,32,512]{2,1,0:T(8,128)S(1)}, u32[]{:S(2)}) copy-start(f32[40,32,512]{2,1,0:T(8,128)S(1)} %shard_map.106.near_out.refs_8_) | copy-start | bytes 7864324
  25.6 32.7 %copy-start.11 = (bf16[2,256,128]{2,1,0:T(8,128)(2,1)S(1)}, bf16[2,256,128]{2,1,0:T(8,128)(2,1)}, u32[]{:S(2)}) copy-start(bf16[2,256,128]{2,1,0:T(8,128)(2,1)} %constant.13.clone.refs_2_) | copy-start | bytes 393220
  25.6 32.7 %copy-start.12 = (bf16[2,256,128]{2,1,0:T(8,128)(2,1)S(1)}, bf16[2,256,128]{2,1,0:T(8,128)(2,1)}, u32[]{:S(2)}) copy-start(bf16[2,256,128]{2,1,0:T(8,128)(2,1)} %constant.12.clone.refs_1_) | copy-start | bytes 393220
  25.6 32.7 %copy-start.13 = (bf16[96,144]{1,0:T(8,128)(2,1)S(1)}, bf16[96,144]{1,0:T(8,128)(2,1)}, u32[]{:S(2)}) copy-start(bf16[96,144]{1,0:T(8,128)(2,1)} %constant.14.clone.refs_3_) | copy-start | bytes 82948
  25.9 4.1 %copy-start.7 = (f32[10,32,512]{2,1,0:T(8,128)}, f32[10,32,512]{2,1,0:T(8,128)S(1)}, u32[]{:S(2)}) copy-start(f32[10,32,512]{2,1,0:T(8,128)S(1)} %collective-permute-done.2.prev2.refs_6_) | copy-start | bytes 1966084
  25.9 4.1 %copy-start.8 = (f32[10,32,512]{2,1,0:T(8,128)}, f32[10,32,512]{2,1,0:T(8,128)S(1)}, u32[]{:S(2)}) copy-start(f32[10,32,512]{2,1,0:T(8,128)S(1)} %collective-permute-done.3.next2.refs_7_) | copy-start | bytes 1966084
  30.0 35.0 %copy-start.14 = (f32[3,32,512]{2,1,0:T(8,128)}, f32[3,32,512]{2,1,0:T(8,128)S(1)}, u32[]{:S(2)}) copy-start(f32[3,32,512]{2,1,0:T(8,128)S(1)} %collective-permute-done.4.refs_11_) | copy-start | bytes 589828
  30.0 35.0 %copy-start.15 = (f32[3,32,512]{2,1,0:T(8,128)}, f32[3,32,512]{2,1,0:T(8,128)S(1)}, u32[]{:S(2)}) copy-start(f32[3,32,512]{2,1,0:T(8,128)S(1)} %collective-permute-done.5.refs_12_) | copy-start | bytes 589828
  30.0 28.3 %all-to-all-start = ((f32[16,48,128]{2,1,0:T(8,128)}), f32[16,48,128]{2,1,0:T(8,128)S(1)}, u32[]{:S(2)}, u32[]{:S(2)}) async-start(f32[16,48,128]{2,1,0:T(8,128)} %shard_map.107), calls=%async_computation | async-start | bytes 786432 | tf_op jit(solution)/shard_map/all_to_all | solution.py:481
  44.0 14.3 %collective-permute-start.6 = (f32[3,32,512]{2,1,0:T(8,128)S(1)}, f32[3,32,512]{2,1,0:T(8,128)S(1)}, u32[]{:S(2)}, u32[]{:S(2)}) collective-permute-start(f32[3,32,512]{2,1,0:T(8,128)S(1)} %get-tuple-element.58), channel_id=1, source_target_pairs={{0,1},{1,2},{2,3},{3,4},{4,5},{5,6},{6,7},{7,8},{8,9},{9,10},{10,1... | collective-permute-start | bytes 589832 | tf_op jit(solution)/shard_map/ppermute | solution.py:452
  44.4 13.9 %collective-permute-start.7 = (f32[3,32,512]{2,1,0:T(8,128)S(1)}, f32[3,32,512]{2,1,0:T(8,128)S(1)}, u32[]{:S(2)}, u32[]{:S(2)}) collective-permute-start(f32[3,32,512]{2,1,0:T(8,128)S(1)} %get-tuple-element.59), channel_id=1, source_target_pairs={{1,0},{2,1},{3,2},{4,3},{5,4},{6,5},{7,6},{8,7},{9,8},{10,9},{11,1... | collective-permute-start | bytes 589832 | tf_op jit(solution)/shard_map/ppermute | solution.py:453
  58.3 6.7 %copy-start.16 = (f32[3,32,512]{2,1,0:T(8,128)}, f32[3,32,512]{2,1,0:T(8,128)S(1)}, u32[]{:S(2)}) copy-start(f32[3,32,512]{2,1,0:T(8,128)S(1)} %collective-permute-done.6.refs_13_) | copy-start | bytes 589828
  58.3 6.7 %copy-start.17 = (f32[3,32,512]{2,1,0:T(8,128)}, f32[3,32,512]{2,1,0:T(8,128)S(1)}, u32[]{:S(2)}) copy-start(f32[3,32,512]{2,1,0:T(8,128)S(1)} %collective-permute-done.7.refs_14_) | copy-start | bytes 589828
  61.2 15.7 %all-to-all-start.1 = ((f32[16,48,128]{2,1,0:T(8,128)}), f32[16,48,128]{2,1,0:T(8,128)S(1)}, u32[]{:S(2)}, u32[]{:S(2)}) async-start(f32[16,48,128]{2,1,0:T(8,128)} %bitcast.1), calls=%async_computation.1 | async-start | bytes 786432 | tf_op jit(solution)/shard_map/all_to_all | solution.py:501
  65.0 11.9 %copy-start.9 = (bf16[512,512]{1,0:T(8,128)(2,1)S(1)}, bf16[512,512]{1,0:T(8,128)(2,1)}, u32[]{:S(2)}) copy-start(bf16[512,512]{1,0:T(8,128)(2,1)} %constant.11.clone.low_any.low) | copy-start | bytes 1572868
  65.0 11.9 %copy-start.10 = (bf16[512,512]{1,0:T(8,128)(2,1)S(1)}, bf16[512,512]{1,0:T(8,128)(2,1)}, u32[]{:S(2)}) copy-start(bf16[512,512]{1,0:T(8,128)(2,1)} %constant.10.clone.high_any.high) | copy-start | bytes 1572868

commit v9 on v8

--- a/solution.py
+++ b/solution.py
@@ -449,8 +449,6 @@
     r0, r2, l0, l2, prev1, next1 = lax.optimization_barrier((r0, r2, l0, l2, prev1, next1))
     prev3 = lax.ppermute(r0, "gx", up)
     next3 = lax.ppermute(r2, "gx", down)
-    prev4 = lax.ppermute(l0, "gx", up)
-    next4 = lax.ppermute(l2, "gx", down)
     near_out = call(
         near_kernel,
         shape(5 * GRAINS, depth, width),
@@ -482,7 +480,9 @@
     else:
         lines = lax.all_to_all(packed, "gx", split_axis=1, concat_axis=0, tiled=True)
     lines = lines.reshape(total_x * share, lanes)
-    lines, prev4, next4 = lax.optimization_barrier((lines, prev4, next4))
+    lines, l0, l2 = lax.optimization_barrier((lines, l0, l2))
+    prev4 = lax.ppermute(l0, "gx", up)
+    next4 = lax.ppermute(l2, "gx", down)
     def lines_body(*refs):
         line_kernel(*refs, scale=1.0 / (count * count))
 
@@ -516,7 +516,7 @@
             pltpu.VMEM((2, *plane), F32),
             pltpu.SemaphoreType.DMA((len(late),)),
         ],
-        flops=2**26, moved=2**24, limit=24,
+        flops=2**37, moved=2**24, limit=24,
     )
     correlation = call(
         finish_kernel,

time: 78.7 us -> 79.9 us (1.015)
  blocking collectives: 0 us -> 26 us
  starting transfers between devices: 37.3 us -> 23.3 us
  waiting for transfers between devices: 17.3 us -> 6.26 us
  local copies, waits for them, and re-layouts: 0.09 us -> 1.43 us
  Pallas kernels: 22.6 us -> 21.7 us
    all_to_all x0 -> x1, blocking collectives: none -> 26 us  [shards(): lax.all_to_all(packed, 'gx', split_axis=0, concat_axis=0, tiled=True)]
    all_to_all x1 -> x0, starting transfers between devices: 14 us -> none  [shards(): lax.all_to_all(packed, 'gx', split_axis=0, concat_axis=0, tiled=True)]
    ppermute x1, waiting for transfers between devices: 9.81 us -> 0.01 us  [shards(): prev4 = lax.ppermute(l0, 'gx', up)]
    unnamed x36, local copies, waits for them, and re-layouts: 0.09 us -> 1.43 us
    all_to_all x1, waiting for transfers between devices: 2.41 us -> 1.16 us  [shards(): lax.all_to_all(back, 'gx', split_axis=0, concat_axis=0, tiled=True)]
    pallas_call x7, Pallas kernels: 22.6 us -> 21.7 us  [call(): pl.pallas_call(kernel, out_shape=outs, in_specs=in_specs, out_specs=jax.t...]
  transfers between devices with their start and end apart: 10 -> 9, of which waited for: 5 -> 4; matrix products, arithmetic and copies ran while one was open for 0% -> 0% of each run, Pallas kernels for 22% -> 24%
where the time goes in v9:
time: 79.9 us; the launch traced here: 79.6 us
  blocking collectives  26 us (33%)
  starting transfers between devices  23.3 us (29%)
  Pallas kernels  21.7 us (27%)
  waiting for transfers between devices  6.26 us (8%)
  local copies, waits for them, and re-layouts  1.43 us (2%)
  between operations  0.91 us (1%)
    all_to_all x1, blocking collectives, shards(): lax.all_to_all(packed, 'gx', split_axis=0, concat_axis=0, tiled=True)  26 us
    pallas_call x7, Pallas kernels, call(): pl.pallas_call(kernel, out_shape=outs, in_specs=in_specs, out_specs=jax.t...  21.7 us
    ppermute x1, starting transfers between devices, shards(): next1 = lax.ppermute(p0, 'gx', down)  5.5 us
    ppermute x1, starting transfers between devices, shards(): prev3 = lax.ppermute(r0, 'gx', up)  5.07 us
    ppermute x1, waiting for transfers between devices, shards(): prev1 = lax.ppermute(p2, 'gx', up)  4.7 us
    ppermute x1, starting transfers between devices, shards(): next2 = lax.ppermute(down2, 'gx', down)  4.49 us
    ppermute x1, starting transfers between devices, shards(): next4 = lax.ppermute(l2, 'gx', down)  4.33 us
    all_to_all x1, starting transfers between devices, shards(): lax.all_to_all(back, 'gx', split_axis=0, concat_axis=0, tiled=True)  3.73 us
  transfers between devices with their start and end apart: 9, of which 4 were waited for; matrix products, arithmetic and copies ran while one was open for 0% of the time, Pallas kernels for 24%

profile of v9, /device:TPU:0, one launch (start us, length us, event | category | flops | bytes accessed | tf_op | source)
XLA Modules:
  0.0 79.6 jit_solution(16779570825982747898)
XLA Ops:
  0.6 1.3 %shard_map.104 = (f32[8,32,512]{2,1,0:T(8,128)S(1)}, f32[8,32,512]{2,1,0:T(8,128)S(1)}, f32[8,32,512]{2,1,0:T(8,128)S(1)}) custom-call(bf16[8,3,32,512]{3,2,1,0:T(8,128)(2,1)} %jitter_any.1, s32[3,32,512]{2,1,0:T(8,128)} %ids_any.1), custom_call_target="tpu_custom_call" | custom-call | flops 2097152 | bytes 4194304 | tf_op jit(solution)/shard_map/pallas_call | solution.py:385
  1.9 0.0 copy-start.2
  1.9 0.0 copy-start.3
  1.9 5.5 %collective-permute-start.1 = (f32[8,32,512]{2,1,0:T(8,128)S(1)}, f32[8,32,512]{2,1,0:T(8,128)S(1)}, u32[]{:S(2)}, u32[]{:S(2)}) collective-permute-start(f32[8,32,512]{2,1,0:T(8,128)S(1)} %get-tuple-element.65.p0.refs_2_), channel_id=1, source_target_pairs={{1,0},{2,1},{3,2},{4,3},{5,4},{6,5},{7,6},{8,7},{9,8},{10,9},{11,1... | collective-permute-start | bytes 1572872 | tf_op jit(solution)/shard_map/ppermute | solution.py:435
  7.4 0.0 collective-permute-start
  7.4 2.0 %shard_map.105 = (f32[10,32,512]{2,1,0:T(8,128)S(1)}, f32[10,32,512]{2,1,0:T(8,128)S(1)}, f32[3,32,512]{2,1,0:T(8,128)S(1)}, f32[3,32,512]{2,1,0:T(8,128)S(1)}, ...) custom-call(s32[2]{0:T(128)} %refs_0_, ...), custom_call_target="tpu_custom_call" | custom-call | flops 16777216 | bytes 4194304 | tf_op jit(solution)/shard_map/pallas_call | solution.py:385
  9.4 0.0 copy-start.1
  9.4 0.0 copy-start.8
  9.4 0.1 collective-permute-start.2
  9.5 4.5 %collective-permute-start.3 = (f32[10,32,512]{2,1,0:T(8,128)S(1)}, f32[10,32,512]{2,1,0:T(8,128)S(1)}, u32[]{:S(2)}, u32[]{:S(2)}) collective-permute-start(f32[10,32,512]{2,1,0:T(8,128)S(1)} %get-tuple-element.50), channel_id=1, source_target_pairs={{1,0},{2,1},{3,2},{4,3},{5,4},{6,5},{7,6},{8,7},{9,8},{10,9},{11,1... | collective-permute-start | bytes 1966088 | tf_op jit(solution)/shard_map/ppermute | solution.py:448
  14.0 0.2 collective-permute-done.1.next1.refs_5_
  14.1 0.0 copy-start.6
  14.1 4.7 %collective-permute-done.prev1.refs_4_ = f32[8,32,512]{2,1,0:T(8,128)S(1)} collective-permute-done((f32[8,32,512]{2,1,0:T(8,128)S(1)}, f32[8,32,512]{2,1,0:T(8,128)S(1)}, u32[]{:S(2)}, u32[]{:S(2)}) %collective-permute-start) | collective-permute-done | bytes 524320 | tf_op jit(solution)/shard_map/ppermute | solution.py:434
  18.8 0.0 copy-start.7
  18.8 5.1 %collective-permute-start.4 = (f32[3,32,512]{2,1,0:T(8,128)S(1)}, f32[3,32,512]{2,1,0:T(8,128)S(1)}, u32[]{:S(2)}, u32[]{:S(2)}) collective-permute-start(f32[3,32,512]{2,1,0:T(8,128)S(1)} %get-tuple-element.53), channel_id=1, source_target_pairs={{0,1},{1,2},{2,3},{3,4},{4,5},{5,6},{6,7},{7,8},{8,9},{9,10},{10,1... | collective-permute-start | bytes 589832 | tf_op jit(solution)/shard_map/ppermute | solution.py:450
  23.9 0.0 collective-permute-start.5
  23.9 1.7 %shard_map.106.near_out.refs_8_ = f32[40,32,512]{2,1,0:T(8,128)S(1)} custom-call(s32[8,8]{1,0:T(8,128)} %refs_1_.1, f32[8,32,512]{2,1,0:T(8,128)S(1)} %get-tuple-element.65.p0.refs_2_, f32[8,32,512]{2,1,0:T(8,128)S(1)} %get-tuple-element.42.p1, f32[8,32,512]{2,1,0:T(8,128)S(1)} %get-tuple-element.66.p2.refs_3_, ...), custom_call_target="tpu_custom_call" | custom-call | flops 33554432 | bytes 16777216 | tf_op jit(solution)/shard_map/pallas_call | solution.py:385
  25.6 0.0 copy-start
  25.6 0.0 copy-start.11
  25.6 0.0 copy-start.12
  25.6 0.0 copy-start.13
  25.6 0.2 collective-permute-done.2.prev2.refs_6_
  25.9 0.0 copy-start.9
  25.9 0.0 collective-permute-done.3.next2.refs_7_
  25.9 0.0 copy-done.2
  25.9 0.0 copy-done.3
  25.9 0.0 copy-done.1
  25.9 0.0 copy-done.8
  25.9 0.0 copy-done.6
  25.9 0.0 copy-done.7
  25.9 0.0 copy-start.10
  25.9 3.3 %shard_map.107 = f32[16,48,128]{2,1,0:T(8,128)S(1)} custom-call(s32[2]{0:T(128)} %refs_0_, s32[8,8]{1,0:T(8,128)} %refs_1_.1, f32[8,32,512]{2,1,0:T(8,128)S(1)} %get-tuple-element.65.p0.refs_2_, f32[8,32,512]{2,1,0:T(8,128)S(1)} %get-tuple-element.66.p2.refs_3_, f32[8,32,512]{2,1,0:T(8,128)S(1)} %collective-permute-done.prev1.refs_4_, ...), custom_call_target="tpu_custom_call" | custom-call | flops 268435456 | bytes 8388608 | tf_op jit(solution)/shard_map/pallas_call | solution.py:385
  29.2 0.0 copy-done
  29.2 0.0 copy-done.9
  29.2 0.0 copy-done.10
  29.2 0.0 collective-permute-done.4.refs_11_
  29.2 0.0 copy-start.14
  29.3 0.0 collective-permute-done.5.refs_12_
  29.3 0.0 copy-start.15
  29.3 26.0 %all_to_all.10 = f32[16,48,128]{2,1,0:T(8,128)S(1)} all-to-all(f32[16,48,128]{2,1,0:T(8,128)S(1)} %shard_map.107), channel_id=1, replica_groups=mesh['grp'=2,'gx'=16] {'gx'}, dimensions={0} | all-to-all | bytes 786432 | tf_op jit(solution)/shard_map/all_to_all | solution.py:479
  55.2 0.1 collective-permute-start.6
  55.3 4.3 %collective-permute-start.7 = (f32[3,32,512]{2,1,0:T(8,128)S(1)}, f32[3,32,512]{2,1,0:T(8,128)S(1)}, u32[]{:S(2)}, u32[]{:S(2)}) collective-permute-start(f32[3,32,512]{2,1,0:T(8,128)S(1)} %get-tuple-element.61), channel_id=1, source_target_pairs={{1,0},{2,1},{3,2},{4,3},{5,4},{6,5},{7,6},{8,7},{9,8},{10,9},{11,1... | collective-permute-start | bytes 589832 | tf_op jit(solution)/shard_map/ppermute | solution.py:485
  59.7 0.0 copy-done.11
  59.7 0.0 copy-done.12
  59.7 0.0 copy-done.13
  59.7 2.9 %shard_map.108 = f32[768,128]{1,0:T(8,128)} custom-call(f32[768,128]{1,0:T(8,128)S(1)} %bitcast.2, bf16[2,256,128]{2,1,0:T(8,128)(2,1)S(1)} %copy-done.12, bf16[2,256,128]{2,1,0:T(8,128)(2,1)S(1)} %copy-done.11, bf16[96,144]{1,0:T(8,128)(2,1)S(1)} %copy-done.13), custom_call_target="tpu_custom_call" | custom-call | flops 268435456 | bytes 4194304 | tf_op jit(solution)/shard_map/pallas_call | solution.py:385
  62.6 0.0 copy-done.14
  62.6 0.0 copy-done.15
  62.6 3.7 %all-to-all-start.1 = ((f32[16,48,128]{2,1,0:T(8,128)}), f32[16,48,128]{2,1,0:T(8,128)S(1)}, u32[]{:S(2)}, u32[]{:S(2)}) async-start(f32[16,48,128]{2,1,0:T(8,128)} %bitcast.1), calls=%async_computation.1 | async-start | bytes 786432 | tf_op jit(solution)/shard_map/all_to_all | solution.py:501
  66.3 0.0 copy-start.4
  66.3 0.0 copy-start.5
  66.3 0.0 collective-permute-done.6.refs_13_
  66.3 0.0 copy-start.16
  66.3 0.0 collective-permute-done.7.refs_14_
  66.4 0.7 copy-done.16
  67.0 0.0 copy-start.17
  67.0 0.7 copy-done.17
  67.7 9.4 %shard_map.109 = f32[8,3,32,512]{3,2,1,0:T(8,128)} custom-call(s32[2]{0:T(128)} %refs_0_, s32[8,8]{1,0:T(8,128)} %refs_1_.1, f32[8,32,512]{2,1,0:T(8,128)} %copy-done.2, f32[8,32,512]{2,1,0:T(8,128)} %copy-done.3, f32[8,32,512]{2,1,0:T(8,128)} %copy-done.7, f32[8,32,512]{2,1,0:T(8,128)} %copy-done.6, f32[10,32,512]{2,1,0:T(8,128)} %copy-done.9, ...), custom_call_target="tpu_custom_call" | custom-call | flops 137438953472 | bytes 16777216 | tf_op jit(solution)/shard_map/pallas_call | solution.py:385
  77.1 1.2 %all-to-all-done.1.returned = f32[16,48,128]{2,1,0:T(8,128)S(1)} async-done(((f32[16,48,128]{2,1,0:T(8,128)}), f32[16,48,128]{2,1,0:T(8,128)S(1)}, u32[]{:S(2)}, u32[]{:S(2)}) %all-to-all-start.1) | async-done | bytes 393248 | tf_op jit(solution)/shard_map/all_to_all | solution.py:501
  78.3 0.0 copy-done.4
  78.3 0.0 copy-done.5
  78.3 1.3 %shard_map.110 = f32[2,3,32,512]{3,2,1,0:T(8,128)} custom-call(f32[16,48,128]{2,1,0:T(8,128)S(1)} %all-to-all-done.1.returned, bf16[512,512]{1,0:T(8,128)(2,1)S(1)} %copy-done.5, bf16[512,512]{1,0:T(8,128)(2,1)S(1)} %copy-done.4), custom_call_target="tpu_custom_call" | custom-call | flops 268435456 | bytes 4194304 | tf_op jit(solution)/shard_map/pallas_call | solution.py:385
Async XLA Ops:
  1.9 24.0 %copy-start.2 = (f32[8,32,512]{2,1,0:T(8,128)}, f32[8,32,512]{2,1,0:T(8,128)S(1)}, u32[]{:S(2)}) copy-start(f32[8,32,512]{2,1,0:T(8,128)S(1)} %get-tuple-element.65.p0.refs_2_) | copy-start | bytes 1572868
  1.9 23.9 %copy-start.3 = (f32[8,32,512]{2,1,0:T(8,128)}, f32[8,32,512]{2,1,0:T(8,128)S(1)}, u32[]{:S(2)}) copy-start(f32[8,32,512]{2,1,0:T(8,128)S(1)} %get-tuple-element.66.p2.refs_3_) | copy-start | bytes 1572868
  1.9 12.2 %collective-permute-start.1 = (f32[8,32,512]{2,1,0:T(8,128)S(1)}, f32[8,32,512]{2,1,0:T(8,128)S(1)}, u32[]{:S(2)}, u32[]{:S(2)}) collective-permute-start(f32[8,32,512]{2,1,0:T(8,128)S(1)} %get-tuple-element.65.p0.refs_2_), channel_id=1, source_target_pairs={{1,0},{2,1},{3,2},{4,3},{5,4},{6,5},{7,6},{8,7},{9,8},{10,9},{11,1... | collective-permute-start | bytes 1572872 | tf_op jit(solution)/shard_map/ppermute | solution.py:435
  7.4 11.4 %collective-permute-start = (f32[8,32,512]{2,1,0:T(8,128)S(1)}, f32[8,32,512]{2,1,0:T(8,128)S(1)}, u32[]{:S(2)}, u32[]{:S(2)}) collective-permute-start(f32[8,32,512]{2,1,0:T(8,128)S(1)} %get-tuple-element.66.p2.refs_3_), channel_id=1, source_target_pairs={{0,1},{1,2},{2,3},{3,4},{4,5},{5,6},{6,7},{7,8},{8,9},{9,10},{10,1... | collective-permute-start | bytes 1572872 | tf_op jit(solution)/shard_map/ppermute | solution.py:434
  9.4 16.5 %copy-start.1 = (f32[3,8,32,512]{3,2,1,0:T(8,128)}, f32[3,8,32,512]{3,2,1,0:T(8,128)S(1)}, u32[]{:S(2)}) copy-start(f32[3,8,32,512]{3,2,1,0:T(8,128)S(1)} %get-tuple-element.73.rates.refs_10_) | copy-start | bytes 4718596
  9.4 16.5 %copy-start.8 = (f32[8,32,512]{2,1,0:T(8,128)}, f32[8,32,512]{2,1,0:T(8,128)S(1)}, u32[]{:S(2)}) copy-start(f32[8,32,512]{2,1,0:T(8,128)S(1)} %get-tuple-element.72.middle.refs_9_) | copy-start | bytes 1572868
  9.4 16.4 %collective-permute-start.2 = (f32[10,32,512]{2,1,0:T(8,128)S(1)}, f32[10,32,512]{2,1,0:T(8,128)S(1)}, u32[]{:S(2)}, u32[]{:S(2)}) collective-permute-start(f32[10,32,512]{2,1,0:T(8,128)S(1)} %get-tuple-element.49), channel_id=1, source_target_pairs={{0,1},{1,2},{2,3},{3,4},{4,5},{5,6},{6,7},{7,8},{8,9},{9,10},{10,1... | collective-permute-start | bytes 1966088 | tf_op jit(solution)/shard_map/ppermute | solution.py:447
  9.5 16.4 %collective-permute-start.3 = (f32[10,32,512]{2,1,0:T(8,128)S(1)}, f32[10,32,512]{2,1,0:T(8,128)S(1)}, u32[]{:S(2)}, u32[]{:S(2)}) collective-permute-start(f32[10,32,512]{2,1,0:T(8,128)S(1)} %get-tuple-element.50), channel_id=1, source_target_pairs={{1,0},{2,1},{3,2},{4,3},{5,4},{6,5},{7,6},{8,7},{9,8},{10,9},{11,1... | collective-permute-start | bytes 1966088 | tf_op jit(solution)/shard_map/ppermute | solution.py:448
  14.1 11.8 %copy-start.6 = (f32[8,32,512]{2,1,0:T(8,128)}, f32[8,32,512]{2,1,0:T(8,128)S(1)}, u32[]{:S(2)}) copy-start(f32[8,32,512]{2,1,0:T(8,128)S(1)} %collective-permute-done.1.next1.refs_5_) | copy-start | bytes 1572868
  18.8 7.1 %copy-start.7 = (f32[8,32,512]{2,1,0:T(8,128)}, f32[8,32,512]{2,1,0:T(8,128)S(1)}, u32[]{:S(2)}) copy-start(f32[8,32,512]{2,1,0:T(8,128)S(1)} %collective-permute-done.prev1.refs_4_) | copy-start | bytes 1572868
  18.8 10.4 %collective-permute-start.4 = (f32[3,32,512]{2,1,0:T(8,128)S(1)}, f32[3,32,512]{2,1,0:T(8,128)S(1)}, u32[]{:S(2)}, u32[]{:S(2)}) collective-permute-start(f32[3,32,512]{2,1,0:T(8,128)S(1)} %get-tuple-element.53), channel_id=1, source_target_pairs={{0,1},{1,2},{2,3},{3,4},{4,5},{5,6},{6,7},{7,8},{8,9},{9,10},{10,1... | collective-permute-start | bytes 589832 | tf_op jit(solution)/shard_map/ppermute | solution.py:450
  23.9 5.3 %collective-permute-start.5 = (f32[3,32,512]{2,1,0:T(8,128)S(1)}, f32[3,32,512]{2,1,0:T(8,128)S(1)}, u32[]{:S(2)}, u32[]{:S(2)}) collective-permute-start(f32[3,32,512]{2,1,0:T(8,128)S(1)} %get-tuple-element.54), channel_id=1, source_target_pairs={{1,0},{2,1},{3,2},{4,3},{5,4},{6,5},{7,6},{8,7},{9,8},{10,9},{11,1... | collective-permute-start | bytes 589832 | tf_op jit(solution)/shard_map/ppermute | solution.py:451
  25.6 3.6 %copy-start = (f32[40,32,512]{2,1,0:T(8,128)}, f32[40,32,512]{2,1,0:T(8,128)S(1)}, u32[]{:S(2)}) copy-start(f32[40,32,512]{2,1,0:T(8,128)S(1)} %shard_map.106.near_out.refs_8_) | copy-start | bytes 7864324
  25.6 34.1 %copy-start.11 = (bf16[2,256,128]{2,1,0:T(8,128)(2,1)S(1)}, bf16[2,256,128]{2,1,0:T(8,128)(2,1)}, u32[]{:S(2)}) copy-start(bf16[2,256,128]{2,1,0:T(8,128)(2,1)} %constant.13.clone.refs_2_) | copy-start | bytes 393220
  25.6 34.1 %copy-start.12 = (bf16[2,256,128]{2,1,0:T(8,128)(2,1)S(1)}, bf16[2,256,128]{2,1,0:T(8,128)(2,1)}, u32[]{:S(2)}) copy-start(bf16[2,256,128]{2,1,0:T(8,128)(2,1)} %constant.12.clone.refs_1_) | copy-start | bytes 393220
  25.6 34.1 %copy-start.13 = (bf16[96,144]{1,0:T(8,128)(2,1)S(1)}, bf16[96,144]{1,0:T(8,128)(2,1)}, u32[]{:S(2)}) copy-start(bf16[96,144]{1,0:T(8,128)(2,1)} %constant.14.clone.refs_3_) | copy-start | bytes 82948
  25.9 3.4 %copy-start.9 = (f32[10,32,512]{2,1,0:T(8,128)}, f32[10,32,512]{2,1,0:T(8,128)S(1)}, u32[]{:S(2)}) copy-start(f32[10,32,512]{2,1,0:T(8,128)S(1)} %collective-permute-done.2.prev2.refs_6_) | copy-start | bytes 1966084
  25.9 3.3 %copy-start.10 = (f32[10,32,512]{2,1,0:T(8,128)}, f32[10,32,512]{2,1,0:T(8,128)S(1)}, u32[]{:S(2)}) copy-start(f32[10,32,512]{2,1,0:T(8,128)S(1)} %collective-permute-done.3.next2.refs_7_) | copy-start | bytes 1966084
  29.2 33.3 %copy-start.14 = (f32[3,32,512]{2,1,0:T(8,128)}, f32[3,32,512]{2,1,0:T(8,128)S(1)}, u32[]{:S(2)}) copy-start(f32[3,32,512]{2,1,0:T(8,128)S(1)} %collective-permute-done.4.refs_11_) | copy-start | bytes 589828
  29.3 33.3 %copy-start.15 = (f32[3,32,512]{2,1,0:T(8,128)}, f32[3,32,512]{2,1,0:T(8,128)S(1)}, u32[]{:S(2)}) copy-start(f32[3,32,512]{2,1,0:T(8,128)S(1)} %collective-permute-done.5.refs_12_) | copy-start | bytes 589828
  55.2 11.1 %collective-permute-start.6 = (f32[3,32,512]{2,1,0:T(8,128)S(1)}, f32[3,32,512]{2,1,0:T(8,128)S(1)}, u32[]{:S(2)}, u32[]{:S(2)}) collective-permute-start(f32[3,32,512]{2,1,0:T(8,128)S(1)} %get-tuple-element.60), channel_id=1, source_target_pairs={{0,1},{1,2},{2,3},{3,4},{4,5},{5,6},{6,7},{7,8},{8,9},{9,10},{10,1... | collective-permute-start | bytes 589832 | tf_op jit(solution)/shard_map/ppermute | solution.py:484
  55.3 11.0 %collective-permute-start.7 = (f32[3,32,512]{2,1,0:T(8,128)S(1)}, f32[3,32,512]{2,1,0:T(8,128)S(1)}, u32[]{:S(2)}, u32[]{:S(2)}) collective-permute-start(f32[3,32,512]{2,1,0:T(8,128)S(1)} %get-tuple-element.61), channel_id=1, source_target_pairs={{1,0},{2,1},{3,2},{4,3},{5,4},{6,5},{7,6},{8,7},{9,8},{10,9},{11,1... | collective-permute-start | bytes 589832 | tf_op jit(solution)/shard_map/ppermute | solution.py:485
  62.6 15.7 %all-to-all-start.1 = ((f32[16,48,128]{2,1,0:T(8,128)}), f32[16,48,128]{2,1,0:T(8,128)S(1)}, u32[]{:S(2)}, u32[]{:S(2)}) async-start(f32[16,48,128]{2,1,0:T(8,128)} %bitcast.1), calls=%async_computation.1 | async-start | bytes 786432 | tf_op jit(solution)/shard_map/all_to_all | solution.py:501
  66.3 12.0 %copy-start.4 = (bf16[512,512]{1,0:T(8,128)(2,1)S(1)}, bf16[512,512]{1,0:T(8,128)(2,1)}, u32[]{:S(2)}) copy-start(bf16[512,512]{1,0:T(8,128)(2,1)} %constant.11.clone.low_any.low) | copy-start | bytes 1572868
  66.3 12.0 %copy-start.5 = (bf16[512,512]{1,0:T(8,128)(2,1)S(1)}, bf16[512,512]{1,0:T(8,128)(2,1)}, u32[]{:S(2)}) copy-start(bf16[512,512]{1,0:T(8,128)(2,1)} %constant.10.clone.high_any.high) | copy-start | bytes 1572868
  66.3 0.7 copy-start.16
  67.0 0.7 copy-start.17

commit v10 on v8

--- a/solution.py
+++ b/solution.py
@@ -202,7 +202,7 @@
 
 def pair_kernel(
     chosen_any, classes_any, p0, p2, prev1, next1, prev2, next2, rates, middle, near_out, high_any, low_any,
-    packed, chosen, classes, high, low, second, edge, fields, semaphores,
+    packed_any, chosen, classes, high, low, second, edge, fields, packed, semaphores,
 ):
     copies = fetch(
         ((chosen_any, chosen), (classes_any, classes), (high_any, high), (low_any, low)), semaphores
@@ -243,6 +243,7 @@
     lanes = 4 * depth
     half = lanes // 2
     real_lane = lax.broadcasted_iota(jnp.int32, (slots, lanes), 1) < half
+    out_copies = []
     for k in range(3):
         at = slice(k // 2 * lanes, k // 2 * lanes + lanes)
         cosine, sine = full[:slots, at], full[slots:, at]
@@ -253,10 +254,16 @@
         part = jnp.where(real_lane, cosine, sine)
         if packed.shape[0] == 3:
             packed[k] = part
+            piece = (packed.at[k], packed_any.at[k])
         else:
             devices, rows, _ = packed.shape
             rows = rows // 3
-            packed[:, k * rows : (k + 1) * rows, :] = part.reshape(devices, rows, lanes)
+            at = slice(k * rows, (k + 1) * rows)
+            packed[:, at, :] = part.reshape(devices, rows, lanes)
+            piece = (packed.at[:, at], packed_any.at[:, at])
+        out_copies += fetch((piece,), semaphores.at[pl.ds(4 + k, 1)])
+    for copy in out_copies:
+        copy.wait()
 
 
 def rest_kernel(*refs):
@@ -300,15 +307,17 @@
     slots = rows // total_x
     half = lanes // 2
 
-    def over_x(pieces):
-        for j, piece in enumerate(pieces):
-            at = slice(j * lanes, (j + 1) * lanes)
-            high, low = split(piece)
-            wide[:total_x, at] = high
-            wide[total_x : 2 * total_x, at] = low
-            wide[2 * total_x :, at] = high
-        both = jnp.dot(x_both[...], wide[...], preferred_element_type=F32)
-        return both[:total_x], both[total_x:]
+    def over_x(pieces, chunk=2):
+        results = []
+        for j in range(0, slots, chunk):
+            group = pieces[j : j + chunk]
+            high, low = split(jnp.concatenate(group, axis=1))
+            stacked = jnp.concatenate([high, low, high], axis=0)
+            both = jnp.dot(x_both[...], stacked, preferred_element_type=F32)
+            for k in range(len(group)):
+                at = slice(k * lanes, (k + 1) * lanes)
+                results.append((both[:total_x, at], both[total_x:, at]))
+        return results
 
     def put(row, even, odd):
         at = slice(row * total_x, (row + 1) * total_x)
@@ -318,23 +327,27 @@
             tall[1, at, base : base + lanes] = low
 
     real_lane = lax.broadcasted_iota(jnp.int32, (total_x, lanes), 1) < half
-    even, odd = over_x([lines[pl.ds(j, total_x, stride=slots), :] for j in range(slots)])
-    for j in range(slots):
-        at = slice(j * lanes, (j + 1) * lanes)
-        put(j, even[:, at], odd[:, at])
-    first_even, first_odd = even[:, :lanes], odd[:, :lanes]
+    turned = over_x([lines[pl.ds(j, total_x, stride=slots), :] for j in range(slots)])
+    for j, (even, odd) in enumerate(turned):
+        put(j, even, odd)
+    first_even, first_odd = turned[0]
     put(slots, jnp.where(real_lane, first_even, 0.0), jnp.where(real_lane, first_odd, 0.0))
     put(
         slots + 1,
         jnp.where(real_lane, pltpu.roll(first_even, half, 1), 0.0),
         jnp.where(real_lane, pltpu.roll(first_odd, half, 1), 0.0),
     )
-    spectrum = dot3((tall[0], tall[1]), (z_forward[0], z_forward[1]))
-    spectrum = spectrum * spectrum
-    spectrum = spectrum + pltpu.roll(spectrum, half, 1)
+    step = 2 * total_x
+    parts = []
+    for row in range(0, (slots + 2) * total_x, step):
+        at = slice(row, row + step)
+        part = dot3((tall[0, at], tall[1, at]), (z_forward[0], z_forward[1]))
+        part = part * part
+        part = part + pltpu.roll(part, half, 1)
+        parts += [part[:total_x], part[total_x:]]
 
     def power(j):
-        return spectrum[j * total_x : (j + 1) * total_x]
+        return parts[j]
 
     first = lax.axis_index("gx") == 0
     lane = lax.broadcasted_iota(jnp.int32, (total_x, lanes), 1)
@@ -348,16 +361,16 @@
             special = jnp.where(constant, 0.0, special)
             value = jnp.where(first, special, value)
         powers.append(value)
-    even, odd = over_x(powers)
-    for j in range(slots):
-        at = slice(j * lanes, (j + 1) * lanes)
-        put(j, even[:, at], odd[:, at])
-    back = dot3((tall[0, :rows], tall[1, :rows]), (z_inverse[0], z_inverse[1]))
-    for j in range(slots):
-        out[pl.ds(j, total_x, stride=slots), :] = back[j * total_x : (j + 1) * total_x]
-
-
-def finish_kernel(returned, high, low, out):
+    for j, (even, odd) in enumerate(over_x(powers)):
+        put(j, even, odd)
+    for j in range(0, slots, 2):
+        at = slice(j * total_x, (j + 2) * total_x)
+        back = dot3((tall[0, at], tall[1, at]), (z_inverse[0], z_inverse[1]))
+        out[pl.ds(j, total_x, stride=slots), :] = back[:total_x]
+        out[pl.ds(j + 1, total_x, stride=slots), :] = back[total_x:]
+
+
+def finish_kernel(returned, high, low, out_any, out, semaphores):
     fields, planes, depth, width = out.shape
     lanes = 2 * fields * depth
     half = lanes // 2
@@ -373,20 +386,26 @@
         part = part.T
         stacked.append(jnp.concatenate([part[:half], part[half:]], axis=1))
     stacked = split(jnp.concatenate(stacked, axis=0))
-    result = dot3(stacked, (high[...], low[...]))
-    for k in range(planes):
-        for f in range(fields):
-            base = k * half + f * depth
-            out[f, k] = result[base : base + depth]
-
-
-def call(kernel, outs, in_specs, *args, scratch=(), flops=0, moved=0, limit=12):
+    copies = []
+    for piece in range(2):
+        at = slice(piece * slots, (piece + 1) * slots)
+        result = dot3(stacked, (high[:, at], low[:, at]))
+        for k in range(planes):
+            for f in range(fields):
+                base = k * half + f * depth
+                out[f, k, :, at] = result[base : base + depth]
+        copies += fetch(((out.at[:, :, :, at], out_any.at[:, :, :, at]),), semaphores.at[pl.ds(piece, 1)])
+    for copy in copies:
+        copy.wait()
+
+
+def call(kernel, outs, in_specs, *args, scratch=(), flops=0, moved=0, limit=12, out_specs=None):
     args = [pltpu.with_memory_space_constraint(a, pltpu.HBM) if b is ANY else a for a, b in zip(args, in_specs)]
     return pl.pallas_call(
         kernel,
         out_shape=outs,
         in_specs=in_specs,
-        out_specs=jax.tree.map(lambda _: VMEM, outs),
+        out_specs=out_specs or jax.tree.map(lambda _: VMEM, outs),
         scratch_shapes=scratch,
         compiler_params=pltpu.CompilerParams(vmem_limit_bytes=limit * MIB),
         cost_estimate=pl.CostEstimate(flops=flops, bytes_accessed=moved, transcendentals=0),
@@ -446,11 +465,6 @@
     )
     prev2 = lax.ppermute(up2, "gx", up)
     next2 = lax.ppermute(down2, "gx", down)
-    r0, r2, l0, l2, prev1, next1 = lax.optimization_barrier((r0, r2, l0, l2, prev1, next1))
-    prev3 = lax.ppermute(r0, "gx", up)
-    next3 = lax.ppermute(r2, "gx", down)
-    prev4 = lax.ppermute(l0, "gx", up)
-    next4 = lax.ppermute(l2, "gx", down)
     near_out = call(
         near_kernel,
         shape(5 * GRAINS, depth, width),
@@ -459,6 +473,11 @@
         scratch=[small[1], pltpu.SemaphoreType.DMA((1,))],
         flops=2**25, moved=2**24,
     )
+    r0, r2, l0, l2, near_out = lax.optimization_barrier((r0, r2, l0, l2, near_out))
+    prev3 = lax.ppermute(r0, "gx", up)
+    next3 = lax.ppermute(r2, "gx", down)
+    prev4 = lax.ppermute(l0, "gx", up)
+    next4 = lax.ppermute(l2, "gx", down)
     packed_shape = (devices, planes * share, lanes) if aligned else (planes, slots, lanes)
     packed = call(
         pair_kernel,
@@ -472,9 +491,10 @@
             pltpu.VMEM((4 * GRAINS, depth, width), F32),
             pltpu.VMEM((2, 2, depth, width), F32),
             pltpu.VMEM(((planes + 1) // 2 * lanes, width), F32),
-            pltpu.SemaphoreType.DMA((4,)),
+            pltpu.VMEM(packed_shape, F32),
+            pltpu.SemaphoreType.DMA((4 + planes,)),
         ],
-        flops=2**28, moved=2**23,
+        out_specs=ANY, flops=2**28, moved=2**23,
     )
     packed, prev3, next3 = lax.optimization_barrier((packed, prev3, next3))
     if aligned:
@@ -523,6 +543,8 @@
         shape(2, planes, depth, width),
         [VMEM] * 3,
         returned, *table,
+        scratch=[pltpu.VMEM((2, planes, depth, width), F32), pltpu.SemaphoreType.DMA((2,))],
+        out_specs=ANY,
         flops=2**28, moved=2**22,
     )
     return (order_params, correlation)

time: 78.7 us -> 78.1 us (level)
  no operation moved by 1% of the time
where the time goes in v10:
time: 78.1 us; the launch traced here: 77.7 us
  starting transfers between devices  37.4 us (48%)
  Pallas kernels  21.9 us (28%)
  waiting for transfers between devices  17.3 us (22%)
  between operations  1.11 us (1%)
    pallas_call x7, Pallas kernels, call(): pl.pallas_call(kernel, out_shape=outs, in_specs=in_specs, out_specs=out_s...  21.9 us
    all_to_all x1, starting transfers between devices, shards(): lax.all_to_all(packed, 'gx', split_axis=0, concat_axis=0, tiled=True)  14 us
    ppermute x1, waiting for transfers between devices, shards(): prev4 = lax.ppermute(l0, 'gx', up)  9.81 us
    ppermute x1, starting transfers between devices, shards(): next1 = lax.ppermute(p0, 'gx', down)  5.5 us
    ppermute x1, starting transfers between devices, shards(): prev3 = lax.ppermute(r0, 'gx', up)  5.12 us
    ppermute x1, waiting for transfers between devices, shards(): prev1 = lax.ppermute(p2, 'gx', up)  4.7 us
    ppermute x1, starting transfers between devices, shards(): next2 = lax.ppermute(down2, 'gx', down)  4.49 us
    ppermute x1, starting transfers between devices, shards(): next4 = lax.ppermute(l2, 'gx', down)  4.08 us
  transfers between devices with their start and end apart: 10, of which 5 were waited for; matrix products, arithmetic and copies ran while one was open for 0% of the time, Pallas kernels for 22%

profile of v10, /device:TPU:0, one launch (start us, length us, event | category | flops | bytes accessed | tf_op | source)
XLA Modules:
  0.0 77.7 jit_solution(12704943300133802924)
XLA Ops:
  0.6 1.3 %shard_map.104 = (f32[8,32,512]{2,1,0:T(8,128)S(1)}, f32[8,32,512]{2,1,0:T(8,128)S(1)}, f32[8,32,512]{2,1,0:T(8,128)S(1)}) custom-call(bf16[8,3,32,512]{3,2,1,0:T(8,128)(2,1)} %jitter_any.1, s32[3,32,512]{2,1,0:T(8,128)} %ids_any.1), custom_call_target="tpu_custom_call" | custom-call | flops 2097152 | bytes 4194304 | tf_op jit(solution)/shard_map/pallas_call | solution.py:404
  1.9 0.0 copy-start.2
  1.9 0.0 copy-start.3
  1.9 5.5 %collective-permute-start.1 = (f32[8,32,512]{2,1,0:T(8,128)S(1)}, f32[8,32,512]{2,1,0:T(8,128)S(1)}, u32[]{:S(2)}, u32[]{:S(2)}) collective-permute-start(f32[8,32,512]{2,1,0:T(8,128)S(1)} %get-tuple-element.63.p0.refs_2_), channel_id=1, source_target_pairs={{1,0},{2,1},{3,2},{4,3},{5,4},{6,5},{7,6},{8,7},{9,8},{10,9},{11,1... | collective-permute-start | bytes 1572872 | tf_op jit(solution)/shard_map/ppermute | solution.py:454
  7.4 0.0 collective-permute-start
  7.4 2.0 %shard_map.105 = (f32[10,32,512]{2,1,0:T(8,128)S(1)}, f32[10,32,512]{2,1,0:T(8,128)S(1)}, f32[3,32,512]{2,1,0:T(8,128)S(1)}, f32[3,32,512]{2,1,0:T(8,128)S(1)}, ...) custom-call(s32[2]{0:T(128)} %refs_0_, ...), custom_call_target="tpu_custom_call" | custom-call | flops 16777216 | bytes 4194304 | tf_op jit(solution)/shard_map/pallas_call | solution.py:404
  9.4 0.0 copy-start.1
  9.4 0.0 copy-start.6
  9.4 0.1 collective-permute-start.2
  9.5 4.5 %collective-permute-start.3 = (f32[10,32,512]{2,1,0:T(8,128)S(1)}, f32[10,32,512]{2,1,0:T(8,128)S(1)}, u32[]{:S(2)}, u32[]{:S(2)}) collective-permute-start(f32[10,32,512]{2,1,0:T(8,128)S(1)} %get-tuple-element.43), channel_id=1, source_target_pairs={{1,0},{2,1},{3,2},{4,3},{5,4},{6,5},{7,6},{8,7},{9,8},{10,9},{11,1... | collective-permute-start | bytes 1966088 | tf_op jit(solution)/shard_map/ppermute | solution.py:467
  14.0 0.2 collective-permute-done.1.next1.refs_5_
  14.1 0.0 copy-start.4
  14.1 4.7 %collective-permute-done.prev1.refs_4_ = f32[8,32,512]{2,1,0:T(8,128)S(1)} collective-permute-done((f32[8,32,512]{2,1,0:T(8,128)S(1)}, f32[8,32,512]{2,1,0:T(8,128)S(1)}, u32[]{:S(2)}, u32[]{:S(2)}) %collective-permute-start) | collective-permute-done | bytes 524320 | tf_op jit(solution)/shard_map/ppermute | solution.py:453
  18.8 0.0 copy-start.5
  18.8 1.7 %shard_map.106.near_out.refs_8_ = f32[40,32,512]{2,1,0:T(8,128)S(1)} custom-call(s32[8,8]{1,0:T(8,128)} %refs_1_.1, f32[8,32,512]{2,1,0:T(8,128)S(1)} %get-tuple-element.63.p0.refs_2_, f32[8,32,512]{2,1,0:T(8,128)S(1)} %get-tuple-element.41.p1, f32[8,32,512]{2,1,0:T(8,128)S(1)} %get-tuple-element.64.p2.refs_3_, ...), custom_call_target="tpu_custom_call" | custom-call | flops 33554432 | bytes 16777216 | tf_op jit(solution)/shard_map/pallas_call | solution.py:404
  20.5 0.0 copy-start
  20.5 0.0 copy-start.11
  20.5 0.0 copy-start.12
  20.6 0.0 copy-start.13
  20.6 5.1 %collective-permute-start.4 = (f32[3,32,512]{2,1,0:T(8,128)S(1)}, f32[3,32,512]{2,1,0:T(8,128)S(1)}, u32[]{:S(2)}, u32[]{:S(2)}) collective-permute-start(f32[3,32,512]{2,1,0:T(8,128)S(1)} %get-tuple-element.51), channel_id=1, source_target_pairs={{0,1},{1,2},{2,3},{3,4},{4,5},{5,6},{6,7},{7,8},{8,9},{9,10},{10,1... | collective-permute-start | bytes 589832 | tf_op jit(solution)/shard_map/ppermute | solution.py:477
  25.7 0.0 collective-permute-start.5
  25.7 0.2 collective-permute-done.2.prev2.refs_6_
  25.9 0.0 copy-start.7
  25.9 0.0 collective-permute-done.3.next2.refs_7_
  25.9 0.0 copy-done.2
  25.9 0.0 copy-done.3
  25.9 0.0 copy-done.1
  25.9 0.0 copy-done.6
  25.9 0.0 copy-done.4
  25.9 0.0 copy-done.5
  25.9 0.0 copy-start.8
  25.9 4.0 %shard_map.107 = f32[16,48,128]{2,1,0:T(8,128)} custom-call(s32[2]{0:T(128)} %refs_0_, s32[8,8]{1,0:T(8,128)} %refs_1_.1, f32[8,32,512]{2,1,0:T(8,128)S(1)} %get-tuple-element.63.p0.refs_2_, f32[8,32,512]{2,1,0:T(8,128)S(1)} %get-tuple-element.64.p2.refs_3_, f32[8,32,512]{2,1,0:T(8,128)S(1)} %collective-permute-done.prev1.refs_4_, ...), custom_call_target="tpu_custom_call" | custom-call | flops 268435456 | bytes 8388608 | tf_op jit(solution)/shard_map/pallas_call | solution.py:404
  30.0 0.0 copy-done
  30.0 0.0 copy-done.7
  30.0 0.0 copy-done.8
  30.0 0.0 collective-permute-done.4.refs_11_
  30.0 0.0 copy-start.14
  30.0 0.0 collective-permute-done.5.refs_12_
  30.0 0.0 copy-start.15
  30.0 14.0 %all-to-all-start = ((f32[16,48,128]{2,1,0:T(8,128)}), f32[16,48,128]{2,1,0:T(8,128)S(1)}, u32[]{:S(2)}, u32[]{:S(2)}) async-start(f32[16,48,128]{2,1,0:T(8,128)} %shard_map.107), calls=%async_computation | async-start | bytes 786432 | tf_op jit(solution)/shard_map/all_to_all | solution.py:501
  44.0 0.4 collective-permute-start.6
  44.4 4.1 %collective-permute-start.7 = (f32[3,32,512]{2,1,0:T(8,128)S(1)}, f32[3,32,512]{2,1,0:T(8,128)S(1)}, u32[]{:S(2)}, u32[]{:S(2)}) collective-permute-start(f32[3,32,512]{2,1,0:T(8,128)S(1)} %get-tuple-element.57), channel_id=1, source_target_pairs={{1,0},{2,1},{3,2},{4,3},{5,4},{6,5},{7,6},{8,7},{9,8},{10,9},{11,1... | collective-permute-start | bytes 589832 | tf_op jit(solution)/shard_map/ppermute | solution.py:480
  48.5 9.8 %collective-permute-done.6.refs_13_ = f32[3,32,512]{2,1,0:T(8,128)S(1)} collective-permute-done((f32[3,32,512]{2,1,0:T(8,128)S(1)}, f32[3,32,512]{2,1,0:T(8,128)S(1)}, u32[]{:S(2)}, u32[]{:S(2)}) %collective-permute-start.6) | collective-permute-done | bytes 196640 | tf_op jit(solution)/shard_map/ppermute | solution.py:479
  58.3 0.0 copy-start.16
  58.3 0.0 collective-permute-done.7.refs_14_
  58.3 0.0 copy-start.17
  58.3 0.0 all-to-all-done
  58.3 0.0 copy-done.11
  58.3 0.0 copy-done.12
  58.4 0.0 copy-done.13
  58.4 2.2 %shard_map.108 = f32[768,128]{1,0:T(8,128)} custom-call(f32[768,128]{1,0:T(8,128)S(1)} %bitcast.2, bf16[2,256,128]{2,1,0:T(8,128)(2,1)S(1)} %copy-done.12, bf16[2,256,128]{2,1,0:T(8,128)(2,1)S(1)} %copy-done.11, bf16[96,144]{1,0:T(8,128)(2,1)S(1)} %copy-done.13), custom_call_target="tpu_custom_call" | custom-call | flops 268435456 | bytes 4194304 | tf_op jit(solution)/shard_map/pallas_call | solution.py:404
  60.5 3.7 %all-to-all-start.1 = ((f32[16,48,128]{2,1,0:T(8,128)}), f32[16,48,128]{2,1,0:T(8,128)S(1)}, u32[]{:S(2)}, u32[]{:S(2)}) async-start(f32[16,48,128]{2,1,0:T(8,128)} %bitcast.1), calls=%async_computation.1 | async-start | bytes 786432 | tf_op jit(solution)/shard_map/all_to_all | solution.py:521
  64.3 0.0 copy-done.14
  64.3 0.0 copy-done.15
  64.3 0.0 copy-done.16
  64.3 0.0 copy-done.17
  64.3 0.0 copy-start.9
  64.3 0.0 copy-start.10
  64.3 9.5 %shard_map.109 = f32[8,3,32,512]{3,2,1,0:T(8,128)} custom-call(s32[2]{0:T(128)} %refs_0_, s32[8,8]{1,0:T(8,128)} %refs_1_.1, f32[8,32,512]{2,1,0:T(8,128)} %copy-done.2, f32[8,32,512]{2,1,0:T(8,128)} %copy-done.3, f32[8,32,512]{2,1,0:T(8,128)} %copy-done.5, f32[8,32,512]{2,1,0:T(8,128)} %copy-done.4, f32[10,32,512]{2,1,0:T(8,128)} %copy-done.7, ...), custom_call_target="tpu_custom_call" | custom-call | flops 67108864 | bytes 16777216 | tf_op jit(solution)/shard_map/pallas_call | solution.py:404
  73.8 2.4 %all-to-all-done.1.returned = f32[16,48,128]{2,1,0:T(8,128)S(1)} async-done(((f32[16,48,128]{2,1,0:T(8,128)}), f32[16,48,128]{2,1,0:T(8,128)S(1)}, u32[]{:S(2)}, u32[]{:S(2)}) %all-to-all-start.1) | async-done | bytes 393248 | tf_op jit(solution)/shard_map/all_to_all | solution.py:521
  76.2 0.0 copy-done.9
  76.2 0.0 copy-done.10
  76.2 1.3 %shard_map.110 = f32[2,3,32,512]{3,2,1,0:T(8,128)} custom-call(f32[16,48,128]{2,1,0:T(8,128)S(1)} %all-to-all-done.1.returned, bf16[512,512]{1,0:T(8,128)(2,1)S(1)} %copy-done.10, bf16[512,512]{1,0:T(8,128)(2,1)S(1)} %copy-done.9), custom_call_target="tpu_custom_call" | custom-call | flops 268435456 | bytes 4194304 | tf_op jit(solution)/shard_map/pallas_call | solution.py:404
Async XLA Ops:
  1.9 24.0 %copy-start.2 = (f32[8,32,512]{2,1,0:T(8,128)}, f32[8,32,512]{2,1,0:T(8,128)S(1)}, u32[]{:S(2)}) copy-start(f32[8,32,512]{2,1,0:T(8,128)S(1)} %get-tuple-element.63.p0.refs_2_) | copy-start | bytes 1572868
  1.9 24.0 %copy-start.3 = (f32[8,32,512]{2,1,0:T(8,128)}, f32[8,32,512]{2,1,0:T(8,128)S(1)}, u32[]{:S(2)}) copy-start(f32[8,32,512]{2,1,0:T(8,128)S(1)} %get-tuple-element.64.p2.refs_3_) | copy-start | bytes 1572868
  1.9 12.2 %collective-permute-start.1 = (f32[8,32,512]{2,1,0:T(8,128)S(1)}, f32[8,32,512]{2,1,0:T(8,128)S(1)}, u32[]{:S(2)}, u32[]{:S(2)}) collective-permute-start(f32[8,32,512]{2,1,0:T(8,128)S(1)} %get-tuple-element.63.p0.refs_2_), channel_id=1, source_target_pairs={{1,0},{2,1},{3,2},{4,3},{5,4},{6,5},{7,6},{8,7},{9,8},{10,9},{11,1... | collective-permute-start | bytes 1572872 | tf_op jit(solution)/shard_map/ppermute | solution.py:454
  7.4 11.4 %collective-permute-start = (f32[8,32,512]{2,1,0:T(8,128)S(1)}, f32[8,32,512]{2,1,0:T(8,128)S(1)}, u32[]{:S(2)}, u32[]{:S(2)}) collective-permute-start(f32[8,32,512]{2,1,0:T(8,128)S(1)} %get-tuple-element.64.p2.refs_3_), channel_id=1, source_target_pairs={{0,1},{1,2},{2,3},{3,4},{4,5},{5,6},{6,7},{7,8},{8,9},{9,10},{10,1... | collective-permute-start | bytes 1572872 | tf_op jit(solution)/shard_map/ppermute | solution.py:453
  9.4 16.5 %copy-start.1 = (f32[3,8,32,512]{3,2,1,0:T(8,128)}, f32[3,8,32,512]{3,2,1,0:T(8,128)S(1)}, u32[]{:S(2)}) copy-start(f32[3,8,32,512]{3,2,1,0:T(8,128)S(1)} %get-tuple-element.71.rates.refs_10_) | copy-start | bytes 4718596
  9.4 16.5 %copy-start.6 = (f32[8,32,512]{2,1,0:T(8,128)}, f32[8,32,512]{2,1,0:T(8,128)S(1)}, u32[]{:S(2)}) copy-start(f32[8,32,512]{2,1,0:T(8,128)S(1)} %get-tuple-element.70.middle.refs_9_) | copy-start | bytes 1572868
  9.4 16.4 %collective-permute-start.2 = (f32[10,32,512]{2,1,0:T(8,128)S(1)}, f32[10,32,512]{2,1,0:T(8,128)S(1)}, u32[]{:S(2)}, u32[]{:S(2)}) collective-permute-start(f32[10,32,512]{2,1,0:T(8,128)S(1)} %get-tuple-element.42), channel_id=1, source_target_pairs={{0,1},{1,2},{2,3},{3,4},{4,5},{5,6},{6,7},{7,8},{8,9},{9,10},{10,1... | collective-permute-start | bytes 1966088 | tf_op jit(solution)/shard_map/ppermute | solution.py:466
  9.5 16.4 %collective-permute-start.3 = (f32[10,32,512]{2,1,0:T(8,128)S(1)}, f32[10,32,512]{2,1,0:T(8,128)S(1)}, u32[]{:S(2)}, u32[]{:S(2)}) collective-permute-start(f32[10,32,512]{2,1,0:T(8,128)S(1)} %get-tuple-element.43), channel_id=1, source_target_pairs={{1,0},{2,1},{3,2},{4,3},{5,4},{6,5},{7,6},{8,7},{9,8},{10,9},{11,1... | collective-permute-start | bytes 1966088 | tf_op jit(solution)/shard_map/ppermute | solution.py:467
  14.1 11.8 %copy-start.4 = (f32[8,32,512]{2,1,0:T(8,128)}, f32[8,32,512]{2,1,0:T(8,128)S(1)}, u32[]{:S(2)}) copy-start(f32[8,32,512]{2,1,0:T(8,128)S(1)} %collective-permute-done.1.next1.refs_5_) | copy-start | bytes 1572868
  18.8 7.1 %copy-start.5 = (f32[8,32,512]{2,1,0:T(8,128)}, f32[8,32,512]{2,1,0:T(8,128)S(1)}, u32[]{:S(2)}) copy-start(f32[8,32,512]{2,1,0:T(8,128)S(1)} %collective-permute-done.prev1.refs_4_) | copy-start | bytes 1572868
  20.5 9.5 %copy-start = (f32[40,32,512]{2,1,0:T(8,128)}, f32[40,32,512]{2,1,0:T(8,128)S(1)}, u32[]{:S(2)}) copy-start(f32[40,32,512]{2,1,0:T(8,128)S(1)} %shard_map.106.near_out.refs_8_) | copy-start | bytes 7864324
  20.5 37.8 %copy-start.11 = (bf16[2,256,128]{2,1,0:T(8,128)(2,1)S(1)}, bf16[2,256,128]{2,1,0:T(8,128)(2,1)}, u32[]{:S(2)}) copy-start(bf16[2,256,128]{2,1,0:T(8,128)(2,1)} %constant.13.clone.refs_2_) | copy-start | bytes 393220
  20.5 37.8 %copy-start.12 = (bf16[2,256,128]{2,1,0:T(8,128)(2,1)S(1)}, bf16[2,256,128]{2,1,0:T(8,128)(2,1)}, u32[]{:S(2)}) copy-start(bf16[2,256,128]{2,1,0:T(8,128)(2,1)} %constant.12.clone.refs_1_) | copy-start | bytes 393220
  20.6 37.8 %copy-start.13 = (bf16[96,144]{1,0:T(8,128)(2,1)S(1)}, bf16[96,144]{1,0:T(8,128)(2,1)}, u32[]{:S(2)}) copy-start(bf16[96,144]{1,0:T(8,128)(2,1)} %constant.14.clone.refs_3_) | copy-start | bytes 82948
  20.6 9.4 %collective-permute-start.4 = (f32[3,32,512]{2,1,0:T(8,128)S(1)}, f32[3,32,512]{2,1,0:T(8,128)S(1)}, u32[]{:S(2)}, u32[]{:S(2)}) collective-permute-start(f32[3,32,512]{2,1,0:T(8,128)S(1)} %get-tuple-element.51), channel_id=1, source_target_pairs={{0,1},{1,2},{2,3},{3,4},{4,5},{5,6},{6,7},{7,8},{8,9},{9,10},{10,1... | collective-permute-start | bytes 589832 | tf_op jit(solution)/shard_map/ppermute | solution.py:477
  25.7 4.3 %collective-permute-start.5 = (f32[3,32,512]{2,1,0:T(8,128)S(1)}, f32[3,32,512]{2,1,0:T(8,128)S(1)}, u32[]{:S(2)}, u32[]{:S(2)}) collective-permute-start(f32[3,32,512]{2,1,0:T(8,128)S(1)} %get-tuple-element.52), channel_id=1, source_target_pairs={{1,0},{2,1},{3,2},{4,3},{5,4},{6,5},{7,6},{8,7},{9,8},{10,9},{11,1... | collective-permute-start | bytes 589832 | tf_op jit(solution)/shard_map/ppermute | solution.py:478
  25.9 4.1 %copy-start.7 = (f32[10,32,512]{2,1,0:T(8,128)}, f32[10,32,512]{2,1,0:T(8,128)S(1)}, u32[]{:S(2)}) copy-start(f32[10,32,512]{2,1,0:T(8,128)S(1)} %collective-permute-done.2.prev2.refs_6_) | copy-start | bytes 1966084
  25.9 4.1 %copy-start.8 = (f32[10,32,512]{2,1,0:T(8,128)}, f32[10,32,512]{2,1,0:T(8,128)S(1)}, u32[]{:S(2)}) copy-start(f32[10,32,512]{2,1,0:T(8,128)S(1)} %collective-permute-done.3.next2.refs_7_) | copy-start | bytes 1966084
  30.0 34.2 %copy-start.14 = (f32[3,32,512]{2,1,0:T(8,128)}, f32[3,32,512]{2,1,0:T(8,128)S(1)}, u32[]{:S(2)}) copy-start(f32[3,32,512]{2,1,0:T(8,128)S(1)} %collective-permute-done.4.refs_11_) | copy-start | bytes 589828
  30.0 34.2 %copy-start.15 = (f32[3,32,512]{2,1,0:T(8,128)}, f32[3,32,512]{2,1,0:T(8,128)S(1)}, u32[]{:S(2)}) copy-start(f32[3,32,512]{2,1,0:T(8,128)S(1)} %collective-permute-done.5.refs_12_) | copy-start | bytes 589828
  30.0 28.3 %all-to-all-start = ((f32[16,48,128]{2,1,0:T(8,128)}), f32[16,48,128]{2,1,0:T(8,128)S(1)}, u32[]{:S(2)}, u32[]{:S(2)}) async-start(f32[16,48,128]{2,1,0:T(8,128)} %shard_map.107), calls=%async_computation | async-start | bytes 786432 | tf_op jit(solution)/shard_map/all_to_all | solution.py:501
  44.0 14.3 %collective-permute-start.6 = (f32[3,32,512]{2,1,0:T(8,128)S(1)}, f32[3,32,512]{2,1,0:T(8,128)S(1)}, u32[]{:S(2)}, u32[]{:S(2)}) collective-permute-start(f32[3,32,512]{2,1,0:T(8,128)S(1)} %get-tuple-element.56), channel_id=1, source_target_pairs={{0,1},{1,2},{2,3},{3,4},{4,5},{5,6},{6,7},{7,8},{8,9},{9,10},{10,1... | collective-permute-start | bytes 589832 | tf_op jit(solution)/shard_map/ppermute | solution.py:479
  44.4 13.9 %collective-permute-start.7 = (f32[3,32,512]{2,1,0:T(8,128)S(1)}, f32[3,32,512]{2,1,0:T(8,128)S(1)}, u32[]{:S(2)}, u32[]{:S(2)}) collective-permute-start(f32[3,32,512]{2,1,0:T(8,128)S(1)} %get-tuple-element.57), channel_id=1, source_target_pairs={{1,0},{2,1},{3,2},{4,3},{5,4},{6,5},{7,6},{8,7},{9,8},{10,9},{11,1... | collective-permute-start | bytes 589832 | tf_op jit(solution)/shard_map/ppermute | solution.py:480
  58.3 6.0 %copy-start.16 = (f32[3,32,512]{2,1,0:T(8,128)}, f32[3,32,512]{2,1,0:T(8,128)S(1)}, u32[]{:S(2)}) copy-start(f32[3,32,512]{2,1,0:T(8,128)S(1)} %collective-permute-done.6.refs_13_) | copy-start | bytes 589828
  58.3 6.0 %copy-start.17 = (f32[3,32,512]{2,1,0:T(8,128)}, f32[3,32,512]{2,1,0:T(8,128)S(1)}, u32[]{:S(2)}) copy-start(f32[3,32,512]{2,1,0:T(8,128)S(1)} %collective-permute-done.7.refs_14_) | copy-start | bytes 589828
  60.5 15.7 %all-to-all-start.1 = ((f32[16,48,128]{2,1,0:T(8,128)}), f32[16,48,128]{2,1,0:T(8,128)S(1)}, u32[]{:S(2)}, u32[]{:S(2)}) async-start(f32[16,48,128]{2,1,0:T(8,128)} %bitcast.1), calls=%async_computation.1 | async-start | bytes 786432 | tf_op jit(solution)/shard_map/all_to_all | solution.py:521
  64.3 11.9 %copy-start.9 = (bf16[512,512]{1,0:T(8,128)(2,1)S(1)}, bf16[512,512]{1,0:T(8,128)(2,1)}, u32[]{:S(2)}) copy-start(bf16[512,512]{1,0:T(8,128)(2,1)} %constant.11.clone.low_any.low) | copy-start | bytes 1572868
  64.3 11.9 %copy-start.10 = (bf16[512,512]{1,0:T(8,128)(2,1)S(1)}, bf16[512,512]{1,0:T(8,128)(2,1)}, u32[]{:S(2)}) copy-start(bf16[512,512]{1,0:T(8,128)(2,1)} %constant.10.clone.high_any.high) | copy-start | bytes 1572868

commit v11 on v10

--- a/solution.py
+++ b/solution.py
@@ -202,7 +202,7 @@
 
 def pair_kernel(
     chosen_any, classes_any, p0, p2, prev1, next1, prev2, next2, rates, middle, near_out, high_any, low_any,
-    packed_any, chosen, classes, high, low, second, edge, fields, packed, semaphores,
+    packed, chosen, classes, high, low, second, edge, fields, semaphores,
 ):
     copies = fetch(
         ((chosen_any, chosen), (classes_any, classes), (high_any, high), (low_any, low)), semaphores
@@ -243,7 +243,6 @@
     lanes = 4 * depth
     half = lanes // 2
     real_lane = lax.broadcasted_iota(jnp.int32, (slots, lanes), 1) < half
-    out_copies = []
     for k in range(3):
         at = slice(k // 2 * lanes, k // 2 * lanes + lanes)
         cosine, sine = full[:slots, at], full[slots:, at]
@@ -254,33 +253,61 @@
         part = jnp.where(real_lane, cosine, sine)
         if packed.shape[0] == 3:
             packed[k] = part
-            piece = (packed.at[k], packed_any.at[k])
         else:
             devices, rows, _ = packed.shape
             rows = rows // 3
-            at = slice(k * rows, (k + 1) * rows)
-            packed[:, at, :] = part.reshape(devices, rows, lanes)
-            piece = (packed.at[:, at], packed_any.at[:, at])
-        out_copies += fetch((piece,), semaphores.at[pl.ds(4 + k, 1)])
-    for copy in out_copies:
-        copy.wait()
-
-
-def rest_kernel(*refs):
-    count = (len(refs) - 4) // 2
-    sources, out, targets = refs[:count], refs[count], refs[count + 1 : 2 * count + 1]
-    second, edge, semaphores = refs[-3:]
-    copies = fetch(list(zip(sources, targets)), semaphores)
-    chosen, classes, p0, p2, prev1, next1, prev2, next2, near_out, middle, rates, prev3, next3, prev4, next4 = targets
-    near_state = groups(near_out, 5)
+            packed[:, k * rows : (k + 1) * rows, :] = part.reshape(devices, rows, lanes)
+
+
+def rest_kernel(
+    prev3, next3, prev4, next4,
+    chosen_any, classes_any, p0_any, p2_any, prev1_any, next1_any, prev2_any, next2_any, near_any, middle_any,
+    rates_any, out_any,
+    chosen, classes, p0, p2, prev1, next1, prev2, next2, near_out, middle, rates, second, edge, out, semaphores,
+):
+    near_state, near_source = groups(near_out, 5), groups(near_any, 5)
     edge_rates, inner1, middle2 = near_state[:2], near_state[2:4], near_state[4]
     outer1, side2 = groups(second, 2), groups(second, 2, 2 * GRAINS)
-    for copy in copies:
-        copy.wait()
-    second_step(p0, p2, prev1, next1, prev2, next2, rates, middle, near_state, outer1, side2)
+    copies = fetch(
+        (
+            (prev1_any, prev1), (prev2_any, prev2), (p0_any, p0), (near_source[0], near_state[0]),
+            (next1_any, next1), (next2_any, next2), (p2_any, p2), (near_source[1], near_state[1]),
+            (near_source[2], near_state[2]), (middle_any, middle), (rates_any.at[0], rates.at[0]),
+            (near_source[3], near_state[3]), (rates_any.at[2], rates.at[2]),
+            (chosen_any, chosen), (classes_any, classes),
+            (near_source[4], near_state[4]), (rates_any.at[1], rates.at[1]),
+        ),
+        semaphores,
+    )
+
+    def wait(first, last):
+        for copy in copies[first:last]:
+            copy.wait()
+
+    wait(0, 4)
+    step_plane(prev1, prev2, p0, edge_rates[0], outer1[0])
+    wait(4, 8)
+    step_plane(next1, p2, next2, edge_rates[1], outer1[1])
+    wait(8, 11)
+    step_plane(inner1[0], outer1[0], middle, rates.at[0], side2[0])
+    wait(11, 13)
+    step_plane(inner1[1], middle, outer1[1], rates.at[2], side2[1])
+    wait(13, 17)
     other = others_of(chosen)
     pair = pair_of(chosen)
     places = [(pair[k], GRAINS + k, None) for k in range(2)] + [(other(r), None, r) for r in range(GRAINS - 2)]
+    eta2 = (side2[0], middle2, side2[1])
+    outs = []
+
+    def finish(plane):
+        total = squares(eta2[plane])
+        for k, (i, _, _) in enumerate(places):
+            before = edge[0, k] if plane == 0 else eta2[plane - 1][i]
+            after = edge[1, k] if plane == 2 else eta2[plane + 1][i]
+            out[i, plane] = update(eta2[plane][i], before, after, total, rates[plane, i])
+        outs.extend(fetch(((out.at[:, plane], out_any.at[:, plane]),), semaphores.at[pl.ds(17 + plane, 1)]))
+
+    finish(1)
     for side, (soon, far, mid, near) in enumerate(((prev3, prev4, prev2, prev1), (next3, next4, next2, next1))):
         ids = grain_of(mid)
         total0 = squares(mid)
@@ -292,13 +319,9 @@
                 third = soon[late] if late < SOON else far[late - SOON]
             first = update(mid[i], third, near[i], total0, rate(classes, ids, i))
             edge[side, k] = update(outer1[side][i], first, inner1[side][i], total1, edge_rates[side][i])
-    eta2 = (side2[0], middle2, side2[1])
-    for plane in range(3):
-        total = squares(eta2[plane])
-        for k, (i, _, _) in enumerate(places):
-            before = edge[0, k] if plane == 0 else eta2[plane - 1][i]
-            after = edge[1, k] if plane == 2 else eta2[plane + 1][i]
-            out[i, plane] = update(eta2[plane][i], before, after, total, rates[plane, i])
+        finish(2 * side)
+    for copy in outs:
+        copy.wait()
 
 
 def line_kernel(lines, z_forward, z_inverse, x_both, out, wide, tall, scale):
@@ -473,11 +496,9 @@
         scratch=[small[1], pltpu.SemaphoreType.DMA((1,))],
         flops=2**25, moved=2**24,
     )
-    r0, r2, l0, l2, near_out = lax.optimization_barrier((r0, r2, l0, l2, near_out))
+    r0, r2, near_out = lax.optimization_barrier((r0, r2, near_out))
     prev3 = lax.ppermute(r0, "gx", up)
     next3 = lax.ppermute(r2, "gx", down)
-    prev4 = lax.ppermute(l0, "gx", up)
-    next4 = lax.ppermute(l2, "gx", down)
     packed_shape = (devices, planes * share, lanes) if aligned else (planes, slots, lanes)
     packed = call(
         pair_kernel,
@@ -491,10 +512,9 @@
             pltpu.VMEM((4 * GRAINS, depth, width), F32),
             pltpu.VMEM((2, 2, depth, width), F32),
             pltpu.VMEM(((planes + 1) // 2 * lanes, width), F32),
-            pltpu.VMEM(packed_shape, F32),
-            pltpu.SemaphoreType.DMA((4 + planes,)),
+            pltpu.SemaphoreType.DMA((4,)),
         ],
-        out_specs=ANY, flops=2**28, moved=2**23,
+        flops=2**28, moved=2**23,
     )
     packed, prev3, next3 = lax.optimization_barrier((packed, prev3, next3))
     if aligned:
@@ -502,7 +522,9 @@
     else:
         lines = lax.all_to_all(packed, "gx", split_axis=1, concat_axis=0, tiled=True)
     lines = lines.reshape(total_x * share, lanes)
-    lines, prev4, next4 = lax.optimization_barrier((lines, prev4, next4))
+    lines, l0, l2 = lax.optimization_barrier((lines, l0, l2))
+    prev4 = lax.ppermute(l0, "gx", up)
+    next4 = lax.ppermute(l2, "gx", down)
     def lines_body(*refs):
         line_kernel(*refs, scale=1.0 / (count * count))
 
@@ -522,21 +544,25 @@
     if not aligned:
         returned = returned.reshape(devices, planes, share, lanes).transpose(1, 0, 2, 3)
         returned = returned.reshape(planes, slots, lanes)
-    late = (chosen, class_table, p0, p2, prev1, next1, prev2, next2, near_out, middle, rates, prev3, next3, prev4, next4)
+    late = (
+        prev3, next3, prev4, next4,
+        chosen, class_table, p0, p2, prev1, next1, prev2, next2, near_out, middle, rates,
+    )
     late, _ = lax.optimization_barrier((late, back))
     order_params = call(
         rest_kernel,
         shape(GRAINS, planes, depth, width),
-        [ANY] * len(late),
+        [VMEM] * 4 + [ANY] * (len(late) - 4),
         *late,
         scratch=[
             *small,
-            *[pltpu.VMEM(value.shape, F32) for value in late[2:]],
+            *[pltpu.VMEM(value.shape, F32) for value in late[6:]],
             pltpu.VMEM((4 * GRAINS, depth, width), F32),
             pltpu.VMEM((2, *plane), F32),
-            pltpu.SemaphoreType.DMA((len(late),)),
+            pltpu.VMEM((GRAINS, planes, depth, width), F32),
+            pltpu.SemaphoreType.DMA((17 + planes,)),
         ],
-        flops=2**26, moved=2**24, limit=24,
+        out_specs=ANY, flops=2**37, moved=2**24, limit=24,
     )
     correlation = call(
         finish_kernel,

time: 78.1 us -> 79.4 us (1.017)
  blocking collectives: 0 us -> 25.9 us
  starting transfers between devices: 37.4 us -> 23.3 us
  waiting for transfers between devices: 17.3 us -> 8.37 us
  Pallas kernels: 21.9 us -> 19.2 us
  local copies, waits for them, and re-layouts: 0.09 us -> 1.08 us
    all_to_all x0 -> x1, blocking collectives: none -> 25.9 us  [shards(): lax.all_to_all(packed, 'gx', split_axis=0, concat_axis=0, tiled=True)]
    all_to_all x1 -> x0, starting transfers between devices: 14 us -> none  [shards(): lax.all_to_all(packed, 'gx', split_axis=0, concat_axis=0, tiled=True)]
    ppermute x1, waiting for transfers between devices: 9.81 us -> 0.01 us  [shards(): prev4 = lax.ppermute(l0, 'gx', up)]
    pallas_call x7, Pallas kernels: 21.9 us -> 19.2 us  [call(): pl.pallas_call(kernel, out_shape=outs, in_specs=in_specs, out_specs=out_s...]
    unnamed x36, local copies, waits for them, and re-layouts: 0.09 us -> 1.08 us
    all_to_all x1, waiting for transfers between devices: 2.41 us -> 3.32 us  [shards(): lax.all_to_all(back, 'gx', split_axis=0, concat_axis=0, tiled=True)]
  transfers between devices with their start and end apart: 10 -> 9, of which waited for: 5 -> 4; matrix products, arithmetic and copies ran while one was open for 0% -> 0% of each run, Pallas kernels for 22% -> 21%
where the time goes in v11:
time: 79.4 us; the launch traced here: 79.1 us
  blocking collectives  25.9 us (33%)
  starting transfers between devices  23.3 us (29%)
  Pallas kernels  19.2 us (24%)
  waiting for transfers between devices  8.37 us (11%)
  local copies, waits for them, and re-layouts  1.08 us (1%)
  between operations  1.08 us (1%)
    all_to_all x1, blocking collectives, shards(): lax.all_to_all(packed, 'gx', split_axis=0, concat_axis=0, tiled=True)  25.9 us
    pallas_call x7, Pallas kernels, call(): pl.pallas_call(kernel, out_shape=outs, in_specs=in_specs, out_specs=out_s...  19.2 us
    ppermute x1, starting transfers between devices, shards(): next1 = lax.ppermute(p0, 'gx', down)  5.5 us
    ppermute x1, starting transfers between devices, shards(): prev3 = lax.ppermute(r0, 'gx', up)  5.12 us
    ppermute x1, waiting for transfers between devices, shards(): prev1 = lax.ppermute(p2, 'gx', up)  4.7 us
    ppermute x1, starting transfers between devices, shards(): next2 = lax.ppermute(down2, 'gx', down)  4.49 us
    ppermute x1, starting transfers between devices, shards(): next4 = lax.ppermute(l2, 'gx', down)  4.33 us
    all_to_all x1, starting transfers between devices, shards(): lax.all_to_all(back, 'gx', split_axis=0, concat_axis=0, tiled=True)  3.73 us
  transfers between devices with their start and end apart: 9, of which 4 were waited for; matrix products, arithmetic and copies ran while one was open for 0% of the time, Pallas kernels for 21%

profile of v11, /device:TPU:0, one launch (start us, length us, event | category | flops | bytes accessed | tf_op | source)
XLA Modules:
  0.0 79.1 jit_solution(17578891934264254535)
XLA Ops:
  0.6 1.3 %shard_map.104 = (f32[8,32,512]{2,1,0:T(8,128)S(1)}, f32[8,32,512]{2,1,0:T(8,128)S(1)}, f32[8,32,512]{2,1,0:T(8,128)S(1)}) custom-call(bf16[8,3,32,512]{3,2,1,0:T(8,128)(2,1)} %jitter_any.1, s32[3,32,512]{2,1,0:T(8,128)} %ids_any.1), custom_call_target="tpu_custom_call" | custom-call | flops 2097152 | bytes 4194304 | tf_op jit(solution)/shard_map/pallas_call | solution.py:427
  1.9 0.0 copy-start.2
  1.9 0.0 copy-start.3
  1.9 5.5 %collective-permute-start.1 = (f32[8,32,512]{2,1,0:T(8,128)S(1)}, f32[8,32,512]{2,1,0:T(8,128)S(1)}, u32[]{:S(2)}, u32[]{:S(2)}) collective-permute-start(f32[8,32,512]{2,1,0:T(8,128)S(1)} %get-tuple-element.63.p0.p0_any), channel_id=1, source_target_pairs={{1,0},{2,1},{3,2},{4,3},{5,4},{6,5},{7,6},{8,7},{9,8},{10,9},{11,1... | collective-permute-start | bytes 1572872 | tf_op jit(solution)/shard_map/ppermute | solution.py:477
  7.4 0.0 collective-permute-start
  7.4 2.0 %shard_map.105 = (f32[10,32,512]{2,1,0:T(8,128)S(1)}, f32[10,32,512]{2,1,0:T(8,128)S(1)}, f32[3,32,512]{2,1,0:T(8,128)S(1)}, f32[3,32,512]{2,1,0:T(8,128)S(1)}, ...) custom-call(s32[2]{0:T(128)} %chosen_any.4, ...), custom_call_target="tpu_custom_call" | custom-call | flops 16777216 | bytes 4194304 | tf_op jit(solution)/shard_map/pallas_call | solution.py:427
  9.4 0.0 copy-start.1
  9.4 0.0 copy-start.8
  9.4 0.1 collective-permute-start.2
  9.5 4.5 %collective-permute-start.3 = (f32[10,32,512]{2,1,0:T(8,128)S(1)}, f32[10,32,512]{2,1,0:T(8,128)S(1)}, u32[]{:S(2)}, u32[]{:S(2)}) collective-permute-start(f32[10,32,512]{2,1,0:T(8,128)S(1)} %get-tuple-element.41), channel_id=1, source_target_pairs={{1,0},{2,1},{3,2},{4,3},{5,4},{6,5},{7,6},{8,7},{9,8},{10,9},{11,1... | collective-permute-start | bytes 1966088 | tf_op jit(solution)/shard_map/ppermute | solution.py:490
  14.0 0.2 collective-permute-done.1.next1.next1_any
  14.1 0.0 copy-start.6
  14.1 4.7 %collective-permute-done.prev1.prev1_any = f32[8,32,512]{2,1,0:T(8,128)S(1)} collective-permute-done((f32[8,32,512]{2,1,0:T(8,128)S(1)}, f32[8,32,512]{2,1,0:T(8,128)S(1)}, u32[]{:S(2)}, u32[]{:S(2)}) %collective-permute-start) | collective-permute-done | bytes 524320 | tf_op jit(solution)/shard_map/ppermute | solution.py:476
  18.8 0.0 copy-start.7
  18.8 1.7 %shard_map.106.near_out.near_any = f32[40,32,512]{2,1,0:T(8,128)S(1)} custom-call(s32[8,8]{1,0:T(8,128)} %classes_any.6, f32[8,32,512]{2,1,0:T(8,128)S(1)} %get-tuple-element.63.p0.p0_any, f32[8,32,512]{2,1,0:T(8,128)S(1)} %get-tuple-element.39.p1, f32[8,32,512]{2,1,0:T(8,128)S(1)} %get-tuple-element.64.p2.p2_any, ...), custom_call_target="tpu_custom_call" | custom-call | flops 33554432 | bytes 16777216 | tf_op jit(solution)/shard_map/pallas_call | solution.py:427
  20.5 0.0 copy-start
  20.5 0.0 copy-start.11
  20.5 0.0 copy-start.12
  20.6 0.0 copy-start.13
  20.6 5.1 %collective-permute-start.4 = (f32[3,32,512]{2,1,0:T(8,128)S(1)}, f32[3,32,512]{2,1,0:T(8,128)S(1)}, u32[]{:S(2)}, u32[]{:S(2)}) collective-permute-start(f32[3,32,512]{2,1,0:T(8,128)S(1)} %get-tuple-element.47), channel_id=1, source_target_pairs={{0,1},{1,2},{2,3},{3,4},{4,5},{5,6},{6,7},{7,8},{8,9},{9,10},{10,1... | collective-permute-start | bytes 589832 | tf_op jit(solution)/shard_map/ppermute | solution.py:500
  25.7 0.0 collective-permute-start.5
  25.7 0.2 collective-permute-done.2.prev2.prev2_any
  25.9 0.0 copy-start.9
  25.9 0.0 collective-permute-done.3.next2.next2_any
  25.9 0.0 copy-done.2
  25.9 0.0 copy-done.3
  25.9 0.0 copy-done.1
  25.9 0.0 copy-done.8
  25.9 0.0 copy-done.6
  25.9 0.0 copy-done.7
  25.9 0.0 copy-start.10
  25.9 3.3 %shard_map.107 = f32[16,48,128]{2,1,0:T(8,128)S(1)} custom-call(s32[2]{0:T(128)} %chosen_any.4, s32[8,8]{1,0:T(8,128)} %classes_any.6, f32[8,32,512]{2,1,0:T(8,128)S(1)} %get-tuple-element.63.p0.p0_any, f32[8,32,512]{2,1,0:T(8,128)S(1)} %get-tuple-element.64.p2.p2_any, f32[8,32,512]{2,1,0:T(8,128)S(1)} %collective-permute-done.prev1.prev1_any, ...), custom_call_target="tpu_custom_call" | custom-call | flops 268435456 | bytes 8388608 | tf_op jit(solution)/shard_map/pallas_call | solution.py:427
  29.2 0.0 copy-done
  29.2 0.0 copy-done.9
  29.2 0.0 copy-done.10
  29.2 0.0 collective-permute-done.4.prev3
  29.3 0.0 copy-start.14
  29.3 0.0 collective-permute-done.5.next3
  29.3 0.0 copy-start.16
  29.3 25.9 %all_to_all.10 = f32[16,48,128]{2,1,0:T(8,128)S(1)} all-to-all(f32[16,48,128]{2,1,0:T(8,128)S(1)} %shard_map.107), channel_id=1, replica_groups=mesh['grp'=2,'gx'=16] {'gx'}, dimensions={0} | all-to-all | bytes 786432 | tf_op jit(solution)/shard_map/all_to_all | solution.py:521
  55.2 0.1 collective-permute-start.6
  55.3 0.0 copy-done.14
  55.4 4.3 %collective-permute-start.7 = (f32[3,32,512]{2,1,0:T(8,128)S(1)}, f32[3,32,512]{2,1,0:T(8,128)S(1)}, u32[]{:S(2)}, u32[]{:S(2)}) collective-permute-start(f32[3,32,512]{2,1,0:T(8,128)S(1)} %get-tuple-element.55), channel_id=1, source_target_pairs={{1,0},{2,1},{3,2},{4,3},{5,4},{6,5},{7,6},{8,7},{9,8},{10,9},{11,1... | collective-permute-start | bytes 589832 | tf_op jit(solution)/shard_map/ppermute | solution.py:527
  59.7 0.0 copy-done.11
  59.7 0.0 copy-done.12
  59.7 0.0 copy-done.13
  59.7 0.0 copy-start.15
  59.7 2.2 %shard_map.108 = f32[768,128]{1,0:T(8,128)} custom-call(f32[768,128]{1,0:T(8,128)S(1)} %bitcast.2, bf16[2,256,128]{2,1,0:T(8,128)(2,1)S(1)} %copy-done.12, bf16[2,256,128]{2,1,0:T(8,128)(2,1)S(1)} %copy-done.11, bf16[96,144]{1,0:T(8,128)(2,1)S(1)} %copy-done.13), custom_call_target="tpu_custom_call" | custom-call | flops 268435456 | bytes 4194304 | tf_op jit(solution)/shard_map/pallas_call | solution.py:427
  61.9 0.0 copy-done.16
  61.9 3.7 %all-to-all-start.1 = ((f32[16,48,128]{2,1,0:T(8,128)}), f32[16,48,128]{2,1,0:T(8,128)S(1)}, u32[]{:S(2)}, u32[]{:S(2)}) async-start(f32[16,48,128]{2,1,0:T(8,128)} %bitcast.1), calls=%async_computation.1 | async-start | bytes 786432 | tf_op jit(solution)/shard_map/all_to_all | solution.py:543
  65.6 0.0 copy-start.4
  65.6 0.0 copy-start.5
  65.6 0.0 collective-permute-done.6.prev4
  65.6 0.0 collective-permute-done.7.next4
  65.6 0.0 copy-done.15
  65.7 0.0 copy-start.17
  65.7 1.0 %copy-done.17 = f32[3,32,512]{2,1,0:T(8,128)S(1)} copy-done((f32[3,32,512]{2,1,0:T(8,128)S(1)}, f32[3,32,512]{2,1,0:T(8,128)}, u32[]{:S(2)}) %copy-start.17) | copy-done | bytes 196632
  66.7 7.6 %shard_map.109 = f32[8,3,32,512]{3,2,1,0:T(8,128)} custom-call(f32[3,32,512]{2,1,0:T(8,128)S(1)} %copy-done.15, f32[3,32,512]{2,1,0:T(8,128)S(1)} %copy-done.17, f32[3,32,512]{2,1,0:T(8,128)S(1)} %collective-permute-done.6.prev4, f32[3,32,512]{2,1,0:T(8,128)S(1)} %collective-permute-done.7.next4, s32[2]{0:T(128)} %chosen_any.4, s32[8,8]{1,0:T(8,128)} %classes_any.6, ...), custom_call_target="tpu_custom_call" | custom-call | flops 137438953472 | bytes 16777216 | tf_op jit(solution)/shard_map/pallas_call | solution.py:427
  74.3 3.3 %all-to-all-done.1.returned = f32[16,48,128]{2,1,0:T(8,128)S(1)} async-done(((f32[16,48,128]{2,1,0:T(8,128)}), f32[16,48,128]{2,1,0:T(8,128)S(1)}, u32[]{:S(2)}, u32[]{:S(2)}) %all-to-all-start.1) | async-done | bytes 393248 | tf_op jit(solution)/shard_map/all_to_all | solution.py:543
  77.6 0.0 copy-done.4
  77.6 0.0 copy-done.5
  77.6 1.3 %shard_map.110 = f32[2,3,32,512]{3,2,1,0:T(8,128)} custom-call(f32[16,48,128]{2,1,0:T(8,128)S(1)} %all-to-all-done.1.returned, bf16[512,512]{1,0:T(8,128)(2,1)S(1)} %copy-done.5, bf16[512,512]{1,0:T(8,128)(2,1)S(1)} %copy-done.4), custom_call_target="tpu_custom_call" | custom-call | flops 268435456 | bytes 4194304 | tf_op jit(solution)/shard_map/pallas_call | solution.py:427
Async XLA Ops:
  1.9 24.0 %copy-start.2 = (f32[8,32,512]{2,1,0:T(8,128)}, f32[8,32,512]{2,1,0:T(8,128)S(1)}, u32[]{:S(2)}) copy-start(f32[8,32,512]{2,1,0:T(8,128)S(1)} %get-tuple-element.63.p0.p0_any) | copy-start | bytes 1572868
  1.9 24.0 %copy-start.3 = (f32[8,32,512]{2,1,0:T(8,128)}, f32[8,32,512]{2,1,0:T(8,128)S(1)}, u32[]{:S(2)}) copy-start(f32[8,32,512]{2,1,0:T(8,128)S(1)} %get-tuple-element.64.p2.p2_any) | copy-start | bytes 1572868
  1.9 12.2 %collective-permute-start.1 = (f32[8,32,512]{2,1,0:T(8,128)S(1)}, f32[8,32,512]{2,1,0:T(8,128)S(1)}, u32[]{:S(2)}, u32[]{:S(2)}) collective-permute-start(f32[8,32,512]{2,1,0:T(8,128)S(1)} %get-tuple-element.63.p0.p0_any), channel_id=1, source_target_pairs={{1,0},{2,1},{3,2},{4,3},{5,4},{6,5},{7,6},{8,7},{9,8},{10,9},{11,1... | collective-permute-start | bytes 1572872 | tf_op jit(solution)/shard_map/ppermute | solution.py:477
  7.4 11.4 %collective-permute-start = (f32[8,32,512]{2,1,0:T(8,128)S(1)}, f32[8,32,512]{2,1,0:T(8,128)S(1)}, u32[]{:S(2)}, u32[]{:S(2)}) collective-permute-start(f32[8,32,512]{2,1,0:T(8,128)S(1)} %get-tuple-element.64.p2.p2_any), channel_id=1, source_target_pairs={{0,1},{1,2},{2,3},{3,4},{4,5},{5,6},{6,7},{7,8},{8,9},{9,10},{10,1... | collective-permute-start | bytes 1572872 | tf_op jit(solution)/shard_map/ppermute | solution.py:476
  9.4 16.5 %copy-start.1 = (f32[3,8,32,512]{3,2,1,0:T(8,128)}, f32[3,8,32,512]{3,2,1,0:T(8,128)S(1)}, u32[]{:S(2)}) copy-start(f32[3,8,32,512]{3,2,1,0:T(8,128)S(1)} %get-tuple-element.71.rates.rates_any) | copy-start | bytes 4718596
  9.4 16.5 %copy-start.8 = (f32[8,32,512]{2,1,0:T(8,128)}, f32[8,32,512]{2,1,0:T(8,128)S(1)}, u32[]{:S(2)}) copy-start(f32[8,32,512]{2,1,0:T(8,128)S(1)} %get-tuple-element.70.middle.middle_any) | copy-start | bytes 1572868
  9.4 16.4 %collective-permute-start.2 = (f32[10,32,512]{2,1,0:T(8,128)S(1)}, f32[10,32,512]{2,1,0:T(8,128)S(1)}, u32[]{:S(2)}, u32[]{:S(2)}) collective-permute-start(f32[10,32,512]{2,1,0:T(8,128)S(1)} %get-tuple-element.40), channel_id=1, source_target_pairs={{0,1},{1,2},{2,3},{3,4},{4,5},{5,6},{6,7},{7,8},{8,9},{9,10},{10,1... | collective-permute-start | bytes 1966088 | tf_op jit(solution)/shard_map/ppermute | solution.py:489
  9.5 16.4 %collective-permute-start.3 = (f32[10,32,512]{2,1,0:T(8,128)S(1)}, f32[10,32,512]{2,1,0:T(8,128)S(1)}, u32[]{:S(2)}, u32[]{:S(2)}) collective-permute-start(f32[10,32,512]{2,1,0:T(8,128)S(1)} %get-tuple-element.41), channel_id=1, source_target_pairs={{1,0},{2,1},{3,2},{4,3},{5,4},{6,5},{7,6},{8,7},{9,8},{10,9},{11,1... | collective-permute-start | bytes 1966088 | tf_op jit(solution)/shard_map/ppermute | solution.py:490
  14.1 11.8 %copy-start.6 = (f32[8,32,512]{2,1,0:T(8,128)}, f32[8,32,512]{2,1,0:T(8,128)S(1)}, u32[]{:S(2)}) copy-start(f32[8,32,512]{2,1,0:T(8,128)S(1)} %collective-permute-done.1.next1.next1_any) | copy-start | bytes 1572868
  18.8 7.1 %copy-start.7 = (f32[8,32,512]{2,1,0:T(8,128)}, f32[8,32,512]{2,1,0:T(8,128)S(1)}, u32[]{:S(2)}) copy-start(f32[8,32,512]{2,1,0:T(8,128)S(1)} %collective-permute-done.prev1.prev1_any) | copy-start | bytes 1572868
  20.5 8.7 %copy-start = (f32[40,32,512]{2,1,0:T(8,128)}, f32[40,32,512]{2,1,0:T(8,128)S(1)}, u32[]{:S(2)}) copy-start(f32[40,32,512]{2,1,0:T(8,128)S(1)} %shard_map.106.near_out.near_any) | copy-start | bytes 7864324
  20.5 39.2 %copy-start.11 = (bf16[2,256,128]{2,1,0:T(8,128)(2,1)S(1)}, bf16[2,256,128]{2,1,0:T(8,128)(2,1)}, u32[]{:S(2)}) copy-start(bf16[2,256,128]{2,1,0:T(8,128)(2,1)} %constant.13.clone.refs_2_) | copy-start | bytes 393220
  20.5 39.1 %copy-start.12 = (bf16[2,256,128]{2,1,0:T(8,128)(2,1)S(1)}, bf16[2,256,128]{2,1,0:T(8,128)(2,1)}, u32[]{:S(2)}) copy-start(bf16[2,256,128]{2,1,0:T(8,128)(2,1)} %constant.12.clone.refs_1_) | copy-start | bytes 393220
  20.6 39.1 %copy-start.13 = (bf16[96,144]{1,0:T(8,128)(2,1)S(1)}, bf16[96,144]{1,0:T(8,128)(2,1)}, u32[]{:S(2)}) copy-start(bf16[96,144]{1,0:T(8,128)(2,1)} %constant.14.clone.refs_3_) | copy-start | bytes 82948
  20.6 8.7 %collective-permute-start.4 = (f32[3,32,512]{2,1,0:T(8,128)S(1)}, f32[3,32,512]{2,1,0:T(8,128)S(1)}, u32[]{:S(2)}, u32[]{:S(2)}) collective-permute-start(f32[3,32,512]{2,1,0:T(8,128)S(1)} %get-tuple-element.47), channel_id=1, source_target_pairs={{0,1},{1,2},{2,3},{3,4},{4,5},{5,6},{6,7},{7,8},{8,9},{9,10},{10,1... | collective-permute-start | bytes 589832 | tf_op jit(solution)/shard_map/ppermute | solution.py:500
  25.7 3.6 %collective-permute-start.5 = (f32[3,32,512]{2,1,0:T(8,128)S(1)}, f32[3,32,512]{2,1,0:T(8,128)S(1)}, u32[]{:S(2)}, u32[]{:S(2)}) collective-permute-start(f32[3,32,512]{2,1,0:T(8,128)S(1)} %get-tuple-element.48), channel_id=1, source_target_pairs={{1,0},{2,1},{3,2},{4,3},{5,4},{6,5},{7,6},{8,7},{9,8},{10,9},{11,1... | collective-permute-start | bytes 589832 | tf_op jit(solution)/shard_map/ppermute | solution.py:501
  25.9 3.4 %copy-start.9 = (f32[10,32,512]{2,1,0:T(8,128)}, f32[10,32,512]{2,1,0:T(8,128)S(1)}, u32[]{:S(2)}) copy-start(f32[10,32,512]{2,1,0:T(8,128)S(1)} %collective-permute-done.2.prev2.prev2_any) | copy-start | bytes 1966084
  25.9 3.3 %copy-start.10 = (f32[10,32,512]{2,1,0:T(8,128)}, f32[10,32,512]{2,1,0:T(8,128)S(1)}, u32[]{:S(2)}) copy-start(f32[10,32,512]{2,1,0:T(8,128)S(1)} %collective-permute-done.3.next2.next2_any) | copy-start | bytes 1966084
  29.3 26.1 %copy-start.14 = (f32[3,32,512]{2,1,0:T(8,128)}, f32[3,32,512]{2,1,0:T(8,128)S(1)}, u32[]{:S(2)}) copy-start(f32[3,32,512]{2,1,0:T(8,128)S(1)} %collective-permute-done.4.prev3) | copy-start | bytes 589828
  29.3 32.6 %copy-start.16 = (f32[3,32,512]{2,1,0:T(8,128)}, f32[3,32,512]{2,1,0:T(8,128)S(1)}, u32[]{:S(2)}) copy-start(f32[3,32,512]{2,1,0:T(8,128)S(1)} %collective-permute-done.5.next3) | copy-start | bytes 589828
  55.2 10.4 %collective-permute-start.6 = (f32[3,32,512]{2,1,0:T(8,128)S(1)}, f32[3,32,512]{2,1,0:T(8,128)S(1)}, u32[]{:S(2)}, u32[]{:S(2)}) collective-permute-start(f32[3,32,512]{2,1,0:T(8,128)S(1)} %get-tuple-element.54), channel_id=1, source_target_pairs={{0,1},{1,2},{2,3},{3,4},{4,5},{5,6},{6,7},{7,8},{8,9},{9,10},{10,1... | collective-permute-start | bytes 589832 | tf_op jit(solution)/shard_map/ppermute | solution.py:526
  55.4 10.3 %collective-permute-start.7 = (f32[3,32,512]{2,1,0:T(8,128)S(1)}, f32[3,32,512]{2,1,0:T(8,128)S(1)}, u32[]{:S(2)}, u32[]{:S(2)}) collective-permute-start(f32[3,32,512]{2,1,0:T(8,128)S(1)} %get-tuple-element.55), channel_id=1, source_target_pairs={{1,0},{2,1},{3,2},{4,3},{5,4},{6,5},{7,6},{8,7},{9,8},{10,9},{11,1... | collective-permute-start | bytes 589832 | tf_op jit(solution)/shard_map/ppermute | solution.py:527
  59.7 6.0 %copy-start.15 = (f32[3,32,512]{2,1,0:T(8,128)S(1)}, f32[3,32,512]{2,1,0:T(8,128)}, u32[]{:S(2)}) copy-start(f32[3,32,512]{2,1,0:T(8,128)} %copy-done.14) | copy-start | bytes 589828
  61.9 15.7 %all-to-all-start.1 = ((f32[16,48,128]{2,1,0:T(8,128)}), f32[16,48,128]{2,1,0:T(8,128)S(1)}, u32[]{:S(2)}, u32[]{:S(2)}) async-start(f32[16,48,128]{2,1,0:T(8,128)} %bitcast.1), calls=%async_computation.1 | async-start | bytes 786432 | tf_op jit(solution)/shard_map/all_to_all | solution.py:543
  65.6 12.0 %copy-start.4 = (bf16[512,512]{1,0:T(8,128)(2,1)S(1)}, bf16[512,512]{1,0:T(8,128)(2,1)}, u32[]{:S(2)}) copy-start(bf16[512,512]{1,0:T(8,128)(2,1)} %constant.11.clone.low_any.low) | copy-start | bytes 1572868
  65.6 12.0 %copy-start.5 = (bf16[512,512]{1,0:T(8,128)(2,1)S(1)}, bf16[512,512]{1,0:T(8,128)(2,1)}, u32[]{:S(2)}) copy-start(bf16[512,512]{1,0:T(8,128)(2,1)} %constant.10.clone.high_any.high) | copy-start | bytes 1572868
  65.7 1.0 %copy-start.17 = (f32[3,32,512]{2,1,0:T(8,128)S(1)}, f32[3,32,512]{2,1,0:T(8,128)}, u32[]{:S(2)}) copy-start(f32[3,32,512]{2,1,0:T(8,128)} %copy-done.16) | copy-start | bytes 589828

commit v12 on v11

--- a/solution.py
+++ b/solution.py
@@ -260,9 +260,9 @@
 
 
 def rest_kernel(
-    prev3, next3, prev4, next4,
+    prev3, next3,
     chosen_any, classes_any, p0_any, p2_any, prev1_any, next1_any, prev2_any, next2_any, near_any, middle_any,
-    rates_any, out_any,
+    rates_any, out_any, linear,
     chosen, classes, p0, p2, prev1, next1, prev2, next2, near_out, middle, rates, second, edge, out, semaphores,
 ):
     near_state, near_source = groups(near_out, 5), groups(near_any, 5)
@@ -299,28 +299,51 @@
     eta2 = (side2[0], middle2, side2[1])
     outs = []
 
-    def finish(plane):
+    def finish(plane, entries):
         total = squares(eta2[plane])
-        for k, (i, _, _) in enumerate(places):
+        for k, i in entries:
             before = edge[0, k] if plane == 0 else eta2[plane - 1][i]
             after = edge[1, k] if plane == 2 else eta2[plane + 1][i]
             out[i, plane] = update(eta2[plane][i], before, after, total, rates[plane, i])
         outs.extend(fetch(((out.at[:, plane], out_any.at[:, plane]),), semaphores.at[pl.ds(17 + plane, 1)]))
 
-    finish(1)
-    for side, (soon, far, mid, near) in enumerate(((prev3, prev4, prev2, prev1), (next3, next4, next2, next1))):
+    everyone = list(enumerate(place[0] for place in places))
+    finish(1, everyone)
+    none = jnp.zeros(p0.shape[1:], F32)
+    for side, (soon, mid, near) in enumerate(((prev3, prev2, prev1), (next3, next2, next1))):
         ids = grain_of(mid)
         total0 = squares(mid)
         total1 = squares(outer1[side])
+        total2 = squares(eta2[2 * side])
         for k, (i, early, late) in enumerate(places):
-            if early is not None:
-                third = mid[early]
-            else:
-                third = soon[late] if late < SOON else far[late - SOON]
-            first = update(mid[i], third, near[i], total0, rate(classes, ids, i))
-            edge[side, k] = update(outer1[side][i], first, inner1[side][i], total1, edge_rates[side][i])
-        finish(2 * side)
+            known = early is not None or late < SOON
+            third = none if not known else soon[late] if early is None else mid[early]
+            slope = rate(classes, ids, i)
+            first = update(mid[i], third, near[i], total0, slope)
+            second_value = update(outer1[side][i], first, inner1[side][i], total1, edge_rates[side][i])
+            edge[side, k] = second_value
+            if not known:
+                linear[side, 0, late - SOON] = update(
+                    eta2[2 * side][i], second_value, eta2[1][i], total2, rates[2 * side, i]
+                )
+                linear[side, 1, late - SOON] = slope * edge_rates[side][i] * rates[2 * side, i]
+        finish(2 * side, everyone[: 2 + SOON])
     for copy in outs:
+        copy.wait()
+
+
+def last_kernel(prev4, next4, linear, chosen_any, partial_any, out_any, chosen, values, semaphores):
+    copies = fetch(((chosen_any, chosen),), semaphores.at[pl.ds(0, 1)])
+    count = prev4.shape[0]
+    for side, far in enumerate((prev4, next4)):
+        for r in range(count):
+            values[side, r] = linear[side, 0, r] + linear[side, 1, r] * far[r]
+    copies[0].wait()
+    other = others_of(chosen)
+    pieces = [
+        (values.at[side, r], out_any.at[other(SOON + r), 2 * side]) for side in range(2) for r in range(count)
+    ]
+    for copy in fetch(pieces, semaphores.at[pl.ds(1, 2 * count)]):
         copy.wait()
 
 
@@ -522,9 +545,7 @@
     else:
         lines = lax.all_to_all(packed, "gx", split_axis=1, concat_axis=0, tiled=True)
     lines = lines.reshape(total_x * share, lanes)
-    lines, l0, l2 = lax.optimization_barrier((lines, l0, l2))
-    prev4 = lax.ppermute(l0, "gx", up)
-    next4 = lax.ppermute(l2, "gx", down)
+
     def lines_body(*refs):
         line_kernel(*refs, scale=1.0 / (count * count))
 
@@ -544,26 +565,40 @@
     if not aligned:
         returned = returned.reshape(devices, planes, share, lanes).transpose(1, 0, 2, 3)
         returned = returned.reshape(planes, slots, lanes)
-    late = (
-        prev3, next3, prev4, next4,
-        chosen, class_table, p0, p2, prev1, next1, prev2, next2, near_out, middle, rates,
-    )
+    l0, l2, back = lax.optimization_barrier((l0, l2, back))
+    prev4 = lax.ppermute(l0, "gx", up)
+    next4 = lax.ppermute(l2, "gx", down)
+    late = (prev3, next3, chosen, class_table, p0, p2, prev1, next1, prev2, next2, near_out, middle, rates)
     late, _ = lax.optimization_barrier((late, back))
-    order_params = call(
+    partial, linear = call(
         rest_kernel,
-        shape(GRAINS, planes, depth, width),
-        [VMEM] * 4 + [ANY] * (len(late) - 4),
+        (shape(GRAINS, planes, depth, width), shape(2, 2, *last)),
+        [VMEM] * 2 + [ANY] * (len(late) - 2),
         *late,
         scratch=[
             *small,
-            *[pltpu.VMEM(value.shape, F32) for value in late[6:]],
+            *[pltpu.VMEM(value.shape, F32) for value in late[4:]],
             pltpu.VMEM((4 * GRAINS, depth, width), F32),
             pltpu.VMEM((2, *plane), F32),
             pltpu.VMEM((GRAINS, planes, depth, width), F32),
             pltpu.SemaphoreType.DMA((17 + planes,)),
         ],
-        out_specs=ANY, flops=2**37, moved=2**24, limit=24,
-    )
+        out_specs=(ANY, VMEM), flops=2**26, moved=2**24, limit=24,
+    )
+    order_params = pl.pallas_call(
+        last_kernel,
+        out_shape=shape(GRAINS, planes, depth, width),
+        in_specs=[VMEM] * 3 + [ANY] * 2,
+        out_specs=ANY,
+        scratch_shapes=[
+            small[0],
+            pltpu.VMEM((2, *last), F32),
+            pltpu.SemaphoreType.DMA((1 + 2 * last[0],)),
+        ],
+        input_output_aliases={4: 0},
+        compiler_params=pltpu.CompilerParams(vmem_limit_bytes=12 * MIB),
+        cost_estimate=pl.CostEstimate(flops=2**20, bytes_accessed=2**21, transcendentals=0),
+    )(prev4, next4, linear, pltpu.with_memory_space_constraint(chosen, pltpu.HBM), partial)
     correlation = call(
         finish_kernel,
         shape(2, planes, depth, width),

time: 79.4 us -> 78.9 us (level)
  Pallas kernels: 19.2 us -> 20.9 us
  waiting for transfers between devices: 8.37 us -> 6.94 us
  local copies, waits for them, and re-layouts: 1.08 us -> 0.09 us
    all_to_all x1, waiting for transfers between devices: 3.32 us -> 0.01 us  [shards(): lax.all_to_all(back, 'gx', split_axis=0, concat_axis=0, tiled=True)]
    ppermute x1, waiting for transfers between devices: 0.01 us -> 1.93 us  [shards(): prev4 = lax.ppermute(l0, 'gx', up)]
    pallas_call x0 -> x1, Pallas kernels: none -> 1.6 us  [shards(): pl.pallas_call(last_kernel, out_shape=shape(GRAINS, planes, depth, width)...]
    unnamed x36, local copies, waits for them, and re-layouts: 1.08 us -> 0.09 us
where the time goes in v12:
time: 78.9 us; the launch traced here: 78.5 us
  blocking collectives  26.1 us (33%)
  starting transfers between devices  23.4 us (30%)
  Pallas kernels  20.9 us (26%)
  waiting for transfers between devices  6.94 us (9%)
  between operations  1.1 us (1%)
    all_to_all x1, blocking collectives, shards(): lax.all_to_all(packed, 'gx', split_axis=0, concat_axis=0, tiled=True)  26.1 us
    pallas_call x7, Pallas kernels, call(): pl.pallas_call(kernel, out_shape=outs, in_specs=in_specs, out_specs=out_s...  19.3 us
    ppermute x1, starting transfers between devices, shards(): next1 = lax.ppermute(p0, 'gx', down)  5.5 us
    ppermute x1, starting transfers between devices, shards(): prev3 = lax.ppermute(r0, 'gx', up)  5.12 us
    ppermute x1, waiting for transfers between devices, shards(): prev1 = lax.ppermute(p2, 'gx', up)  4.7 us
    ppermute x1, starting transfers between devices, shards(): next2 = lax.ppermute(down2, 'gx', down)  4.49 us
    ppermute x1, starting transfers between devices, shards(): next4 = lax.ppermute(l2, 'gx', down)  4.23 us
    all_to_all x1, starting transfers between devices, shards(): lax.all_to_all(back, 'gx', split_axis=0, concat_axis=0, tiled=True)  3.55 us
  transfers between devices with their start and end apart: 9, of which 4 were waited for; matrix products, arithmetic and copies ran while one was open for 0% of the time, Pallas kernels for 21%

profile of v12, /device:TPU:0, one launch (start us, length us, event | category | flops | bytes accessed | tf_op | source)
XLA Modules:
  0.0 78.5 jit_solution(4207222625197937774)
XLA Ops:
  0.6 1.3 %shard_map.104 = (f32[8,32,512]{2,1,0:T(8,128)S(1)}, f32[8,32,512]{2,1,0:T(8,128)S(1)}, f32[8,32,512]{2,1,0:T(8,128)S(1)}) custom-call(bf16[8,3,32,512]{3,2,1,0:T(8,128)(2,1)} %jitter_any.1, s32[3,32,512]{2,1,0:T(8,128)} %ids_any.1), custom_call_target="tpu_custom_call" | custom-call | flops 2097152 | bytes 4194304 | tf_op jit(solution)/shard_map/pallas_call | solution.py:450
  1.9 0.0 copy-start.2
  1.9 0.0 copy-start.3
  1.9 5.5 %collective-permute-start.1 = (f32[8,32,512]{2,1,0:T(8,128)S(1)}, f32[8,32,512]{2,1,0:T(8,128)S(1)}, u32[]{:S(2)}, u32[]{:S(2)}) collective-permute-start(f32[8,32,512]{2,1,0:T(8,128)S(1)} %get-tuple-element.59.p0.p0_any), channel_id=1, source_target_pairs={{1,0},{2,1},{3,2},{4,3},{5,4},{6,5},{7,6},{8,7},{9,8},{10,9},{11,1... | collective-permute-start | bytes 1572872 | tf_op jit(solution)/shard_map/ppermute | solution.py:500
  7.4 0.0 collective-permute-start
  7.4 2.0 %shard_map.105 = (f32[10,32,512]{2,1,0:T(8,128)S(1)}, f32[10,32,512]{2,1,0:T(8,128)S(1)}, f32[3,32,512]{2,1,0:T(8,128)S(1)}, f32[3,32,512]{2,1,0:T(8,128)S(1)}, ...) custom-call(s32[2]{0:T(128)} %chosen_any.6, ...), custom_call_target="tpu_custom_call" | custom-call | flops 16777216 | bytes 4194304 | tf_op jit(solution)/shard_map/pallas_call | solution.py:450
  9.4 0.0 copy-start.14
  9.4 0.0 copy-start.16
  9.4 0.0 copy-start.1
  9.4 0.0 copy-start.6
  9.4 0.1 collective-permute-start.2
  9.5 4.5 %collective-permute-start.3 = (f32[10,32,512]{2,1,0:T(8,128)S(1)}, f32[10,32,512]{2,1,0:T(8,128)S(1)}, u32[]{:S(2)}, u32[]{:S(2)}) collective-permute-start(f32[10,32,512]{2,1,0:T(8,128)S(1)} %get-tuple-element.42), channel_id=1, source_target_pairs={{1,0},{2,1},{3,2},{4,3},{5,4},{6,5},{7,6},{8,7},{9,8},{10,9},{11,1... | collective-permute-start | bytes 1966088 | tf_op jit(solution)/shard_map/ppermute | solution.py:513
  14.0 0.1 collective-permute-done.1.next1.next1_any
  14.1 0.0 copy-start.4
  14.1 4.7 %collective-permute-done.prev1.prev1_any = f32[8,32,512]{2,1,0:T(8,128)S(1)} collective-permute-done((f32[8,32,512]{2,1,0:T(8,128)S(1)}, f32[8,32,512]{2,1,0:T(8,128)S(1)}, u32[]{:S(2)}, u32[]{:S(2)}) %collective-permute-start) | collective-permute-done | bytes 524320 | tf_op jit(solution)/shard_map/ppermute | solution.py:499
  18.8 0.0 copy-start.5
  18.8 1.7 %shard_map.106.near_out.near_any = f32[40,32,512]{2,1,0:T(8,128)S(1)} custom-call(s32[8,8]{1,0:T(8,128)} %classes_any.6, f32[8,32,512]{2,1,0:T(8,128)S(1)} %get-tuple-element.59.p0.p0_any, f32[8,32,512]{2,1,0:T(8,128)S(1)} %get-tuple-element.37.p1, f32[8,32,512]{2,1,0:T(8,128)S(1)} %get-tuple-element.60.p2.p2_any, ...), custom_call_target="tpu_custom_call" | custom-call | flops 33554432 | bytes 16777216 | tf_op jit(solution)/shard_map/pallas_call | solution.py:450
  20.5 0.0 copy-done.14
  20.5 0.0 copy-done.16
  20.5 0.0 copy-start
  20.6 0.0 copy-start.11
  20.6 0.0 copy-start.12
  20.6 0.0 copy-start.13
  20.6 5.1 %collective-permute-start.4 = (f32[3,32,512]{2,1,0:T(8,128)S(1)}, f32[3,32,512]{2,1,0:T(8,128)S(1)}, u32[]{:S(2)}, u32[]{:S(2)}) collective-permute-start(f32[3,32,512]{2,1,0:T(8,128)S(1)} %get-tuple-element.48), channel_id=1, source_target_pairs={{0,1},{1,2},{2,3},{3,4},{4,5},{5,6},{6,7},{7,8},{8,9},{9,10},{10,1... | collective-permute-start | bytes 589832 | tf_op jit(solution)/shard_map/ppermute | solution.py:523
  25.7 0.0 collective-permute-start.5
  25.7 0.2 collective-permute-done.2.prev2.prev2_any
  25.9 0.0 copy-start.7
  25.9 0.0 collective-permute-done.3.next2.next2_any
  25.9 0.0 copy-done.2
  25.9 0.0 copy-done.3
  25.9 0.0 copy-done.1
  25.9 0.0 copy-done.6
  25.9 0.0 copy-done.4
  25.9 0.0 copy-done.5
  25.9 0.0 copy-start.8
  25.9 3.3 %shard_map.107 = f32[16,48,128]{2,1,0:T(8,128)S(1)} custom-call(s32[2]{0:T(128)} %chosen_any.6, s32[8,8]{1,0:T(8,128)} %classes_any.6, f32[8,32,512]{2,1,0:T(8,128)S(1)} %get-tuple-element.59.p0.p0_any, f32[8,32,512]{2,1,0:T(8,128)S(1)} %get-tuple-element.60.p2.p2_any, f32[8,32,512]{2,1,0:T(8,128)S(1)} %collective-permute-done.prev1.prev1_any, ...), custom_call_target="tpu_custom_call" | custom-call | flops 268435456 | bytes 8388608 | tf_op jit(solution)/shard_map/pallas_call | solution.py:450
  29.2 0.0 copy-done
  29.2 0.0 copy-done.7
  29.2 0.0 copy-done.8
  29.2 0.0 copy-start.17
  29.3 0.0 copy-start.15
  29.3 0.0 collective-permute-done.4.prev3
  29.3 0.0 collective-permute-done.5.next3
  29.3 26.1 %all_to_all.10 = f32[16,48,128]{2,1,0:T(8,128)S(1)} all-to-all(f32[16,48,128]{2,1,0:T(8,128)S(1)} %shard_map.107), channel_id=1, replica_groups=mesh['grp'=2,'gx'=16] {'gx'}, dimensions={0} | all-to-all | bytes 786432 | tf_op jit(solution)/shard_map/all_to_all | solution.py:544
  55.4 0.0 copy-done.11
  55.4 0.0 copy-done.12
  55.4 0.0 copy-done.13
  55.4 2.2 %shard_map.108 = f32[768,128]{1,0:T(8,128)} custom-call(f32[768,128]{1,0:T(8,128)S(1)} %bitcast.2, bf16[2,256,128]{2,1,0:T(8,128)(2,1)S(1)} %copy-done.12, bf16[2,256,128]{2,1,0:T(8,128)(2,1)S(1)} %copy-done.11, bf16[96,144]{1,0:T(8,128)(2,1)S(1)} %copy-done.13), custom_call_target="tpu_custom_call" | custom-call | flops 268435456 | bytes 4194304 | tf_op jit(solution)/shard_map/pallas_call | solution.py:450
  57.5 3.6 %all-to-all-start.1 = ((f32[16,48,128]{2,1,0:T(8,128)}), f32[16,48,128]{2,1,0:T(8,128)S(1)}, u32[]{:S(2)}, u32[]{:S(2)}) async-start(f32[16,48,128]{2,1,0:T(8,128)} %bitcast.1), calls=%async_computation.1 | async-start | bytes 786432 | tf_op jit(solution)/shard_map/all_to_all | solution.py:564
  61.1 0.0 copy-done.17
  61.1 0.4 collective-permute-start.6
  61.5 0.0 copy-done.15
  61.5 4.2 %collective-permute-start.7 = (f32[3,32,512]{2,1,0:T(8,128)S(1)}, f32[3,32,512]{2,1,0:T(8,128)S(1)}, u32[]{:S(2)}, u32[]{:S(2)}) collective-permute-start(f32[3,32,512]{2,1,0:T(8,128)S(1)} %copy-done.15), channel_id=1, source_target_pairs={{1,0},{2,1},{3,2},{4,3},{5,4},{6,5},{7,6},{8,7},{9,8},{10,9},{11,1... | collective-permute-start | bytes 589832 | tf_op jit(solution)/shard_map/ppermute | solution.py:570
  65.8 7.7 %shard_map.109 = (f32[8,3,32,512]{3,2,1,0:T(8,128)}, f32[2,2,3,32,512]{4,3,2,1,0:T(8,128)S(1)}) custom-call(f32[3,32,512]{2,1,0:T(8,128)S(1)} %collective-permute-done.4.prev3, f32[3,32,512]{2,1,0:T(8,128)S(1)} %collective-permute-done.5.next3, s32[2]{0:T(128)} %chosen_any.6, s32[8,8]{1,0:T(8,128)} %classes_any.6, f32[8,32,512]{2,1,0:T(8,128)} %copy-done.2, ...), custom_call_target="tpu_custom_call" | custom-call | flops 67108864 | bytes 16777216 | tf_op jit(solution)/shard_map/pallas_call | solution.py:450
  73.4 1.9 %collective-permute-done.6.prev4 = f32[3,32,512]{2,1,0:T(8,128)S(1)} collective-permute-done((f32[3,32,512]{2,1,0:T(8,128)S(1)}, f32[3,32,512]{2,1,0:T(8,128)S(1)}, u32[]{:S(2)}, u32[]{:S(2)}) %collective-permute-start.6) | collective-permute-done | bytes 196640 | tf_op jit(solution)/shard_map/ppermute | solution.py:569
  75.4 0.0 collective-permute-done.7.next4
  75.4 0.0 copy-start.9
  75.4 0.0 copy-start.10
  75.4 1.6 %shard_map.110 = f32[8,3,32,512]{3,2,1,0:T(8,128)} custom-call(f32[3,32,512]{2,1,0:T(8,128)S(1)} %collective-permute-done.6.prev4, f32[3,32,512]{2,1,0:T(8,128)S(1)} %collective-permute-done.7.next4, f32[2,2,3,32,512]{4,3,2,1,0:T(8,128)S(1)} %get-tuple-element.68.linear, s32[2]{0:T(128)} %chosen_any.6, ...), custom_call_target="tpu_custom_call", output_to_operand_aliasing={{}: (4, {})} | custom-call | flops 1048576 | bytes 2097152 | tf_op jit(solution)/shard_map/pallas_call | solution.py:588
  77.0 0.0 all-to-all-done.1.returned
  77.0 0.0 copy-done.9
  77.0 0.0 copy-done.10
  77.0 1.3 %shard_map.111 = f32[2,3,32,512]{3,2,1,0:T(8,128)} custom-call(f32[16,48,128]{2,1,0:T(8,128)S(1)} %all-to-all-done.1.returned, bf16[512,512]{1,0:T(8,128)(2,1)S(1)} %copy-done.10, bf16[512,512]{1,0:T(8,128)(2,1)S(1)} %copy-done.9), custom_call_target="tpu_custom_call" | custom-call | flops 268435456 | bytes 4194304 | tf_op jit(solution)/shard_map/pallas_call | solution.py:450
Async XLA Ops:
  1.9 24.0 %copy-start.2 = (f32[8,32,512]{2,1,0:T(8,128)}, f32[8,32,512]{2,1,0:T(8,128)S(1)}, u32[]{:S(2)}) copy-start(f32[8,32,512]{2,1,0:T(8,128)S(1)} %get-tuple-element.59.p0.p0_any) | copy-start | bytes 1572868
  1.9 24.0 %copy-start.3 = (f32[8,32,512]{2,1,0:T(8,128)}, f32[8,32,512]{2,1,0:T(8,128)S(1)}, u32[]{:S(2)}) copy-start(f32[8,32,512]{2,1,0:T(8,128)S(1)} %get-tuple-element.60.p2.p2_any) | copy-start | bytes 1572868
  1.9 12.2 %collective-permute-start.1 = (f32[8,32,512]{2,1,0:T(8,128)S(1)}, f32[8,32,512]{2,1,0:T(8,128)S(1)}, u32[]{:S(2)}, u32[]{:S(2)}) collective-permute-start(f32[8,32,512]{2,1,0:T(8,128)S(1)} %get-tuple-element.59.p0.p0_any), channel_id=1, source_target_pairs={{1,0},{2,1},{3,2},{4,3},{5,4},{6,5},{7,6},{8,7},{9,8},{10,9},{11,1... | collective-permute-start | bytes 1572872 | tf_op jit(solution)/shard_map/ppermute | solution.py:500
  7.4 11.4 %collective-permute-start = (f32[8,32,512]{2,1,0:T(8,128)S(1)}, f32[8,32,512]{2,1,0:T(8,128)S(1)}, u32[]{:S(2)}, u32[]{:S(2)}) collective-permute-start(f32[8,32,512]{2,1,0:T(8,128)S(1)} %get-tuple-element.60.p2.p2_any), channel_id=1, source_target_pairs={{0,1},{1,2},{2,3},{3,4},{4,5},{5,6},{6,7},{7,8},{8,9},{9,10},{10,1... | collective-permute-start | bytes 1572872 | tf_op jit(solution)/shard_map/ppermute | solution.py:499
  9.4 11.1 %copy-start.14 = (f32[3,32,512]{2,1,0:T(8,128)}, f32[3,32,512]{2,1,0:T(8,128)S(1)}, u32[]{:S(2)}) copy-start(f32[3,32,512]{2,1,0:T(8,128)S(1)} %get-tuple-element.52) | copy-start | bytes 589828
  9.4 11.1 %copy-start.16 = (f32[3,32,512]{2,1,0:T(8,128)}, f32[3,32,512]{2,1,0:T(8,128)S(1)}, u32[]{:S(2)}) copy-start(f32[3,32,512]{2,1,0:T(8,128)S(1)} %get-tuple-element.51) | copy-start | bytes 589828
  9.4 16.5 %copy-start.1 = (f32[3,8,32,512]{3,2,1,0:T(8,128)}, f32[3,8,32,512]{3,2,1,0:T(8,128)S(1)}, u32[]{:S(2)}) copy-start(f32[3,8,32,512]{3,2,1,0:T(8,128)S(1)} %get-tuple-element.67.rates.rates_any) | copy-start | bytes 4718596
  9.4 16.5 %copy-start.6 = (f32[8,32,512]{2,1,0:T(8,128)}, f32[8,32,512]{2,1,0:T(8,128)S(1)}, u32[]{:S(2)}) copy-start(f32[8,32,512]{2,1,0:T(8,128)S(1)} %get-tuple-element.66.middle.middle_any) | copy-start | bytes 1572868
  9.4 16.4 %collective-permute-start.2 = (f32[10,32,512]{2,1,0:T(8,128)S(1)}, f32[10,32,512]{2,1,0:T(8,128)S(1)}, u32[]{:S(2)}, u32[]{:S(2)}) collective-permute-start(f32[10,32,512]{2,1,0:T(8,128)S(1)} %get-tuple-element.41), channel_id=1, source_target_pairs={{0,1},{1,2},{2,3},{3,4},{4,5},{5,6},{6,7},{7,8},{8,9},{9,10},{10,1... | collective-permute-start | bytes 1966088 | tf_op jit(solution)/shard_map/ppermute | solution.py:512
  9.5 16.4 %collective-permute-start.3 = (f32[10,32,512]{2,1,0:T(8,128)S(1)}, f32[10,32,512]{2,1,0:T(8,128)S(1)}, u32[]{:S(2)}, u32[]{:S(2)}) collective-permute-start(f32[10,32,512]{2,1,0:T(8,128)S(1)} %get-tuple-element.42), channel_id=1, source_target_pairs={{1,0},{2,1},{3,2},{4,3},{5,4},{6,5},{7,6},{8,7},{9,8},{10,9},{11,1... | collective-permute-start | bytes 1966088 | tf_op jit(solution)/shard_map/ppermute | solution.py:513
  14.1 11.8 %copy-start.4 = (f32[8,32,512]{2,1,0:T(8,128)}, f32[8,32,512]{2,1,0:T(8,128)S(1)}, u32[]{:S(2)}) copy-start(f32[8,32,512]{2,1,0:T(8,128)S(1)} %collective-permute-done.1.next1.next1_any) | copy-start | bytes 1572868
  18.8 7.1 %copy-start.5 = (f32[8,32,512]{2,1,0:T(8,128)}, f32[8,32,512]{2,1,0:T(8,128)S(1)}, u32[]{:S(2)}) copy-start(f32[8,32,512]{2,1,0:T(8,128)S(1)} %collective-permute-done.prev1.prev1_any) | copy-start | bytes 1572868
  20.5 8.7 %copy-start = (f32[40,32,512]{2,1,0:T(8,128)}, f32[40,32,512]{2,1,0:T(8,128)S(1)}, u32[]{:S(2)}) copy-start(f32[40,32,512]{2,1,0:T(8,128)S(1)} %shard_map.106.near_out.near_any) | copy-start | bytes 7864324
  20.6 34.8 %copy-start.11 = (bf16[2,256,128]{2,1,0:T(8,128)(2,1)S(1)}, bf16[2,256,128]{2,1,0:T(8,128)(2,1)}, u32[]{:S(2)}) copy-start(bf16[2,256,128]{2,1,0:T(8,128)(2,1)} %constant.13.clone.refs_2_) | copy-start | bytes 393220
  20.6 34.8 %copy-start.12 = (bf16[2,256,128]{2,1,0:T(8,128)(2,1)S(1)}, bf16[2,256,128]{2,1,0:T(8,128)(2,1)}, u32[]{:S(2)}) copy-start(bf16[2,256,128]{2,1,0:T(8,128)(2,1)} %constant.12.clone.refs_1_) | copy-start | bytes 393220
  20.6 34.8 %copy-start.13 = (bf16[96,144]{1,0:T(8,128)(2,1)S(1)}, bf16[96,144]{1,0:T(8,128)(2,1)}, u32[]{:S(2)}) copy-start(bf16[96,144]{1,0:T(8,128)(2,1)} %constant.14.clone.refs_3_) | copy-start | bytes 82948
  20.6 8.7 %collective-permute-start.4 = (f32[3,32,512]{2,1,0:T(8,128)S(1)}, f32[3,32,512]{2,1,0:T(8,128)S(1)}, u32[]{:S(2)}, u32[]{:S(2)}) collective-permute-start(f32[3,32,512]{2,1,0:T(8,128)S(1)} %get-tuple-element.48), channel_id=1, source_target_pairs={{0,1},{1,2},{2,3},{3,4},{4,5},{5,6},{6,7},{7,8},{8,9},{9,10},{10,1... | collective-permute-start | bytes 589832 | tf_op jit(solution)/shard_map/ppermute | solution.py:523
  25.7 3.6 %collective-permute-start.5 = (f32[3,32,512]{2,1,0:T(8,128)S(1)}, f32[3,32,512]{2,1,0:T(8,128)S(1)}, u32[]{:S(2)}, u32[]{:S(2)}) collective-permute-start(f32[3,32,512]{2,1,0:T(8,128)S(1)} %get-tuple-element.49), channel_id=1, source_target_pairs={{1,0},{2,1},{3,2},{4,3},{5,4},{6,5},{7,6},{8,7},{9,8},{10,9},{11,1... | collective-permute-start | bytes 589832 | tf_op jit(solution)/shard_map/ppermute | solution.py:524
  25.9 3.4 %copy-start.7 = (f32[10,32,512]{2,1,0:T(8,128)}, f32[10,32,512]{2,1,0:T(8,128)S(1)}, u32[]{:S(2)}) copy-start(f32[10,32,512]{2,1,0:T(8,128)S(1)} %collective-permute-done.2.prev2.prev2_any) | copy-start | bytes 1966084
  25.9 3.3 %copy-start.8 = (f32[10,32,512]{2,1,0:T(8,128)}, f32[10,32,512]{2,1,0:T(8,128)S(1)}, u32[]{:S(2)}) copy-start(f32[10,32,512]{2,1,0:T(8,128)S(1)} %collective-permute-done.3.next2.next2_any) | copy-start | bytes 1966084
  29.2 31.9 %copy-start.17 = (f32[3,32,512]{2,1,0:T(8,128)S(1)}, f32[3,32,512]{2,1,0:T(8,128)}, u32[]{:S(2)}) copy-start(f32[3,32,512]{2,1,0:T(8,128)} %copy-done.16) | copy-start | bytes 589828
  29.3 32.3 %copy-start.15 = (f32[3,32,512]{2,1,0:T(8,128)S(1)}, f32[3,32,512]{2,1,0:T(8,128)}, u32[]{:S(2)}) copy-start(f32[3,32,512]{2,1,0:T(8,128)} %copy-done.14) | copy-start | bytes 589828
  57.5 19.5 %all-to-all-start.1 = ((f32[16,48,128]{2,1,0:T(8,128)}), f32[16,48,128]{2,1,0:T(8,128)S(1)}, u32[]{:S(2)}, u32[]{:S(2)}) async-start(f32[16,48,128]{2,1,0:T(8,128)} %bitcast.1), calls=%async_computation.1 | async-start | bytes 786432 | tf_op jit(solution)/shard_map/all_to_all | solution.py:564
  61.1 14.3 %collective-permute-start.6 = (f32[3,32,512]{2,1,0:T(8,128)S(1)}, f32[3,32,512]{2,1,0:T(8,128)S(1)}, u32[]{:S(2)}, u32[]{:S(2)}) collective-permute-start(f32[3,32,512]{2,1,0:T(8,128)S(1)} %copy-done.17), channel_id=1, source_target_pairs={{0,1},{1,2},{2,3},{3,4},{4,5},{5,6},{6,7},{7,8},{8,9},{9,10},{10,1... | collective-permute-start | bytes 589832 | tf_op jit(solution)/shard_map/ppermute | solution.py:569
  61.5 13.8 %collective-permute-start.7 = (f32[3,32,512]{2,1,0:T(8,128)S(1)}, f32[3,32,512]{2,1,0:T(8,128)S(1)}, u32[]{:S(2)}, u32[]{:S(2)}) collective-permute-start(f32[3,32,512]{2,1,0:T(8,128)S(1)} %copy-done.15), channel_id=1, source_target_pairs={{1,0},{2,1},{3,2},{4,3},{5,4},{6,5},{7,6},{8,7},{9,8},{10,9},{11,1... | collective-permute-start | bytes 589832 | tf_op jit(solution)/shard_map/ppermute | solution.py:570
  75.4 1.6 %copy-start.9 = (bf16[512,512]{1,0:T(8,128)(2,1)S(1)}, bf16[512,512]{1,0:T(8,128)(2,1)}, u32[]{:S(2)}) copy-start(bf16[512,512]{1,0:T(8,128)(2,1)} %constant.11.clone.low_any.low) | copy-start | bytes 1572868
  75.4 1.6 %copy-start.10 = (bf16[512,512]{1,0:T(8,128)(2,1)S(1)}, bf16[512,512]{1,0:T(8,128)(2,1)}, u32[]{:S(2)}) copy-start(bf16[512,512]{1,0:T(8,128)(2,1)} %constant.10.clone.high_any.high) | copy-start | bytes 1572868

commit v13 on v12

--- a/solution.py
+++ b/solution.py
@@ -10,7 +10,7 @@
 from jax.sharding import PartitionSpec as P
 
 STEPS = 3
-SOON = 3
+SOON = 4
 GRAINS = 8
 F32 = jnp.float32
 BF16 = jnp.bfloat16

time: 78.9 us -> 78.8 us (level)
  waiting for transfers between devices: 6.94 us -> 5.67 us
  local copies, waits for them, and re-layouts: 0.09 us -> 1.03 us
    ppermute x1, waiting for transfers between devices: 1.93 us -> 0.32 us  [shards(): prev4 = lax.ppermute(l0, 'gx', up)]
    unnamed x36, local copies, waits for them, and re-layouts: 0.09 us -> 1.03 us
  transfers between devices with their start and end apart: 9 -> 9, of which waited for: 4 -> 5; matrix products, arithmetic and copies ran while one was open for 0% -> 0% of each run, Pallas kernels for 21% -> 20%
where the time goes in v13:
time: 78.8 us; the launch traced here: 78.4 us
  blocking collectives  26.5 us (34%)
  starting transfers between devices  23.4 us (30%)
  Pallas kernels  20.8 us (26%)
  waiting for transfers between devices  5.67 us (7%)
  between operations  1.07 us (1%)
  local copies, waits for them, and re-layouts  1.03 us (1%)
    all_to_all x1, blocking collectives, shards(): lax.all_to_all(packed, 'gx', split_axis=0, concat_axis=0, tiled=True)  26.5 us
    pallas_call x7, Pallas kernels, call(): pl.pallas_call(kernel, out_shape=outs, in_specs=in_specs, out_specs=out_s...  19.3 us
    ppermute x1, starting transfers between devices, shards(): next1 = lax.ppermute(p0, 'gx', down)  5.5 us
    ppermute x1, starting transfers between devices, shards(): prev3 = lax.ppermute(r0, 'gx', up)  5.12 us
    ppermute x1, waiting for transfers between devices, shards(): prev1 = lax.ppermute(p2, 'gx', up)  4.7 us
    ppermute x1, starting transfers between devices, shards(): next2 = lax.ppermute(down2, 'gx', down)  4.49 us
    ppermute x1, starting transfers between devices, shards(): next4 = lax.ppermute(l2, 'gx', down)  4.22 us
    all_to_all x1, starting transfers between devices, shards(): lax.all_to_all(back, 'gx', split_axis=0, concat_axis=0, tiled=True)  3.55 us
  transfers between devices with their start and end apart: 9, of which 5 were waited for; matrix products, arithmetic and copies ran while one was open for 0% of the time, Pallas kernels for 20%

profile of v13, /device:TPU:0, one launch (start us, length us, event | category | flops | bytes accessed | tf_op | source)
XLA Modules:
  0.0 78.4 jit_solution(17238620475434235873)
XLA Ops:
  0.6 1.3 %shard_map.104 = (f32[8,32,512]{2,1,0:T(8,128)S(1)}, f32[8,32,512]{2,1,0:T(8,128)S(1)}, f32[8,32,512]{2,1,0:T(8,128)S(1)}) custom-call(bf16[8,3,32,512]{3,2,1,0:T(8,128)(2,1)} %jitter_any.1, s32[3,32,512]{2,1,0:T(8,128)} %ids_any.1), custom_call_target="tpu_custom_call" | custom-call | flops 2097152 | bytes 4194304 | tf_op jit(solution)/shard_map/pallas_call | solution.py:450
  1.9 0.0 copy-start.2
  1.9 0.0 copy-start.3
  1.9 5.5 %collective-permute-start.1 = (f32[8,32,512]{2,1,0:T(8,128)S(1)}, f32[8,32,512]{2,1,0:T(8,128)S(1)}, u32[]{:S(2)}, u32[]{:S(2)}) collective-permute-start(f32[8,32,512]{2,1,0:T(8,128)S(1)} %get-tuple-element.59.p0.p0_any), channel_id=1, source_target_pairs={{1,0},{2,1},{3,2},{4,3},{5,4},{6,5},{7,6},{8,7},{9,8},{10,9},{11,1... | collective-permute-start | bytes 1572872 | tf_op jit(solution)/shard_map/ppermute | solution.py:500
  7.4 0.0 collective-permute-start
  7.4 2.0 %shard_map.105 = (f32[10,32,512]{2,1,0:T(8,128)S(1)}, f32[10,32,512]{2,1,0:T(8,128)S(1)}, f32[4,32,512]{2,1,0:T(8,128)S(1)}, f32[4,32,512]{2,1,0:T(8,128)S(1)}, ...) custom-call(s32[2]{0:T(128)} %chosen_any.6, ...), custom_call_target="tpu_custom_call" | custom-call | flops 16777216 | bytes 4194304 | tf_op jit(solution)/shard_map/pallas_call | solution.py:450
  9.4 0.0 copy-start.16
  9.4 0.0 copy-start.1
  9.4 0.0 copy-start.6
  9.4 0.1 collective-permute-start.2
  9.5 4.5 %collective-permute-start.3 = (f32[10,32,512]{2,1,0:T(8,128)S(1)}, f32[10,32,512]{2,1,0:T(8,128)S(1)}, u32[]{:S(2)}, u32[]{:S(2)}) collective-permute-start(f32[10,32,512]{2,1,0:T(8,128)S(1)} %get-tuple-element.42), channel_id=1, source_target_pairs={{1,0},{2,1},{3,2},{4,3},{5,4},{6,5},{7,6},{8,7},{9,8},{10,9},{11,1... | collective-permute-start | bytes 1966088 | tf_op jit(solution)/shard_map/ppermute | solution.py:513
  14.0 0.1 collective-permute-done.1.next1.next1_any
  14.1 0.0 copy-start.4
  14.1 4.7 %collective-permute-done.prev1.prev1_any = f32[8,32,512]{2,1,0:T(8,128)S(1)} collective-permute-done((f32[8,32,512]{2,1,0:T(8,128)S(1)}, f32[8,32,512]{2,1,0:T(8,128)S(1)}, u32[]{:S(2)}, u32[]{:S(2)}) %collective-permute-start) | collective-permute-done | bytes 524320 | tf_op jit(solution)/shard_map/ppermute | solution.py:499
  18.8 0.0 copy-start.5
  18.8 1.7 %shard_map.106.near_out.near_any = f32[40,32,512]{2,1,0:T(8,128)S(1)} custom-call(s32[8,8]{1,0:T(8,128)} %classes_any.6, f32[8,32,512]{2,1,0:T(8,128)S(1)} %get-tuple-element.59.p0.p0_any, f32[8,32,512]{2,1,0:T(8,128)S(1)} %get-tuple-element.37.p1, f32[8,32,512]{2,1,0:T(8,128)S(1)} %get-tuple-element.60.p2.p2_any, ...), custom_call_target="tpu_custom_call" | custom-call | flops 33554432 | bytes 16777216 | tf_op jit(solution)/shard_map/pallas_call | solution.py:450
  20.5 0.0 copy-done.16
  20.5 0.0 copy-start
  20.5 0.0 copy-start.13
  20.6 0.0 copy-start.14
  20.6 0.0 copy-start.15
  20.6 5.1 %collective-permute-start.4 = (f32[4,32,512]{2,1,0:T(8,128)S(1)}, f32[4,32,512]{2,1,0:T(8,128)S(1)}, u32[]{:S(2)}, u32[]{:S(2)}) collective-permute-start(f32[4,32,512]{2,1,0:T(8,128)S(1)} %get-tuple-element.48), channel_id=1, source_target_pairs={{0,1},{1,2},{2,3},{3,4},{4,5},{5,6},{6,7},{7,8},{8,9},{9,10},{10,1... | collective-permute-start | bytes 786440 | tf_op jit(solution)/shard_map/ppermute | solution.py:523
  25.7 0.0 collective-permute-start.5
  25.7 0.2 collective-permute-done.2.prev2.prev2_any
  25.9 0.0 copy-start.7
  25.9 0.0 collective-permute-done.3.next2.next2_any
  25.9 0.0 copy-done.2
  25.9 0.0 copy-done.3
  25.9 0.0 copy-done.1
  25.9 0.0 copy-done.6
  25.9 0.0 copy-done.4
  25.9 0.0 copy-done.5
  25.9 0.0 copy-start.8
  25.9 3.3 %shard_map.107 = f32[16,48,128]{2,1,0:T(8,128)S(1)} custom-call(s32[2]{0:T(128)} %chosen_any.6, s32[8,8]{1,0:T(8,128)} %classes_any.6, f32[8,32,512]{2,1,0:T(8,128)S(1)} %get-tuple-element.59.p0.p0_any, f32[8,32,512]{2,1,0:T(8,128)S(1)} %get-tuple-element.60.p2.p2_any, f32[8,32,512]{2,1,0:T(8,128)S(1)} %collective-permute-done.prev1.prev1_any, ...), custom_call_target="tpu_custom_call" | custom-call | flops 268435456 | bytes 8388608 | tf_op jit(solution)/shard_map/pallas_call | solution.py:450
  29.2 0.0 copy-done
  29.2 0.0 copy-done.7
  29.2 0.0 copy-done.8
  29.2 0.0 copy-start.17
  29.3 0.0 collective-permute-done.4.prev3
  29.3 0.3 collective-permute-done.5.next3
  29.6 0.0 copy-start.11
  29.6 26.5 %all_to_all.10 = f32[16,48,128]{2,1,0:T(8,128)S(1)} all-to-all(f32[16,48,128]{2,1,0:T(8,128)S(1)} %shard_map.107), channel_id=1, replica_groups=mesh['grp'=2,'gx'=16] {'gx'}, dimensions={0} | all-to-all | bytes 786432 | tf_op jit(solution)/shard_map/all_to_all | solution.py:544
  56.1 0.0 copy-done.13
  56.1 0.0 copy-done.14
  56.1 0.0 copy-done.15
  56.1 2.2 %shard_map.108 = f32[768,128]{1,0:T(8,128)} custom-call(f32[768,128]{1,0:T(8,128)S(1)} %bitcast.2, bf16[2,256,128]{2,1,0:T(8,128)(2,1)S(1)} %copy-done.14, bf16[2,256,128]{2,1,0:T(8,128)(2,1)S(1)} %copy-done.13, bf16[96,144]{1,0:T(8,128)(2,1)S(1)} %copy-done.15), custom_call_target="tpu_custom_call" | custom-call | flops 268435456 | bytes 4194304 | tf_op jit(solution)/shard_map/pallas_call | solution.py:450
  58.2 0.0 copy-done.11
  58.2 3.6 %all-to-all-start.1 = ((f32[16,48,128]{2,1,0:T(8,128)}), f32[16,48,128]{2,1,0:T(8,128)S(1)}, u32[]{:S(2)}, u32[]{:S(2)}) async-start(f32[16,48,128]{2,1,0:T(8,128)} %bitcast.1), calls=%async_computation.1 | async-start | bytes 786432 | tf_op jit(solution)/shard_map/all_to_all | solution.py:564
  61.8 0.0 copy-done.17
  61.8 0.4 collective-permute-start.6
  62.2 4.2 %collective-permute-start.7 = (f32[2,32,512]{2,1,0:T(8,128)S(1)}, f32[2,32,512]{2,1,0:T(8,128)S(1)}, u32[]{:S(2)}, u32[]{:S(2)}) collective-permute-start(f32[2,32,512]{2,1,0:T(8,128)S(1)} %get-tuple-element.52), channel_id=1, source_target_pairs={{1,0},{2,1},{3,2},{4,3},{5,4},{6,5},{7,6},{8,7},{9,8},{10,9},{11,1... | collective-permute-start | bytes 393224 | tf_op jit(solution)/shard_map/ppermute | solution.py:570
  66.5 0.0 copy-start.12
  66.5 0.9 %copy-done.12 = f32[4,32,512]{2,1,0:T(8,128)S(1)} copy-done((f32[4,32,512]{2,1,0:T(8,128)S(1)}, f32[4,32,512]{2,1,0:T(8,128)}, u32[]{:S(2)}) %copy-start.12) | copy-done | bytes 262168
  67.4 7.6 %shard_map.109 = (f32[8,3,32,512]{3,2,1,0:T(8,128)}, f32[2,2,2,32,512]{4,3,2,1,0:T(8,128)S(1)}) custom-call(f32[4,32,512]{2,1,0:T(8,128)S(1)} %collective-permute-done.4.prev3, f32[4,32,512]{2,1,0:T(8,128)S(1)} %copy-done.12, s32[2]{0:T(128)} %chosen_any.6, s32[8,8]{1,0:T(8,128)} %classes_any.6, f32[8,32,512]{2,1,0:T(8,128)} %copy-done.2, ...), custom_call_target="tpu_custom_call" | custom-call | flops 67108864 | bytes 16777216 | tf_op jit(solution)/shard_map/pallas_call | solution.py:450
  75.1 0.3 collective-permute-done.6.prev4
  75.4 0.0 collective-permute-done.7.next4
  75.4 0.0 copy-start.9
  75.4 0.0 copy-start.10
  75.4 1.5 %shard_map.110 = f32[8,3,32,512]{3,2,1,0:T(8,128)} custom-call(f32[2,32,512]{2,1,0:T(8,128)S(1)} %collective-permute-done.6.prev4, f32[2,32,512]{2,1,0:T(8,128)S(1)} %collective-permute-done.7.next4, f32[2,2,2,32,512]{4,3,2,1,0:T(8,128)S(1)} %get-tuple-element.68.linear, s32[2]{0:T(128)} %chosen_any.6, ...), custom_call_target="tpu_custom_call", output_to_operand_aliasing={{}: (4, {})} | custom-call | flops 1048576 | bytes 2097152 | tf_op jit(solution)/shard_map/pallas_call | solution.py:588
  76.9 0.0 all-to-all-done.1.returned
  76.9 0.0 copy-done.9
  76.9 0.0 copy-done.10
  77.0 1.3 %shard_map.111 = f32[2,3,32,512]{3,2,1,0:T(8,128)} custom-call(f32[16,48,128]{2,1,0:T(8,128)S(1)} %all-to-all-done.1.returned, bf16[512,512]{1,0:T(8,128)(2,1)S(1)} %copy-done.10, bf16[512,512]{1,0:T(8,128)(2,1)S(1)} %copy-done.9), custom_call_target="tpu_custom_call" | custom-call | flops 268435456 | bytes 4194304 | tf_op jit(solution)/shard_map/pallas_call | solution.py:450
Async XLA Ops:
  1.9 24.0 %copy-start.2 = (f32[8,32,512]{2,1,0:T(8,128)}, f32[8,32,512]{2,1,0:T(8,128)S(1)}, u32[]{:S(2)}) copy-start(f32[8,32,512]{2,1,0:T(8,128)S(1)} %get-tuple-element.59.p0.p0_any) | copy-start | bytes 1572868
  1.9 24.0 %copy-start.3 = (f32[8,32,512]{2,1,0:T(8,128)}, f32[8,32,512]{2,1,0:T(8,128)S(1)}, u32[]{:S(2)}) copy-start(f32[8,32,512]{2,1,0:T(8,128)S(1)} %get-tuple-element.60.p2.p2_any) | copy-start | bytes 1572868
  1.9 12.2 %collective-permute-start.1 = (f32[8,32,512]{2,1,0:T(8,128)S(1)}, f32[8,32,512]{2,1,0:T(8,128)S(1)}, u32[]{:S(2)}, u32[]{:S(2)}) collective-permute-start(f32[8,32,512]{2,1,0:T(8,128)S(1)} %get-tuple-element.59.p0.p0_any), channel_id=1, source_target_pairs={{1,0},{2,1},{3,2},{4,3},{5,4},{6,5},{7,6},{8,7},{9,8},{10,9},{11,1... | collective-permute-start | bytes 1572872 | tf_op jit(solution)/shard_map/ppermute | solution.py:500
  7.4 11.4 %collective-permute-start = (f32[8,32,512]{2,1,0:T(8,128)S(1)}, f32[8,32,512]{2,1,0:T(8,128)S(1)}, u32[]{:S(2)}, u32[]{:S(2)}) collective-permute-start(f32[8,32,512]{2,1,0:T(8,128)S(1)} %get-tuple-element.60.p2.p2_any), channel_id=1, source_target_pairs={{0,1},{1,2},{2,3},{3,4},{4,5},{5,6},{6,7},{7,8},{8,9},{9,10},{10,1... | collective-permute-start | bytes 1572872 | tf_op jit(solution)/shard_map/ppermute | solution.py:499
  9.4 11.1 %copy-start.16 = (f32[2,32,512]{2,1,0:T(8,128)}, f32[2,32,512]{2,1,0:T(8,128)S(1)}, u32[]{:S(2)}) copy-start(f32[2,32,512]{2,1,0:T(8,128)S(1)} %get-tuple-element.51) | copy-start | bytes 393220
  9.4 16.5 %copy-start.1 = (f32[3,8,32,512]{3,2,1,0:T(8,128)}, f32[3,8,32,512]{3,2,1,0:T(8,128)S(1)}, u32[]{:S(2)}) copy-start(f32[3,8,32,512]{3,2,1,0:T(8,128)S(1)} %get-tuple-element.67.rates.rates_any) | copy-start | bytes 4718596
  9.4 16.5 %copy-start.6 = (f32[8,32,512]{2,1,0:T(8,128)}, f32[8,32,512]{2,1,0:T(8,128)S(1)}, u32[]{:S(2)}) copy-start(f32[8,32,512]{2,1,0:T(8,128)S(1)} %get-tuple-element.66.middle.middle_any) | copy-start | bytes 1572868
  9.4 16.4 %collective-permute-start.2 = (f32[10,32,512]{2,1,0:T(8,128)S(1)}, f32[10,32,512]{2,1,0:T(8,128)S(1)}, u32[]{:S(2)}, u32[]{:S(2)}) collective-permute-start(f32[10,32,512]{2,1,0:T(8,128)S(1)} %get-tuple-element.41), channel_id=1, source_target_pairs={{0,1},{1,2},{2,3},{3,4},{4,5},{5,6},{6,7},{7,8},{8,9},{9,10},{10,1... | collective-permute-start | bytes 1966088 | tf_op jit(solution)/shard_map/ppermute | solution.py:512
  9.5 16.4 %collective-permute-start.3 = (f32[10,32,512]{2,1,0:T(8,128)S(1)}, f32[10,32,512]{2,1,0:T(8,128)S(1)}, u32[]{:S(2)}, u32[]{:S(2)}) collective-permute-start(f32[10,32,512]{2,1,0:T(8,128)S(1)} %get-tuple-element.42), channel_id=1, source_target_pairs={{1,0},{2,1},{3,2},{4,3},{5,4},{6,5},{7,6},{8,7},{9,8},{10,9},{11,1... | collective-permute-start | bytes 1966088 | tf_op jit(solution)/shard_map/ppermute | solution.py:513
  14.1 11.8 %copy-start.4 = (f32[8,32,512]{2,1,0:T(8,128)}, f32[8,32,512]{2,1,0:T(8,128)S(1)}, u32[]{:S(2)}) copy-start(f32[8,32,512]{2,1,0:T(8,128)S(1)} %collective-permute-done.1.next1.next1_any) | copy-start | bytes 1572868
  18.8 7.1 %copy-start.5 = (f32[8,32,512]{2,1,0:T(8,128)}, f32[8,32,512]{2,1,0:T(8,128)S(1)}, u32[]{:S(2)}) copy-start(f32[8,32,512]{2,1,0:T(8,128)S(1)} %collective-permute-done.prev1.prev1_any) | copy-start | bytes 1572868
  20.5 8.7 %copy-start = (f32[40,32,512]{2,1,0:T(8,128)}, f32[40,32,512]{2,1,0:T(8,128)S(1)}, u32[]{:S(2)}) copy-start(f32[40,32,512]{2,1,0:T(8,128)S(1)} %shard_map.106.near_out.near_any) | copy-start | bytes 7864324
  20.5 35.5 %copy-start.13 = (bf16[2,256,128]{2,1,0:T(8,128)(2,1)S(1)}, bf16[2,256,128]{2,1,0:T(8,128)(2,1)}, u32[]{:S(2)}) copy-start(bf16[2,256,128]{2,1,0:T(8,128)(2,1)} %constant.13.clone.refs_2_) | copy-start | bytes 393220
  20.6 35.5 %copy-start.14 = (bf16[2,256,128]{2,1,0:T(8,128)(2,1)S(1)}, bf16[2,256,128]{2,1,0:T(8,128)(2,1)}, u32[]{:S(2)}) copy-start(bf16[2,256,128]{2,1,0:T(8,128)(2,1)} %constant.12.clone.refs_1_) | copy-start | bytes 393220
  20.6 35.5 %copy-start.15 = (bf16[96,144]{1,0:T(8,128)(2,1)S(1)}, bf16[96,144]{1,0:T(8,128)(2,1)}, u32[]{:S(2)}) copy-start(bf16[96,144]{1,0:T(8,128)(2,1)} %constant.14.clone.refs_3_) | copy-start | bytes 82948
  20.6 8.7 %collective-permute-start.4 = (f32[4,32,512]{2,1,0:T(8,128)S(1)}, f32[4,32,512]{2,1,0:T(8,128)S(1)}, u32[]{:S(2)}, u32[]{:S(2)}) collective-permute-start(f32[4,32,512]{2,1,0:T(8,128)S(1)} %get-tuple-element.48), channel_id=1, source_target_pairs={{0,1},{1,2},{2,3},{3,4},{4,5},{5,6},{6,7},{7,8},{8,9},{9,10},{10,1... | collective-permute-start | bytes 786440 | tf_op jit(solution)/shard_map/ppermute | solution.py:523
  25.7 3.9 %collective-permute-start.5 = (f32[4,32,512]{2,1,0:T(8,128)S(1)}, f32[4,32,512]{2,1,0:T(8,128)S(1)}, u32[]{:S(2)}, u32[]{:S(2)}) collective-permute-start(f32[4,32,512]{2,1,0:T(8,128)S(1)} %get-tuple-element.49), channel_id=1, source_target_pairs={{1,0},{2,1},{3,2},{4,3},{5,4},{6,5},{7,6},{8,7},{9,8},{10,9},{11,1... | collective-permute-start | bytes 786440 | tf_op jit(solution)/shard_map/ppermute | solution.py:524
  25.9 3.4 %copy-start.7 = (f32[10,32,512]{2,1,0:T(8,128)}, f32[10,32,512]{2,1,0:T(8,128)S(1)}, u32[]{:S(2)}) copy-start(f32[10,32,512]{2,1,0:T(8,128)S(1)} %collective-permute-done.2.prev2.prev2_any) | copy-start | bytes 1966084
  25.9 3.3 %copy-start.8 = (f32[10,32,512]{2,1,0:T(8,128)}, f32[10,32,512]{2,1,0:T(8,128)S(1)}, u32[]{:S(2)}) copy-start(f32[10,32,512]{2,1,0:T(8,128)S(1)} %collective-permute-done.3.next2.next2_any) | copy-start | bytes 1966084
  29.2 32.6 %copy-start.17 = (f32[2,32,512]{2,1,0:T(8,128)S(1)}, f32[2,32,512]{2,1,0:T(8,128)}, u32[]{:S(2)}) copy-start(f32[2,32,512]{2,1,0:T(8,128)} %copy-done.16) | copy-start | bytes 393220
  29.6 28.6 %copy-start.11 = (f32[4,32,512]{2,1,0:T(8,128)}, f32[4,32,512]{2,1,0:T(8,128)S(1)}, u32[]{:S(2)}) copy-start(f32[4,32,512]{2,1,0:T(8,128)S(1)} %collective-permute-done.5.next3) | copy-start | bytes 786436
  58.2 18.7 %all-to-all-start.1 = ((f32[16,48,128]{2,1,0:T(8,128)}), f32[16,48,128]{2,1,0:T(8,128)S(1)}, u32[]{:S(2)}, u32[]{:S(2)}) async-start(f32[16,48,128]{2,1,0:T(8,128)} %bitcast.1), calls=%async_computation.1 | async-start | bytes 786432 | tf_op jit(solution)/shard_map/all_to_all | solution.py:564
  61.8 13.6 %collective-permute-start.6 = (f32[2,32,512]{2,1,0:T(8,128)S(1)}, f32[2,32,512]{2,1,0:T(8,128)S(1)}, u32[]{:S(2)}, u32[]{:S(2)}) collective-permute-start(f32[2,32,512]{2,1,0:T(8,128)S(1)} %copy-done.17), channel_id=1, source_target_pairs={{0,1},{1,2},{2,3},{3,4},{4,5},{5,6},{6,7},{7,8},{8,9},{9,10},{10,1... | collective-permute-start | bytes 393224 | tf_op jit(solution)/shard_map/ppermute | solution.py:569
  62.2 13.1 %collective-permute-start.7 = (f32[2,32,512]{2,1,0:T(8,128)S(1)}, f32[2,32,512]{2,1,0:T(8,128)S(1)}, u32[]{:S(2)}, u32[]{:S(2)}) collective-permute-start(f32[2,32,512]{2,1,0:T(8,128)S(1)} %get-tuple-element.52), channel_id=1, source_target_pairs={{1,0},{2,1},{3,2},{4,3},{5,4},{6,5},{7,6},{8,7},{9,8},{10,9},{11,1... | collective-permute-start | bytes 393224 | tf_op jit(solution)/shard_map/ppermute | solution.py:570
  66.5 0.9 %copy-start.12 = (f32[4,32,512]{2,1,0:T(8,128)S(1)}, f32[4,32,512]{2,1,0:T(8,128)}, u32[]{:S(2)}) copy-start(f32[4,32,512]{2,1,0:T(8,128)} %copy-done.11) | copy-start | bytes 786436
  75.4 1.6 %copy-start.9 = (bf16[512,512]{1,0:T(8,128)(2,1)S(1)}, bf16[512,512]{1,0:T(8,128)(2,1)}, u32[]{:S(2)}) copy-start(bf16[512,512]{1,0:T(8,128)(2,1)} %constant.11.clone.low_any.low) | copy-start | bytes 1572868
  75.4 1.6 %copy-start.10 = (bf16[512,512]{1,0:T(8,128)(2,1)S(1)}, bf16[512,512]{1,0:T(8,128)(2,1)}, u32[]{:S(2)}) copy-start(bf16[512,512]{1,0:T(8,128)(2,1)} %constant.10.clone.high_any.high) | copy-start | bytes 1572868

commit v14 on v11

--- a/solution.py
+++ b/solution.py
@@ -10,7 +10,6 @@
 from jax.sharding import PartitionSpec as P
 
 STEPS = 3
-SOON = 3
 GRAINS = 8
 F32 = jnp.float32
 BF16 = jnp.bfloat16
@@ -153,7 +152,7 @@
 
 
 def inner_kernel(
-    chosen_any, classes_any, p0, p1, p2, up2, down2, r0, r2, l0, l2, rates, middle, chosen, classes, semaphores
+    chosen_any, classes_any, p0, p1, p2, up2, down2, r0, r2, rates, middle, chosen, classes, semaphores
 ):
     copies = fetch(((chosen_any, chosen), (classes_any, classes)), semaphores)
     for i in range(GRAINS):
@@ -167,11 +166,8 @@
     other = others_of(chosen)
     for r in range(GRAINS - 2):
         i = other(r)
-        for soon, late, start in ((r0, l0, p0), (r2, l2, p2)):
-            if r < SOON:
-                soon[r] = start[i]
-            else:
-                late[r - SOON] = start[i]
+        r0[r] = p0[i]
+        r2[r] = p2[i]
     for k, start in enumerate((p0, p1, p2)):
         rates_plane(classes, start, rates.at[k])
     step_plane(p1, p0, p2, rates.at[1], middle)
@@ -260,7 +256,7 @@
 
 
 def rest_kernel(
-    prev3, next3, prev4, next4,
+    prev3, next3,
     chosen_any, classes_any, p0_any, p2_any, prev1_any, next1_any, prev2_any, next2_any, near_any, middle_any,
     rates_any, out_any,
     chosen, classes, p0, p2, prev1, next1, prev2, next2, near_out, middle, rates, second, edge, out, semaphores,
@@ -308,15 +304,12 @@
         outs.extend(fetch(((out.at[:, plane], out_any.at[:, plane]),), semaphores.at[pl.ds(17 + plane, 1)]))
 
     finish(1)
-    for side, (soon, far, mid, near) in enumerate(((prev3, prev4, prev2, prev1), (next3, next4, next2, next1))):
+    for side, (far, mid, near) in enumerate(((prev3, prev2, prev1), (next3, next2, next1))):
         ids = grain_of(mid)
         total0 = squares(mid)
         total1 = squares(outer1[side])
         for k, (i, early, late) in enumerate(places):
-            if early is not None:
-                third = mid[early]
-            else:
-                third = soon[late] if late < SOON else far[late - SOON]
+            third = far[late] if early is None else mid[early]
             first = update(mid[i], third, near[i], total0, rate(classes, ids, i))
             edge[side, k] = update(outer1[side][i], first, inner1[side][i], total1, edge_rates[side][i])
         finish(2 * side)
@@ -458,7 +451,7 @@
     x_both = jnp.asarray(np.concatenate([x_high, x_high, x_low], axis=1))
 
     two = (2, *plane)
-    soon, last = (SOON, depth, width), (GRAINS - 2 - SOON, depth, width)
+    six = (GRAINS - 2, depth, width)
     small = [pltpu.SMEM((2,), jnp.int32), pltpu.SMEM((GRAINS, GRAINS), jnp.int32)]
     ten = (GRAINS + 2, depth, width)
     p0, p1, p2 = call(
@@ -475,10 +468,10 @@
     )
     prev1 = lax.ppermute(p2, "gx", up)
     next1 = lax.ppermute(p0, "gx", down)
-    up2, down2, r0, r2, l0, l2, rates, middle = call(
+    up2, down2, r0, r2, rates, middle = call(
         inner_kernel,
         (
-            shape(*ten), shape(*ten), shape(*soon), shape(*soon), shape(*last), shape(*last),
+            shape(*ten), shape(*ten), shape(*six), shape(*six),
             shape(planes, *plane), shape(*plane),
         ),
         [ANY] * 2 + [VMEM] * 3,
@@ -488,6 +481,9 @@
     )
     prev2 = lax.ppermute(up2, "gx", up)
     next2 = lax.ppermute(down2, "gx", down)
+    r0, r2, prev1, next1 = lax.optimization_barrier((r0, r2, prev1, next1))
+    prev3 = lax.ppermute(r0, "gx", up)
+    next3 = lax.ppermute(r2, "gx", down)
     near_out = call(
         near_kernel,
         shape(5 * GRAINS, depth, width),
@@ -496,9 +492,6 @@
         scratch=[small[1], pltpu.SemaphoreType.DMA((1,))],
         flops=2**25, moved=2**24,
     )
-    r0, r2, near_out = lax.optimization_barrier((r0, r2, near_out))
-    prev3 = lax.ppermute(r0, "gx", up)
-    next3 = lax.ppermute(r2, "gx", down)
     packed_shape = (devices, planes * share, lanes) if aligned else (planes, slots, lanes)
     packed = call(
         pair_kernel,
@@ -522,9 +515,7 @@
     else:
         lines = lax.all_to_all(packed, "gx", split_axis=1, concat_axis=0, tiled=True)
     lines = lines.reshape(total_x * share, lanes)
-    lines, l0, l2 = lax.optimization_barrier((lines, l0, l2))
-    prev4 = lax.ppermute(l0, "gx", up)
-    next4 = lax.ppermute(l2, "gx", down)
+
     def lines_body(*refs):
         line_kernel(*refs, scale=1.0 / (count * count))
 
@@ -545,18 +536,18 @@
         returned = returned.reshape(devices, planes, share, lanes).transpose(1, 0, 2, 3)
         returned = returned.reshape(planes, slots, lanes)
     late = (
-        prev3, next3, prev4, next4,
+        prev3, next3,
         chosen, class_table, p0, p2, prev1, next1, prev2, next2, near_out, middle, rates,
     )
     late, _ = lax.optimization_barrier((late, back))
     order_params = call(
         rest_kernel,
         shape(GRAINS, planes, depth, width),
-        [VMEM] * 4 + [ANY] * (len(late) - 4),
+        [VMEM] * 2 + [ANY] * (len(late) - 2),
         *late,
         scratch=[
             *small,
-            *[pltpu.VMEM(value.shape, F32) for value in late[6:]],
+            *[pltpu.VMEM(value.shape, F32) for value in late[4:]],
             pltpu.VMEM((4 * GRAINS, depth, width), F32),
             pltpu.VMEM((2, *plane), F32),
             pltpu.VMEM((GRAINS, planes, depth, width), F32),

time: 79.4 us -> 77.9 us (0.981)
  starting transfers between devices: 23.3 us -> 18.9 us
  blocking collectives: 25.9 us -> 28 us
  waiting for transfers between devices: 8.37 us -> 9.25 us
    ppermute x2 -> x0, starting transfers between devices: 4.44 us -> none  [the longest x1 4.33 us: shards(): next4 = lax.ppermute(l2, 'gx', down)]
    all_to_all x1, blocking collectives: 25.9 us -> 28 us  [shards(): lax.all_to_all(packed, 'gx', split_axis=0, concat_axis=0, tiled=True)]
    ppermute x1, waiting for transfers between devices: 0.01 us -> 0.85 us  [shards(): prev3 = lax.ppermute(r0, 'gx', up)]
  transfers between devices with their start and end apart: 9 -> 7, of which waited for: 4 -> 5; matrix products, arithmetic and copies ran while one was open for 0% -> 0% of each run, Pallas kernels for 21% -> 19%
where the time goes in v14:
time: 77.9 us; the launch traced here: 77.6 us
  blocking collectives  28 us (36%)
  Pallas kernels  19.4 us (25%)
  starting transfers between devices  18.9 us (24%)
  waiting for transfers between devices  9.25 us (12%)
  local copies, waits for them, and re-layouts  1.06 us (1%)
  between operations  1.01 us (1%)
    all_to_all x1, blocking collectives, shards(): lax.all_to_all(packed, 'gx', split_axis=0, concat_axis=0, tiled=True)  28 us
    pallas_call x7, Pallas kernels, call(): pl.pallas_call(kernel, out_shape=outs, in_specs=in_specs, out_specs=out_s...  19.4 us
    ppermute x1, starting transfers between devices, shards(): next1 = lax.ppermute(p0, 'gx', down)  5.5 us
    ppermute x1, starting transfers between devices, shards(): prev3 = lax.ppermute(r0, 'gx', up)  5.07 us
    ppermute x1, waiting for transfers between devices, shards(): prev1 = lax.ppermute(p2, 'gx', up)  4.7 us
    ppermute x1, starting transfers between devices, shards(): next2 = lax.ppermute(down2, 'gx', down)  4.49 us
    all_to_all x1, starting transfers between devices, shards(): lax.all_to_all(back, 'gx', split_axis=0, concat_axis=0, tiled=True)  3.73 us
    all_to_all x1, waiting for transfers between devices, shards(): lax.all_to_all(back, 'gx', split_axis=0, concat_axis=0, tiled=True)  3.3 us
  transfers between devices with their start and end apart: 7, of which 5 were waited for; matrix products, arithmetic and copies ran while one was open for 0% of the time, Pallas kernels for 19%

profile of v14, /device:TPU:0, one launch (start us, length us, event | category | flops | bytes accessed | tf_op | source)
XLA Modules:
  0.0 77.6 jit_solution(10623263836300281157)
XLA Ops:
  0.6 1.3 %shard_map.104 = (f32[8,32,512]{2,1,0:T(8,128)S(1)}, f32[8,32,512]{2,1,0:T(8,128)S(1)}, f32[8,32,512]{2,1,0:T(8,128)S(1)}) custom-call(bf16[8,3,32,512]{3,2,1,0:T(8,128)(2,1)} %jitter_any.1, s32[3,32,512]{2,1,0:T(8,128)} %ids_any.1), custom_call_target="tpu_custom_call" | custom-call | flops 2097152 | bytes 4194304 | tf_op jit(solution)/shard_map/pallas_call | solution.py:420
  1.9 0.0 copy-start.2
  1.9 0.0 copy-start.3
  1.9 5.5 %collective-permute-start.1 = (f32[8,32,512]{2,1,0:T(8,128)S(1)}, f32[8,32,512]{2,1,0:T(8,128)S(1)}, u32[]{:S(2)}, u32[]{:S(2)}) collective-permute-start(f32[8,32,512]{2,1,0:T(8,128)S(1)} %get-tuple-element.51.p0.p0_any), channel_id=1, source_target_pairs={{1,0},{2,1},{3,2},{4,3},{5,4},{6,5},{7,6},{8,7},{9,8},{10,9},{11,1... | collective-permute-start | bytes 1572872 | tf_op jit(solution)/shard_map/ppermute | solution.py:470
  7.4 0.0 collective-permute-start
  7.4 2.0 %shard_map.105 = (f32[10,32,512]{2,1,0:T(8,128)S(1)}, f32[10,32,512]{2,1,0:T(8,128)S(1)}, f32[6,32,512]{2,1,0:T(8,128)S(1)}, f32[6,32,512]{2,1,0:T(8,128)S(1)}, ...) custom-call(s32[2]{0:T(128)} %chosen_any.4, s32[8,8]{1,0:T(8,128)} %classes_any.6, ...), custom_call_target="tpu_custom_call" | custom-call | flops 16777216 | bytes 4194304 | tf_op jit(solution)/shard_map/pallas_call | solution.py:420
  9.4 0.0 copy-start.1
  9.4 0.0 copy-start.8
  9.4 0.1 collective-permute-start.2
  9.5 4.5 %collective-permute-start.3 = (f32[10,32,512]{2,1,0:T(8,128)S(1)}, f32[10,32,512]{2,1,0:T(8,128)S(1)}, u32[]{:S(2)}, u32[]{:S(2)}) collective-permute-start(f32[10,32,512]{2,1,0:T(8,128)S(1)} %get-tuple-element.39), channel_id=1, source_target_pairs={{1,0},{2,1},{3,2},{4,3},{5,4},{6,5},{7,6},{8,7},{9,8},{10,9},{11,1... | collective-permute-start | bytes 1966088 | tf_op jit(solution)/shard_map/ppermute | solution.py:483
  14.0 0.2 collective-permute-done.1.next1.next1_any
  14.1 0.0 copy-start.6
  14.1 4.7 %collective-permute-done.prev1.prev1_any = f32[8,32,512]{2,1,0:T(8,128)S(1)} collective-permute-done((f32[8,32,512]{2,1,0:T(8,128)S(1)}, f32[8,32,512]{2,1,0:T(8,128)S(1)}, u32[]{:S(2)}, u32[]{:S(2)}) %collective-permute-start) | collective-permute-done | bytes 524320 | tf_op jit(solution)/shard_map/ppermute | solution.py:469
  18.8 0.0 copy-start.7
  18.8 5.1 %collective-permute-start.4 = (f32[6,32,512]{2,1,0:T(8,128)S(1)}, f32[6,32,512]{2,1,0:T(8,128)S(1)}, u32[]{:S(2)}, u32[]{:S(2)}) collective-permute-start(f32[6,32,512]{2,1,0:T(8,128)S(1)} %get-tuple-element.42), channel_id=1, source_target_pairs={{0,1},{1,2},{2,3},{3,4},{4,5},{5,6},{6,7},{7,8},{8,9},{9,10},{10,1... | collective-permute-start | bytes 1179656 | tf_op jit(solution)/shard_map/ppermute | solution.py:485
  23.9 0.0 collective-permute-start.5
  23.9 1.7 %shard_map.106.near_out.near_any = f32[40,32,512]{2,1,0:T(8,128)S(1)} custom-call(s32[8,8]{1,0:T(8,128)} %classes_any.6, f32[8,32,512]{2,1,0:T(8,128)S(1)} %get-tuple-element.51.p0.p0_any, f32[8,32,512]{2,1,0:T(8,128)S(1)} %get-tuple-element.33.p1, f32[8,32,512]{2,1,0:T(8,128)S(1)} %get-tuple-element.52.p2.p2_any, ...), custom_call_target="tpu_custom_call" | custom-call | flops 33554432 | bytes 16777216 | tf_op jit(solution)/shard_map/pallas_call | solution.py:420
  25.6 0.0 copy-start
  25.6 0.0 copy-start.11
  25.6 0.0 copy-start.12
  25.6 0.0 copy-start.13
  25.6 0.2 collective-permute-done.2.prev2.prev2_any
  25.9 0.0 copy-start.9
  25.9 0.0 collective-permute-done.3.next2.next2_any
  25.9 0.0 copy-done.2
  25.9 0.0 copy-done.3
  25.9 0.0 copy-done.1
  25.9 0.0 copy-done.8
  25.9 0.0 copy-done.6
  25.9 0.0 copy-done.7
  25.9 0.0 copy-start.10
  25.9 3.3 %shard_map.107 = f32[16,48,128]{2,1,0:T(8,128)S(1)} custom-call(s32[2]{0:T(128)} %chosen_any.4, s32[8,8]{1,0:T(8,128)} %classes_any.6, f32[8,32,512]{2,1,0:T(8,128)S(1)} %get-tuple-element.51.p0.p0_any, f32[8,32,512]{2,1,0:T(8,128)S(1)} %get-tuple-element.52.p2.p2_any, f32[8,32,512]{2,1,0:T(8,128)S(1)} %collective-permute-done.prev1.prev1_any, ...), custom_call_target="tpu_custom_call" | custom-call | flops 268435456 | bytes 8388608 | tf_op jit(solution)/shard_map/pallas_call | solution.py:420
  29.2 0.0 copy-done
  29.2 0.0 copy-done.9
  29.2 0.0 copy-done.10
  29.2 0.8 %collective-permute-done.4.prev3 = f32[6,32,512]{2,1,0:T(8,128)S(1)} collective-permute-done((f32[6,32,512]{2,1,0:T(8,128)S(1)}, f32[6,32,512]{2,1,0:T(8,128)S(1)}, u32[]{:S(2)}, u32[]{:S(2)}) %collective-permute-start.4) | collective-permute-done | bytes 393248 | tf_op jit(solution)/shard_map/ppermute | solution.py:485
  30.1 0.0 collective-permute-done.5.next3
  30.1 0.0 copy-start.14
  30.1 28.0 %all_to_all.10 = f32[16,48,128]{2,1,0:T(8,128)S(1)} all-to-all(f32[16,48,128]{2,1,0:T(8,128)S(1)} %shard_map.107), channel_id=1, replica_groups=mesh['grp'=2,'gx'=16] {'gx'}, dimensions={0} | all-to-all | bytes 786432 | tf_op jit(solution)/shard_map/all_to_all | solution.py:514
  58.1 0.0 copy-done.11
  58.1 0.0 copy-done.12
  58.1 0.0 copy-done.13
  58.1 2.2 %shard_map.108 = f32[768,128]{1,0:T(8,128)} custom-call(f32[768,128]{1,0:T(8,128)S(1)} %bitcast.2, bf16[2,256,128]{2,1,0:T(8,128)(2,1)S(1)} %copy-done.12, bf16[2,256,128]{2,1,0:T(8,128)(2,1)S(1)} %copy-done.11, bf16[96,144]{1,0:T(8,128)(2,1)S(1)} %copy-done.13), custom_call_target="tpu_custom_call" | custom-call | flops 268435456 | bytes 4194304 | tf_op jit(solution)/shard_map/pallas_call | solution.py:420
  60.3 0.0 copy-done.14
  60.3 3.7 %all-to-all-start.1 = ((f32[16,48,128]{2,1,0:T(8,128)}), f32[16,48,128]{2,1,0:T(8,128)S(1)}, u32[]{:S(2)}, u32[]{:S(2)}) async-start(f32[16,48,128]{2,1,0:T(8,128)} %bitcast.1), calls=%async_computation.1 | async-start | bytes 786432 | tf_op jit(solution)/shard_map/all_to_all | solution.py:534
  64.1 0.0 copy-start.15
  64.1 1.0 %copy-done.15 = f32[6,32,512]{2,1,0:T(8,128)S(1)} copy-done((f32[6,32,512]{2,1,0:T(8,128)S(1)}, f32[6,32,512]{2,1,0:T(8,128)}, u32[]{:S(2)}) %copy-start.15) | copy-done | bytes 393240
  65.1 0.0 copy-start.4
  65.1 0.0 copy-start.5
  65.1 7.7 %shard_map.109 = f32[8,3,32,512]{3,2,1,0:T(8,128)} custom-call(f32[6,32,512]{2,1,0:T(8,128)S(1)} %collective-permute-done.4.prev3, f32[6,32,512]{2,1,0:T(8,128)S(1)} %copy-done.15, s32[2]{0:T(128)} %chosen_any.4, s32[8,8]{1,0:T(8,128)} %classes_any.6, f32[8,32,512]{2,1,0:T(8,128)} %copy-done.2, f32[8,32,512]{2,1,0:T(8,128)} %copy-done.3, ...), custom_call_target="tpu_custom_call" | custom-call | flops 137438953472 | bytes 16777216 | tf_op jit(solution)/shard_map/pallas_call | solution.py:420
  72.8 3.3 %all-to-all-done.1.returned = f32[16,48,128]{2,1,0:T(8,128)S(1)} async-done(((f32[16,48,128]{2,1,0:T(8,128)}), f32[16,48,128]{2,1,0:T(8,128)S(1)}, u32[]{:S(2)}, u32[]{:S(2)}) %all-to-all-start.1) | async-done | bytes 393248 | tf_op jit(solution)/shard_map/all_to_all | solution.py:534
  76.1 0.0 copy-done.4
  76.1 0.0 copy-done.5
  76.1 1.3 %shard_map.110 = f32[2,3,32,512]{3,2,1,0:T(8,128)} custom-call(f32[16,48,128]{2,1,0:T(8,128)S(1)} %all-to-all-done.1.returned, bf16[512,512]{1,0:T(8,128)(2,1)S(1)} %copy-done.5, bf16[512,512]{1,0:T(8,128)(2,1)S(1)} %copy-done.4), custom_call_target="tpu_custom_call" | custom-call | flops 268435456 | bytes 4194304 | tf_op jit(solution)/shard_map/pallas_call | solution.py:420
Async XLA Ops:
  1.9 24.0 %copy-start.2 = (f32[8,32,512]{2,1,0:T(8,128)}, f32[8,32,512]{2,1,0:T(8,128)S(1)}, u32[]{:S(2)}) copy-start(f32[8,32,512]{2,1,0:T(8,128)S(1)} %get-tuple-element.51.p0.p0_any) | copy-start | bytes 1572868
  1.9 23.9 %copy-start.3 = (f32[8,32,512]{2,1,0:T(8,128)}, f32[8,32,512]{2,1,0:T(8,128)S(1)}, u32[]{:S(2)}) copy-start(f32[8,32,512]{2,1,0:T(8,128)S(1)} %get-tuple-element.52.p2.p2_any) | copy-start | bytes 1572868
  1.9 12.2 %collective-permute-start.1 = (f32[8,32,512]{2,1,0:T(8,128)S(1)}, f32[8,32,512]{2,1,0:T(8,128)S(1)}, u32[]{:S(2)}, u32[]{:S(2)}) collective-permute-start(f32[8,32,512]{2,1,0:T(8,128)S(1)} %get-tuple-element.51.p0.p0_any), channel_id=1, source_target_pairs={{1,0},{2,1},{3,2},{4,3},{5,4},{6,5},{7,6},{8,7},{9,8},{10,9},{11,1... | collective-permute-start | bytes 1572872 | tf_op jit(solution)/shard_map/ppermute | solution.py:470
  7.4 11.4 %collective-permute-start = (f32[8,32,512]{2,1,0:T(8,128)S(1)}, f32[8,32,512]{2,1,0:T(8,128)S(1)}, u32[]{:S(2)}, u32[]{:S(2)}) collective-permute-start(f32[8,32,512]{2,1,0:T(8,128)S(1)} %get-tuple-element.52.p2.p2_any), channel_id=1, source_target_pairs={{0,1},{1,2},{2,3},{3,4},{4,5},{5,6},{6,7},{7,8},{8,9},{9,10},{10,1... | collective-permute-start | bytes 1572872 | tf_op jit(solution)/shard_map/ppermute | solution.py:469
  9.4 16.5 %copy-start.1 = (f32[3,8,32,512]{3,2,1,0:T(8,128)}, f32[3,8,32,512]{3,2,1,0:T(8,128)S(1)}, u32[]{:S(2)}) copy-start(f32[3,8,32,512]{3,2,1,0:T(8,128)S(1)} %get-tuple-element.59.rates.rates_any) | copy-start | bytes 4718596
  9.4 16.5 %copy-start.8 = (f32[8,32,512]{2,1,0:T(8,128)}, f32[8,32,512]{2,1,0:T(8,128)S(1)}, u32[]{:S(2)}) copy-start(f32[8,32,512]{2,1,0:T(8,128)S(1)} %get-tuple-element.58.middle.middle_any) | copy-start | bytes 1572868
  9.4 16.4 %collective-permute-start.2 = (f32[10,32,512]{2,1,0:T(8,128)S(1)}, f32[10,32,512]{2,1,0:T(8,128)S(1)}, u32[]{:S(2)}, u32[]{:S(2)}) collective-permute-start(f32[10,32,512]{2,1,0:T(8,128)S(1)} %get-tuple-element.38), channel_id=1, source_target_pairs={{0,1},{1,2},{2,3},{3,4},{4,5},{5,6},{6,7},{7,8},{8,9},{9,10},{10,1... | collective-permute-start | bytes 1966088 | tf_op jit(solution)/shard_map/ppermute | solution.py:482
  9.5 16.4 %collective-permute-start.3 = (f32[10,32,512]{2,1,0:T(8,128)S(1)}, f32[10,32,512]{2,1,0:T(8,128)S(1)}, u32[]{:S(2)}, u32[]{:S(2)}) collective-permute-start(f32[10,32,512]{2,1,0:T(8,128)S(1)} %get-tuple-element.39), channel_id=1, source_target_pairs={{1,0},{2,1},{3,2},{4,3},{5,4},{6,5},{7,6},{8,7},{9,8},{10,9},{11,1... | collective-permute-start | bytes 1966088 | tf_op jit(solution)/shard_map/ppermute | solution.py:483
  14.1 11.8 %copy-start.6 = (f32[8,32,512]{2,1,0:T(8,128)}, f32[8,32,512]{2,1,0:T(8,128)S(1)}, u32[]{:S(2)}) copy-start(f32[8,32,512]{2,1,0:T(8,128)S(1)} %collective-permute-done.1.next1.next1_any) | copy-start | bytes 1572868
  18.8 7.1 %copy-start.7 = (f32[8,32,512]{2,1,0:T(8,128)}, f32[8,32,512]{2,1,0:T(8,128)S(1)}, u32[]{:S(2)}) copy-start(f32[8,32,512]{2,1,0:T(8,128)S(1)} %collective-permute-done.prev1.prev1_any) | copy-start | bytes 1572868
  18.8 11.2 %collective-permute-start.4 = (f32[6,32,512]{2,1,0:T(8,128)S(1)}, f32[6,32,512]{2,1,0:T(8,128)S(1)}, u32[]{:S(2)}, u32[]{:S(2)}) collective-permute-start(f32[6,32,512]{2,1,0:T(8,128)S(1)} %get-tuple-element.42), channel_id=1, source_target_pairs={{0,1},{1,2},{2,3},{3,4},{4,5},{5,6},{6,7},{7,8},{8,9},{9,10},{10,1... | collective-permute-start | bytes 1179656 | tf_op jit(solution)/shard_map/ppermute | solution.py:485
  23.9 6.2 %collective-permute-start.5 = (f32[6,32,512]{2,1,0:T(8,128)S(1)}, f32[6,32,512]{2,1,0:T(8,128)S(1)}, u32[]{:S(2)}, u32[]{:S(2)}) collective-permute-start(f32[6,32,512]{2,1,0:T(8,128)S(1)} %get-tuple-element.43), channel_id=1, source_target_pairs={{1,0},{2,1},{3,2},{4,3},{5,4},{6,5},{7,6},{8,7},{9,8},{10,9},{11,1... | collective-permute-start | bytes 1179656 | tf_op jit(solution)/shard_map/ppermute | solution.py:486
  25.6 3.6 %copy-start = (f32[40,32,512]{2,1,0:T(8,128)}, f32[40,32,512]{2,1,0:T(8,128)S(1)}, u32[]{:S(2)}) copy-start(f32[40,32,512]{2,1,0:T(8,128)S(1)} %shard_map.106.near_out.near_any) | copy-start | bytes 7864324
  25.6 32.5 %copy-start.11 = (bf16[2,256,128]{2,1,0:T(8,128)(2,1)S(1)}, bf16[2,256,128]{2,1,0:T(8,128)(2,1)}, u32[]{:S(2)}) copy-start(bf16[2,256,128]{2,1,0:T(8,128)(2,1)} %constant.13.clone.refs_2_) | copy-start | bytes 393220
  25.6 32.5 %copy-start.12 = (bf16[2,256,128]{2,1,0:T(8,128)(2,1)S(1)}, bf16[2,256,128]{2,1,0:T(8,128)(2,1)}, u32[]{:S(2)}) copy-start(bf16[2,256,128]{2,1,0:T(8,128)(2,1)} %constant.12.clone.refs_1_) | copy-start | bytes 393220
  25.6 32.5 %copy-start.13 = (bf16[96,144]{1,0:T(8,128)(2,1)S(1)}, bf16[96,144]{1,0:T(8,128)(2,1)}, u32[]{:S(2)}) copy-start(bf16[96,144]{1,0:T(8,128)(2,1)} %constant.14.clone.refs_3_) | copy-start | bytes 82948
  25.9 3.4 %copy-start.9 = (f32[10,32,512]{2,1,0:T(8,128)}, f32[10,32,512]{2,1,0:T(8,128)S(1)}, u32[]{:S(2)}) copy-start(f32[10,32,512]{2,1,0:T(8,128)S(1)} %collective-permute-done.2.prev2.prev2_any) | copy-start | bytes 1966084
  25.9 3.3 %copy-start.10 = (f32[10,32,512]{2,1,0:T(8,128)}, f32[10,32,512]{2,1,0:T(8,128)S(1)}, u32[]{:S(2)}) copy-start(f32[10,32,512]{2,1,0:T(8,128)S(1)} %collective-permute-done.3.next2.next2_any) | copy-start | bytes 1966084
  30.1 30.3 %copy-start.14 = (f32[6,32,512]{2,1,0:T(8,128)}, f32[6,32,512]{2,1,0:T(8,128)S(1)}, u32[]{:S(2)}) copy-start(f32[6,32,512]{2,1,0:T(8,128)S(1)} %collective-permute-done.5.next3) | copy-start | bytes 1179652
  60.3 15.7 %all-to-all-start.1 = ((f32[16,48,128]{2,1,0:T(8,128)}), f32[16,48,128]{2,1,0:T(8,128)S(1)}, u32[]{:S(2)}, u32[]{:S(2)}) async-start(f32[16,48,128]{2,1,0:T(8,128)} %bitcast.1), calls=%async_computation.1 | async-start | bytes 786432 | tf_op jit(solution)/shard_map/all_to_all | solution.py:534
  64.1 1.0 %copy-start.15 = (f32[6,32,512]{2,1,0:T(8,128)S(1)}, f32[6,32,512]{2,1,0:T(8,128)}, u32[]{:S(2)}) copy-start(f32[6,32,512]{2,1,0:T(8,128)} %copy-done.14) | copy-start | bytes 1179652
  65.1 11.0 %copy-start.4 = (bf16[512,512]{1,0:T(8,128)(2,1)S(1)}, bf16[512,512]{1,0:T(8,128)(2,1)}, u32[]{:S(2)}) copy-start(bf16[512,512]{1,0:T(8,128)(2,1)} %constant.11.clone.low_any.low) | copy-start | bytes 1572868
  65.1 11.0 %copy-start.5 = (bf16[512,512]{1,0:T(8,128)(2,1)S(1)}, bf16[512,512]{1,0:T(8,128)(2,1)}, u32[]{:S(2)}) copy-start(bf16[512,512]{1,0:T(8,128)(2,1)} %constant.10.clone.high_any.high) | copy-start | bytes 1572868

commit v15 on v14

--- a/solution.py
+++ b/solution.py
@@ -91,20 +91,23 @@
     return other
 
 
-def start_kernel(jitter_any, ids_any, p0, p1, p2, jitter, grain_ids, semaphores):
-    planes = grain_ids.shape[0]
+def start_plane(jitter, grain_ids, out):
+    ids = grain_ids[...]
+    for i in range(GRAINS):
+        base = jnp.where(ids == i, jnp.float32(0.6), jnp.float32(0.0))
+        out[i] = base + jitter[i].astype(F32)
+
+
+def start_kernel(jitter_any, ids_any, p0, p2, jitter, grain_ids, semaphores):
     pairs = []
-    for k in range(planes):
-        pairs.append((jitter_any.at[:, k], jitter.at[:, k]))
-        pairs.append((ids_any.at[k], grain_ids.at[k]))
+    for k in range(2):
+        pairs.append((jitter_any.at[:, 2 * k], jitter.at[:, k]))
+        pairs.append((ids_any.at[2 * k], grain_ids.at[k]))
     copies = fetch(pairs, semaphores)
-    for k, out in enumerate((p0, p1, p2)):
+    for k, out in enumerate((p0, p2)):
         copies[2 * k].wait()
         copies[2 * k + 1].wait()
-        ids = grain_ids[k]
-        for i in range(GRAINS):
-            base = jnp.where(ids == i, jnp.float32(0.6), jnp.float32(0.0))
-            out[i] = base + jitter[i, k].astype(F32)
+        start_plane(jitter.at[:, k], grain_ids.at[k], out)
 
 
 def grain_of(start):
@@ -152,13 +155,20 @@
 
 
 def inner_kernel(
-    chosen_any, classes_any, p0, p1, p2, up2, down2, r0, r2, rates, middle, chosen, classes, semaphores
+    chosen_any, classes_any, jitter_any, ids_any, p0, p2,
+    p1, up2, down2, r0, r2, rates, middle, chosen, classes, jitter, grain_ids, semaphores,
 ):
-    copies = fetch(((chosen_any, chosen), (classes_any, classes)), semaphores)
+    copies = fetch(
+        ((jitter_any.at[:, 1], jitter), (ids_any.at[1], grain_ids), (chosen_any, chosen), (classes_any, classes)),
+        semaphores,
+    )
+    copies[0].wait()
+    copies[1].wait()
+    start_plane(jitter, grain_ids, p1)
     for i in range(GRAINS):
         up2[i] = p1[i]
         down2[i] = p1[i]
-    for copy in copies:
+    for copy in copies[2:]:
         copy.wait()
     for k, i in enumerate(pair_of(chosen)):
         up2[GRAINS + k] = p0[i]
@@ -454,29 +464,34 @@
     six = (GRAINS - 2, depth, width)
     small = [pltpu.SMEM((2,), jnp.int32), pltpu.SMEM((GRAINS, GRAINS), jnp.int32)]
     ten = (GRAINS + 2, depth, width)
-    p0, p1, p2 = call(
+    p0, p2 = call(
         start_kernel,
-        (shape(*plane), shape(*plane), shape(*plane)),
+        (shape(*plane), shape(*plane)),
         [ANY] * 2,
         jitter, grain_ids,
         scratch=[
-            pltpu.VMEM(jitter.shape, jitter.dtype),
-            pltpu.VMEM(grain_ids.shape, jnp.int32),
-            pltpu.SemaphoreType.DMA((2 * planes,)),
+            pltpu.VMEM((GRAINS, 2, depth, width), jitter.dtype),
+            pltpu.VMEM((2, depth, width), jnp.int32),
+            pltpu.SemaphoreType.DMA((4,)),
         ],
         flops=2**21, moved=2**22,
     )
     prev1 = lax.ppermute(p2, "gx", up)
     next1 = lax.ppermute(p0, "gx", down)
-    up2, down2, r0, r2, rates, middle = call(
+    p1, up2, down2, r0, r2, rates, middle = call(
         inner_kernel,
         (
-            shape(*ten), shape(*ten), shape(*six), shape(*six),
+            shape(*plane), shape(*ten), shape(*ten), shape(*six), shape(*six),
             shape(planes, *plane), shape(*plane),
         ),
-        [ANY] * 2 + [VMEM] * 3,
-        chosen, class_table, p0, p1, p2,
-        scratch=[*small, pltpu.SemaphoreType.DMA((2,))],
+        [ANY] * 4 + [VMEM] * 2,
+        chosen, class_table, jitter, grain_ids, p0, p2,
+        scratch=[
+            *small,
+            pltpu.VMEM((GRAINS, depth, width), jitter.dtype),
+            pltpu.VMEM((depth, width), jnp.int32),
+            pltpu.SemaphoreType.DMA((4,)),
+        ],
         flops=2**24, moved=2**22,
     )
     prev2 = lax.ppermute(up2, "gx", up)

time: 77.9 us -> 77.8 us (level)
  transfers between devices with their start and end apart: 7 -> 7, of which waited for: 5 -> 4; matrix products, arithmetic and copies ran while one was open for 0% -> 0% of each run, Pallas kernels for 19% -> 19%
where the time goes in v15:
time: 77.8 us; the launch traced here: 77.5 us
  blocking collectives  28 us (36%)
  Pallas kernels  19.6 us (25%)
  starting transfers between devices  18.9 us (24%)
  waiting for transfers between devices  8.85 us (11%)
  local copies, waits for them, and re-layouts  1.06 us (1%)
  between operations  1.01 us (1%)
    all_to_all x1, blocking collectives, shards(): lax.all_to_all(packed, 'gx', split_axis=0, concat_axis=0, tiled=True)  28 us
    pallas_call x7, Pallas kernels, call(): pl.pallas_call(kernel, out_shape=outs, in_specs=in_specs, out_specs=out_s...  19.6 us
    ppermute x1, starting transfers between devices, shards(): next1 = lax.ppermute(p0, 'gx', down)  5.5 us
    ppermute x1, starting transfers between devices, shards(): prev3 = lax.ppermute(r0, 'gx', up)  5.07 us
    ppermute x1, starting transfers between devices, shards(): next2 = lax.ppermute(down2, 'gx', down)  4.49 us
    ppermute x1, waiting for transfers between devices, shards(): prev1 = lax.ppermute(p2, 'gx', up)  4.47 us
    all_to_all x1, starting transfers between devices, shards(): lax.all_to_all(back, 'gx', split_axis=0, concat_axis=0, tiled=True)  3.73 us
    all_to_all x1, waiting for transfers between devices, shards(): lax.all_to_all(back, 'gx', split_axis=0, concat_axis=0, tiled=True)  3.3 us
  transfers between devices with their start and end apart: 7, of which 4 were waited for; matrix products, arithmetic and copies ran while one was open for 0% of the time, Pallas kernels for 19%

profile of v15, /device:TPU:0, one launch (start us, length us, event | category | flops | bytes accessed | tf_op | source)
XLA Modules:
  0.0 77.5 jit_solution(258800505476273939)
XLA Ops:
  0.6 1.2 %shard_map.104 = (f32[8,32,512]{2,1,0:T(8,128)S(1)}, f32[8,32,512]{2,1,0:T(8,128)S(1)}) custom-call(bf16[8,3,32,512]{3,2,1,0:T(8,128)(2,1)} %jitter_any.3, s32[3,32,512]{2,1,0:T(8,128)} %ids_any.3), custom_call_target="tpu_custom_call" | custom-call | flops 2097152 | bytes 4194304 | tf_op jit(solution)/shard_map/pallas_call | solution.py:430
  1.8 0.0 copy-start.2
  1.8 0.0 copy-start.3
  1.8 5.5 %collective-permute-start.1 = (f32[8,32,512]{2,1,0:T(8,128)S(1)}, f32[8,32,512]{2,1,0:T(8,128)S(1)}, u32[]{:S(2)}, u32[]{:S(2)}) collective-permute-start(f32[8,32,512]{2,1,0:T(8,128)S(1)} %get-tuple-element.51.p0.p0_any), channel_id=1, source_target_pairs={{1,0},{2,1},{3,2},{4,3},{5,4},{6,5},{7,6},{8,7},{9,8},{10,9},{11,1... | collective-permute-start | bytes 1572872 | tf_op jit(solution)/shard_map/ppermute | solution.py:480
  7.3 0.0 collective-permute-start
  7.3 2.3 %shard_map.105 = (f32[8,32,512]{2,1,0:T(8,128)S(1)}, f32[10,32,512]{2,1,0:T(8,128)S(1)}, f32[10,32,512]{2,1,0:T(8,128)S(1)}, f32[6,32,512]{2,1,0:T(8,128)S(1)}, ...) custom-call(s32[2]{0:T(128)} %chosen_any.4, s32[8,8]{1,0:T(8,128)} %classes_any.6, ...), custom_call_target="tpu_custom_call" | custom-call | flops 16777216 | bytes 4194304 | tf_op jit(solution)/shard_map/pallas_call | solution.py:430
  9.7 0.0 copy-start.1
  9.7 0.0 copy-start.8
  9.7 0.1 collective-permute-start.2
  9.8 4.5 %collective-permute-start.3 = (f32[10,32,512]{2,1,0:T(8,128)S(1)}, f32[10,32,512]{2,1,0:T(8,128)S(1)}, u32[]{:S(2)}, u32[]{:S(2)}) collective-permute-start(f32[10,32,512]{2,1,0:T(8,128)S(1)} %get-tuple-element.38), channel_id=1, source_target_pairs={{1,0},{2,1},{3,2},{4,3},{5,4},{6,5},{7,6},{8,7},{9,8},{10,9},{11,1... | collective-permute-start | bytes 1966088 | tf_op jit(solution)/shard_map/ppermute | solution.py:498
  14.3 0.0 collective-permute-done.1.next1.next1_any
  14.3 0.0 copy-start.6
  14.3 4.5 %collective-permute-done.prev1.prev1_any = f32[8,32,512]{2,1,0:T(8,128)S(1)} collective-permute-done((f32[8,32,512]{2,1,0:T(8,128)S(1)}, f32[8,32,512]{2,1,0:T(8,128)S(1)}, u32[]{:S(2)}, u32[]{:S(2)}) %collective-permute-start) | collective-permute-done | bytes 524320 | tf_op jit(solution)/shard_map/ppermute | solution.py:479
  18.7 0.0 copy-start.7
  18.7 5.1 %collective-permute-start.4 = (f32[6,32,512]{2,1,0:T(8,128)S(1)}, f32[6,32,512]{2,1,0:T(8,128)S(1)}, u32[]{:S(2)}, u32[]{:S(2)}) collective-permute-start(f32[6,32,512]{2,1,0:T(8,128)S(1)} %get-tuple-element.42), channel_id=1, source_target_pairs={{0,1},{1,2},{2,3},{3,4},{4,5},{5,6},{6,7},{7,8},{8,9},{9,10},{10,1... | collective-permute-start | bytes 1179656 | tf_op jit(solution)/shard_map/ppermute | solution.py:500
  23.8 0.0 collective-permute-start.5
  23.8 1.7 %shard_map.106.near_out.near_any = f32[40,32,512]{2,1,0:T(8,128)S(1)} custom-call(s32[8,8]{1,0:T(8,128)} %classes_any.6, f32[8,32,512]{2,1,0:T(8,128)S(1)} %get-tuple-element.51.p0.p0_any, f32[8,32,512]{2,1,0:T(8,128)S(1)} %get-tuple-element.41.p1, f32[8,32,512]{2,1,0:T(8,128)S(1)} %get-tuple-element.52.p2.p2_any, ...), custom_call_target="tpu_custom_call" | custom-call | flops 33554432 | bytes 16777216 | tf_op jit(solution)/shard_map/pallas_call | solution.py:430
  25.5 0.0 copy-start
  25.5 0.0 copy-start.11
  25.5 0.0 copy-start.12
  25.5 0.0 copy-start.13
  25.5 0.2 collective-permute-done.2.prev2.prev2_any
  25.8 0.0 copy-start.9
  25.8 0.0 collective-permute-done.3.next2.next2_any
  25.8 0.0 copy-done.2
  25.8 0.0 copy-done.3
  25.8 0.0 copy-done.1
  25.8 0.0 copy-done.8
  25.8 0.0 copy-done.6
  25.8 0.0 copy-done.7
  25.8 0.0 copy-start.10
  25.8 3.3 %shard_map.107 = f32[16,48,128]{2,1,0:T(8,128)S(1)} custom-call(s32[2]{0:T(128)} %chosen_any.4, s32[8,8]{1,0:T(8,128)} %classes_any.6, f32[8,32,512]{2,1,0:T(8,128)S(1)} %get-tuple-element.51.p0.p0_any, f32[8,32,512]{2,1,0:T(8,128)S(1)} %get-tuple-element.52.p2.p2_any, f32[8,32,512]{2,1,0:T(8,128)S(1)} %collective-permute-done.prev1.prev1_any, ...), custom_call_target="tpu_custom_call" | custom-call | flops 268435456 | bytes 8388608 | tf_op jit(solution)/shard_map/pallas_call | solution.py:430
  29.1 0.0 copy-done
  29.1 0.0 copy-done.9
  29.1 0.0 copy-done.10
  29.1 0.9 %collective-permute-done.4.prev3 = f32[6,32,512]{2,1,0:T(8,128)S(1)} collective-permute-done((f32[6,32,512]{2,1,0:T(8,128)S(1)}, f32[6,32,512]{2,1,0:T(8,128)S(1)}, u32[]{:S(2)}, u32[]{:S(2)}) %collective-permute-start.4) | collective-permute-done | bytes 393248 | tf_op jit(solution)/shard_map/ppermute | solution.py:500
  30.0 0.0 collective-permute-done.5.next3
  30.0 0.0 copy-start.14
  30.0 28.0 %all_to_all.10 = f32[16,48,128]{2,1,0:T(8,128)S(1)} all-to-all(f32[16,48,128]{2,1,0:T(8,128)S(1)} %shard_map.107), channel_id=1, replica_groups=mesh['grp'=2,'gx'=16] {'gx'}, dimensions={0} | all-to-all | bytes 786432 | tf_op jit(solution)/shard_map/all_to_all | solution.py:529
  58.0 0.0 copy-done.11
  58.0 0.0 copy-done.12
  58.0 0.0 copy-done.13
  58.0 2.2 %shard_map.108 = f32[768,128]{1,0:T(8,128)} custom-call(f32[768,128]{1,0:T(8,128)S(1)} %bitcast.2, bf16[2,256,128]{2,1,0:T(8,128)(2,1)S(1)} %copy-done.12, bf16[2,256,128]{2,1,0:T(8,128)(2,1)S(1)} %copy-done.11, bf16[96,144]{1,0:T(8,128)(2,1)S(1)} %copy-done.13), custom_call_target="tpu_custom_call" | custom-call | flops 268435456 | bytes 4194304 | tf_op jit(solution)/shard_map/pallas_call | solution.py:430
  60.2 0.0 copy-done.14
  60.2 3.7 %all-to-all-start.1 = ((f32[16,48,128]{2,1,0:T(8,128)}), f32[16,48,128]{2,1,0:T(8,128)S(1)}, u32[]{:S(2)}, u32[]{:S(2)}) async-start(f32[16,48,128]{2,1,0:T(8,128)} %bitcast.1), calls=%async_computation.1 | async-start | bytes 786432 | tf_op jit(solution)/shard_map/all_to_all | solution.py:549
  64.0 0.0 copy-start.15
  64.0 1.0 %copy-done.15 = f32[6,32,512]{2,1,0:T(8,128)S(1)} copy-done((f32[6,32,512]{2,1,0:T(8,128)S(1)}, f32[6,32,512]{2,1,0:T(8,128)}, u32[]{:S(2)}) %copy-start.15) | copy-done | bytes 393240
  65.0 0.0 copy-start.4
  65.0 0.0 copy-start.5
  65.0 7.7 %shard_map.109 = f32[8,3,32,512]{3,2,1,0:T(8,128)} custom-call(f32[6,32,512]{2,1,0:T(8,128)S(1)} %collective-permute-done.4.prev3, f32[6,32,512]{2,1,0:T(8,128)S(1)} %copy-done.15, s32[2]{0:T(128)} %chosen_any.4, s32[8,8]{1,0:T(8,128)} %classes_any.6, f32[8,32,512]{2,1,0:T(8,128)} %copy-done.2, f32[8,32,512]{2,1,0:T(8,128)} %copy-done.3, ...), custom_call_target="tpu_custom_call" | custom-call | flops 137438953472 | bytes 16777216 | tf_op jit(solution)/shard_map/pallas_call | solution.py:430
  72.7 3.3 %all-to-all-done.1.returned = f32[16,48,128]{2,1,0:T(8,128)S(1)} async-done(((f32[16,48,128]{2,1,0:T(8,128)}), f32[16,48,128]{2,1,0:T(8,128)S(1)}, u32[]{:S(2)}, u32[]{:S(2)}) %all-to-all-start.1) | async-done | bytes 393248 | tf_op jit(solution)/shard_map/all_to_all | solution.py:549
  76.0 0.0 copy-done.4
  76.0 0.0 copy-done.5
  76.0 1.3 %shard_map.110 = f32[2,3,32,512]{3,2,1,0:T(8,128)} custom-call(f32[16,48,128]{2,1,0:T(8,128)S(1)} %all-to-all-done.1.returned, bf16[512,512]{1,0:T(8,128)(2,1)S(1)} %copy-done.5, bf16[512,512]{1,0:T(8,128)(2,1)S(1)} %copy-done.4), custom_call_target="tpu_custom_call" | custom-call | flops 268435456 | bytes 4194304 | tf_op jit(solution)/shard_map/pallas_call | solution.py:430
Async XLA Ops:
  1.8 24.0 %copy-start.2 = (f32[8,32,512]{2,1,0:T(8,128)}, f32[8,32,512]{2,1,0:T(8,128)S(1)}, u32[]{:S(2)}) copy-start(f32[8,32,512]{2,1,0:T(8,128)S(1)} %get-tuple-element.51.p0.p0_any) | copy-start | bytes 1572868
  1.8 23.9 %copy-start.3 = (f32[8,32,512]{2,1,0:T(8,128)}, f32[8,32,512]{2,1,0:T(8,128)S(1)}, u32[]{:S(2)}) copy-start(f32[8,32,512]{2,1,0:T(8,128)S(1)} %get-tuple-element.52.p2.p2_any) | copy-start | bytes 1572868
  1.8 12.4 %collective-permute-start.1 = (f32[8,32,512]{2,1,0:T(8,128)S(1)}, f32[8,32,512]{2,1,0:T(8,128)S(1)}, u32[]{:S(2)}, u32[]{:S(2)}) collective-permute-start(f32[8,32,512]{2,1,0:T(8,128)S(1)} %get-tuple-element.51.p0.p0_any), channel_id=1, source_target_pairs={{1,0},{2,1},{3,2},{4,3},{5,4},{6,5},{7,6},{8,7},{9,8},{10,9},{11,1... | collective-permute-start | bytes 1572872 | tf_op jit(solution)/shard_map/ppermute | solution.py:480
  7.3 11.4 %collective-permute-start = (f32[8,32,512]{2,1,0:T(8,128)S(1)}, f32[8,32,512]{2,1,0:T(8,128)S(1)}, u32[]{:S(2)}, u32[]{:S(2)}) collective-permute-start(f32[8,32,512]{2,1,0:T(8,128)S(1)} %get-tuple-element.52.p2.p2_any), channel_id=1, source_target_pairs={{0,1},{1,2},{2,3},{3,4},{4,5},{5,6},{6,7},{7,8},{8,9},{9,10},{10,1... | collective-permute-start | bytes 1572872 | tf_op jit(solution)/shard_map/ppermute | solution.py:479
  9.7 16.1 %copy-start.1 = (f32[3,8,32,512]{3,2,1,0:T(8,128)}, f32[3,8,32,512]{3,2,1,0:T(8,128)S(1)}, u32[]{:S(2)}) copy-start(f32[3,8,32,512]{3,2,1,0:T(8,128)S(1)} %get-tuple-element.59.rates.rates_any) | copy-start | bytes 4718596
  9.7 16.1 %copy-start.8 = (f32[8,32,512]{2,1,0:T(8,128)}, f32[8,32,512]{2,1,0:T(8,128)S(1)}, u32[]{:S(2)}) copy-start(f32[8,32,512]{2,1,0:T(8,128)S(1)} %get-tuple-element.58.middle.middle_any) | copy-start | bytes 1572868
  9.7 16.1 %collective-permute-start.2 = (f32[10,32,512]{2,1,0:T(8,128)S(1)}, f32[10,32,512]{2,1,0:T(8,128)S(1)}, u32[]{:S(2)}, u32[]{:S(2)}) collective-permute-start(f32[10,32,512]{2,1,0:T(8,128)S(1)} %get-tuple-element.37), channel_id=1, source_target_pairs={{0,1},{1,2},{2,3},{3,4},{4,5},{5,6},{6,7},{7,8},{8,9},{9,10},{10,1... | collective-permute-start | bytes 1966088 | tf_op jit(solution)/shard_map/ppermute | solution.py:497
  9.8 16.0 %collective-permute-start.3 = (f32[10,32,512]{2,1,0:T(8,128)S(1)}, f32[10,32,512]{2,1,0:T(8,128)S(1)}, u32[]{:S(2)}, u32[]{:S(2)}) collective-permute-start(f32[10,32,512]{2,1,0:T(8,128)S(1)} %get-tuple-element.38), channel_id=1, source_target_pairs={{1,0},{2,1},{3,2},{4,3},{5,4},{6,5},{7,6},{8,7},{9,8},{10,9},{11,1... | collective-permute-start | bytes 1966088 | tf_op jit(solution)/shard_map/ppermute | solution.py:498
  14.3 11.5 %copy-start.6 = (f32[8,32,512]{2,1,0:T(8,128)}, f32[8,32,512]{2,1,0:T(8,128)S(1)}, u32[]{:S(2)}) copy-start(f32[8,32,512]{2,1,0:T(8,128)S(1)} %collective-permute-done.1.next1.next1_any) | copy-start | bytes 1572868
  18.7 7.1 %copy-start.7 = (f32[8,32,512]{2,1,0:T(8,128)}, f32[8,32,512]{2,1,0:T(8,128)S(1)}, u32[]{:S(2)}) copy-start(f32[8,32,512]{2,1,0:T(8,128)S(1)} %collective-permute-done.prev1.prev1_any) | copy-start | bytes 1572868
  18.7 11.2 %collective-permute-start.4 = (f32[6,32,512]{2,1,0:T(8,128)S(1)}, f32[6,32,512]{2,1,0:T(8,128)S(1)}, u32[]{:S(2)}, u32[]{:S(2)}) collective-permute-start(f32[6,32,512]{2,1,0:T(8,128)S(1)} %get-tuple-element.42), channel_id=1, source_target_pairs={{0,1},{1,2},{2,3},{3,4},{4,5},{5,6},{6,7},{7,8},{8,9},{9,10},{10,1... | collective-permute-start | bytes 1179656 | tf_op jit(solution)/shard_map/ppermute | solution.py:500
  23.8 6.2 %collective-permute-start.5 = (f32[6,32,512]{2,1,0:T(8,128)S(1)}, f32[6,32,512]{2,1,0:T(8,128)S(1)}, u32[]{:S(2)}, u32[]{:S(2)}) collective-permute-start(f32[6,32,512]{2,1,0:T(8,128)S(1)} %get-tuple-element.43), channel_id=1, source_target_pairs={{1,0},{2,1},{3,2},{4,3},{5,4},{6,5},{7,6},{8,7},{9,8},{10,9},{11,1... | collective-permute-start | bytes 1179656 | tf_op jit(solution)/shard_map/ppermute | solution.py:501
  25.5 3.6 %copy-start = (f32[40,32,512]{2,1,0:T(8,128)}, f32[40,32,512]{2,1,0:T(8,128)S(1)}, u32[]{:S(2)}) copy-start(f32[40,32,512]{2,1,0:T(8,128)S(1)} %shard_map.106.near_out.near_any) | copy-start | bytes 7864324
  25.5 32.5 %copy-start.11 = (bf16[2,256,128]{2,1,0:T(8,128)(2,1)S(1)}, bf16[2,256,128]{2,1,0:T(8,128)(2,1)}, u32[]{:S(2)}) copy-start(bf16[2,256,128]{2,1,0:T(8,128)(2,1)} %constant.13.clone.refs_2_) | copy-start | bytes 393220
  25.5 32.5 %copy-start.12 = (bf16[2,256,128]{2,1,0:T(8,128)(2,1)S(1)}, bf16[2,256,128]{2,1,0:T(8,128)(2,1)}, u32[]{:S(2)}) copy-start(bf16[2,256,128]{2,1,0:T(8,128)(2,1)} %constant.12.clone.refs_1_) | copy-start | bytes 393220
  25.5 32.5 %copy-start.13 = (bf16[96,144]{1,0:T(8,128)(2,1)S(1)}, bf16[96,144]{1,0:T(8,128)(2,1)}, u32[]{:S(2)}) copy-start(bf16[96,144]{1,0:T(8,128)(2,1)} %constant.14.clone.refs_3_) | copy-start | bytes 82948
  25.8 3.3 %copy-start.9 = (f32[10,32,512]{2,1,0:T(8,128)}, f32[10,32,512]{2,1,0:T(8,128)S(1)}, u32[]{:S(2)}) copy-start(f32[10,32,512]{2,1,0:T(8,128)S(1)} %collective-permute-done.2.prev2.prev2_any) | copy-start | bytes 1966084
  25.8 3.3 %copy-start.10 = (f32[10,32,512]{2,1,0:T(8,128)}, f32[10,32,512]{2,1,0:T(8,128)S(1)}, u32[]{:S(2)}) copy-start(f32[10,32,512]{2,1,0:T(8,128)S(1)} %collective-permute-done.3.next2.next2_any) | copy-start | bytes 1966084
  30.0 30.3 %copy-start.14 = (f32[6,32,512]{2,1,0:T(8,128)}, f32[6,32,512]{2,1,0:T(8,128)S(1)}, u32[]{:S(2)}) copy-start(f32[6,32,512]{2,1,0:T(8,128)S(1)} %collective-permute-done.5.next3) | copy-start | bytes 1179652
  60.2 15.7 %all-to-all-start.1 = ((f32[16,48,128]{2,1,0:T(8,128)}), f32[16,48,128]{2,1,0:T(8,128)S(1)}, u32[]{:S(2)}, u32[]{:S(2)}) async-start(f32[16,48,128]{2,1,0:T(8,128)} %bitcast.1), calls=%async_computation.1 | async-start | bytes 786432 | tf_op jit(solution)/shard_map/all_to_all | solution.py:549
  64.0 1.0 %copy-start.15 = (f32[6,32,512]{2,1,0:T(8,128)S(1)}, f32[6,32,512]{2,1,0:T(8,128)}, u32[]{:S(2)}) copy-start(f32[6,32,512]{2,1,0:T(8,128)} %copy-done.14) | copy-start | bytes 1179652
  65.0 11.0 %copy-start.4 = (bf16[512,512]{1,0:T(8,128)(2,1)S(1)}, bf16[512,512]{1,0:T(8,128)(2,1)}, u32[]{:S(2)}) copy-start(bf16[512,512]{1,0:T(8,128)(2,1)} %constant.11.clone.low_any.low) | copy-start | bytes 1572868
  65.0 11.0 %copy-start.5 = (bf16[512,512]{1,0:T(8,128)(2,1)S(1)}, bf16[512,512]{1,0:T(8,128)(2,1)}, u32[]{:S(2)}) copy-start(bf16[512,512]{1,0:T(8,128)(2,1)} %constant.10.clone.high_any.high) | copy-start | bytes 1572868

commit v16 on v14

--- a/solution.py
+++ b/solution.py
@@ -323,7 +323,7 @@
     slots = rows // total_x
     half = lanes // 2
 
-    def over_x(pieces, chunk=2):
+    def over_x(pieces, chunk=4):
         results = []
         for j in range(0, slots, chunk):
             group = pieces[j : j + chunk]

time: 77.9 us -> 77.9 us (level)
  no operation moved by 1% of the time
where the time goes in v16:
time: 77.9 us; the launch traced here: 77.6 us
  blocking collectives  28 us (36%)
  Pallas kernels  19.4 us (25%)
  starting transfers between devices  18.9 us (24%)
  waiting for transfers between devices  9.25 us (12%)
  local copies, waits for them, and re-layouts  1.06 us (1%)
  between operations  1.01 us (1%)
    all_to_all x1, blocking collectives, shards(): lax.all_to_all(packed, 'gx', split_axis=0, concat_axis=0, tiled=True)  28 us
    pallas_call x7, Pallas kernels, call(): pl.pallas_call(kernel, out_shape=outs, in_specs=in_specs, out_specs=out_s...  19.4 us
    ppermute x1, starting transfers between devices, shards(): next1 = lax.ppermute(p0, 'gx', down)  5.5 us
    ppermute x1, starting transfers between devices, shards(): prev3 = lax.ppermute(r0, 'gx', up)  5.07 us
    ppermute x1, waiting for transfers between devices, shards(): prev1 = lax.ppermute(p2, 'gx', up)  4.7 us
    ppermute x1, starting transfers between devices, shards(): next2 = lax.ppermute(down2, 'gx', down)  4.49 us
    all_to_all x1, starting transfers between devices, shards(): lax.all_to_all(back, 'gx', split_axis=0, concat_axis=0, tiled=True)  3.73 us
    all_to_all x1, waiting for transfers between devices, shards(): lax.all_to_all(back, 'gx', split_axis=0, concat_axis=0, tiled=True)  3.3 us
  transfers between devices with their start and end apart: 7, of which 5 were waited for; matrix products, arithmetic and copies ran while one was open for 0% of the time, Pallas kernels for 19%

profile of v16, /device:TPU:0, one launch (start us, length us, event | category | flops | bytes accessed | tf_op | source)
XLA Modules:
  0.0 77.6 jit_solution(10623263836300281157)
XLA Ops:
  0.6 1.3 %shard_map.104 = (f32[8,32,512]{2,1,0:T(8,128)S(1)}, f32[8,32,512]{2,1,0:T(8,128)S(1)}, f32[8,32,512]{2,1,0:T(8,128)S(1)}) custom-call(bf16[8,3,32,512]{3,2,1,0:T(8,128)(2,1)} %jitter_any.1, s32[3,32,512]{2,1,0:T(8,128)} %ids_any.1), custom_call_target="tpu_custom_call" | custom-call | flops 2097152 | bytes 4194304 | tf_op jit(solution)/shard_map/pallas_call | solution.py:420
  1.9 0.0 copy-start.2
  1.9 0.0 copy-start.3
  1.9 5.5 %collective-permute-start.1 = (f32[8,32,512]{2,1,0:T(8,128)S(1)}, f32[8,32,512]{2,1,0:T(8,128)S(1)}, u32[]{:S(2)}, u32[]{:S(2)}) collective-permute-start(f32[8,32,512]{2,1,0:T(8,128)S(1)} %get-tuple-element.51.p0.p0_any), channel_id=1, source_target_pairs={{1,0},{2,1},{3,2},{4,3},{5,4},{6,5},{7,6},{8,7},{9,8},{10,9},{11,1... | collective-permute-start | bytes 1572872 | tf_op jit(solution)/shard_map/ppermute | solution.py:470
  7.4 0.0 collective-permute-start
  7.4 2.0 %shard_map.105 = (f32[10,32,512]{2,1,0:T(8,128)S(1)}, f32[10,32,512]{2,1,0:T(8,128)S(1)}, f32[6,32,512]{2,1,0:T(8,128)S(1)}, f32[6,32,512]{2,1,0:T(8,128)S(1)}, ...) custom-call(s32[2]{0:T(128)} %chosen_any.4, s32[8,8]{1,0:T(8,128)} %classes_any.6, ...), custom_call_target="tpu_custom_call" | custom-call | flops 16777216 | bytes 4194304 | tf_op jit(solution)/shard_map/pallas_call | solution.py:420
  9.4 0.0 copy-start.1
  9.4 0.0 copy-start.8
  9.4 0.1 collective-permute-start.2
  9.5 4.5 %collective-permute-start.3 = (f32[10,32,512]{2,1,0:T(8,128)S(1)}, f32[10,32,512]{2,1,0:T(8,128)S(1)}, u32[]{:S(2)}, u32[]{:S(2)}) collective-permute-start(f32[10,32,512]{2,1,0:T(8,128)S(1)} %get-tuple-element.39), channel_id=1, source_target_pairs={{1,0},{2,1},{3,2},{4,3},{5,4},{6,5},{7,6},{8,7},{9,8},{10,9},{11,1... | collective-permute-start | bytes 1966088 | tf_op jit(solution)/shard_map/ppermute | solution.py:483
  14.0 0.2 collective-permute-done.1.next1.next1_any
  14.1 0.0 copy-start.6
  14.1 4.7 %collective-permute-done.prev1.prev1_any = f32[8,32,512]{2,1,0:T(8,128)S(1)} collective-permute-done((f32[8,32,512]{2,1,0:T(8,128)S(1)}, f32[8,32,512]{2,1,0:T(8,128)S(1)}, u32[]{:S(2)}, u32[]{:S(2)}) %collective-permute-start) | collective-permute-done | bytes 524320 | tf_op jit(solution)/shard_map/ppermute | solution.py:469
  18.8 0.0 copy-start.7
  18.8 5.1 %collective-permute-start.4 = (f32[6,32,512]{2,1,0:T(8,128)S(1)}, f32[6,32,512]{2,1,0:T(8,128)S(1)}, u32[]{:S(2)}, u32[]{:S(2)}) collective-permute-start(f32[6,32,512]{2,1,0:T(8,128)S(1)} %get-tuple-element.42), channel_id=1, source_target_pairs={{0,1},{1,2},{2,3},{3,4},{4,5},{5,6},{6,7},{7,8},{8,9},{9,10},{10,1... | collective-permute-start | bytes 1179656 | tf_op jit(solution)/shard_map/ppermute | solution.py:485
  23.9 0.0 collective-permute-start.5
  23.9 1.7 %shard_map.106.near_out.near_any = f32[40,32,512]{2,1,0:T(8,128)S(1)} custom-call(s32[8,8]{1,0:T(8,128)} %classes_any.6, f32[8,32,512]{2,1,0:T(8,128)S(1)} %get-tuple-element.51.p0.p0_any, f32[8,32,512]{2,1,0:T(8,128)S(1)} %get-tuple-element.33.p1, f32[8,32,512]{2,1,0:T(8,128)S(1)} %get-tuple-element.52.p2.p2_any, ...), custom_call_target="tpu_custom_call" | custom-call | flops 33554432 | bytes 16777216 | tf_op jit(solution)/shard_map/pallas_call | solution.py:420
  25.6 0.0 copy-start
  25.6 0.0 copy-start.11
  25.6 0.0 copy-start.12
  25.6 0.0 copy-start.13
  25.6 0.2 collective-permute-done.2.prev2.prev2_any
  25.9 0.0 copy-start.9
  25.9 0.0 collective-permute-done.3.next2.next2_any
  25.9 0.0 copy-done.2
  25.9 0.0 copy-done.3
  25.9 0.0 copy-done.1
  25.9 0.0 copy-done.8
  25.9 0.0 copy-done.6
  25.9 0.0 copy-done.7
  25.9 0.0 copy-start.10
  25.9 3.3 %shard_map.107 = f32[16,48,128]{2,1,0:T(8,128)S(1)} custom-call(s32[2]{0:T(128)} %chosen_any.4, s32[8,8]{1,0:T(8,128)} %classes_any.6, f32[8,32,512]{2,1,0:T(8,128)S(1)} %get-tuple-element.51.p0.p0_any, f32[8,32,512]{2,1,0:T(8,128)S(1)} %get-tuple-element.52.p2.p2_any, f32[8,32,512]{2,1,0:T(8,128)S(1)} %collective-permute-done.prev1.prev1_any, ...), custom_call_target="tpu_custom_call" | custom-call | flops 268435456 | bytes 8388608 | tf_op jit(solution)/shard_map/pallas_call | solution.py:420
  29.2 0.0 copy-done
  29.2 0.0 copy-done.9
  29.2 0.0 copy-done.10
  29.2 0.8 %collective-permute-done.4.prev3 = f32[6,32,512]{2,1,0:T(8,128)S(1)} collective-permute-done((f32[6,32,512]{2,1,0:T(8,128)S(1)}, f32[6,32,512]{2,1,0:T(8,128)S(1)}, u32[]{:S(2)}, u32[]{:S(2)}) %collective-permute-start.4) | collective-permute-done | bytes 393248 | tf_op jit(solution)/shard_map/ppermute | solution.py:485
  30.1 0.0 collective-permute-done.5.next3
  30.1 0.0 copy-start.14
  30.1 28.0 %all_to_all.10 = f32[16,48,128]{2,1,0:T(8,128)S(1)} all-to-all(f32[16,48,128]{2,1,0:T(8,128)S(1)} %shard_map.107), channel_id=1, replica_groups=mesh['grp'=2,'gx'=16] {'gx'}, dimensions={0} | all-to-all | bytes 786432 | tf_op jit(solution)/shard_map/all_to_all | solution.py:514
  58.1 0.0 copy-done.11
  58.1 0.0 copy-done.12
  58.1 0.0 copy-done.13
  58.1 2.2 %shard_map.108 = f32[768,128]{1,0:T(8,128)} custom-call(f32[768,128]{1,0:T(8,128)S(1)} %bitcast.2, bf16[2,256,128]{2,1,0:T(8,128)(2,1)S(1)} %copy-done.12, bf16[2,256,128]{2,1,0:T(8,128)(2,1)S(1)} %copy-done.11, bf16[96,144]{1,0:T(8,128)(2,1)S(1)} %copy-done.13), custom_call_target="tpu_custom_call" | custom-call | flops 268435456 | bytes 4194304 | tf_op jit(solution)/shard_map/pallas_call | solution.py:420
  60.3 0.0 copy-done.14
  60.3 3.7 %all-to-all-start.1 = ((f32[16,48,128]{2,1,0:T(8,128)}), f32[16,48,128]{2,1,0:T(8,128)S(1)}, u32[]{:S(2)}, u32[]{:S(2)}) async-start(f32[16,48,128]{2,1,0:T(8,128)} %bitcast.1), calls=%async_computation.1 | async-start | bytes 786432 | tf_op jit(solution)/shard_map/all_to_all | solution.py:534
  64.1 0.0 copy-start.15
  64.1 1.0 %copy-done.15 = f32[6,32,512]{2,1,0:T(8,128)S(1)} copy-done((f32[6,32,512]{2,1,0:T(8,128)S(1)}, f32[6,32,512]{2,1,0:T(8,128)}, u32[]{:S(2)}) %copy-start.15) | copy-done | bytes 393240
  65.1 0.0 copy-start.4
  65.1 0.0 copy-start.5
  65.1 7.7 %shard_map.109 = f32[8,3,32,512]{3,2,1,0:T(8,128)} custom-call(f32[6,32,512]{2,1,0:T(8,128)S(1)} %collective-permute-done.4.prev3, f32[6,32,512]{2,1,0:T(8,128)S(1)} %copy-done.15, s32[2]{0:T(128)} %chosen_any.4, s32[8,8]{1,0:T(8,128)} %classes_any.6, f32[8,32,512]{2,1,0:T(8,128)} %copy-done.2, f32[8,32,512]{2,1,0:T(8,128)} %copy-done.3, ...), custom_call_target="tpu_custom_call" | custom-call | flops 137438953472 | bytes 16777216 | tf_op jit(solution)/shard_map/pallas_call | solution.py:420
  72.8 3.3 %all-to-all-done.1.returned = f32[16,48,128]{2,1,0:T(8,128)S(1)} async-done(((f32[16,48,128]{2,1,0:T(8,128)}), f32[16,48,128]{2,1,0:T(8,128)S(1)}, u32[]{:S(2)}, u32[]{:S(2)}) %all-to-all-start.1) | async-done | bytes 393248 | tf_op jit(solution)/shard_map/all_to_all | solution.py:534
  76.1 0.0 copy-done.4
  76.1 0.0 copy-done.5
  76.1 1.3 %shard_map.110 = f32[2,3,32,512]{3,2,1,0:T(8,128)} custom-call(f32[16,48,128]{2,1,0:T(8,128)S(1)} %all-to-all-done.1.returned, bf16[512,512]{1,0:T(8,128)(2,1)S(1)} %copy-done.5, bf16[512,512]{1,0:T(8,128)(2,1)S(1)} %copy-done.4), custom_call_target="tpu_custom_call" | custom-call | flops 268435456 | bytes 4194304 | tf_op jit(solution)/shard_map/pallas_call | solution.py:420
Async XLA Ops:
  1.9 24.0 %copy-start.2 = (f32[8,32,512]{2,1,0:T(8,128)}, f32[8,32,512]{2,1,0:T(8,128)S(1)}, u32[]{:S(2)}) copy-start(f32[8,32,512]{2,1,0:T(8,128)S(1)} %get-tuple-element.51.p0.p0_any) | copy-start | bytes 1572868
  1.9 23.9 %copy-start.3 = (f32[8,32,512]{2,1,0:T(8,128)}, f32[8,32,512]{2,1,0:T(8,128)S(1)}, u32[]{:S(2)}) copy-start(f32[8,32,512]{2,1,0:T(8,128)S(1)} %get-tuple-element.52.p2.p2_any) | copy-start | bytes 1572868
  1.9 12.2 %collective-permute-start.1 = (f32[8,32,512]{2,1,0:T(8,128)S(1)}, f32[8,32,512]{2,1,0:T(8,128)S(1)}, u32[]{:S(2)}, u32[]{:S(2)}) collective-permute-start(f32[8,32,512]{2,1,0:T(8,128)S(1)} %get-tuple-element.51.p0.p0_any), channel_id=1, source_target_pairs={{1,0},{2,1},{3,2},{4,3},{5,4},{6,5},{7,6},{8,7},{9,8},{10,9},{11,1... | collective-permute-start | bytes 1572872 | tf_op jit(solution)/shard_map/ppermute | solution.py:470
  7.4 11.4 %collective-permute-start = (f32[8,32,512]{2,1,0:T(8,128)S(1)}, f32[8,32,512]{2,1,0:T(8,128)S(1)}, u32[]{:S(2)}, u32[]{:S(2)}) collective-permute-start(f32[8,32,512]{2,1,0:T(8,128)S(1)} %get-tuple-element.52.p2.p2_any), channel_id=1, source_target_pairs={{0,1},{1,2},{2,3},{3,4},{4,5},{5,6},{6,7},{7,8},{8,9},{9,10},{10,1... | collective-permute-start | bytes 1572872 | tf_op jit(solution)/shard_map/ppermute | solution.py:469
  9.4 16.5 %copy-start.1 = (f32[3,8,32,512]{3,2,1,0:T(8,128)}, f32[3,8,32,512]{3,2,1,0:T(8,128)S(1)}, u32[]{:S(2)}) copy-start(f32[3,8,32,512]{3,2,1,0:T(8,128)S(1)} %get-tuple-element.59.rates.rates_any) | copy-start | bytes 4718596
  9.4 16.5 %copy-start.8 = (f32[8,32,512]{2,1,0:T(8,128)}, f32[8,32,512]{2,1,0:T(8,128)S(1)}, u32[]{:S(2)}) copy-start(f32[8,32,512]{2,1,0:T(8,128)S(1)} %get-tuple-element.58.middle.middle_any) | copy-start | bytes 1572868
  9.4 16.4 %collective-permute-start.2 = (f32[10,32,512]{2,1,0:T(8,128)S(1)}, f32[10,32,512]{2,1,0:T(8,128)S(1)}, u32[]{:S(2)}, u32[]{:S(2)}) collective-permute-start(f32[10,32,512]{2,1,0:T(8,128)S(1)} %get-tuple-element.38), channel_id=1, source_target_pairs={{0,1},{1,2},{2,3},{3,4},{4,5},{5,6},{6,7},{7,8},{8,9},{9,10},{10,1... | collective-permute-start | bytes 1966088 | tf_op jit(solution)/shard_map/ppermute | solution.py:482
  9.5 16.4 %collective-permute-start.3 = (f32[10,32,512]{2,1,0:T(8,128)S(1)}, f32[10,32,512]{2,1,0:T(8,128)S(1)}, u32[]{:S(2)}, u32[]{:S(2)}) collective-permute-start(f32[10,32,512]{2,1,0:T(8,128)S(1)} %get-tuple-element.39), channel_id=1, source_target_pairs={{1,0},{2,1},{3,2},{4,3},{5,4},{6,5},{7,6},{8,7},{9,8},{10,9},{11,1... | collective-permute-start | bytes 1966088 | tf_op jit(solution)/shard_map/ppermute | solution.py:483
  14.1 11.8 %copy-start.6 = (f32[8,32,512]{2,1,0:T(8,128)}, f32[8,32,512]{2,1,0:T(8,128)S(1)}, u32[]{:S(2)}) copy-start(f32[8,32,512]{2,1,0:T(8,128)S(1)} %collective-permute-done.1.next1.next1_any) | copy-start | bytes 1572868
  18.8 7.1 %copy-start.7 = (f32[8,32,512]{2,1,0:T(8,128)}, f32[8,32,512]{2,1,0:T(8,128)S(1)}, u32[]{:S(2)}) copy-start(f32[8,32,512]{2,1,0:T(8,128)S(1)} %collective-permute-done.prev1.prev1_any) | copy-start | bytes 1572868
  18.8 11.2 %collective-permute-start.4 = (f32[6,32,512]{2,1,0:T(8,128)S(1)}, f32[6,32,512]{2,1,0:T(8,128)S(1)}, u32[]{:S(2)}, u32[]{:S(2)}) collective-permute-start(f32[6,32,512]{2,1,0:T(8,128)S(1)} %get-tuple-element.42), channel_id=1, source_target_pairs={{0,1},{1,2},{2,3},{3,4},{4,5},{5,6},{6,7},{7,8},{8,9},{9,10},{10,1... | collective-permute-start | bytes 1179656 | tf_op jit(solution)/shard_map/ppermute | solution.py:485
  23.9 6.2 %collective-permute-start.5 = (f32[6,32,512]{2,1,0:T(8,128)S(1)}, f32[6,32,512]{2,1,0:T(8,128)S(1)}, u32[]{:S(2)}, u32[]{:S(2)}) collective-permute-start(f32[6,32,512]{2,1,0:T(8,128)S(1)} %get-tuple-element.43), channel_id=1, source_target_pairs={{1,0},{2,1},{3,2},{4,3},{5,4},{6,5},{7,6},{8,7},{9,8},{10,9},{11,1... | collective-permute-start | bytes 1179656 | tf_op jit(solution)/shard_map/ppermute | solution.py:486
  25.6 3.6 %copy-start = (f32[40,32,512]{2,1,0:T(8,128)}, f32[40,32,512]{2,1,0:T(8,128)S(1)}, u32[]{:S(2)}) copy-start(f32[40,32,512]{2,1,0:T(8,128)S(1)} %shard_map.106.near_out.near_any) | copy-start | bytes 7864324
  25.6 32.5 %copy-start.11 = (bf16[2,256,128]{2,1,0:T(8,128)(2,1)S(1)}, bf16[2,256,128]{2,1,0:T(8,128)(2,1)}, u32[]{:S(2)}) copy-start(bf16[2,256,128]{2,1,0:T(8,128)(2,1)} %constant.13.clone.refs_2_) | copy-start | bytes 393220
  25.6 32.5 %copy-start.12 = (bf16[2,256,128]{2,1,0:T(8,128)(2,1)S(1)}, bf16[2,256,128]{2,1,0:T(8,128)(2,1)}, u32[]{:S(2)}) copy-start(bf16[2,256,128]{2,1,0:T(8,128)(2,1)} %constant.12.clone.refs_1_) | copy-start | bytes 393220
  25.6 32.5 %copy-start.13 = (bf16[96,144]{1,0:T(8,128)(2,1)S(1)}, bf16[96,144]{1,0:T(8,128)(2,1)}, u32[]{:S(2)}) copy-start(bf16[96,144]{1,0:T(8,128)(2,1)} %constant.14.clone.refs_3_) | copy-start | bytes 82948
  25.9 3.4 %copy-start.9 = (f32[10,32,512]{2,1,0:T(8,128)}, f32[10,32,512]{2,1,0:T(8,128)S(1)}, u32[]{:S(2)}) copy-start(f32[10,32,512]{2,1,0:T(8,128)S(1)} %collective-permute-done.2.prev2.prev2_any) | copy-start | bytes 1966084
  25.9 3.3 %copy-start.10 = (f32[10,32,512]{2,1,0:T(8,128)}, f32[10,32,512]{2,1,0:T(8,128)S(1)}, u32[]{:S(2)}) copy-start(f32[10,32,512]{2,1,0:T(8,128)S(1)} %collective-permute-done.3.next2.next2_any) | copy-start | bytes 1966084
  30.1 30.3 %copy-start.14 = (f32[6,32,512]{2,1,0:T(8,128)}, f32[6,32,512]{2,1,0:T(8,128)S(1)}, u32[]{:S(2)}) copy-start(f32[6,32,512]{2,1,0:T(8,128)S(1)} %collective-permute-done.5.next3) | copy-start | bytes 1179652
  60.3 15.7 %all-to-all-start.1 = ((f32[16,48,128]{2,1,0:T(8,128)}), f32[16,48,128]{2,1,0:T(8,128)S(1)}, u32[]{:S(2)}, u32[]{:S(2)}) async-start(f32[16,48,128]{2,1,0:T(8,128)} %bitcast.1), calls=%async_computation.1 | async-start | bytes 786432 | tf_op jit(solution)/shard_map/all_to_all | solution.py:534
  64.1 1.0 %copy-start.15 = (f32[6,32,512]{2,1,0:T(8,128)S(1)}, f32[6,32,512]{2,1,0:T(8,128)}, u32[]{:S(2)}) copy-start(f32[6,32,512]{2,1,0:T(8,128)} %copy-done.14) | copy-start | bytes 1179652
  65.1 11.0 %copy-start.4 = (bf16[512,512]{1,0:T(8,128)(2,1)S(1)}, bf16[512,512]{1,0:T(8,128)(2,1)}, u32[]{:S(2)}) copy-start(bf16[512,512]{1,0:T(8,128)(2,1)} %constant.11.clone.low_any.low) | copy-start | bytes 1572868
  65.1 11.0 %copy-start.5 = (bf16[512,512]{1,0:T(8,128)(2,1)S(1)}, bf16[512,512]{1,0:T(8,128)(2,1)}, u32[]{:S(2)}) copy-start(bf16[512,512]{1,0:T(8,128)(2,1)} %constant.10.clone.high_any.high) | copy-start | bytes 1572868
